TPU v7x, 32 devices: a whole 2x2x4 slice. The times are simulated.
32 devices in a mesh: dp: 8 (over z, y), tp: 4 (over x, core).
Axes of the slice: x: 2, y: 2, z: 4, core: 2. Of those that a mesh axis runs over, the one named last changes fastest.
Arguments:
- tokens: bfloat16 [128, 256, 512], P('dp'), may hold values from -6 to 6
- frame_counts: int32 [128], P('dp'), may hold values from 128 to 256, as said below
- rate_groups: int32 [128], P('dp'), may hold values from 0 to 1
- conv_weight: bfloat16 [7, 512], replicated, may hold values from -2 to 2
- conv_bias: bfloat16 [512], replicated, may hold values from -3 to 3
- norm_scale: bfloat16 [2, 512], replicated, may hold values from 0.5 to 1.5
- norm_shift: bfloat16 [2, 512], replicated, may hold values from -2 to 2
- weight_in: bfloat16 [512, 1536], P(None, 'tp'), may hold values from -0.25 to 0.25
- bias_in: bfloat16 [1536], P('tp'), may hold values from -2 to 2
- weight_out: bfloat16 [1536, 512], P('tp'), may hold values from -0.21875 to 0.21875
- bias_out: bfloat16 [512], replicated, may hold values from -2 to 2
- layer_scale: bfloat16 [512], replicated, may hold values from 0.5 to 1.5
- cotangent: bfloat16 [128, 256, 512], P('dp'), may hold values from -6 to 6
Outputs:
- block_out: bfloat16 [128, 256, 512], P('dp')
- grad_tokens: float32 [128, 256, 512], P('dp')
- grad_conv_weight: float32 [7, 512], replicated
- grad_conv_bias: float32 [512], replicated
- grad_norm_scale: float32 [2, 512], replicated
- grad_norm_shift: float32 [2, 512], replicated
- grad_weight_in: float32 [512, 1536], P(None, 'tp')
- grad_bias_in: float32 [1536], P('tp')
- grad_weight_out: float32 [1536, 512], P('tp')
- grad_bias_out: float32 [512], replicated
- grad_layer_scale: float32 [512], replicated
Inputs may be any that keep to these rules, and one draw needn't show every extreme that they name: `frame_counts`: an item of group 0 has at most 256 live frames, one of group 1 at most 240; both bounds are reached, and so is the least.
All inputs are finite; a program needn't handle non-finite values.
Results may differ from a plain program's by a relative error of at most 0.0061.
Values may be sent and summed in bfloat16 or wider, within the bound.
No kernel may reach another device: no remote copies, remote signals or barrier semaphores. Data moves between devices by JAX's collectives and lax.ppermute only.
A program may use at most 192 MiB of HBM per device.

v0:
```python
import functools

import jax
import jax.numpy as jnp
from jax import lax
from jax.experimental import pallas as pl
from jax.experimental.pallas import tpu as pltpu
from jax.sharding import PartitionSpec as P

EPS = 1e-06
BF, F32 = jnp.bfloat16, jnp.float32
TILE = 256
LANES = 128
PAD = 8
CHUNK = 64
VMEM_LIMIT = 12 * 1024 * 1024


def params(**more):
    return pltpu.CompilerParams(vmem_limit_bytes=VMEM_LIMIT, **more)


def struct(shape, dtype):
    return jax.ShapeDtypeStruct(shape, dtype)


def whole(shape):
    return pl.BlockSpec(shape, lambda *_: (0,) * len(shape))


def hbm():
    return pl.BlockSpec(memory_space=pltpu.HBM)


def smem():
    return pl.BlockSpec(memory_space=pltpu.SMEM)


def cost(size):
    return pl.CostEstimate(flops=0, transcendentals=0, bytes_accessed=size)


def vmem():
    return pl.BlockSpec(memory_space=pltpu.VMEM)


def lane(q):
    return slice(q * LANES, (q + 1) * LANES)


def fold(x):
    return jnp.sum(x.reshape(x.shape[0] // 8, 8, x.shape[1]), axis=0)


def pick(table, group):
    rows = table[...].astype(F32)
    value = rows[0:1]
    for r in range(1, rows.shape[0]):
        value = jnp.where(group == r, rows[r:r + 1], value)
    return value


def as_row(ref):
    return ref[...].astype(F32).reshape(1, -1)


def gelu_parts(pre):
    cdf = 0.5 + 0.5 * lax.erf(pre * 0.7071067811865476)
    density = jnp.exp(-0.5 * pre * pre) * 0.3989422804014327
    return pre * cdf, cdf + pre * density


def dot(a, b):
    return jnp.dot(a, b, preferred_element_type=F32)


def dot_t(a, b):
    return lax.dot_general(a, b, (((1,), (1,)), ((), ())), preferred_element_type=F32)


def dot_rows(a, b):
    return lax.dot_general(a, b, (((0,), (0,)), ((), ())), preferred_element_type=F32)


def place_items(n, meta, offs):
    end = jnp.int32(0)
    for j in range(n):
        offs[j] = end
        end = end + ((meta[2 + meta[0] * n + j] + 15) & -16)
    offs[n] = end
    offs[n + 1] = (end + TILE - 1) // TILE


def pack_kernel(wi, bi, wo, out):
    width, h = wi.shape
    hq, wq = h // LANES, width // LANES
    for q in range(hq):
        out[q * width:(q + 1) * width, :] = wi[:, lane(q)]
    base = hq * width
    for q in range(wq):
        out[base + q * h:base + (q + 1) * h, :] = wo[:, lane(q)]
    base += wq * h
    bias = bi[...].astype(F32).reshape(1, h)
    rows = [bias[:, lane(q)] for q in range(hq)] + [jnp.zeros((1, LANES), F32)] * (16 - hq)
    out[base:base + 16, :] = jnp.concatenate(rows, axis=0).astype(BF)


def pack(wi, bi, wo):
    rows = 2 * wi.size // LANES + 16
    return pl.pallas_call(pack_kernel, out_shape=struct((rows, LANES), BF),
                          compiler_params=params())(wi, bi, wo)


def weight_copies(buf, side, win, wout, bias, sems):
    width, h = win.shape[0], win.shape[1] // 2
    hq, wq = h // LANES, width // LANES
    copies = []
    for q in range(hq):
        at = side * h + q * LANES
        copies.append((buf.at[pl.ds(q * width, width), :], win.at[:, pl.ds(at, LANES)]))
    base = hq * width
    for q in range(wq):
        copies.append((buf.at[pl.ds(base + q * h, h), :], wout.at[pl.ds(side * h, h), pl.ds(q * LANES, LANES)]))
    copies.append((buf.at[pl.ds(base + wq * h, 16), :], bias.at[side]))
    return [pltpu.make_async_copy(src, dst, sems.at[side, i]) for i, (src, dst) in enumerate(copies)]


def spread_bias(bias, row):
    hq = row.shape[1] // LANES // 2
    for side in range(2):
        for q in range(hq):
            at = side * hq + q
            row[:, lane(at)] = bias[side, q:q + 1, :].astype(F32)


def conv_norm_kernel(n, meta, tok, cot, cw, cb, ns, nsh, gamma, ad, nrm, low, inv, gbo, offs, pad):
    s = pl.program_id(0)
    frames, width = tok.shape[1], tok.shape[2]
    taps = cw.shape[0]
    half = taps // 2
    wq = width // LANES

    @pl.when(s == 0)
    def _():
        place_items(n, meta, offs)
        gbo[...] = jnp.zeros_like(gbo)
        pad[...] = jnp.zeros_like(pad)

    item = meta[0] * n + s
    count = meta[2 + item]
    group = meta[2 + 2 * n + item]
    off = offs[s]
    rows = lax.broadcasted_iota(jnp.int32, (frames, 1), 0)
    for q in range(wq):
        pad[q, PAD:PAD + frames, :] = jnp.where(rows < count, tok[0, :, lane(q)].astype(F32), 0.0)
    scale, shift = pick(ns, group), pick(nsh, group)
    gam, conv_bias = as_row(gamma), as_row(cb)
    w = cw[...].astype(F32)

    def step(i, acc):
        r0 = pl.multiple_of(i * CHUNK, CHUNK)
        live = (lax.broadcasted_iota(jnp.int32, (CHUNK, 1), 0) + r0) < count
        convs = []
        for q in range(wq):
            conv = conv_bias[:, lane(q)]
            for k in range(taps):
                conv = conv + w[k:k + 1, lane(q)] * pad[q, pl.ds(r0 + (PAD - half + k), CHUNK), :]
            convs.append(conv)
        mean = jnp.sum(sum(convs[1:], convs[0]), axis=-1, keepdims=True) * (1.0 / width)
        cents = [c - mean for c in convs]
        sq = [c * c for c in cents]
        var = jnp.sum(sum(sq[1:], sq[0]), axis=-1, keepdims=True) * (1.0 / width)
        istd = lax.rsqrt(var + EPS)
        dst = pl.ds(pl.multiple_of(off + r0, 16), CHUNK)
        inv[dst, :] = jnp.broadcast_to(istd, (CHUNK, LANES))
        new = []
        for q in range(wq):
            normed = cents[q] * istd
            ad[dst, lane(q)] = (normed * scale[:, lane(q)] + shift[:, lane(q)]).astype(BF)
            nrm[dst, lane(q)] = normed.astype(BF)
            back = jnp.where(live, cot[0, pl.ds(r0, CHUNK), lane(q)].astype(F32), 0.0) * gam[:, lane(q)]
            low[dst, lane(q)] = back.astype(BF)
            new.append(acc[q] + fold(back))
        return tuple(new)

    accs = lax.fori_loop(0, pl.cdiv(count, CHUNK), step, (jnp.zeros((8, LANES), F32),) * wq)
    for q in range(wq):
        gbo[:, lane(q)] += accs[q]

    @pl.when(s == n - 1)
    def _():
        end = pl.ds(pl.multiple_of(offs[n], 16), TILE)
        ad[end, :] = jnp.zeros((TILE, width), BF)
        low[end, :] = jnp.zeros((TILE, width), BF)


def conv_norm(meta, tok, cot, cw, cb, ns, nsh, gamma):
    items, frames, width = tok.shape
    n = items // 2
    rows = n * frames + TILE
    item = pl.BlockSpec((1, frames, width), lambda s, c: (c[0] * n + s, 0, 0))
    return pl.pallas_call(
        functools.partial(conv_norm_kernel, n),
        grid_spec=pltpu.PrefetchScalarGridSpec(
            num_scalar_prefetch=1, grid=(n,),
            in_specs=[item, item] + [whole(v.shape) for v in (cw, cb, ns, nsh, gamma)],
            out_specs=[vmem()] * 5,
            scratch_shapes=[pltpu.SMEM((n + 2,), jnp.int32),
                            pltpu.VMEM((width // LANES, frames + 4 * PAD, LANES), F32)]),
        out_shape=[struct((rows, width), BF)] * 3 + [struct((rows, LANES), F32), struct((8, width), F32)],
        compiler_params=params(), cost_estimate=cost(0),
    )(meta, tok, cot, cw, cb, ns, nsh, gamma)


def hidden_kernel(n, meta, ad, low, buf_a, buf_b, act, pre, win, wout, keep, send, gbi,
                  offs, bias, bias_row, dwo, dwi, sems):
    width, h = win.shape[0], win.shape[1] // 2
    wq = width // LANES
    copies = weight_copies(buf_a, 0, win, wout, bias, sems) + weight_copies(buf_b, 1, win, wout, bias, sems)
    for c in copies:
        c.start()
    place_items(n, meta, offs)
    dwo[...] = jnp.zeros_like(dwo)
    dwi[...] = jnp.zeros_like(dwi)
    gbi[...] = jnp.zeros_like(gbi)
    for c in copies:
        c.wait()
    spread_bias(bias, bias_row)

    def tile(t, _):
        at = pl.ds(pl.multiple_of(t * TILE, TILE), TILE)
        a, b = ad[at, :], low[at, :]
        activation, slope = gelu_parts(dot(a, win[...]) + bias_row[...])
        grad = dot_t(b, wout[...]) * slope
        lo = activation.astype(BF)
        act[at, :] = lo
        dwo[...] += dot_rows(lo, b)
        gbi[...] += fold(grad)
        g = grad.astype(BF)
        pre[at, :] = g
        dwi[...] += dot_rows(a, g)
        return 0

    lax.fori_loop(0, offs[n + 1], tile, 0)
    for side, dst in ((0, keep), (1, send)):
        for q in range(wq):
            dst[q * h:(q + 1) * h, :] = dwo[side * h:(side + 1) * h, lane(q)].astype(dst.dtype)
        base = wq * h
        for q in range(h // LANES):
            dst[base + q * width:base + (q + 1) * width, :] = dwi[:, lane(side * (h // LANES) + q)].astype(dst.dtype)


def hidden(meta, ad, low, buf_a, buf_b, h, n):
    rows, width = ad.shape
    packed = 2 * width * h // LANES
    wq, hq = width // LANES, h // LANES
    return pl.pallas_call(
        functools.partial(hidden_kernel, n),
        in_specs=[smem(), vmem(), vmem(), hbm(), hbm()],
        out_specs=[vmem()] * 7,
        scratch_shapes=[pltpu.SMEM((n + 2,), jnp.int32),
                        pltpu.VMEM((2, 16, LANES), BF), pltpu.VMEM((1, 2 * h), F32),
                        pltpu.VMEM((2 * h, width), F32), pltpu.VMEM((width, 2 * h), F32),
                        pltpu.SemaphoreType.DMA((2, hq + wq + 1))],
        out_shape=[struct((rows, 2 * h), BF)] * 2 + [struct((width, 2 * h), BF), struct((2 * h, width), BF)]
        + [struct((packed, LANES), F32), struct((packed, LANES), BF), struct((8, 2 * h), F32)],
        compiler_params=params(), cost_estimate=cost(0),
    )(meta, ad, low, buf_a, buf_b)


def combine_kernel(dp, meta, keep, recv, stay, leave):
    m = keep.shape[0] // dp
    for d in range(dp):
        src = pl.ds(pl.multiple_of((meta[1] ^ d) * m, m), m)
        total = keep[src, :] + recv[src, :].astype(F32)
        dst = leave if d % 2 else stay
        dst[d // 2 * m:(d // 2 + 1) * m, :] = total.astype(dst.dtype)


def combine(meta, keep, recv, dp):
    rows = keep.shape[0] // 2
    return pl.pallas_call(
        functools.partial(combine_kernel, dp),
        in_specs=[smem(), vmem(), vmem()], out_specs=[vmem(), vmem()],
        out_shape=[struct((rows, LANES), F32), struct((rows, LANES), BF)],
        compiler_params=params())(meta, keep, recv)


def mix_kernel(n, meta, ad, low, act, pre, win1, wout1, bout, buf_c, buf_d, branch, ag,
               offs, win2, wout2, bias, bias_row, sems):
    copies = weight_copies(buf_c, 0, win2, wout2, bias, sems) + weight_copies(buf_d, 1, win2, wout2, bias, sems)
    for c in copies:
        c.start()
    place_items(n, meta, offs)
    for c in copies:
        c.wait()
    spread_bias(bias, bias_row)

    def tile(t, _):
        at = pl.ds(pl.multiple_of(t * TILE, TILE), TILE)
        a, b = ad[at, :], low[at, :]
        activation, slope = gelu_parts(dot(a, win2[...]) + bias_row[...])
        grad = dot_t(b, wout2[...]) * slope
        branch[at, :] = (dot(act[at, :], wout1[...]) + dot(activation.astype(BF), wout2[...])) + as_row(bout)
        ag[at, :] = dot_t(pre[at, :], win1[...]) + dot_t(grad.astype(BF), win2[...])
        return 0

    lax.fori_loop(0, offs[n + 1], tile, 0)


def mix(meta, ad, low, act, pre, win, wout, bout, buf_c, buf_d, n):
    rows, width = ad.shape
    h = act.shape[1] // 2
    wq, hq = width // LANES, h // LANES
    return pl.pallas_call(
        functools.partial(mix_kernel, n),
        in_specs=[smem()] + [vmem()] * 6 + [whole(bout.shape)] + [hbm()] * 2,
        out_specs=[vmem(), vmem()],
        scratch_shapes=[pltpu.SMEM((n + 2,), jnp.int32),
                        pltpu.VMEM((width, 2 * h), BF), pltpu.VMEM((2 * h, width), BF),
                        pltpu.VMEM((2, 16, LANES), BF), pltpu.VMEM((1, 2 * h), F32),
                        pltpu.SemaphoreType.DMA((2, hq + wq + 1))],
        out_shape=[struct((rows, width), F32)] * 2,
        compiler_params=params(), cost_estimate=cost(0),
    )(meta, ad, low, act, pre, win, wout, bout, buf_c, buf_d)


def finish_kernel(n, first, last_part, meta, tok, cot, branch, ag, nrm, inv, sums_in, gbo, gbi, cw, ns,
                  gamma, both, *rest):
    results, (offs, cgp, sums) = rest[:-3], rest[-3:]
    s = pl.program_id(0) + first
    frames, width = tok.shape[1], tok.shape[2]
    taps, rates = cw.shape[0], ns.shape[0]
    half = taps // 2
    wq = width // LANES
    h = gbi.shape[1] // 2

    @pl.when(s == first)
    def _():
        place_items(n, meta, offs)
        sums[...] = sums_in[...] if last_part else jnp.zeros_like(sums)
        cgp[...] = jnp.zeros_like(cgp)

    item = meta[0] * n + s
    count = meta[2 + item]
    group = meta[2 + 2 * n + item]
    off = offs[s]
    scale = pick(ns, group)
    gam = as_row(gamma)
    w = cw[...].astype(F32)
    zero = jnp.zeros((8, LANES), F32)
    steps = pl.cdiv(count, CHUNK)

    def step(i, accs):
        r0 = pl.multiple_of(i * CHUNK, CHUNK)
        here = pl.ds(r0, CHUNK)
        live = (lax.broadcasted_iota(jnp.int32, (CHUNK, 1), 0) + r0) < count
        src = pl.ds(pl.multiple_of(off + r0, 16), CHUNK)
        new = []
        ngs, nrs = [], []
        for q in range(wq):
            a_ls, a_sc, a_sh = accs[3 * q:3 * q + 3]
            br = jnp.where(live, branch[src, lane(q)], 0.0)
            tk = jnp.where(live, tok[0, here, lane(q)].astype(F32), 0.0)
            both[0, 0, here, lane(q)] = (tk + gam[:, lane(q)] * br).astype(BF)
            g = jnp.where(live, ag[src, lane(q)], 0.0)
            nr = nrm[src, lane(q)].astype(F32)
            new += [a_ls + fold(cot[0, here, lane(q)].astype(F32) * br), a_sc + fold(g * nr), a_sh + fold(g)]
            ngs.append(g * scale[:, lane(q)])
            nrs.append(nr)
        cross = [a * b for a, b in zip(ngs, nrs)]
        m1 = jnp.sum(sum(ngs[1:], ngs[0]), axis=-1, keepdims=True) * (1.0 / width)
        m2 = jnp.sum(sum(cross[1:], cross[0]), axis=-1, keepdims=True) * (1.0 / width)
        istd = inv[src, :]
        for q in range(wq):
            cg = istd * (ngs[q] - m1 - nrs[q] * m2)
            cgp[q, pl.ds(pl.multiple_of(r0 + PAD, 8), CHUNK), :] = jnp.where(live, cg, 0.0)
        return tuple(new)

    accs = lax.fori_loop(0, steps, step, (zero,) * (3 * wq))
    for q in range(wq):
        sums[taps + 1, :, lane(q)] += accs[3 * q]
        sums[taps + 2 + group, :, lane(q)] += accs[3 * q + 1]
        sums[taps + 2 + rates + group, :, lane(q)] += accs[3 * q + 2]

    def clear(i, _):
        r0 = pl.multiple_of(i * CHUNK, CHUNK)
        here = pl.ds(r0, CHUNK)
        both[0, 0, here, :] = jnp.zeros((CHUNK, width), BF)
        both[1, 0, here, :] = jnp.zeros((CHUNK, width), BF)
        for q in range(wq):
            cgp[q, pl.ds(pl.multiple_of(r0 + PAD, 8), CHUNK), :] = jnp.zeros((CHUNK, LANES), F32)
        return 0

    lax.fori_loop(steps, frames // CHUNK, clear, 0)

    for q in range(wq):
        wl = w[:, lane(q)]

        def conv_step(i, accs):
            r0 = pl.multiple_of(i * CHUNK, CHUNK)
            here = pl.ds(r0, CHUNK)
            live = (lax.broadcasted_iota(jnp.int32, (CHUNK, 1), 0) + r0) < count
            tk = jnp.where(live, tok[0, here, lane(q)].astype(F32), 0.0)
            total = cot[0, here, lane(q)].astype(F32)
            new = []
            for k in range(taps):
                sh = cgp[q, pl.ds(r0 + (PAD + half - k), CHUNK), :]
                total = total + wl[k:k + 1] * sh
                new.append(accs[k] + fold(tk * sh))
                if k == half:
                    new_bias = accs[taps] + fold(sh)
            both[1, 0, here, lane(q)] = jnp.where(live, total, 0.0).astype(BF)
            return tuple(new) + (new_bias,)

        accs = lax.fori_loop(0, steps, conv_step, (zero,) * (taps + 1))
        for k in range(taps + 1):
            sums[k, :, lane(q)] += accs[k]

    @pl.when(pl.program_id(0) == pl.num_programs(0) - 1)
    def _():
        if not last_part:
            results[0][...] = sums[...]
            return
        small_keep, small_send = results
        last = taps + 2 + 2 * rates
        rows = [jnp.sum(sums[i], axis=0, keepdims=True) for i in range(last)]
        rows.append(jnp.sum(gbo[...], axis=0, keepdims=True))
        gb = jnp.sum(gbi[...], axis=0, keepdims=True)
        fill = jnp.zeros((1, width - h), F32)
        spare = [jnp.zeros((1, width), F32)] * (small_keep.shape[0] - last - 2)
        for side, dst in ((0, small_keep), (1, small_send)):
            tail = [jnp.concatenate([gb[:, side * h:(side + 1) * h], fill], axis=1)]
            dst[...] = jnp.concatenate(rows + tail + spare, axis=0)


def finish(meta, tok, cot, branch, ag, nrm, inv, sums, gbo, gbi, cw, ns, gamma, first, size):
    items, frames, width = tok.shape
    n = items // 2
    last_part = first + size == n
    wq = width // LANES
    taps, rates = cw.shape[0], ns.shape[0]
    n_small = -(-(taps + 4 + 2 * rates) // 8) * 8
    sums_shape = (taps + 2 + 2 * rates, 8, width)
    item = pl.BlockSpec((1, frames, width), lambda s, c: (c[0] * n + first + s, 0, 0))
    mine = pl.BlockSpec((2, 1, frames, width), lambda s, *_: (0, s, 0, 0))
    more = [(n_small, width)] * 2 if last_part else [sums_shape]
    if sums is None:
        sums = gbo
    return pl.pallas_call(
        functools.partial(finish_kernel, n, first, last_part),
        grid_spec=pltpu.PrefetchScalarGridSpec(
            num_scalar_prefetch=1, grid=(size,),
            in_specs=[item, item] + [vmem()] * 7 + [whole(v.shape) for v in (cw, ns, gamma)],
            out_specs=[mine] + [vmem()] * len(more),
            scratch_shapes=[pltpu.SMEM((n + 2,), jnp.int32),
                            pltpu.VMEM((wq, frames + 4 * PAD, LANES), F32),
                            pltpu.VMEM(sums_shape, F32)]),
        out_shape=[struct((2, size, frames, width), BF)] + [struct(v, F32) for v in more],
        compiler_params=params(), cost_estimate=cost(40000000),
    )(meta, tok, cot, branch, ag, nrm, inv, sums, gbo, gbi, cw, ns, gamma)


def merge_kernel(meta, mine, other, *rest):
    out, gtok = rest[-2:]
    for side, src in ((0, mine), (1, other)):
        @pl.when(pl.program_id(0) == side)
        def _():
            out[...] = src[0]
            gtok[...] = src[1].astype(F32)


def merge(meta, mine, other, into, n, first, step=2):
    _, size, frames, width = mine.shape
    blocks = size // step
    spec_a = pl.BlockSpec((2, step, frames, width), lambda side, s, c: (0, s * (1 - side) + (blocks - 1) * side, 0, 0))
    spec_b = pl.BlockSpec((2, step, frames, width), lambda side, s, c: (0, s * side, 0, 0))
    dst = pl.BlockSpec((step, frames, width), lambda side, s, c: (((c[0] ^ side) * n + first) // step + s, 0, 0))
    return pl.pallas_call(
        merge_kernel,
        grid_spec=pltpu.PrefetchScalarGridSpec(
            num_scalar_prefetch=1, grid=(2, blocks),
            in_specs=[spec_a, spec_b] + [pl.BlockSpec(memory_space=pl.ANY)] * len(into), out_specs=[dst, dst]),
        out_shape=[struct((2 * n, frames, width), BF), struct((2 * n, frames, width), F32)],
        input_output_aliases={3: 0, 4: 1} if into else {},
        compiler_params=params(), cost_estimate=cost(20000000),
    )(meta, mine, other, *into)


def shard_kernel(stay, *refs):
    pieces, out = refs[:-1], refs[-1]
    total = stay[:out.shape[0], :]
    for piece in pieces:
        total = total + piece[...].astype(F32)
    out[...] = total.astype(BF)


def make_shard(stay, pieces):
    return pl.pallas_call(shard_kernel, in_specs=[vmem()] * (1 + len(pieces)), out_specs=vmem(),
                          out_shape=struct(pieces[0].shape, BF), compiler_params=params())(stay, *pieces)


def relay_kernel(*refs):
    sources, out = refs[:-1], refs[-1]
    m = sources[0].shape[0]
    for d, src in enumerate(sources):
        out[d * m:(d + 1) * m, :] = src[...]


def relay(sources):
    m = sources[0].shape[0]
    return pl.pallas_call(relay_kernel, in_specs=[vmem()] * len(sources), out_specs=vmem(),
                          out_shape=struct((len(sources) * m, LANES), BF), compiler_params=params())(*sources)


def unpack_kernel(dp, taps, rates, meta, near, far, small, gcw, gcb, gns, gnsh, gwi, gbi, gwo, gbo, gls, full):
    h, width = gwo.shape
    wq, hq = width // LANES, h // LANES
    m = full.shape[0] // dp
    for odd, mess in ((0, near), (1, far)):
        for d in range(dp // 2):
            at = pl.multiple_of((meta[1] ^ (2 * d + odd)) * m, m)
            full[pl.ds(at, m), :] = mess[d * m:(d + 1) * m, :].astype(F32)
    for q in range(wq):
        gwo[:, lane(q)] = full[q * h:(q + 1) * h, :]
    base = wq * h
    for q in range(hq):
        gwi[:, lane(q)] = full[base + q * width:base + (q + 1) * width, :]
    gcw[...] = small[:taps]
    gcb[...] = small[taps]
    gls[...] = small[taps + 1]
    gns[...] = small[taps + 2:taps + 2 + rates]
    gnsh[...] = small[taps + 2 + rates:taps + 2 + 2 * rates]
    at = taps + 2 + 2 * rates
    gbo[...] = small[at]
    gbi[...] = small[at + 1, :h]


def unpack(meta, near, far, small, dp, taps, rates, width, h):
    shapes = [(taps, width), (width,), (rates, width), (rates, width), (width, h), (h,), (h, width), (width,), (width,)]
    return pl.pallas_call(
        functools.partial(unpack_kernel, dp, taps, rates), in_specs=[smem(), vmem(), vmem(), vmem()],
        out_shape=[struct(s, F32) for s in shapes],
        scratch_shapes=[pltpu.VMEM((2 * width * h // LANES, LANES), F32)],
        compiler_params=params())(meta, near, far, small)


def swap(x, step):
    size = lax.axis_size("tp")
    return lax.ppermute(x, "tp", [(i, i ^ step) for i in range(size)])


def across(x, step):
    size = lax.axis_size("dp")
    return lax.ppermute(x, "dp", [(i, i ^ step) for i in range(size)])


def per_device(tokens, frame_counts, rate_groups, conv_weight, conv_bias, norm_scale, norm_shift,
               weight_in, bias_in, weight_out, bias_out, layer_scale, cotangent):
    width, h = weight_in.shape
    n = tokens.shape[0] // 2
    (tokens, cotangent, conv_weight, conv_bias, norm_scale, norm_shift, weight_in, bias_in, weight_out, bias_out,
     layer_scale) = [pltpu.with_memory_space_constraint(v, pltpu.HBM) for v in (
         tokens, cotangent, conv_weight, conv_bias, norm_scale, norm_shift, weight_in, bias_in, weight_out, bias_out,
         layer_scale)]
    taps, rates = conv_weight.shape[0], norm_scale.shape[0]
    dp = lax.axis_size("dp")
    place = jnp.stack([lax.axis_index("tp") & 1, lax.axis_index("dp")]).astype(jnp.int32)
    meta = jnp.concatenate([place, frame_counts, rate_groups])

    buf_a = pack(weight_in, bias_in, weight_out)
    buf_b = swap(buf_a, 1)
    buf_c = swap(buf_a, 2)
    buf_d = swap(buf_c, 1)
    ad, nrm, low, inv, gbo = conv_norm(meta, tokens, cotangent, conv_weight, conv_bias,
                                       norm_scale, norm_shift, layer_scale)
    act, pre, win, wout, keep, send, gbi = hidden(meta, ad, low, buf_a, buf_b, h, n)
    stay, leave = combine(meta, keep, swap(send, 1), dp)
    arrived = across(leave, 1)
    branch, ag = mix(meta, ad, low, act, pre, win, wout, bias_out, buf_c, buf_d, n)
    arrived, branch = lax.optimization_barrier((arrived, branch))
    stay = (stay + arrived.astype(F32)).reshape(dp // 2, -1, LANES)
    pieces = [across(stay[d].astype(BF), 2 * d) for d in range(1, dp // 2)]

    def finish_part(sums, branch, first):
        return finish(meta, tokens, cotangent, branch, ag, nrm, inv, sums,
                      gbo, gbi, conv_weight, norm_scale, layer_scale, first, n // 2)

    both_1, sums = finish_part(None, branch, 0)
    pieces, sums, branch = lax.optimization_barrier((pieces, sums, branch))
    both_2, small_keep, small_send = finish_part(sums, branch, n // 2)
    shard = make_shard(stay.reshape(-1, LANES), pieces)
    near = [shard] + [across(shard, 2 * d) for d in range(1, dp // 2)]
    near, small_send, both_1, both_2 = lax.optimization_barrier((near, small_send, both_1, both_2))
    small_got = swap(small_send, 1)
    small_got, both_1, both_2 = lax.optimization_barrier((small_got, both_1, both_2))
    near = relay(near)
    far = across(near, 1)
    small = small_keep + small_got
    for i in range(dp.bit_length() - 1):
        small = small + across(small, 1 << i)
    done = merge(meta, both_1, swap(both_1, 1), (), n, 0)
    out, gtok = merge(meta, both_2, swap(both_2, 1), done, n, n // 2)
    far, out, gtok = lax.optimization_barrier((far, out, gtok))
    gcw, gcb, gns, gnsh, gwi, gbi, gwo, gbo, gls = unpack(meta, near, far, small, dp, taps, rates, width, h)
    return (out, gtok, gcw, gcb, gns, gnsh, gwi, gbi, gwo, gbo, gls)


def solution(mesh):
    items, copied = P("dp", None, None), P()
    in_specs = (items, P("dp"), P("dp"), copied, copied, copied, copied, P(None, "tp"), P("tp"), P("tp", None),
                copied, copied, items)
    out_specs = (items, items, copied, copied, copied, copied, P(None, "tp"), P("tp"), P("tp", None), copied, copied)
    return jax.shard_map(per_device, mesh=mesh, in_specs=in_specs, out_specs=out_specs, check_vma=False)
```

profile of v0, /device:TPU:0, one launch (start us, length us, event | category | flops | bytes accessed | tf_op | source)
XLA Modules:
  0.0 97.0 jit_solution(827415714465868384)
XLA Ops:
  0.6 1.3 %shard_map.213.buf_a = bf16[3088,128]{1,0:T(8,128)(2,1)S(1)} custom-call(bf16[512,384]{1,0:T(8,128)(2,1)} %wi.1, bf16[384]{0:T(512)(128)(2,1)} %bi.1, bf16[384,512]{1,0:T(8,128)(2,1)} %wo.1), custom_call_target="tpu_custom_call" | custom-call | tf_op jit(solution)/shard_map/pallas_call | solution.py:110
  1.9 0.5 collective-permute-start
  2.4 2.6 %collective-permute-start.3 = (bf16[3088,128]{1,0:T(8,128)(2,1)S(1)}, bf16[3088,128]{1,0:T(8,128)(2,1)S(1)}, u32[]{:S(2)}, u32[]{:S(2)}) collective-permute-start(bf16[3088,128]{1,0:T(8,128)(2,1)S(1)} %shard_map.213.buf_a), channel_id=1, source_target_pairs={{0,2},{1,3},{2,0},{3,1},{4,6},{5,7},{6,4},{7,5},{8,10},{9,11},{10,... | collective-permute-start | bytes 2371592 | tf_op jit(solution)/shard_map/ppermute | solution.py:550
  5.0 0.7 pad_add_fusion.meta
  5.8 9.7 %shard_map.212 = (bf16[2304,512]{1,0:T(8,128)(2,1)S(1)}, bf16[2304,512]{1,0:T(8,128)(2,1)S(1)}, bf16[2304,512]{1,0:T(8,128)(2,1)S(1)}, f32[2304,128]{1,0:T(8,128)S(1)}, f32[8,512]{1,0:T(8,128)S(1)}) custom-call(s32[34]{0:T(128)S(1)} %pad_add_fusion.meta, bf16[16,256,512]{2,1,0:T(8,128)(2,1)} %tok.5, bf16[16,256,512]{2,1,0:T(8,128)(2,1)} %cot.5, ...), custom_call_target="tpu_custom_call" | custom-call | tf_op jit(solution)/shard_map/pallas_call | solution.py:202
  15.4 0.0 collective-permute-done.buf_b
  15.4 8.8 %shard_map.214 = (bf16[2304,768]{1,0:T(8,128)(2,1)S(1)}, bf16[2304,768]{1,0:T(8,128)(2,1)S(1)}, bf16[512,768]{1,0:T(8,128)(2,1)S(1)}, bf16[768,512]{1,0:T(8,128)...) custom-call(s32[34]{0:T(128)S(1)} %pad_add_fusion.meta, ...), custom_call_target="tpu_custom_call" | custom-call | tf_op jit(solution)/shard_map/pallas_call | solution.py:257
  24.2 0.6 collective-permute-start.1
  24.9 0.0 collective-permute-done.3.buf_c
  24.9 0.1 collective-permute-start.4
  24.9 1.8 %collective-permute-done.1.recv = bf16[3072,128]{1,0:T(8,128)(2,1)S(1)} collective-permute-done((bf16[3072,128]{1,0:T(8,128)(2,1)S(1)}, bf16[3072,128]{1,0:T(8,128)(2,1)S(1)}, u32[]{:S(2)}, u32[]{:S(2)}) %collective-permute-start.1) | collective-permute-done | bytes 786464 | tf_op jit(solution)/shard_map/ppermute | solution.py:550
  26.8 0.7 shard_map.215
  27.4 1.8 %collective-permute-start.2 = (bf16[1536,128]{1,0:T(8,128)(2,1)S(1)}, bf16[1536,128]{1,0:T(8,128)(2,1)S(1)}, u32[]{:S(2)}, u32[]{:S(2)}) collective-permute-start(bf16[1536,128]{1,0:T(8,128)(2,1)S(1)} %get-tuple-element.70), channel_id=1, source_target_pairs={{0,4},{4,0},{8,12},{12,8},{16,20},{20,16},{24,28},{28,24},{1,5},{5... | collective-permute-start | bytes 1179656 | tf_op jit(solution)/shard_map/ppermute | solution.py:555
  29.3 0.0 collective-permute-done.4.buf_d
  29.3 11.7 %shard_map.216 = (f32[2304,512]{1,0:T(8,128)S(1)}, f32[2304,512]{1,0:T(8,128)S(1)}) custom-call(s32[34]{0:T(128)S(1)} %pad_add_fusion.meta, bf16[2304,512]{1,0:T(8,128)(2,1)S(1)} %get-tuple-element.65.ad, bf16[2304,512]{1,0:T(8,128)(2,1)S(1)} %get-tuple-element.66.low, bf16[2304,768]{1,0:T(8,128)(2,1)S(1)} %get-tuple-element.71.act, ...), custom_call_target="tpu_custom_call" | custom-call | tf_op jit(solution)/shard_map/pallas_call | solution.py:315
  41.0 0.0 collective-permute-done.2
  41.0 0.1 fusion
  41.2 2.5 %collective-permute-start.7 = (bf16[384,128]{1,0:T(8,128)(2,1)S(1)}, bf16[384,128]{1,0:T(8,128)(2,1)S(1)}, u32[]{:S(2)}, u32[]{:S(2)}) collective-permute-start(bf16[384,128]{1,0:T(8,128)(2,1)S(1)} %get-tuple-element.121), channel_id=1, source_target_pairs={{0,24},{4,28},{8,16},{12,20},{16,8},{20,12},{24,0},{28,4},{1,25},{... | collective-permute-start | bytes 294920 | tf_op jit(solution)/shard_map/ppermute | solution.py:555
  43.7 0.8 collective-permute-start.6
  44.5 1.1 %collective-permute-start.5 = (bf16[384,128]{1,0:T(8,128)(2,1)S(1)}, bf16[384,128]{1,0:T(8,128)(2,1)S(1)}, u32[]{:S(2)}, u32[]{:S(2)}) collective-permute-start(bf16[384,128]{1,0:T(8,128)(2,1)S(1)} %get-tuple-element.123), channel_id=1, source_target_pairs={{0,8},{4,12},{8,0},{12,4},{16,24},{20,28},{24,16},{28,20},{1,9},{5... | collective-permute-start | bytes 294920 | tf_op jit(solution)/shard_map/ppermute | solution.py:555
  45.6 6.8 %shard_map.217 = (bf16[2,4,256,512]{3,2,1,0:T(8,128)(2,1)S(1)}, f32[13,8,512]{2,1,0:T(8,128)S(1)}) custom-call(s32[34]{0:T(128)S(1)} %pad_add_fusion.meta, bf16[16,256,512]{2,1,0:T(8,128)(2,1)} %tok.5, bf16[16,256,512]{2,1,0:T(8,128)(2,1)} %cot.5, f32[2304,512]{1,0:T(8,128)S(1)} %get-tuple-element.87.branch, f32[2304,512]{1,0:T(8,128)S(1)} %get-tuple-element.78.ag, ...), custom_call_target="tpu_custom_call" | custom-call | bytes 40000000 | tf_op jit(solution)/shard_map/pallas_call | solution.py:450
  52.5 0.0 collective-permute-done.7.refs_2_
  52.5 0.7 collective-permute-done.6.refs_1_
  53.1 0.0 collective-permute-done.5.refs_0_
  53.1 0.1 shard_map.218.refs_0_
  53.2 2.2 %collective-permute-start.10 = (bf16[384,128]{1,0:T(8,128)(2,1)S(1)}, bf16[384,128]{1,0:T(8,128)(2,1)S(1)}, u32[]{:S(2)}, u32[]{:S(2)}) collective-permute-start(bf16[384,128]{1,0:T(8,128)(2,1)S(1)} %shard_map.218.refs_0_), channel_id=1, source_target_pairs={{0,24},{4,28},{8,16},{12,20},{16,8},{20,12},{24,0},{28,4},{1,25},{... | collective-permute-start | bytes 294920 | tf_op jit(solution)/shard_map/ppermute | solution.py:555
  55.4 0.0 collective-permute-start.9
  55.4 2.2 %collective-permute-start.8 = (bf16[384,128]{1,0:T(8,128)(2,1)S(1)}, bf16[384,128]{1,0:T(8,128)(2,1)S(1)}, u32[]{:S(2)}, u32[]{:S(2)}) collective-permute-start(bf16[384,128]{1,0:T(8,128)(2,1)S(1)} %shard_map.218.refs_0_), channel_id=1, source_target_pairs={{0,8},{4,12},{8,0},{12,4},{16,24},{20,28},{24,16},{28,20},{1,9},{5... | collective-permute-start | bytes 294920 | tf_op jit(solution)/shard_map/ppermute | solution.py:555
  57.6 6.9 %shard_map.219 = (bf16[2,4,256,512]{3,2,1,0:T(8,128)(2,1)S(1)}, f32[16,512]{1,0:T(8,128)S(1)}, f32[16,512]{1,0:T(8,128)S(1)}) custom-call(s32[34]{0:T(128)S(1)} %pad_add_fusion.meta, bf16[16,256,512]{2,1,0:T(8,128)(2,1)} %tok.5, bf16[16,256,512]{2,1,0:T(8,128)(2,1)} %cot.5, f32[2304,512]{1,0:T(8,128)S(1)} %get-tuple-element.87.branch, ...), custom_call_target="tpu_custom_call" | custom-call | bytes 40000000 | tf_op jit(solution)/shard_map/pallas_call | solution.py:450
  64.5 0.0 collective-permute-done.10.refs_3_
  64.5 0.0 collective-permute-done.9.refs_2_
  64.5 0.0 collective-permute-done.8.refs_1_
  64.6 0.1 collective-permute-start.12
  64.6 1.2 %collective-permute-done.12 = f32[16,512]{1,0:T(8,128)S(1)} collective-permute-done((f32[16,512]{1,0:T(8,128)S(1)}, f32[16,512]{1,0:T(8,128)S(1)}, u32[]{:S(2)}, u32[]{:S(2)}) %collective-permute-start.12) | collective-permute-done | bytes 32800 | tf_op jit(solution)/shard_map/ppermute | solution.py:550
  65.8 0.2 collective-permute-start.14
  66.0 0.3 collective-permute-start.13
  66.4 1.4 %collective-permute-start.11 = (bf16[1536,128]{1,0:T(8,128)(2,1)S(1)}, bf16[1536,128]{1,0:T(8,128)(2,1)S(1)}, u32[]{:S(2)}, u32[]{:S(2)}) collective-permute-start(bf16[1536,128]{1,0:T(8,128)(2,1)S(1)} %shard_map.220.near), channel_id=1, source_target_pairs={{0,4},{4,0},{8,12},{12,8},{16,20},{20,16},{24,28},{28,24},{1,5},{5... | collective-permute-start | bytes 1179656 | tf_op jit(solution)/shard_map/ppermute | solution.py:555
  67.7 0.7 collective-permute-start.15
  68.5 9.9 %collective-permute-done.15 = f32[16,512]{1,0:T(8,128)S(1)} collective-permute-done((f32[16,512]{1,0:T(8,128)S(1)}, f32[16,512]{1,0:T(8,128)S(1)}, u32[]{:S(2)}, u32[]{:S(2)}) %collective-permute-start.15) | collective-permute-done | bytes 32800 | tf_op jit(solution)/shard_map/ppermute | solution.py:555
  78.3 0.3 collective-permute-start.16
  78.7 3.6 %collective-permute-done.16 = f32[16,512]{1,0:T(8,128)S(1)} collective-permute-done((f32[16,512]{1,0:T(8,128)S(1)}, f32[16,512]{1,0:T(8,128)S(1)}, u32[]{:S(2)}, u32[]{:S(2)}) %collective-permute-start.16) | collective-permute-done | bytes 32800 | tf_op jit(solution)/shard_map/ppermute | solution.py:555
  82.3 1.4 %collective-permute-start.17 = (f32[16,512]{1,0:T(8,128)S(1)}, f32[16,512]{1,0:T(8,128)S(1)}, u32[]{:S(2)}, u32[]{:S(2)}) collective-permute-start(f32[16,512]{1,0:T(8,128)S(1)} %add.18), channel_id=1, source_target_pairs={{0,16},{4,20},{8,24},{12,28},{16,0},{20,4},{24,8},{28,12},{1,17},{... | collective-permute-start | bytes 98312 | tf_op jit(solution)/shard_map/ppermute | solution.py:555
  83.6 3.6 %collective-permute-done.17 = f32[16,512]{1,0:T(8,128)S(1)} collective-permute-done((f32[16,512]{1,0:T(8,128)S(1)}, f32[16,512]{1,0:T(8,128)S(1)}, u32[]{:S(2)}, u32[]{:S(2)}) %collective-permute-start.17) | collective-permute-done | bytes 32800 | tf_op jit(solution)/shard_map/ppermute | solution.py:555
  87.2 0.0 collective-permute-done.14.other
  87.2 4.0 %shard_map.221 = (bf16[16,256,512]{2,1,0:T(8,128)(2,1)}, f32[16,256,512]{2,1,0:T(8,128)}) custom-call(s32[34]{0:T(128)S(1)} %pad_add_fusion.meta, bf16[2,4,256,512]{3,2,1,0:T(8,128)(2,1)S(1)} %get-tuple-element.100.mine, bf16[2,4,256,512]{3,2,1,0:T(8,128)(2,1)S(1)} %collective-permute-done.14.other), custom_call_target="tpu_custom_call" | custom-call | bytes 20000000 | tf_op jit(solution)/shard_map/pallas_call | solution.py:479
  91.2 0.0 collective-permute-done.13.other
  91.2 4.0 %shard_map.222 = (bf16[16,256,512]{2,1,0:T(8,128)(2,1)}, f32[16,256,512]{2,1,0:T(8,128)}) custom-call(s32[34]{0:T(128)S(1)} %pad_add_fusion.meta, bf16[2,4,256,512]{3,2,1,0:T(8,128)(2,1)S(1)} %get-tuple-element.99.mine, bf16[2,4,256,512]{3,2,1,0:T(8,128)(2,1)S(1)} %collective-permute-done.13.other, ...), custom_call_target="tpu_custom_call", output_to_operand_aliasing={{0}: (3, {}), {1}: (4, {})} | custom-call | bytes 20000000 | tf_op jit(solution)/shard_map/pallas_call | solution.py:479
  95.1 0.0 collective-permute-done.11.far
  95.1 1.9 %shard_map.223 = (f32[7,512]{1,0:T(8,128)}, f32[512]{0:T(512)}, f32[2,512]{1,0:T(2,128)}, f32[2,512]{1,0:T(2,128)}, f32[512,384]{1,0:T(8,128)}, /*index=5*/f32[3...) custom-call(s32[34]{0:T(128)S(1)} %pad_add_fusion.meta, bf16[1536,128]{1,0:T(8,128)(2,1)S(1)} %shard_map.220.near, ...), custom_call_target="tpu_custom_call" | custom-call | tf_op jit(solution)/shard_map/pallas_call | solution.py:541
  (6 shorter events, 0.1 us)
Async XLA Ops:
  1.9 13.5 %collective-permute-start = (bf16[3088,128]{1,0:T(8,128)(2,1)S(1)}, bf16[3088,128]{1,0:T(8,128)(2,1)S(1)}, u32[]{:S(2)}, u32[]{:S(2)}) collective-permute-start(bf16[3088,128]{1,0:T(8,128)(2,1)S(1)} %shard_map.213.buf_a), channel_id=1, source_target_pairs={{0,1},{1,0},{2,3},{3,2},{4,5},{5,4},{6,7},{7,6},{8,9},{9,8},{10,11... | collective-permute-start | bytes 2371592 | tf_op jit(solution)/shard_map/ppermute | solution.py:550
  2.4 22.4 %collective-permute-start.3 = (bf16[3088,128]{1,0:T(8,128)(2,1)S(1)}, bf16[3088,128]{1,0:T(8,128)(2,1)S(1)}, u32[]{:S(2)}, u32[]{:S(2)}) collective-permute-start(bf16[3088,128]{1,0:T(8,128)(2,1)S(1)} %shard_map.213.buf_a), channel_id=1, source_target_pairs={{0,2},{1,3},{2,0},{3,1},{4,6},{5,7},{6,4},{7,5},{8,10},{9,11},{10,... | collective-permute-start | bytes 2371592 | tf_op jit(solution)/shard_map/ppermute | solution.py:550
  24.2 2.5 %collective-permute-start.1 = (bf16[3072,128]{1,0:T(8,128)(2,1)S(1)}, bf16[3072,128]{1,0:T(8,128)(2,1)S(1)}, u32[]{:S(2)}, u32[]{:S(2)}) collective-permute-start(bf16[3072,128]{1,0:T(8,128)(2,1)S(1)} %get-tuple-element.68), channel_id=1, source_target_pairs={{0,1},{1,0},{2,3},{3,2},{4,5},{5,4},{6,7},{7,6},{8,9},{9,8},{10,11... | collective-permute-start | bytes 2359304 | tf_op jit(solution)/shard_map/ppermute | solution.py:550
  24.9 4.4 %collective-permute-start.4 = (bf16[3088,128]{1,0:T(8,128)(2,1)S(1)}, bf16[3088,128]{1,0:T(8,128)(2,1)S(1)}, u32[]{:S(2)}, u32[]{:S(2)}) collective-permute-start(bf16[3088,128]{1,0:T(8,128)(2,1)S(1)} %collective-permute-done.3.buf_c), channel_id=1, source_target_pairs={{0,1},{1,0},{2,3},{3,2},{4,5},{5,4},{6,7},{7,6},{8,9},{9,8},{10,11... | collective-permute-start | bytes 2371592 | tf_op jit(solution)/shard_map/ppermute | solution.py:550
  27.4 13.6 %collective-permute-start.2 = (bf16[1536,128]{1,0:T(8,128)(2,1)S(1)}, bf16[1536,128]{1,0:T(8,128)(2,1)S(1)}, u32[]{:S(2)}, u32[]{:S(2)}) collective-permute-start(bf16[1536,128]{1,0:T(8,128)(2,1)S(1)} %get-tuple-element.70), channel_id=1, source_target_pairs={{0,4},{4,0},{8,12},{12,8},{16,20},{20,16},{24,28},{28,24},{1,5},{5... | collective-permute-start | bytes 1179656 | tf_op jit(solution)/shard_map/ppermute | solution.py:555
  41.2 11.3 %collective-permute-start.7 = (bf16[384,128]{1,0:T(8,128)(2,1)S(1)}, bf16[384,128]{1,0:T(8,128)(2,1)S(1)}, u32[]{:S(2)}, u32[]{:S(2)}) collective-permute-start(bf16[384,128]{1,0:T(8,128)(2,1)S(1)} %get-tuple-element.121), channel_id=1, source_target_pairs={{0,24},{4,28},{8,16},{12,20},{16,8},{20,12},{24,0},{28,4},{1,25},{... | collective-permute-start | bytes 294920 | tf_op jit(solution)/shard_map/ppermute | solution.py:555
  43.7 9.4 %collective-permute-start.6 = (bf16[384,128]{1,0:T(8,128)(2,1)S(1)}, bf16[384,128]{1,0:T(8,128)(2,1)S(1)}, u32[]{:S(2)}, u32[]{:S(2)}) collective-permute-start(bf16[384,128]{1,0:T(8,128)(2,1)S(1)} %get-tuple-element.122), channel_id=1, source_target_pairs={{0,16},{4,20},{8,24},{12,28},{16,0},{20,4},{24,8},{28,12},{1,17},{... | collective-permute-start | bytes 294920 | tf_op jit(solution)/shard_map/ppermute | solution.py:555
  44.5 8.6 %collective-permute-start.5 = (bf16[384,128]{1,0:T(8,128)(2,1)S(1)}, bf16[384,128]{1,0:T(8,128)(2,1)S(1)}, u32[]{:S(2)}, u32[]{:S(2)}) collective-permute-start(bf16[384,128]{1,0:T(8,128)(2,1)S(1)} %get-tuple-element.123), channel_id=1, source_target_pairs={{0,8},{4,12},{8,0},{12,4},{16,24},{20,28},{24,16},{28,20},{1,9},{5... | collective-permute-start | bytes 294920 | tf_op jit(solution)/shard_map/ppermute | solution.py:555
  53.2 11.3 %collective-permute-start.10 = (bf16[384,128]{1,0:T(8,128)(2,1)S(1)}, bf16[384,128]{1,0:T(8,128)(2,1)S(1)}, u32[]{:S(2)}, u32[]{:S(2)}) collective-permute-start(bf16[384,128]{1,0:T(8,128)(2,1)S(1)} %shard_map.218.refs_0_), channel_id=1, source_target_pairs={{0,24},{4,28},{8,16},{12,20},{16,8},{20,12},{24,0},{28,4},{1,25},{... | collective-permute-start | bytes 294920 | tf_op jit(solution)/shard_map/ppermute | solution.py:555
  55.4 9.1 %collective-permute-start.9 = (bf16[384,128]{1,0:T(8,128)(2,1)S(1)}, bf16[384,128]{1,0:T(8,128)(2,1)S(1)}, u32[]{:S(2)}, u32[]{:S(2)}) collective-permute-start(bf16[384,128]{1,0:T(8,128)(2,1)S(1)} %shard_map.218.refs_0_), channel_id=1, source_target_pairs={{0,16},{4,20},{8,24},{12,28},{16,0},{20,4},{24,8},{28,12},{1,17},{... | collective-permute-start | bytes 294920 | tf_op jit(solution)/shard_map/ppermute | solution.py:555
  55.4 9.1 %collective-permute-start.8 = (bf16[384,128]{1,0:T(8,128)(2,1)S(1)}, bf16[384,128]{1,0:T(8,128)(2,1)S(1)}, u32[]{:S(2)}, u32[]{:S(2)}) collective-permute-start(bf16[384,128]{1,0:T(8,128)(2,1)S(1)} %shard_map.218.refs_0_), channel_id=1, source_target_pairs={{0,8},{4,12},{8,0},{12,4},{16,24},{20,28},{24,16},{28,20},{1,9},{5... | collective-permute-start | bytes 294920 | tf_op jit(solution)/shard_map/ppermute | solution.py:555
  64.6 1.3 %collective-permute-start.12 = (f32[16,512]{1,0:T(8,128)S(1)}, f32[16,512]{1,0:T(8,128)S(1)}, u32[]{:S(2)}, u32[]{:S(2)}) collective-permute-start(f32[16,512]{1,0:T(8,128)S(1)} %get-tuple-element.96), channel_id=1, source_target_pairs={{0,1},{1,0},{2,3},{3,2},{4,5},{5,4},{6,7},{7,6},{8,9},{9,8},{10,11... | collective-permute-start | bytes 98312 | tf_op jit(solution)/shard_map/ppermute | solution.py:550
  65.8 21.4 %collective-permute-start.14 = (bf16[2,4,256,512]{3,2,1,0:T(8,128)(2,1)S(1)}, bf16[2,4,256,512]{3,2,1,0:T(8,128)(2,1)S(1)}, u32[]{:S(2)}, u32[]{:S(2)}) collective-permute-start(bf16[2,4,256,512]{3,2,1,0:T(8,128)(2,1)S(1)} %get-tuple-element.100.mine), channel_id=1, source_target_pairs={{0,1},{1,0},{2,3},{3,2},{4,5},{5,4},{6,7},{7,6},{8,9},{9,8},{10,11... | collective-permute-start | bytes 6291464 | tf_op jit(solution)/shard_map/ppermute | solution.py:550
  66.0 25.2 %collective-permute-start.13 = (bf16[2,4,256,512]{3,2,1,0:T(8,128)(2,1)S(1)}, bf16[2,4,256,512]{3,2,1,0:T(8,128)(2,1)S(1)}, u32[]{:S(2)}, u32[]{:S(2)}) collective-permute-start(bf16[2,4,256,512]{3,2,1,0:T(8,128)(2,1)S(1)} %get-tuple-element.99.mine), channel_id=1, source_target_pairs={{0,1},{1,0},{2,3},{3,2},{4,5},{5,4},{6,7},{7,6},{8,9},{9,8},{10,11... | collective-permute-start | bytes 6291464 | tf_op jit(solution)/shard_map/ppermute | solution.py:550
  66.4 28.8 %collective-permute-start.11 = (bf16[1536,128]{1,0:T(8,128)(2,1)S(1)}, bf16[1536,128]{1,0:T(8,128)(2,1)S(1)}, u32[]{:S(2)}, u32[]{:S(2)}) collective-permute-start(bf16[1536,128]{1,0:T(8,128)(2,1)S(1)} %shard_map.220.near), channel_id=1, source_target_pairs={{0,4},{4,0},{8,12},{12,8},{16,20},{20,16},{24,28},{28,24},{1,5},{5... | collective-permute-start | bytes 1179656 | tf_op jit(solution)/shard_map/ppermute | solution.py:555
  67.7 10.6 %collective-permute-start.15 = (f32[16,512]{1,0:T(8,128)S(1)}, f32[16,512]{1,0:T(8,128)S(1)}, u32[]{:S(2)}, u32[]{:S(2)}) collective-permute-start(f32[16,512]{1,0:T(8,128)S(1)} %add.16), channel_id=1, source_target_pairs={{0,4},{4,0},{8,12},{12,8},{16,20},{20,16},{24,28},{28,24},{1,5},{5... | collective-permute-start | bytes 98312 | tf_op jit(solution)/shard_map/ppermute | solution.py:555
  78.3 3.9 %collective-permute-start.16 = (f32[16,512]{1,0:T(8,128)S(1)}, f32[16,512]{1,0:T(8,128)S(1)}, u32[]{:S(2)}, u32[]{:S(2)}) collective-permute-start(f32[16,512]{1,0:T(8,128)S(1)} %add.17), channel_id=1, source_target_pairs={{0,8},{4,12},{8,0},{12,4},{16,24},{20,28},{24,16},{28,20},{1,9},{5... | collective-permute-start | bytes 98312 | tf_op jit(solution)/shard_map/ppermute | solution.py:555
  82.3 4.9 %collective-permute-start.17 = (f32[16,512]{1,0:T(8,128)S(1)}, f32[16,512]{1,0:T(8,128)S(1)}, u32[]{:S(2)}, u32[]{:S(2)}) collective-permute-start(f32[16,512]{1,0:T(8,128)S(1)} %add.18), channel_id=1, source_target_pairs={{0,16},{4,20},{8,24},{12,28},{16,0},{20,4},{24,8},{28,12},{1,17},{... | collective-permute-start | bytes 98312 | tf_op jit(solution)/shard_map/ppermute | solution.py:555
where the time goes:
time: 98.9 us; the launch traced here: 97 us
  Pallas kernels  55.7 us (56%)
  waiting for transfers between devices  20.7 us (21%)
  starting transfers between devices  18.9 us (19%)
    ppermute x11, waiting for transfers between devices, across(): return lax.ppermute(x, 'dp', [(i, i ^ step) for i in range(size)])  17.7 us
    ppermute x11, starting transfers between devices, across(): return lax.ppermute(x, 'dp', [(i, i ^ step) for i in range(size)])  14.5 us
    pallas_call x2, Pallas kernels, finish(): pl.pallas_call(functools.partial(finish_kernel, n, first, last_part), gri...  13.7 us
    pallas_call x1, Pallas kernels, mix(): pl.pallas_call(functools.partial(mix_kernel, n), in_specs=[smem()] + [vme...  11.7 us
    pallas_call x1, Pallas kernels, conv_norm(): pl.pallas_call(functools.partial(conv_norm_kernel, n), grid_spec=pltpu.Pr...  9.66 us
    pallas_call x1, Pallas kernels, hidden(): pl.pallas_call(functools.partial(hidden_kernel, n), in_specs=[smem(), vme...  8.8 us
    pallas_call x2, Pallas kernels, merge(): pl.pallas_call(merge_kernel, grid_spec=pltpu.PrefetchScalarGridSpec(num_s...  7.92 us
    ppermute x7, starting transfers between devices, swap(): return lax.ppermute(x, 'tp', [(i, i ^ step) for i in range(size)])  4.37 us
  transfers between devices with their start and end apart: 18, of which 6 were waited for; matrix products, arithmetic and copies ran while one was open for 1% of the time, Pallas kernels for 54%

commit v1 on v0

--- a/solution.py
+++ b/solution.py
@@ -597,10 +597,16 @@
     near = relay(near)
     far = across(near, 1)
     small = small_keep + small_got
-    for i in range(dp.bit_length() - 1):
-        small = small + across(small, 1 << i)
+    steps = [1 << i for i in range(1, dp.bit_length() - 1)]
+    got = across(small, steps[0])
     done = merge(meta, both_1, swap(both_1, 1), (), n, 0)
+    got, done = lax.optimization_barrier((got, done))
+    small = small + got
+    for step in steps[1:]:
+        small = small + across(small, step)
     out, gtok = merge(meta, both_2, swap(both_2, 1), done, n, n // 2)
+    small, out, gtok = lax.optimization_barrier((small, out, gtok))
+    small = small + across(small, 1)
     far, out, gtok = lax.optimization_barrier((far, out, gtok))
     gcw, gcb, gns, gnsh, gwi, gbi, gwo, gbo, gls = unpack(meta, near, far, small, dp, taps, rates, width, h)
     return (out, gtok, gcw, gcb, gns, gnsh, gwi, gbi, gwo, gbo, gls)

time: 98.9 us -> 86.5 us (0.87); the launches traced: 97 us -> 86.1 us
  waiting for transfers between devices: 20.7 us -> 7.31 us
  starting transfers between devices: 18.9 us -> 24.8 us
  Pallas kernels: 55.7 us -> 52.3 us
    ppermute x11, waiting for transfers between devices: 17.7 us -> 3.79 us  [across(): return lax.ppermute(x, 'dp', [(i, i ^ step) for i in range(size)])]
    ppermute x11, starting transfers between devices: 14.5 us -> 20.6 us  [across(): return lax.ppermute(x, 'dp', [(i, i ^ step) for i in range(size)])]
    pallas_call x1, Pallas kernels: 11.7 us -> 10.2 us  [mix(): pl.pallas_call(functools.partial(mix_kernel, n), in_specs=[smem()] + [vme...]
    pallas_call x1, Pallas kernels: 8.8 us -> 7.74 us  [hidden(): pl.pallas_call(functools.partial(hidden_kernel, n), in_specs=[smem(), vme...]
  transfers between devices with their start and end apart: 18 -> 18, of which waited for: 6 -> 6; matrix products, arithmetic and copies ran while one was open for 1% -> 1% of each run, Pallas kernels for 54% -> 57%
where the time goes in v1:
time: 86.5 us; the launch traced here: 86.1 us
  Pallas kernels  52.3 us (60%)
  starting transfers between devices  24.8 us (29%)
  waiting for transfers between devices  7.31 us (8%)
  other arithmetic  0.88 us (1%)
    ppermute x11, starting transfers between devices, across(): return lax.ppermute(x, 'dp', [(i, i ^ step) for i in range(size)])  20.6 us
    pallas_call x2, Pallas kernels, finish(): pl.pallas_call(functools.partial(finish_kernel, n, first, last_part), gri...  13 us
    pallas_call x1, Pallas kernels, mix(): pl.pallas_call(functools.partial(mix_kernel, n), in_specs=[smem()] + [vme...  10.2 us
    pallas_call x1, Pallas kernels, conv_norm(): pl.pallas_call(functools.partial(conv_norm_kernel, n), grid_spec=pltpu.Pr...  9.45 us
    pallas_call x2, Pallas kernels, merge(): pl.pallas_call(merge_kernel, grid_spec=pltpu.PrefetchScalarGridSpec(num_s...  7.91 us
    pallas_call x1, Pallas kernels, hidden(): pl.pallas_call(functools.partial(hidden_kernel, n), in_specs=[smem(), vme...  7.74 us
    ppermute x7, starting transfers between devices, swap(): return lax.ppermute(x, 'tp', [(i, i ^ step) for i in range(size)])  4.17 us
    ppermute x11, waiting for transfers between devices, across(): return lax.ppermute(x, 'dp', [(i, i ^ step) for i in range(size)])  3.79 us
  transfers between devices with their start and end apart: 18, of which 6 were waited for; matrix products, arithmetic and copies ran while one was open for 1% of the time, Pallas kernels for 57%

profile of v1, /device:TPU:0, one launch (start us, length us, event | category | flops | bytes accessed | tf_op | source)
XLA Modules:
  0.0 86.1 jit_solution(14470545665434342972)
XLA Ops:
  0.6 1.3 %shard_map.213.buf_a = bf16[3088,128]{1,0:T(8,128)(2,1)S(1)} custom-call(bf16[512,384]{1,0:T(8,128)(2,1)} %wi.1, bf16[384]{0:T(512)(128)(2,1)} %bi.1, bf16[384,512]{1,0:T(8,128)(2,1)} %wo.1), custom_call_target="tpu_custom_call" | custom-call | tf_op jit(solution)/shard_map/pallas_call | solution.py:110
  1.9 0.5 collective-permute-start
  2.4 2.6 %collective-permute-start.3 = (bf16[3088,128]{1,0:T(8,128)(2,1)S(1)}, bf16[3088,128]{1,0:T(8,128)(2,1)S(1)}, u32[]{:S(2)}, u32[]{:S(2)}) collective-permute-start(bf16[3088,128]{1,0:T(8,128)(2,1)S(1)} %shard_map.213.buf_a), channel_id=1, source_target_pairs={{0,2},{1,3},{2,0},{3,1},{4,6},{5,7},{6,4},{7,5},{8,10},{9,11},{10,... | collective-permute-start | bytes 2371592 | tf_op jit(solution)/shard_map/ppermute | solution.py:550
  5.0 0.7 pad_add_fusion.meta
  5.8 9.4 %shard_map.212 = (bf16[2304,512]{1,0:T(8,128)(2,1)S(1)}, bf16[2304,512]{1,0:T(8,128)(2,1)S(1)}, bf16[2304,512]{1,0:T(8,128)(2,1)S(1)}, f32[2304,128]{1,0:T(8,128)S(1)}, f32[8,512]{1,0:T(8,128)S(1)}) custom-call(s32[34]{0:T(128)S(1)} %pad_add_fusion.meta, bf16[16,256,512]{2,1,0:T(8,128)(2,1)} %tok.5, bf16[16,256,512]{2,1,0:T(8,128)(2,1)} %cot.5, ...), custom_call_target="tpu_custom_call" | custom-call | tf_op jit(solution)/shard_map/pallas_call | solution.py:202
  15.2 0.0 collective-permute-done.buf_b
  15.2 7.7 %shard_map.214 = (bf16[2304,768]{1,0:T(8,128)(2,1)S(1)}, bf16[2304,768]{1,0:T(8,128)(2,1)S(1)}, bf16[512,768]{1,0:T(8,128)(2,1)S(1)}, bf16[768,512]{1,0:T(8,128)...) custom-call(s32[34]{0:T(128)S(1)} %pad_add_fusion.meta, ...), custom_call_target="tpu_custom_call" | custom-call | tf_op jit(solution)/shard_map/pallas_call | solution.py:257
  23.0 0.5 collective-permute-start.1
  23.4 0.0 collective-permute-done.3.buf_c
  23.4 0.1 collective-permute-start.4
  23.5 1.8 %collective-permute-done.1.recv = bf16[3072,128]{1,0:T(8,128)(2,1)S(1)} collective-permute-done((bf16[3072,128]{1,0:T(8,128)(2,1)S(1)}, bf16[3072,128]{1,0:T(8,128)(2,1)S(1)}, u32[]{:S(2)}, u32[]{:S(2)}) %collective-permute-start.1) | collective-permute-done | bytes 786464 | tf_op jit(solution)/shard_map/ppermute | solution.py:550
  25.3 0.7 shard_map.215
  26.0 3.4 %collective-permute-start.2 = (bf16[1536,128]{1,0:T(8,128)(2,1)S(1)}, bf16[1536,128]{1,0:T(8,128)(2,1)S(1)}, u32[]{:S(2)}, u32[]{:S(2)}) collective-permute-start(bf16[1536,128]{1,0:T(8,128)(2,1)S(1)} %get-tuple-element.76), channel_id=1, source_target_pairs={{0,4},{4,0},{8,12},{12,8},{16,20},{20,16},{24,28},{28,24},{1,5},{5... | collective-permute-start | bytes 1179656 | tf_op jit(solution)/shard_map/ppermute | solution.py:555
  29.4 0.0 collective-permute-done.4.buf_d
  29.4 10.2 %shard_map.216 = (f32[2304,512]{1,0:T(8,128)S(1)}, f32[2304,512]{1,0:T(8,128)S(1)}) custom-call(s32[34]{0:T(128)S(1)} %pad_add_fusion.meta, bf16[2304,512]{1,0:T(8,128)(2,1)S(1)} %get-tuple-element.71.ad, bf16[2304,512]{1,0:T(8,128)(2,1)S(1)} %get-tuple-element.72.low, bf16[2304,768]{1,0:T(8,128)(2,1)S(1)} %get-tuple-element.77.act, ...), custom_call_target="tpu_custom_call" | custom-call | tf_op jit(solution)/shard_map/pallas_call | solution.py:315
  39.6 0.0 collective-permute-done.2
  39.6 0.1 fusion
  39.7 5.1 %collective-permute-start.7 = (bf16[384,128]{1,0:T(8,128)(2,1)S(1)}, bf16[384,128]{1,0:T(8,128)(2,1)S(1)}, u32[]{:S(2)}, u32[]{:S(2)}) collective-permute-start(bf16[384,128]{1,0:T(8,128)(2,1)S(1)} %get-tuple-element.133), channel_id=1, source_target_pairs={{0,24},{4,28},{8,16},{12,20},{16,8},{20,12},{24,0},{28,4},{1,25},{... | collective-permute-start | bytes 294920 | tf_op jit(solution)/shard_map/ppermute | solution.py:555
  44.9 0.0 collective-permute-start.6
  44.9 0.6 collective-permute-start.5
  45.5 6.5 %shard_map.217 = (bf16[2,4,256,512]{3,2,1,0:T(8,128)(2,1)S(1)}, f32[13,8,512]{2,1,0:T(8,128)S(1)}) custom-call(s32[34]{0:T(128)S(1)} %pad_add_fusion.meta, bf16[16,256,512]{2,1,0:T(8,128)(2,1)} %tok.5, bf16[16,256,512]{2,1,0:T(8,128)(2,1)} %cot.5, f32[2304,512]{1,0:T(8,128)S(1)} %get-tuple-element.93.branch, f32[2304,512]{1,0:T(8,128)S(1)} %get-tuple-element.84.ag, ...), custom_call_target="tpu_custom_call" | custom-call | bytes 40000000 | tf_op jit(solution)/shard_map/pallas_call | solution.py:450
  52.0 0.0 collective-permute-done.7.refs_2_
  52.0 0.6 collective-permute-done.6.refs_1_
  52.5 0.0 collective-permute-done.5.refs_0_
  52.5 0.1 shard_map.218.refs_0_
  52.6 3.9 %collective-permute-start.10 = (bf16[384,128]{1,0:T(8,128)(2,1)S(1)}, bf16[384,128]{1,0:T(8,128)(2,1)S(1)}, u32[]{:S(2)}, u32[]{:S(2)}) collective-permute-start(bf16[384,128]{1,0:T(8,128)(2,1)S(1)} %shard_map.218.refs_0_), channel_id=1, source_target_pairs={{0,24},{4,28},{8,16},{12,20},{16,8},{20,12},{24,0},{28,4},{1,25},{... | collective-permute-start | bytes 294920 | tf_op jit(solution)/shard_map/ppermute | solution.py:555
  56.5 0.0 collective-permute-start.9
  56.5 0.6 collective-permute-start.8
  57.2 6.5 %shard_map.219 = (bf16[2,4,256,512]{3,2,1,0:T(8,128)(2,1)S(1)}, f32[16,512]{1,0:T(8,128)S(1)}, f32[16,512]{1,0:T(8,128)S(1)}) custom-call(s32[34]{0:T(128)S(1)} %pad_add_fusion.meta, bf16[16,256,512]{2,1,0:T(8,128)(2,1)} %tok.5, bf16[16,256,512]{2,1,0:T(8,128)(2,1)} %cot.5, f32[2304,512]{1,0:T(8,128)S(1)} %get-tuple-element.93.branch, ...), custom_call_target="tpu_custom_call" | custom-call | bytes 40000000 | tf_op jit(solution)/shard_map/pallas_call | solution.py:450
  63.7 0.0 collective-permute-done.10.refs_3_
  63.8 0.1 collective-permute-done.9.refs_2_
  63.9 0.0 collective-permute-done.8.refs_1_
  63.9 0.0 collective-permute-start.12
  63.9 1.2 %collective-permute-done.12 = f32[16,512]{1,0:T(8,128)S(1)} collective-permute-done((f32[16,512]{1,0:T(8,128)S(1)}, f32[16,512]{1,0:T(8,128)S(1)}, u32[]{:S(2)}, u32[]{:S(2)}) %collective-permute-start.12) | collective-permute-done | bytes 32800 | tf_op jit(solution)/shard_map/ppermute | solution.py:550
  65.1 0.2 collective-permute-start.14
  65.3 0.3 collective-permute-start.16
  65.6 1.8 %collective-permute-start.11 = (bf16[1536,128]{1,0:T(8,128)(2,1)S(1)}, bf16[1536,128]{1,0:T(8,128)(2,1)S(1)}, u32[]{:S(2)}, u32[]{:S(2)}) collective-permute-start(bf16[1536,128]{1,0:T(8,128)(2,1)S(1)} %shard_map.220.near), channel_id=1, source_target_pairs={{0,4},{4,0},{8,12},{12,8},{16,20},{20,16},{24,28},{28,24},{1,5},{5... | collective-permute-start | bytes 1179656 | tf_op jit(solution)/shard_map/ppermute | solution.py:555
  67.5 1.3 %collective-permute-start.13 = (f32[16,512]{1,0:T(8,128)S(1)}, f32[16,512]{1,0:T(8,128)S(1)}, u32[]{:S(2)}, u32[]{:S(2)}) collective-permute-start(f32[16,512]{1,0:T(8,128)S(1)} %add.16), channel_id=1, source_target_pairs={{0,8},{4,12},{8,0},{12,4},{16,24},{20,28},{24,16},{28,20},{1,9},{5... | collective-permute-start | bytes 98312 | tf_op jit(solution)/shard_map/ppermute | solution.py:555
  68.7 0.5 collective-permute-done.14.other
  69.3 4.0 %shard_map.221 = (bf16[16,256,512]{2,1,0:T(8,128)(2,1)}, f32[16,256,512]{2,1,0:T(8,128)}) custom-call(s32[34]{0:T(128)S(1)} %pad_add_fusion.meta, bf16[2,4,256,512]{3,2,1,0:T(8,128)(2,1)S(1)} %get-tuple-element.107.mine, bf16[2,4,256,512]{3,2,1,0:T(8,128)(2,1)S(1)} %collective-permute-done.14.other), custom_call_target="tpu_custom_call" | custom-call | bytes 20000000 | tf_op jit(solution)/shard_map/pallas_call | solution.py:479
  73.2 0.0 collective-permute-done.13
  73.2 3.0 %collective-permute-start.15 = (f32[16,512]{1,0:T(8,128)S(1)}, f32[16,512]{1,0:T(8,128)S(1)}, u32[]{:S(2)}, u32[]{:S(2)}) collective-permute-start(f32[16,512]{1,0:T(8,128)S(1)} %add.17), channel_id=1, source_target_pairs={{0,16},{4,20},{8,24},{12,28},{16,0},{20,4},{24,8},{28,12},{1,17},{... | collective-permute-start | bytes 98312 | tf_op jit(solution)/shard_map/ppermute | solution.py:555
  76.2 0.0 collective-permute-done.16.other
  76.2 4.0 %shard_map.222 = (bf16[16,256,512]{2,1,0:T(8,128)(2,1)}, f32[16,256,512]{2,1,0:T(8,128)}) custom-call(s32[34]{0:T(128)S(1)} %pad_add_fusion.meta, bf16[2,4,256,512]{3,2,1,0:T(8,128)(2,1)S(1)} %get-tuple-element.111.mine, bf16[2,4,256,512]{3,2,1,0:T(8,128)(2,1)S(1)} %collective-permute-done.16.other, ...), custom_call_target="tpu_custom_call", output_to_operand_aliasing={{0}: (3, {}), {1}: (4, {})} | custom-call | bytes 20000000 | tf_op jit(solution)/shard_map/pallas_call | solution.py:479
  80.2 0.0 collective-permute-done.15
  80.2 0.9 %collective-permute-start.17 = (f32[16,512]{1,0:T(8,128)S(1)}, f32[16,512]{1,0:T(8,128)S(1)}, u32[]{:S(2)}, u32[]{:S(2)}) collective-permute-start(f32[16,512]{1,0:T(8,128)S(1)} %add.18), channel_id=1, source_target_pairs={{0,4},{4,0},{8,12},{12,8},{16,20},{20,16},{24,28},{28,24},{1,5},{5... | collective-permute-start | bytes 98312 | tf_op jit(solution)/shard_map/ppermute | solution.py:555
  81.1 0.0 collective-permute-done.11.far
  81.1 3.1 %collective-permute-done.17 = f32[16,512]{1,0:T(8,128)S(1)} collective-permute-done((f32[16,512]{1,0:T(8,128)S(1)}, f32[16,512]{1,0:T(8,128)S(1)}, u32[]{:S(2)}, u32[]{:S(2)}) %collective-permute-start.17) | collective-permute-done | bytes 32800 | tf_op jit(solution)/shard_map/ppermute | solution.py:555
  84.2 1.9 %shard_map.223 = (f32[7,512]{1,0:T(8,128)}, f32[512]{0:T(512)}, f32[2,512]{1,0:T(2,128)}, f32[2,512]{1,0:T(2,128)}, f32[512,384]{1,0:T(8,128)}, /*index=5*/f32[3...) custom-call(s32[34]{0:T(128)S(1)} %pad_add_fusion.meta, bf16[1536,128]{1,0:T(8,128)(2,1)S(1)} %shard_map.220.near, ...), custom_call_target="tpu_custom_call" | custom-call | tf_op jit(solution)/shard_map/pallas_call | solution.py:541
  (6 shorter events, 0.1 us)
Async XLA Ops:
  1.9 13.3 %collective-permute-start = (bf16[3088,128]{1,0:T(8,128)(2,1)S(1)}, bf16[3088,128]{1,0:T(8,128)(2,1)S(1)}, u32[]{:S(2)}, u32[]{:S(2)}) collective-permute-start(bf16[3088,128]{1,0:T(8,128)(2,1)S(1)} %shard_map.213.buf_a), channel_id=1, source_target_pairs={{0,1},{1,0},{2,3},{3,2},{4,5},{5,4},{6,7},{7,6},{8,9},{9,8},{10,11... | collective-permute-start | bytes 2371592 | tf_op jit(solution)/shard_map/ppermute | solution.py:550
  2.4 21.0 %collective-permute-start.3 = (bf16[3088,128]{1,0:T(8,128)(2,1)S(1)}, bf16[3088,128]{1,0:T(8,128)(2,1)S(1)}, u32[]{:S(2)}, u32[]{:S(2)}) collective-permute-start(bf16[3088,128]{1,0:T(8,128)(2,1)S(1)} %shard_map.213.buf_a), channel_id=1, source_target_pairs={{0,2},{1,3},{2,0},{3,1},{4,6},{5,7},{6,4},{7,5},{8,10},{9,11},{10,... | collective-permute-start | bytes 2371592 | tf_op jit(solution)/shard_map/ppermute | solution.py:550
  23.0 2.4 %collective-permute-start.1 = (bf16[3072,128]{1,0:T(8,128)(2,1)S(1)}, bf16[3072,128]{1,0:T(8,128)(2,1)S(1)}, u32[]{:S(2)}, u32[]{:S(2)}) collective-permute-start(bf16[3072,128]{1,0:T(8,128)(2,1)S(1)} %get-tuple-element.74), channel_id=1, source_target_pairs={{0,1},{1,0},{2,3},{3,2},{4,5},{5,4},{6,7},{7,6},{8,9},{9,8},{10,11... | collective-permute-start | bytes 2359304 | tf_op jit(solution)/shard_map/ppermute | solution.py:550
  23.4 5.9 %collective-permute-start.4 = (bf16[3088,128]{1,0:T(8,128)(2,1)S(1)}, bf16[3088,128]{1,0:T(8,128)(2,1)S(1)}, u32[]{:S(2)}, u32[]{:S(2)}) collective-permute-start(bf16[3088,128]{1,0:T(8,128)(2,1)S(1)} %collective-permute-done.3.buf_c), channel_id=1, source_target_pairs={{0,1},{1,0},{2,3},{3,2},{4,5},{5,4},{6,7},{7,6},{8,9},{9,8},{10,11... | collective-permute-start | bytes 2371592 | tf_op jit(solution)/shard_map/ppermute | solution.py:550
  26.0 13.6 %collective-permute-start.2 = (bf16[1536,128]{1,0:T(8,128)(2,1)S(1)}, bf16[1536,128]{1,0:T(8,128)(2,1)S(1)}, u32[]{:S(2)}, u32[]{:S(2)}) collective-permute-start(bf16[1536,128]{1,0:T(8,128)(2,1)S(1)} %get-tuple-element.76), channel_id=1, source_target_pairs={{0,4},{4,0},{8,12},{12,8},{16,20},{20,16},{24,28},{28,24},{1,5},{5... | collective-permute-start | bytes 1179656 | tf_op jit(solution)/shard_map/ppermute | solution.py:555
  39.7 12.2 %collective-permute-start.7 = (bf16[384,128]{1,0:T(8,128)(2,1)S(1)}, bf16[384,128]{1,0:T(8,128)(2,1)S(1)}, u32[]{:S(2)}, u32[]{:S(2)}) collective-permute-start(bf16[384,128]{1,0:T(8,128)(2,1)S(1)} %get-tuple-element.133), channel_id=1, source_target_pairs={{0,24},{4,28},{8,16},{12,20},{16,8},{20,12},{24,0},{28,4},{1,25},{... | collective-permute-start | bytes 294920 | tf_op jit(solution)/shard_map/ppermute | solution.py:555
  44.9 7.7 %collective-permute-start.6 = (bf16[384,128]{1,0:T(8,128)(2,1)S(1)}, bf16[384,128]{1,0:T(8,128)(2,1)S(1)}, u32[]{:S(2)}, u32[]{:S(2)}) collective-permute-start(bf16[384,128]{1,0:T(8,128)(2,1)S(1)} %get-tuple-element.134), channel_id=1, source_target_pairs={{0,16},{4,20},{8,24},{12,28},{16,0},{20,4},{24,8},{28,12},{1,17},{... | collective-permute-start | bytes 294920 | tf_op jit(solution)/shard_map/ppermute | solution.py:555
  44.9 7.7 %collective-permute-start.5 = (bf16[384,128]{1,0:T(8,128)(2,1)S(1)}, bf16[384,128]{1,0:T(8,128)(2,1)S(1)}, u32[]{:S(2)}, u32[]{:S(2)}) collective-permute-start(bf16[384,128]{1,0:T(8,128)(2,1)S(1)} %get-tuple-element.135), channel_id=1, source_target_pairs={{0,8},{4,12},{8,0},{12,4},{16,24},{20,28},{24,16},{28,20},{1,9},{5... | collective-permute-start | bytes 294920 | tf_op jit(solution)/shard_map/ppermute | solution.py:555
  52.6 11.1 %collective-permute-start.10 = (bf16[384,128]{1,0:T(8,128)(2,1)S(1)}, bf16[384,128]{1,0:T(8,128)(2,1)S(1)}, u32[]{:S(2)}, u32[]{:S(2)}) collective-permute-start(bf16[384,128]{1,0:T(8,128)(2,1)S(1)} %shard_map.218.refs_0_), channel_id=1, source_target_pairs={{0,24},{4,28},{8,16},{12,20},{16,8},{20,12},{24,0},{28,4},{1,25},{... | collective-permute-start | bytes 294920 | tf_op jit(solution)/shard_map/ppermute | solution.py:555
  56.5 7.3 %collective-permute-start.9 = (bf16[384,128]{1,0:T(8,128)(2,1)S(1)}, bf16[384,128]{1,0:T(8,128)(2,1)S(1)}, u32[]{:S(2)}, u32[]{:S(2)}) collective-permute-start(bf16[384,128]{1,0:T(8,128)(2,1)S(1)} %shard_map.218.refs_0_), channel_id=1, source_target_pairs={{0,16},{4,20},{8,24},{12,28},{16,0},{20,4},{24,8},{28,12},{1,17},{... | collective-permute-start | bytes 294920 | tf_op jit(solution)/shard_map/ppermute | solution.py:555
  56.5 7.3 %collective-permute-start.8 = (bf16[384,128]{1,0:T(8,128)(2,1)S(1)}, bf16[384,128]{1,0:T(8,128)(2,1)S(1)}, u32[]{:S(2)}, u32[]{:S(2)}) collective-permute-start(bf16[384,128]{1,0:T(8,128)(2,1)S(1)} %shard_map.218.refs_0_), channel_id=1, source_target_pairs={{0,8},{4,12},{8,0},{12,4},{16,24},{20,28},{24,16},{28,20},{1,9},{5... | collective-permute-start | bytes 294920 | tf_op jit(solution)/shard_map/ppermute | solution.py:555
  63.9 1.2 %collective-permute-start.12 = (f32[16,512]{1,0:T(8,128)S(1)}, f32[16,512]{1,0:T(8,128)S(1)}, u32[]{:S(2)}, u32[]{:S(2)}) collective-permute-start(f32[16,512]{1,0:T(8,128)S(1)} %get-tuple-element.103), channel_id=1, source_target_pairs={{0,1},{1,0},{2,3},{3,2},{4,5},{5,4},{6,7},{7,6},{8,9},{9,8},{10,11... | collective-permute-start | bytes 98312 | tf_op jit(solution)/shard_map/ppermute | solution.py:550
  65.1 4.2 %collective-permute-start.14 = (bf16[2,4,256,512]{3,2,1,0:T(8,128)(2,1)S(1)}, bf16[2,4,256,512]{3,2,1,0:T(8,128)(2,1)S(1)}, u32[]{:S(2)}, u32[]{:S(2)}) collective-permute-start(bf16[2,4,256,512]{3,2,1,0:T(8,128)(2,1)S(1)} %get-tuple-element.107.mine), channel_id=1, source_target_pairs={{0,1},{1,0},{2,3},{3,2},{4,5},{5,4},{6,7},{7,6},{8,9},{9,8},{10,11... | collective-permute-start | bytes 6291464 | tf_op jit(solution)/shard_map/ppermute | solution.py:550
  65.3 10.9 %collective-permute-start.16 = (bf16[2,4,256,512]{3,2,1,0:T(8,128)(2,1)S(1)}, bf16[2,4,256,512]{3,2,1,0:T(8,128)(2,1)S(1)}, u32[]{:S(2)}, u32[]{:S(2)}) collective-permute-start(bf16[2,4,256,512]{3,2,1,0:T(8,128)(2,1)S(1)} %get-tuple-element.111.mine), channel_id=1, source_target_pairs={{0,1},{1,0},{2,3},{3,2},{4,5},{5,4},{6,7},{7,6},{8,9},{9,8},{10,11... | collective-permute-start | bytes 6291464 | tf_op jit(solution)/shard_map/ppermute | solution.py:550
  65.6 15.4 %collective-permute-start.11 = (bf16[1536,128]{1,0:T(8,128)(2,1)S(1)}, bf16[1536,128]{1,0:T(8,128)(2,1)S(1)}, u32[]{:S(2)}, u32[]{:S(2)}) collective-permute-start(bf16[1536,128]{1,0:T(8,128)(2,1)S(1)} %shard_map.220.near), channel_id=1, source_target_pairs={{0,4},{4,0},{8,12},{12,8},{16,20},{20,16},{24,28},{28,24},{1,5},{5... | collective-permute-start | bytes 1179656 | tf_op jit(solution)/shard_map/ppermute | solution.py:555
  67.5 5.8 %collective-permute-start.13 = (f32[16,512]{1,0:T(8,128)S(1)}, f32[16,512]{1,0:T(8,128)S(1)}, u32[]{:S(2)}, u32[]{:S(2)}) collective-permute-start(f32[16,512]{1,0:T(8,128)S(1)} %add.16), channel_id=1, source_target_pairs={{0,8},{4,12},{8,0},{12,4},{16,24},{20,28},{24,16},{28,20},{1,9},{5... | collective-permute-start | bytes 98312 | tf_op jit(solution)/shard_map/ppermute | solution.py:555
  73.2 6.9 %collective-permute-start.15 = (f32[16,512]{1,0:T(8,128)S(1)}, f32[16,512]{1,0:T(8,128)S(1)}, u32[]{:S(2)}, u32[]{:S(2)}) collective-permute-start(f32[16,512]{1,0:T(8,128)S(1)} %add.17), channel_id=1, source_target_pairs={{0,16},{4,20},{8,24},{12,28},{16,0},{20,4},{24,8},{28,12},{1,17},{... | collective-permute-start | bytes 98312 | tf_op jit(solution)/shard_map/ppermute | solution.py:555
  80.2 4.0 %collective-permute-start.17 = (f32[16,512]{1,0:T(8,128)S(1)}, f32[16,512]{1,0:T(8,128)S(1)}, u32[]{:S(2)}, u32[]{:S(2)}) collective-permute-start(f32[16,512]{1,0:T(8,128)S(1)} %add.18), channel_id=1, source_target_pairs={{0,4},{4,0},{8,12},{12,8},{16,20},{20,16},{24,28},{28,24},{1,5},{5... | collective-permute-start | bytes 98312 | tf_op jit(solution)/shard_map/ppermute | solution.py:555

commit v2 on v0

--- a/solution.py
+++ b/solution.py
@@ -13,6 +13,7 @@
 LANES = 128
 PAD = 8
 CHUNK = 64
+WIDE_CHUNK = 128
 VMEM_LIMIT = 12 * 1024 * 1024
 
 
@@ -133,33 +134,59 @@
             row[:, lane(at)] = bias[side, q:q + 1, :].astype(F32)
 
 
-def conv_norm_kernel(n, meta, tok, cot, cw, cb, ns, nsh, gamma, ad, nrm, low, inv, gbo, offs, pad):
+def front_kernel(n, meta, tok, cot, cw, cb, ns, nsh, gamma, buf_a, buf_b,
+                 ad, nrm, low, inv, act, pre, win, wout, keep, send, gbo, gbi,
+                 offs, pad, ad_s, nrm_s, low_s, inv_s, bias, bias_row, dwo, dwi, sems):
     s = pl.program_id(0)
     frames, width = tok.shape[1], tok.shape[2]
     taps = cw.shape[0]
     half = taps // 2
     wq = width // LANES
+    h = win.shape[1] // 2
+    copies = weight_copies(buf_a, 0, win, wout, bias, sems) + weight_copies(buf_b, 1, win, wout, bias, sems)
 
     @pl.when(s == 0)
     def _():
+        for c in copies:
+            c.start()
         place_items(n, meta, offs)
+        offs[n + 2] = 0
         gbo[...] = jnp.zeros_like(gbo)
         pad[...] = jnp.zeros_like(pad)
+
+    def flush(j):
+        dst = pl.ds(pl.multiple_of(offs[j], 16), frames)
+        for whole_ref, stage in ((ad, ad_s), (nrm, nrm_s), (low, low_s), (inv, inv_s)):
+            whole_ref[dst, :] = stage[...]
+
+    @pl.when(s > 0)
+    def _():
+        flush(s - 1)
+
+    @pl.when(s == 1)
+    def _():
+        for c in copies:
+            c.wait()
+        spread_bias(bias, bias_row)
+        dwo[...] = jnp.zeros_like(dwo)
+        dwi[...] = jnp.zeros_like(dwi)
+        gbi[...] = jnp.zeros_like(gbi)
 
     item = meta[0] * n + s
     count = meta[2 + item]
     group = meta[2 + 2 * n + item]
-    off = offs[s]
-    rows = lax.broadcasted_iota(jnp.int32, (frames, 1), 0)
-    for q in range(wq):
-        pad[q, PAD:PAD + frames, :] = jnp.where(rows < count, tok[0, :, lane(q)].astype(F32), 0.0)
-    scale, shift = pick(ns, group), pick(nsh, group)
-    gam, conv_bias = as_row(gamma), as_row(cb)
-    w = cw[...].astype(F32)
-
-    def step(i, acc):
-        r0 = pl.multiple_of(i * CHUNK, CHUNK)
-        live = (lax.broadcasted_iota(jnp.int32, (CHUNK, 1), 0) + r0) < count
+
+    def setup():
+        rows = lax.broadcasted_iota(jnp.int32, (frames, LANES), 0)
+        for q in range(wq):
+            pad[q, PAD:PAD + frames, :] = jnp.where(rows < count, tok[0, :, lane(q)].astype(F32), 0.0)
+        return pick(ns, group), pick(nsh, group), as_row(gamma), as_row(cb), cw[...].astype(F32)
+
+    def conv_step(i, acc, consts):
+        scale, shift, gam, conv_bias, w = consts
+        r0 = i * CHUNK if isinstance(i, int) else pl.multiple_of(i * CHUNK, CHUNK)
+        here = pl.ds(r0, CHUNK)
+        live = (lax.broadcasted_iota(jnp.int32, (CHUNK, LANES), 0) + r0) < count
         convs = []
         for q in range(wq):
             conv = conv_bias[:, lane(q)]
@@ -171,101 +198,114 @@
         sq = [c * c for c in cents]
         var = jnp.sum(sum(sq[1:], sq[0]), axis=-1, keepdims=True) * (1.0 / width)
         istd = lax.rsqrt(var + EPS)
-        dst = pl.ds(pl.multiple_of(off + r0, 16), CHUNK)
-        inv[dst, :] = jnp.broadcast_to(istd, (CHUNK, LANES))
+        inv_s[here, :] = jnp.broadcast_to(istd, (CHUNK, LANES))
         new = []
         for q in range(wq):
             normed = cents[q] * istd
-            ad[dst, lane(q)] = (normed * scale[:, lane(q)] + shift[:, lane(q)]).astype(BF)
-            nrm[dst, lane(q)] = normed.astype(BF)
-            back = jnp.where(live, cot[0, pl.ds(r0, CHUNK), lane(q)].astype(F32), 0.0) * gam[:, lane(q)]
-            low[dst, lane(q)] = back.astype(BF)
+            ad_s[here, lane(q)] = (normed * scale[:, lane(q)] + shift[:, lane(q)]).astype(BF)
+            nrm_s[here, lane(q)] = normed.astype(BF)
+            back = jnp.where(live, cot[0, here, lane(q)].astype(F32), 0.0) * gam[:, lane(q)]
+            low_s[here, lane(q)] = back.astype(BF)
             new.append(acc[q] + fold(back))
         return tuple(new)
 
-    accs = lax.fori_loop(0, pl.cdiv(count, CHUNK), step, (jnp.zeros((8, LANES), F32),) * wq)
-    for q in range(wq):
-        gbo[:, lane(q)] += accs[q]
-
-    @pl.when(s == n - 1)
-    def _():
-        end = pl.ds(pl.multiple_of(offs[n], 16), TILE)
-        ad[end, :] = jnp.zeros((TILE, width), BF)
-        low[end, :] = jnp.zeros((TILE, width), BF)
-
-
-def conv_norm(meta, tok, cot, cw, cb, ns, nsh, gamma):
-    items, frames, width = tok.shape
-    n = items // 2
-    rows = n * frames + TILE
-    item = pl.BlockSpec((1, frames, width), lambda s, c: (c[0] * n + s, 0, 0))
-    return pl.pallas_call(
-        functools.partial(conv_norm_kernel, n),
-        grid_spec=pltpu.PrefetchScalarGridSpec(
-            num_scalar_prefetch=1, grid=(n,),
-            in_specs=[item, item] + [whole(v.shape) for v in (cw, cb, ns, nsh, gamma)],
-            out_specs=[vmem()] * 5,
-            scratch_shapes=[pltpu.SMEM((n + 2,), jnp.int32),
-                            pltpu.VMEM((width // LANES, frames + 4 * PAD, LANES), F32)]),
-        out_shape=[struct((rows, width), BF)] * 3 + [struct((rows, LANES), F32), struct((8, width), F32)],
-        compiler_params=params(), cost_estimate=cost(0),
-    )(meta, tok, cot, cw, cb, ns, nsh, gamma)
-
-
-def hidden_kernel(n, meta, ad, low, buf_a, buf_b, act, pre, win, wout, keep, send, gbi,
-                  offs, bias, bias_row, dwo, dwi, sems):
-    width, h = win.shape[0], win.shape[1] // 2
-    wq = width // LANES
-    copies = weight_copies(buf_a, 0, win, wout, bias, sems) + weight_copies(buf_b, 1, win, wout, bias, sems)
-    for c in copies:
-        c.start()
-    place_items(n, meta, offs)
-    dwo[...] = jnp.zeros_like(dwo)
-    dwi[...] = jnp.zeros_like(dwi)
-    gbi[...] = jnp.zeros_like(gbi)
-    for c in copies:
-        c.wait()
-    spread_bias(bias, bias_row)
-
-    def tile(t, _):
+    def add_gbo(accs):
+        for q in range(wq):
+            gbo[:, lane(q)] += accs[q]
+
+    def tile(t, between=()):
+        between = list(between)
         at = pl.ds(pl.multiple_of(t * TILE, TILE), TILE)
         a, b = ad[at, :], low[at, :]
         activation, slope = gelu_parts(dot(a, win[...]) + bias_row[...])
+        if between:
+            between.pop(0)()
         grad = dot_t(b, wout[...]) * slope
         lo = activation.astype(BF)
         act[at, :] = lo
+        if between:
+            between.pop(0)()
         dwo[...] += dot_rows(lo, b)
         gbi[...] += fold(grad)
         g = grad.astype(BF)
         pre[at, :] = g
+        if between:
+            between.pop(0)()
         dwi[...] += dot_rows(a, g)
-        return 0
-
-    lax.fori_loop(0, offs[n + 1], tile, 0)
-    for side, dst in ((0, keep), (1, send)):
-        for q in range(wq):
-            dst[q * h:(q + 1) * h, :] = dwo[side * h:(side + 1) * h, lane(q)].astype(dst.dtype)
-        base = wq * h
-        for q in range(h // LANES):
-            dst[base + q * width:base + (q + 1) * width, :] = dwi[:, lane(side * (h // LANES) + q)].astype(dst.dtype)
-
-
-def hidden(meta, ad, low, buf_a, buf_b, h, n):
-    rows, width = ad.shape
+        if between:
+            between.pop(0)()
+
+    done = offs[n + 2]
+    ready = offs[s] >= (done + 1) * TILE
+    none = (jnp.zeros((8, LANES), F32),) * wq
+
+    @pl.when(ready)
+    def _():
+        consts = setup()
+        state = [none]
+
+        def part(lo_i, hi_i):
+            def run():
+                for i in range(lo_i, hi_i):
+                    state[0] = conv_step(i, state[0], consts)
+            return run
+
+        count_c = frames // CHUNK
+        cuts = [count_c * k // 4 for k in range(5)]
+        tile(done, [part(cuts[k], cuts[k + 1]) for k in range(4)])
+        add_gbo(state[0])
+        offs[n + 2] = done + 1
+
+    @pl.when(jnp.logical_not(ready))
+    def _():
+        consts = setup()
+        add_gbo(lax.fori_loop(0, pl.cdiv(count, CHUNK), lambda i, acc: conv_step(i, acc, consts), none))
+
+    @pl.when(s == n - 1)
+    def _():
+        flush(s)
+        end = pl.ds(pl.multiple_of(offs[n], 16), TILE)
+        ad[end, :] = jnp.zeros((TILE, width), BF)
+        low[end, :] = jnp.zeros((TILE, width), BF)
+
+        def rest(t, _):
+            tile(t)
+            return 0
+
+        lax.fori_loop(offs[n + 2], offs[n + 1], rest, 0)
+        for side, dst in ((0, keep), (1, send)):
+            for q in range(wq):
+                dst[q * h:(q + 1) * h, :] = dwo[side * h:(side + 1) * h, lane(q)].astype(dst.dtype)
+            base = wq * h
+            for q in range(h // LANES):
+                dst[base + q * width:base + (q + 1) * width, :] = dwi[:, lane(side * (h // LANES) + q)].astype(dst.dtype)
+
+
+def front(meta, tok, cot, cw, cb, ns, nsh, gamma, buf_a, buf_b, h):
+    items, frames, width = tok.shape
+    n = items // 2
+    rows = n * frames + TILE
     packed = 2 * width * h // LANES
     wq, hq = width // LANES, h // LANES
+    item = pl.BlockSpec((1, frames, width), lambda s, c: (c[0] * n + s, 0, 0))
     return pl.pallas_call(
-        functools.partial(hidden_kernel, n),
-        in_specs=[smem(), vmem(), vmem(), hbm(), hbm()],
-        out_specs=[vmem()] * 7,
-        scratch_shapes=[pltpu.SMEM((n + 2,), jnp.int32),
-                        pltpu.VMEM((2, 16, LANES), BF), pltpu.VMEM((1, 2 * h), F32),
-                        pltpu.VMEM((2 * h, width), F32), pltpu.VMEM((width, 2 * h), F32),
-                        pltpu.SemaphoreType.DMA((2, hq + wq + 1))],
-        out_shape=[struct((rows, 2 * h), BF)] * 2 + [struct((width, 2 * h), BF), struct((2 * h, width), BF)]
-        + [struct((packed, LANES), F32), struct((packed, LANES), BF), struct((8, 2 * h), F32)],
+        functools.partial(front_kernel, n),
+        grid_spec=pltpu.PrefetchScalarGridSpec(
+            num_scalar_prefetch=1, grid=(n,),
+            in_specs=[item, item] + [whole(v.shape) for v in (cw, cb, ns, nsh, gamma)] + [hbm()] * 2,
+            out_specs=[vmem()] * 12,
+            scratch_shapes=[pltpu.SMEM((n + 3,), jnp.int32),
+                            pltpu.VMEM((wq, frames + 4 * PAD, LANES), F32),
+                            pltpu.VMEM((frames, width), BF), pltpu.VMEM((frames, width), BF),
+                            pltpu.VMEM((frames, width), BF), pltpu.VMEM((frames, LANES), F32),
+                            pltpu.VMEM((2, 16, LANES), BF), pltpu.VMEM((1, 2 * h), F32),
+                            pltpu.VMEM((2 * h, width), F32), pltpu.VMEM((width, 2 * h), F32),
+                            pltpu.SemaphoreType.DMA((2, hq + wq + 1))]),
+        out_shape=[struct((rows, width), BF)] * 3 + [struct((rows, LANES), F32)]
+        + [struct((rows, 2 * h), BF)] * 2 + [struct((width, 2 * h), BF), struct((2 * h, width), BF)]
+        + [struct((packed, LANES), F32), struct((packed, LANES), BF), struct((8, width), F32), struct((8, 2 * h), F32)],
         compiler_params=params(), cost_estimate=cost(0),
-    )(meta, ad, low, buf_a, buf_b)
+    )(meta, tok, cot, cw, cb, ns, nsh, gamma, buf_a, buf_b)
 
 
 def combine_kernel(dp, meta, keep, recv, stay, leave):
@@ -326,9 +366,28 @@
 
 
 def finish_kernel(n, first, last_part, meta, tok, cot, branch, ag, nrm, inv, sums_in, gbo, gbi, cw, ns,
-                  gamma, both, *rest):
-    results, (offs, cgp, sums) = rest[:-3], rest[-3:]
+                  gamma, *rest):
+    other = rest[0]
+    (out, gtok, both), results, (offs, cgp, sums) = rest[3:6] if last_part else rest[:3], rest[6 if last_part else 3:-3], rest[-3:]
     s = pl.program_id(0) + first
+
+    if last_part:
+        @pl.when(pl.program_id(1) == 1)
+        def _():
+            out[...] = other[0]
+            gtok[...] = other[1].astype(F32)
+
+        @pl.when(pl.program_id(1) == 0)
+        def _():
+            finish_item(n, s, first, last_part, meta, tok, cot, branch, ag, nrm, inv, sums_in, gbo, gbi, cw, ns, gamma,
+                        out, gtok, both, results, offs, cgp, sums)
+    else:
+        finish_item(n, s, first, last_part, meta, tok, cot, branch, ag, nrm, inv, sums_in, gbo, gbi, cw, ns, gamma,
+                    out, gtok, both, results, offs, cgp, sums)
+
+
+def finish_item(n, s, first, last_part, meta, tok, cot, branch, ag, nrm, inv, sums_in, gbo, gbi, cw, ns, gamma,
+                out, gtok, both, results, offs, cgp, sums):
     frames, width = tok.shape[1], tok.shape[2]
     taps, rates = cw.shape[0], ns.shape[0]
     half = taps // 2
@@ -349,20 +408,22 @@
     gam = as_row(gamma)
     w = cw[...].astype(F32)
     zero = jnp.zeros((8, LANES), F32)
-    steps = pl.cdiv(count, CHUNK)
+    steps = pl.cdiv(count, WIDE_CHUNK)
 
     def step(i, accs):
-        r0 = pl.multiple_of(i * CHUNK, CHUNK)
-        here = pl.ds(r0, CHUNK)
-        live = (lax.broadcasted_iota(jnp.int32, (CHUNK, 1), 0) + r0) < count
-        src = pl.ds(pl.multiple_of(off + r0, 16), CHUNK)
+        r0 = pl.multiple_of(i * WIDE_CHUNK, WIDE_CHUNK)
+        here = pl.ds(r0, WIDE_CHUNK)
+        live = (lax.broadcasted_iota(jnp.int32, (WIDE_CHUNK, 1), 0) + r0) < count
+        src = pl.ds(pl.multiple_of(off + r0, 16), WIDE_CHUNK)
         new = []
         ngs, nrs = [], []
         for q in range(wq):
             a_ls, a_sc, a_sh = accs[3 * q:3 * q + 3]
             br = jnp.where(live, branch[src, lane(q)], 0.0)
             tk = jnp.where(live, tok[0, here, lane(q)].astype(F32), 0.0)
-            both[0, 0, here, lane(q)] = (tk + gam[:, lane(q)] * br).astype(BF)
+            value = (tk + gam[:, lane(q)] * br).astype(BF)
+            both[0, 0, here, lane(q)] = value
+            out[0, here, lane(q)] = value
             g = jnp.where(live, ag[src, lane(q)], 0.0)
             nr = nrm[src, lane(q)].astype(F32)
             new += [a_ls + fold(cot[0, here, lane(q)].astype(F32) * br), a_sc + fold(g * nr), a_sh + fold(g)]
@@ -374,7 +435,7 @@
         istd = inv[src, :]
         for q in range(wq):
             cg = istd * (ngs[q] - m1 - nrs[q] * m2)
-            cgp[q, pl.ds(pl.multiple_of(r0 + PAD, 8), CHUNK), :] = jnp.where(live, cg, 0.0)
+            cgp[q, pl.ds(pl.multiple_of(r0 + PAD, 8), WIDE_CHUNK), :] = jnp.where(live, cg, 0.0)
         return tuple(new)
 
     accs = lax.fori_loop(0, steps, step, (zero,) * (3 * wq))
@@ -384,33 +445,35 @@
         sums[taps + 2 + rates + group, :, lane(q)] += accs[3 * q + 2]
 
     def clear(i, _):
-        r0 = pl.multiple_of(i * CHUNK, CHUNK)
-        here = pl.ds(r0, CHUNK)
-        both[0, 0, here, :] = jnp.zeros((CHUNK, width), BF)
-        both[1, 0, here, :] = jnp.zeros((CHUNK, width), BF)
+        r0 = pl.multiple_of(i * WIDE_CHUNK, WIDE_CHUNK)
+        here = pl.ds(r0, WIDE_CHUNK)
+        for ref in (both.at[0, 0], both.at[1, 0], out.at[0], gtok.at[0]):
+            ref[here, :] = jnp.zeros((WIDE_CHUNK, width), ref.dtype)
         for q in range(wq):
-            cgp[q, pl.ds(pl.multiple_of(r0 + PAD, 8), CHUNK), :] = jnp.zeros((CHUNK, LANES), F32)
+            cgp[q, pl.ds(pl.multiple_of(r0 + PAD, 8), WIDE_CHUNK), :] = jnp.zeros((WIDE_CHUNK, LANES), F32)
         return 0
 
-    lax.fori_loop(steps, frames // CHUNK, clear, 0)
+    lax.fori_loop(steps, frames // WIDE_CHUNK, clear, 0)
 
     for q in range(wq):
         wl = w[:, lane(q)]
 
         def conv_step(i, accs):
-            r0 = pl.multiple_of(i * CHUNK, CHUNK)
-            here = pl.ds(r0, CHUNK)
-            live = (lax.broadcasted_iota(jnp.int32, (CHUNK, 1), 0) + r0) < count
+            r0 = pl.multiple_of(i * WIDE_CHUNK, WIDE_CHUNK)
+            here = pl.ds(r0, WIDE_CHUNK)
+            live = (lax.broadcasted_iota(jnp.int32, (WIDE_CHUNK, 1), 0) + r0) < count
             tk = jnp.where(live, tok[0, here, lane(q)].astype(F32), 0.0)
             total = cot[0, here, lane(q)].astype(F32)
             new = []
             for k in range(taps):
-                sh = cgp[q, pl.ds(r0 + (PAD + half - k), CHUNK), :]
+                sh = cgp[q, pl.ds(r0 + (PAD + half - k), WIDE_CHUNK), :]
                 total = total + wl[k:k + 1] * sh
                 new.append(accs[k] + fold(tk * sh))
                 if k == half:
                     new_bias = accs[taps] + fold(sh)
-            both[1, 0, here, lane(q)] = jnp.where(live, total, 0.0).astype(BF)
+            total = jnp.where(live, total, 0.0).astype(BF)
+            both[1, 0, here, lane(q)] = total
+            gtok[0, here, lane(q)] = total.astype(F32)
             return tuple(new) + (new_bias,)
 
         accs = lax.fori_loop(0, steps, conv_step, (zero,) * (taps + 1))
@@ -434,7 +497,7 @@
             dst[...] = jnp.concatenate(rows + tail + spare, axis=0)
 
 
-def finish(meta, tok, cot, branch, ag, nrm, inv, sums, gbo, gbi, cw, ns, gamma, first, size):
+def finish(meta, tok, cot, branch, ag, nrm, inv, sums, gbo, gbi, cw, ns, gamma, first, size, other=None, into=()):
     items, frames, width = tok.shape
     n = items // 2
     last_part = first + size == n
@@ -442,49 +505,48 @@
     taps, rates = cw.shape[0], ns.shape[0]
     n_small = -(-(taps + 4 + 2 * rates) // 8) * 8
     sums_shape = (taps + 2 + 2 * rates, 8, width)
-    item = pl.BlockSpec((1, frames, width), lambda s, c: (c[0] * n + first + s, 0, 0))
-    mine = pl.BlockSpec((2, 1, frames, width), lambda s, *_: (0, s, 0, 0))
+    item = pl.BlockSpec((1, frames, width), lambda s, p, c: (c[0] * n + first + s, 0, 0))
+    mine = pl.BlockSpec((2, 1, frames, width), lambda s, p, c: (0, s, 0, 0))
+    dst = pl.BlockSpec((1, frames, width), lambda s, p, c: ((c[0] ^ p) * n + first * (1 - p) + s, 0, 0))
     more = [(n_small, width)] * 2 if last_part else [sums_shape]
     if sums is None:
         sums = gbo
+    fixed = [meta, tok, cot, branch, ag, nrm, inv, sums, gbo, gbi, cw, ns, gamma]
+    extra = [mine] + [pl.BlockSpec(memory_space=pl.ANY)] * 2 if last_part else []
     return pl.pallas_call(
         functools.partial(finish_kernel, n, first, last_part),
         grid_spec=pltpu.PrefetchScalarGridSpec(
-            num_scalar_prefetch=1, grid=(size,),
-            in_specs=[item, item] + [vmem()] * 7 + [whole(v.shape) for v in (cw, ns, gamma)],
-            out_specs=[mine] + [vmem()] * len(more),
+            num_scalar_prefetch=1, grid=(size, 2 if last_part else 1),
+            in_specs=[item, item] + [vmem()] * 7 + [whole(v.shape) for v in (cw, ns, gamma)] + extra,
+            out_specs=[dst, dst, mine] + [vmem()] * len(more),
             scratch_shapes=[pltpu.SMEM((n + 2,), jnp.int32),
                             pltpu.VMEM((wq, frames + 4 * PAD, LANES), F32),
                             pltpu.VMEM(sums_shape, F32)]),
-        out_shape=[struct((2, size, frames, width), BF)] + [struct(v, F32) for v in more],
+        out_shape=[struct((items, frames, width), BF), struct((items, frames, width), F32),
+                   struct((2, size, frames, width), BF)] + [struct(v, F32) for v in more],
+        input_output_aliases={14: 0, 15: 1} if last_part else {},
         compiler_params=params(), cost_estimate=cost(40000000),
-    )(meta, tok, cot, branch, ag, nrm, inv, sums, gbo, gbi, cw, ns, gamma)
-
-
-def merge_kernel(meta, mine, other, *rest):
-    out, gtok = rest[-2:]
-    for side, src in ((0, mine), (1, other)):
-        @pl.when(pl.program_id(0) == side)
-        def _():
-            out[...] = src[0]
-            gtok[...] = src[1].astype(F32)
-
-
-def merge(meta, mine, other, into, n, first, step=2):
-    _, size, frames, width = mine.shape
-    blocks = size // step
-    spec_a = pl.BlockSpec((2, step, frames, width), lambda side, s, c: (0, s * (1 - side) + (blocks - 1) * side, 0, 0))
-    spec_b = pl.BlockSpec((2, step, frames, width), lambda side, s, c: (0, s * side, 0, 0))
-    dst = pl.BlockSpec((step, frames, width), lambda side, s, c: (((c[0] ^ side) * n + first) // step + s, 0, 0))
+    )(*fixed, *((other,) + tuple(into) if last_part else ()))
+
+
+def merge_kernel(meta, other, out_in, gtok_in, out, gtok):
+    out[...] = other[0]
+    gtok[...] = other[1].astype(F32)
+
+
+def merge(meta, other, into, n, first, step=2):
+    _, size, frames, width = other.shape
+    src = pl.BlockSpec((2, step, frames, width), lambda s, c: (0, s, 0, 0))
+    dst = pl.BlockSpec((step, frames, width), lambda s, c: (((1 - c[0]) * n + first) // step + s, 0, 0))
     return pl.pallas_call(
         merge_kernel,
         grid_spec=pltpu.PrefetchScalarGridSpec(
-            num_scalar_prefetch=1, grid=(2, blocks),
-            in_specs=[spec_a, spec_b] + [pl.BlockSpec(memory_space=pl.ANY)] * len(into), out_specs=[dst, dst]),
-        out_shape=[struct((2 * n, frames, width), BF), struct((2 * n, frames, width), F32)],
-        input_output_aliases={3: 0, 4: 1} if into else {},
+            num_scalar_prefetch=1, grid=(size // step,),
+            in_specs=[src] + [pl.BlockSpec(memory_space=pl.ANY)] * 2, out_specs=[dst, dst]),
+        out_shape=[struct(v.shape, v.dtype) for v in into],
+        input_output_aliases={2: 0, 3: 1},
         compiler_params=params(), cost_estimate=cost(20000000),
-    )(meta, mine, other, *into)
+    )(meta, other, *into)
 
 
 def shard_kernel(stay, *refs):
@@ -572,9 +634,8 @@
     buf_b = swap(buf_a, 1)
     buf_c = swap(buf_a, 2)
     buf_d = swap(buf_c, 1)
-    ad, nrm, low, inv, gbo = conv_norm(meta, tokens, cotangent, conv_weight, conv_bias,
-                                       norm_scale, norm_shift, layer_scale)
-    act, pre, win, wout, keep, send, gbi = hidden(meta, ad, low, buf_a, buf_b, h, n)
+    ad, nrm, low, inv, act, pre, win, wout, keep, send, gbo, gbi = front(
+        meta, tokens, cotangent, conv_weight, conv_bias, norm_scale, norm_shift, layer_scale, buf_a, buf_b, h)
     stay, leave = combine(meta, keep, swap(send, 1), dp)
     arrived = across(leave, 1)
     branch, ag = mix(meta, ad, low, act, pre, win, wout, bias_out, buf_c, buf_d, n)
@@ -582,25 +643,29 @@
     stay = (stay + arrived.astype(F32)).reshape(dp // 2, -1, LANES)
     pieces = [across(stay[d].astype(BF), 2 * d) for d in range(1, dp // 2)]
 
-    def finish_part(sums, branch, first):
-        return finish(meta, tokens, cotangent, branch, ag, nrm, inv, sums,
-                      gbo, gbi, conv_weight, norm_scale, layer_scale, first, n // 2)
-
-    both_1, sums = finish_part(None, branch, 0)
-    pieces, sums, branch = lax.optimization_barrier((pieces, sums, branch))
-    both_2, small_keep, small_send = finish_part(sums, branch, n // 2)
+    def finish_part(sums, branch, first, *more):
+        return finish(meta, tokens, cotangent, branch, ag, nrm, inv, sums, gbo, gbi, conv_weight, norm_scale,
+                      layer_scale, first, n // 2, *more)
+
+    *parts, both, sums = finish_part(None, branch, 0)
+    pieces, sums, branch, both = lax.optimization_barrier((pieces, sums, branch, both))
+    other = swap(both, 1)
     shard = make_shard(stay.reshape(-1, LANES), pieces)
     near = [shard] + [across(shard, 2 * d) for d in range(1, dp // 2)]
-    near, small_send, both_1, both_2 = lax.optimization_barrier((near, small_send, both_1, both_2))
+    *parts, both, small_keep, small_send = finish_part(sums, branch, n // 2, other, parts)
+    near, small_send, both = lax.optimization_barrier((near, small_send, both))
     small_got = swap(small_send, 1)
-    small_got, both_1, both_2 = lax.optimization_barrier((small_got, both_1, both_2))
+    small_got, both = lax.optimization_barrier((small_got, both))
     near = relay(near)
     far = across(near, 1)
     small = small_keep + small_got
-    for i in range(dp.bit_length() - 1):
+    got = across(small, 2)
+    out, gtok = merge(meta, swap(both, 1), parts, n, n // 2)
+    got, out, gtok = lax.optimization_barrier((got, out, gtok))
+    small = small + got
+    for i in range(2, dp.bit_length() - 1):
         small = small + across(small, 1 << i)
-    done = merge(meta, both_1, swap(both_1, 1), (), n, 0)
-    out, gtok = merge(meta, both_2, swap(both_2, 1), done, n, n // 2)
+    small = small + across(small, 1)
     far, out, gtok = lax.optimization_barrier((far, out, gtok))
     gcw, gcb, gns, gnsh, gwi, gbi, gwo, gbo, gls = unpack(meta, near, far, small, dp, taps, rates, width, h)
     return (out, gtok, gcw, gcb, gns, gnsh, gwi, gbi, gwo, gbo, gls)

time: 98.9 us -> 88 us (0.89); the launches traced: 97 us -> 87.9 us
  waiting for transfers between devices: 20.7 us -> 13.8 us
  starting transfers between devices: 18.9 us -> 16.5 us
    ppermute x11, waiting for transfers between devices: 17.7 us -> 7.59 us  [across(): return lax.ppermute(x, 'dp', [(i, i ^ step) for i in range(size)])]
    pallas_call x2, Pallas kernels: 13.7 us -> 20.6 us  [finish(): pl.pallas_call(functools.partial(finish_kernel, n, first, last_part), gri...]
    pallas_call x2 -> x1, Pallas kernels: 7.92 us -> 2.47 us  [merge(): pl.pallas_call(merge_kernel, grid_spec=pltpu.PrefetchScalarGridSpec(num_s...]
    ppermute x7, waiting for transfers between devices: 3.03 us -> 6.2 us  [swap(): return lax.ppermute(x, 'tp', [(i, i ^ step) for i in range(size)])]
    ppermute x11, starting transfers between devices: 14.5 us -> 12.8 us  [across(): return lax.ppermute(x, 'dp', [(i, i ^ step) for i in range(size)])]
    pallas_call x2 -> x1, Pallas kernels: 18.5 us -> 17.1 us  [front(): pl.pallas_call(functools.partial(front_kernel, n), grid_spec=pltpu.Prefet...]
  transfers between devices with their start and end apart: 18 -> 18, of which waited for: 6 -> 6; matrix products, arithmetic and copies ran while one was open for 1% -> 1% of each run, Pallas kernels for 54% -> 60%
where the time goes in v2:
time: 88 us; the launch traced here: 87.9 us
  Pallas kernels  55.9 us (64%)
  starting transfers between devices  16.5 us (19%)
  waiting for transfers between devices  13.8 us (16%)
  other arithmetic  0.88 us (1%)
    pallas_call x2, Pallas kernels, finish(): pl.pallas_call(functools.partial(finish_kernel, n, first, last_part), gri...  20.6 us
    pallas_call x1, Pallas kernels, front(): pl.pallas_call(functools.partial(front_kernel, n), grid_spec=pltpu.Prefet...  17.1 us
    ppermute x11, starting transfers between devices, across(): return lax.ppermute(x, 'dp', [(i, i ^ step) for i in range(size)])  12.8 us
    pallas_call x1, Pallas kernels, mix(): pl.pallas_call(functools.partial(mix_kernel, n), in_specs=[smem()] + [vme...  11.8 us
    ppermute x11, waiting for transfers between devices, across(): return lax.ppermute(x, 'dp', [(i, i ^ step) for i in range(size)])  7.59 us
    ppermute x7, waiting for transfers between devices, swap(): return lax.ppermute(x, 'tp', [(i, i ^ step) for i in range(size)])  6.2 us
    ppermute x7, starting transfers between devices, swap(): return lax.ppermute(x, 'tp', [(i, i ^ step) for i in range(size)])  3.66 us
    pallas_call x1, Pallas kernels, merge(): pl.pallas_call(merge_kernel, grid_spec=pltpu.PrefetchScalarGridSpec(num_s...  2.47 us
  transfers between devices with their start and end apart: 18, of which 6 were waited for; matrix products, arithmetic and copies ran while one was open for 1% of the time, Pallas kernels for 60%

profile of v2, /device:TPU:0, one launch (start us, length us, event | category | flops | bytes accessed | tf_op | source)
XLA Modules:
  0.0 87.9 jit_solution(15088307188317284205)
XLA Ops:
  0.6 1.3 %shard_map.212.buf_a = bf16[3088,128]{1,0:T(8,128)(2,1)S(1)} custom-call(bf16[512,384]{1,0:T(8,128)(2,1)} %wi.1, bf16[384]{0:T(512)(128)(2,1)} %bi.1, bf16[384,512]{1,0:T(8,128)(2,1)} %wo.1), custom_call_target="tpu_custom_call" | custom-call | tf_op jit(solution)/shard_map/pallas_call | solution.py:111
  1.9 0.5 collective-permute-start
  2.4 2.6 %collective-permute-start.3 = (bf16[3088,128]{1,0:T(8,128)(2,1)S(1)}, bf16[3088,128]{1,0:T(8,128)(2,1)S(1)}, u32[]{:S(2)}, u32[]{:S(2)}) collective-permute-start(bf16[3088,128]{1,0:T(8,128)(2,1)S(1)} %shard_map.212.buf_a), channel_id=1, source_target_pairs={{0,2},{1,3},{2,0},{3,1},{4,6},{5,7},{6,4},{7,5},{8,10},{9,11},{10,... | collective-permute-start | bytes 2371592 | tf_op jit(solution)/shard_map/ppermute | solution.py:612
  5.0 0.7 pad_add_fusion.meta
  5.8 0.0 collective-permute-done.buf_b
  5.8 17.1 %shard_map.213 = (bf16[2304,512]{1,0:T(8,128)(2,1)S(1)}, bf16[2304,512]{1,0:T(8,128)(2,1)S(1)}, bf16[2304,512]{1,0:T(8,128)(2,1)S(1)}, f32[2304,128]{1,0:T(8,128...) custom-call(s32[34]{0:T(128)S(1)} %pad_add_fusion.meta, ...), custom_call_target="tpu_custom_call" | custom-call | tf_op jit(solution)/shard_map/pallas_call | solution.py:291
  22.8 0.1 collective-permute-start.1
  22.9 0.3 collective-permute-done.3.buf_c
  23.2 0.2 collective-permute-start.4
  23.4 1.8 %collective-permute-done.1.recv = bf16[3072,128]{1,0:T(8,128)(2,1)S(1)} collective-permute-done((bf16[3072,128]{1,0:T(8,128)(2,1)S(1)}, bf16[3072,128]{1,0:T(8,128)(2,1)S(1)}, u32[]{:S(2)}, u32[]{:S(2)}) %collective-permute-start.1) | collective-permute-done | bytes 786464 | tf_op jit(solution)/shard_map/ppermute | solution.py:612
  25.2 0.7 shard_map.214
  25.9 1.4 %collective-permute-start.2 = (bf16[1536,128]{1,0:T(8,128)(2,1)S(1)}, bf16[1536,128]{1,0:T(8,128)(2,1)S(1)}, u32[]{:S(2)}, u32[]{:S(2)}) collective-permute-start(bf16[1536,128]{1,0:T(8,128)(2,1)S(1)} %get-tuple-element.72), channel_id=1, source_target_pairs={{0,4},{4,0},{8,12},{12,8},{16,20},{20,16},{24,28},{28,24},{1,5},{5... | collective-permute-start | bytes 1179656 | tf_op jit(solution)/shard_map/ppermute | solution.py:617
  27.3 0.0 collective-permute-done.4.buf_d
  27.3 11.8 %shard_map.215 = (f32[2304,512]{1,0:T(8,128)S(1)}, f32[2304,512]{1,0:T(8,128)S(1)}) custom-call(s32[34]{0:T(128)S(1)} %pad_add_fusion.meta, bf16[2304,512]{1,0:T(8,128)(2,1)S(1)} %get-tuple-element.73.ad, bf16[2304,512]{1,0:T(8,128)(2,1)S(1)} %get-tuple-element.74.low, bf16[2304,768]{1,0:T(8,128)(2,1)S(1)} %get-tuple-element.75.act, ...), custom_call_target="tpu_custom_call" | custom-call | tf_op jit(solution)/shard_map/pallas_call | solution.py:355
  39.1 0.0 collective-permute-done.2
  39.1 0.1 fusion
  39.2 2.4 %collective-permute-start.7 = (bf16[384,128]{1,0:T(8,128)(2,1)S(1)}, bf16[384,128]{1,0:T(8,128)(2,1)S(1)}, u32[]{:S(2)}, u32[]{:S(2)}) collective-permute-start(bf16[384,128]{1,0:T(8,128)(2,1)S(1)} %get-tuple-element.129), channel_id=1, source_target_pairs={{0,24},{4,28},{8,16},{12,20},{16,8},{20,12},{24,0},{28,4},{1,25},{... | collective-permute-start | bytes 294920 | tf_op jit(solution)/shard_map/ppermute | solution.py:617
  41.7 0.9 %collective-permute-start.6 = (bf16[384,128]{1,0:T(8,128)(2,1)S(1)}, bf16[384,128]{1,0:T(8,128)(2,1)S(1)}, u32[]{:S(2)}, u32[]{:S(2)}) collective-permute-start(bf16[384,128]{1,0:T(8,128)(2,1)S(1)} %get-tuple-element.130), channel_id=1, source_target_pairs={{0,16},{4,20},{8,24},{12,28},{16,0},{20,4},{24,8},{28,12},{1,17},{... | collective-permute-start | bytes 294920 | tf_op jit(solution)/shard_map/ppermute | solution.py:617
  42.6 1.1 %collective-permute-start.5 = (bf16[384,128]{1,0:T(8,128)(2,1)S(1)}, bf16[384,128]{1,0:T(8,128)(2,1)S(1)}, u32[]{:S(2)}, u32[]{:S(2)}) collective-permute-start(bf16[384,128]{1,0:T(8,128)(2,1)S(1)} %get-tuple-element.131), channel_id=1, source_target_pairs={{0,8},{4,12},{8,0},{12,4},{16,24},{20,28},{24,16},{28,20},{1,9},{5... | collective-permute-start | bytes 294920 | tf_op jit(solution)/shard_map/ppermute | solution.py:617
  43.7 8.1 %shard_map.216 = (bf16[16,256,512]{2,1,0:T(8,128)(2,1)}, f32[16,256,512]{2,1,0:T(8,128)}, bf16[2,4,256,512]{3,2,1,0:T(8,128)(2,1)S(1)}, f32[13,8,512]{2,1,0:T(8,128)S(1)}) custom-call(s32[34]{0:T(128)S(1)} %pad_add_fusion.meta, bf16[16,256,512]{2,1,0:T(8,128)(2,1)} %tok.5, bf16[16,256,512]{2,1,0:T(8,128)(2,1)} %cot.5, ...), custom_call_target="tpu_custom_call" | custom-call | bytes 40000000 | tf_op jit(solution)/shard_map/pallas_call | solution.py:516
  51.8 0.0 collective-permute-done.7.refs_2_
  51.8 0.0 collective-permute-done.6.refs_1_
  51.8 0.0 collective-permute-done.5.refs_0_
  51.8 0.1 collective-permute-start.11
  51.9 0.1 shard_map.217.refs_0_
  51.9 2.2 %collective-permute-start.10 = (bf16[384,128]{1,0:T(8,128)(2,1)S(1)}, bf16[384,128]{1,0:T(8,128)(2,1)S(1)}, u32[]{:S(2)}, u32[]{:S(2)}) collective-permute-start(bf16[384,128]{1,0:T(8,128)(2,1)S(1)} %shard_map.217.refs_0_), channel_id=1, source_target_pairs={{0,24},{4,28},{8,16},{12,20},{16,8},{20,12},{24,0},{28,4},{1,25},{... | collective-permute-start | bytes 294920 | tf_op jit(solution)/shard_map/ppermute | solution.py:617
  54.2 0.2 collective-permute-start.9
  54.4 2.0 %collective-permute-start.8 = (bf16[384,128]{1,0:T(8,128)(2,1)S(1)}, bf16[384,128]{1,0:T(8,128)(2,1)S(1)}, u32[]{:S(2)}, u32[]{:S(2)}) collective-permute-start(bf16[384,128]{1,0:T(8,128)(2,1)S(1)} %shard_map.217.refs_0_), channel_id=1, source_target_pairs={{0,8},{4,12},{8,0},{12,4},{16,24},{20,28},{24,16},{28,20},{1,9},{5... | collective-permute-start | bytes 294920 | tf_op jit(solution)/shard_map/ppermute | solution.py:617
  56.4 0.0 collective-permute-done.11.rest_0_
  56.4 12.5 %shard_map.218 = (bf16[16,256,512]{2,1,0:T(8,128)(2,1)}, f32[16,256,512]{2,1,0:T(8,128)}, bf16[2,4,256,512]{3,2,1,0:T(8,128)(2,1)S(1)}, f32[16,512]{1,0:T(8,128)S(1)}, f32[16,512]{1,0:T(8,128)S(1)}) custom-call(s32[34]{0:T(128)S(1)} %pad_add_fusion.meta, bf16[16,256,512]{2,1,0:T(8,128)(2,1)} %tok.5, ...), custom_call_target="tpu_custom_call", output_to_operand_aliasing={{0}: (14, {}), {1}: (15, {})} | custom-call | bytes 40000000 | tf_op jit(solution)/shard_map/pallas_call | solution.py:516
  68.9 0.0 collective-permute-done.10.refs_3_
  68.9 0.0 collective-permute-done.9.refs_2_
  68.9 0.0 collective-permute-done.8.refs_1_
  68.9 0.1 collective-permute-start.13
  69.0 1.2 %collective-permute-done.13 = f32[16,512]{1,0:T(8,128)S(1)} collective-permute-done((f32[16,512]{1,0:T(8,128)S(1)}, f32[16,512]{1,0:T(8,128)S(1)}, u32[]{:S(2)}, u32[]{:S(2)}) %collective-permute-start.13) | collective-permute-done | bytes 32800 | tf_op jit(solution)/shard_map/ppermute | solution.py:612
  70.2 0.2 collective-permute-start.15
  70.4 0.8 collective-permute-start.12
  71.2 0.2 collective-permute-start.14
  71.4 2.9 %collective-permute-done.15.other = bf16[2,4,256,512]{3,2,1,0:T(8,128)(2,1)S(1)} collective-permute-done((bf16[2,4,256,512]{3,2,1,0:T(8,128)(2,1)S(1)}, bf16[2,4,256,512]{3,2,1,0:T(8,128)(2,1)S(1)}, u32[]{:S(2)}, u32[]{:S(2)}) %collective-permute-start.15) | collective-permute-done | bytes 2097184 | tf_op jit(solution)/shard_map/ppermute | solution.py:612
  74.4 2.5 %shard_map.220 = (bf16[16,256,512]{2,1,0:T(8,128)(2,1)}, f32[16,256,512]{2,1,0:T(8,128)}) custom-call(s32[34]{0:T(128)S(1)} %pad_add_fusion.meta, bf16[2,4,256,512]{3,2,1,0:T(8,128)(2,1)S(1)} %collective-permute-done.15.other, bf16[16,256,512]{2,1,0:T(8,128)(2,1)} %get-tuple-element.108.out_in, ...), custom_call_target="tpu_custom_call", output_to_operand_aliasing={{0}: (2, {}), {1}: (3, {})} | custom-call | bytes 20000000 | tf_op jit(solution)/shard_map/pallas_call | solution.py:541
  76.8 0.0 collective-permute-done.14
  76.9 0.8 collective-permute-start.16
  77.6 4.4 %collective-permute-done.16 = f32[16,512]{1,0:T(8,128)S(1)} collective-permute-done((f32[16,512]{1,0:T(8,128)S(1)}, f32[16,512]{1,0:T(8,128)S(1)}, u32[]{:S(2)}, u32[]{:S(2)}) %collective-permute-start.16) | collective-permute-done | bytes 32800 | tf_op jit(solution)/shard_map/ppermute | solution.py:617
  82.1 0.8 collective-permute-start.17
  82.8 0.0 collective-permute-done.12.far
  82.8 3.1 %collective-permute-done.17 = f32[16,512]{1,0:T(8,128)S(1)} collective-permute-done((f32[16,512]{1,0:T(8,128)S(1)}, f32[16,512]{1,0:T(8,128)S(1)}, u32[]{:S(2)}, u32[]{:S(2)}) %collective-permute-start.17) | collective-permute-done | bytes 32800 | tf_op jit(solution)/shard_map/ppermute | solution.py:617
  86.0 1.9 %shard_map.221 = (f32[7,512]{1,0:T(8,128)}, f32[512]{0:T(512)}, f32[2,512]{1,0:T(2,128)}, f32[2,512]{1,0:T(2,128)}, f32[512,384]{1,0:T(8,128)}, /*index=5*/f32[3...) custom-call(s32[34]{0:T(128)S(1)} %pad_add_fusion.meta, bf16[1536,128]{1,0:T(8,128)(2,1)S(1)} %shard_map.219.near, ...), custom_call_target="tpu_custom_call" | custom-call | tf_op jit(solution)/shard_map/pallas_call | solution.py:603
  (6 shorter events, 0.1 us)
Async XLA Ops:
  1.9 3.8 %collective-permute-start = (bf16[3088,128]{1,0:T(8,128)(2,1)S(1)}, bf16[3088,128]{1,0:T(8,128)(2,1)S(1)}, u32[]{:S(2)}, u32[]{:S(2)}) collective-permute-start(bf16[3088,128]{1,0:T(8,128)(2,1)S(1)} %shard_map.212.buf_a), channel_id=1, source_target_pairs={{0,1},{1,0},{2,3},{3,2},{4,5},{5,4},{6,7},{7,6},{8,9},{9,8},{10,11... | collective-permute-start | bytes 2371592 | tf_op jit(solution)/shard_map/ppermute | solution.py:612
  2.4 20.8 %collective-permute-start.3 = (bf16[3088,128]{1,0:T(8,128)(2,1)S(1)}, bf16[3088,128]{1,0:T(8,128)(2,1)S(1)}, u32[]{:S(2)}, u32[]{:S(2)}) collective-permute-start(bf16[3088,128]{1,0:T(8,128)(2,1)S(1)} %shard_map.212.buf_a), channel_id=1, source_target_pairs={{0,2},{1,3},{2,0},{3,1},{4,6},{5,7},{6,4},{7,5},{8,10},{9,11},{10,... | collective-permute-start | bytes 2371592 | tf_op jit(solution)/shard_map/ppermute | solution.py:612
  22.8 2.4 %collective-permute-start.1 = (bf16[3072,128]{1,0:T(8,128)(2,1)S(1)}, bf16[3072,128]{1,0:T(8,128)(2,1)S(1)}, u32[]{:S(2)}, u32[]{:S(2)}) collective-permute-start(bf16[3072,128]{1,0:T(8,128)(2,1)S(1)} %get-tuple-element.70), channel_id=1, source_target_pairs={{0,1},{1,0},{2,3},{3,2},{4,5},{5,4},{6,7},{7,6},{8,9},{9,8},{10,11... | collective-permute-start | bytes 2359304 | tf_op jit(solution)/shard_map/ppermute | solution.py:612
  23.2 4.0 %collective-permute-start.4 = (bf16[3088,128]{1,0:T(8,128)(2,1)S(1)}, bf16[3088,128]{1,0:T(8,128)(2,1)S(1)}, u32[]{:S(2)}, u32[]{:S(2)}) collective-permute-start(bf16[3088,128]{1,0:T(8,128)(2,1)S(1)} %collective-permute-done.3.buf_c), channel_id=1, source_target_pairs={{0,1},{1,0},{2,3},{3,2},{4,5},{5,4},{6,7},{7,6},{8,9},{9,8},{10,11... | collective-permute-start | bytes 2371592 | tf_op jit(solution)/shard_map/ppermute | solution.py:612
  25.9 13.2 %collective-permute-start.2 = (bf16[1536,128]{1,0:T(8,128)(2,1)S(1)}, bf16[1536,128]{1,0:T(8,128)(2,1)S(1)}, u32[]{:S(2)}, u32[]{:S(2)}) collective-permute-start(bf16[1536,128]{1,0:T(8,128)(2,1)S(1)} %get-tuple-element.72), channel_id=1, source_target_pairs={{0,4},{4,0},{8,12},{12,8},{16,20},{20,16},{24,28},{28,24},{1,5},{5... | collective-permute-start | bytes 1179656 | tf_op jit(solution)/shard_map/ppermute | solution.py:617
  39.2 12.5 %collective-permute-start.7 = (bf16[384,128]{1,0:T(8,128)(2,1)S(1)}, bf16[384,128]{1,0:T(8,128)(2,1)S(1)}, u32[]{:S(2)}, u32[]{:S(2)}) collective-permute-start(bf16[384,128]{1,0:T(8,128)(2,1)S(1)} %get-tuple-element.129), channel_id=1, source_target_pairs={{0,24},{4,28},{8,16},{12,20},{16,8},{20,12},{24,0},{28,4},{1,25},{... | collective-permute-start | bytes 294920 | tf_op jit(solution)/shard_map/ppermute | solution.py:617
  41.7 10.1 %collective-permute-start.6 = (bf16[384,128]{1,0:T(8,128)(2,1)S(1)}, bf16[384,128]{1,0:T(8,128)(2,1)S(1)}, u32[]{:S(2)}, u32[]{:S(2)}) collective-permute-start(bf16[384,128]{1,0:T(8,128)(2,1)S(1)} %get-tuple-element.130), channel_id=1, source_target_pairs={{0,16},{4,20},{8,24},{12,28},{16,0},{20,4},{24,8},{28,12},{1,17},{... | collective-permute-start | bytes 294920 | tf_op jit(solution)/shard_map/ppermute | solution.py:617
  42.6 9.2 %collective-permute-start.5 = (bf16[384,128]{1,0:T(8,128)(2,1)S(1)}, bf16[384,128]{1,0:T(8,128)(2,1)S(1)}, u32[]{:S(2)}, u32[]{:S(2)}) collective-permute-start(bf16[384,128]{1,0:T(8,128)(2,1)S(1)} %get-tuple-element.131), channel_id=1, source_target_pairs={{0,8},{4,12},{8,0},{12,4},{16,24},{20,28},{24,16},{28,20},{1,9},{5... | collective-permute-start | bytes 294920 | tf_op jit(solution)/shard_map/ppermute | solution.py:617
  51.8 4.6 %collective-permute-start.11 = (bf16[2,4,256,512]{3,2,1,0:T(8,128)(2,1)S(1)}, bf16[2,4,256,512]{3,2,1,0:T(8,128)(2,1)S(1)}, u32[]{:S(2)}, u32[]{:S(2)}) collective-permute-start(bf16[2,4,256,512]{3,2,1,0:T(8,128)(2,1)S(1)} %get-tuple-element.94), channel_id=1, source_target_pairs={{0,1},{1,0},{2,3},{3,2},{4,5},{5,4},{6,7},{7,6},{8,9},{9,8},{10,11... | collective-permute-start | bytes 6291464 | tf_op jit(solution)/shard_map/ppermute | solution.py:612
  51.9 17.0 %collective-permute-start.10 = (bf16[384,128]{1,0:T(8,128)(2,1)S(1)}, bf16[384,128]{1,0:T(8,128)(2,1)S(1)}, u32[]{:S(2)}, u32[]{:S(2)}) collective-permute-start(bf16[384,128]{1,0:T(8,128)(2,1)S(1)} %shard_map.217.refs_0_), channel_id=1, source_target_pairs={{0,24},{4,28},{8,16},{12,20},{16,8},{20,12},{24,0},{28,4},{1,25},{... | collective-permute-start | bytes 294920 | tf_op jit(solution)/shard_map/ppermute | solution.py:617
  54.2 14.8 %collective-permute-start.9 = (bf16[384,128]{1,0:T(8,128)(2,1)S(1)}, bf16[384,128]{1,0:T(8,128)(2,1)S(1)}, u32[]{:S(2)}, u32[]{:S(2)}) collective-permute-start(bf16[384,128]{1,0:T(8,128)(2,1)S(1)} %shard_map.217.refs_0_), channel_id=1, source_target_pairs={{0,16},{4,20},{8,24},{12,28},{16,0},{20,4},{24,8},{28,12},{1,17},{... | collective-permute-start | bytes 294920 | tf_op jit(solution)/shard_map/ppermute | solution.py:617
  54.4 14.6 %collective-permute-start.8 = (bf16[384,128]{1,0:T(8,128)(2,1)S(1)}, bf16[384,128]{1,0:T(8,128)(2,1)S(1)}, u32[]{:S(2)}, u32[]{:S(2)}) collective-permute-start(bf16[384,128]{1,0:T(8,128)(2,1)S(1)} %shard_map.217.refs_0_), channel_id=1, source_target_pairs={{0,8},{4,12},{8,0},{12,4},{16,24},{20,28},{24,16},{28,20},{1,9},{5... | collective-permute-start | bytes 294920 | tf_op jit(solution)/shard_map/ppermute | solution.py:617
  68.9 1.3 %collective-permute-start.13 = (f32[16,512]{1,0:T(8,128)S(1)}, f32[16,512]{1,0:T(8,128)S(1)}, u32[]{:S(2)}, u32[]{:S(2)}) collective-permute-start(f32[16,512]{1,0:T(8,128)S(1)} %get-tuple-element.104), channel_id=1, source_target_pairs={{0,1},{1,0},{2,3},{3,2},{4,5},{5,4},{6,7},{7,6},{8,9},{9,8},{10,11... | collective-permute-start | bytes 98312 | tf_op jit(solution)/shard_map/ppermute | solution.py:612
  70.2 4.2 %collective-permute-start.15 = (bf16[2,4,256,512]{3,2,1,0:T(8,128)(2,1)S(1)}, bf16[2,4,256,512]{3,2,1,0:T(8,128)(2,1)S(1)}, u32[]{:S(2)}, u32[]{:S(2)}) collective-permute-start(bf16[2,4,256,512]{3,2,1,0:T(8,128)(2,1)S(1)} %get-tuple-element.107), channel_id=1, source_target_pairs={{0,1},{1,0},{2,3},{3,2},{4,5},{5,4},{6,7},{7,6},{8,9},{9,8},{10,11... | collective-permute-start | bytes 6291464 | tf_op jit(solution)/shard_map/ppermute | solution.py:612
  70.4 12.4 %collective-permute-start.12 = (bf16[1536,128]{1,0:T(8,128)(2,1)S(1)}, bf16[1536,128]{1,0:T(8,128)(2,1)S(1)}, u32[]{:S(2)}, u32[]{:S(2)}) collective-permute-start(bf16[1536,128]{1,0:T(8,128)(2,1)S(1)} %shard_map.219.near), channel_id=1, source_target_pairs={{0,4},{4,0},{8,12},{12,8},{16,20},{20,16},{24,28},{28,24},{1,5},{5... | collective-permute-start | bytes 1179656 | tf_op jit(solution)/shard_map/ppermute | solution.py:617
  71.2 5.6 %collective-permute-start.14 = (f32[16,512]{1,0:T(8,128)S(1)}, f32[16,512]{1,0:T(8,128)S(1)}, u32[]{:S(2)}, u32[]{:S(2)}) collective-permute-start(f32[16,512]{1,0:T(8,128)S(1)} %add.16), channel_id=1, source_target_pairs={{0,8},{4,12},{8,0},{12,4},{16,24},{20,28},{24,16},{28,20},{1,9},{5... | collective-permute-start | bytes 98312 | tf_op jit(solution)/shard_map/ppermute | solution.py:617
  76.9 5.2 %collective-permute-start.16 = (f32[16,512]{1,0:T(8,128)S(1)}, f32[16,512]{1,0:T(8,128)S(1)}, u32[]{:S(2)}, u32[]{:S(2)}) collective-permute-start(f32[16,512]{1,0:T(8,128)S(1)} %add.17), channel_id=1, source_target_pairs={{0,16},{4,20},{8,24},{12,28},{16,0},{20,4},{24,8},{28,12},{1,17},{... | collective-permute-start | bytes 98312 | tf_op jit(solution)/shard_map/ppermute | solution.py:617
  82.1 3.9 %collective-permute-start.17 = (f32[16,512]{1,0:T(8,128)S(1)}, f32[16,512]{1,0:T(8,128)S(1)}, u32[]{:S(2)}, u32[]{:S(2)}) collective-permute-start(f32[16,512]{1,0:T(8,128)S(1)} %add.18), channel_id=1, source_target_pairs={{0,4},{4,0},{8,12},{12,8},{16,20},{20,16},{24,28},{28,24},{1,5},{5... | collective-permute-start | bytes 98312 | tf_op jit(solution)/shard_map/ppermute | solution.py:617

commit v3 on v2

--- a/solution.py
+++ b/solution.py
@@ -365,40 +365,22 @@
     )(meta, ad, low, act, pre, win, wout, bout, buf_c, buf_d)
 
 
-def finish_kernel(n, first, last_part, meta, tok, cot, branch, ag, nrm, inv, sums_in, gbo, gbi, cw, ns,
-                  gamma, *rest):
-    other = rest[0]
-    (out, gtok, both), results, (offs, cgp, sums) = rest[3:6] if last_part else rest[:3], rest[6 if last_part else 3:-3], rest[-3:]
-    s = pl.program_id(0) + first
-
-    if last_part:
-        @pl.when(pl.program_id(1) == 1)
-        def _():
-            out[...] = other[0]
-            gtok[...] = other[1].astype(F32)
-
-        @pl.when(pl.program_id(1) == 0)
-        def _():
-            finish_item(n, s, first, last_part, meta, tok, cot, branch, ag, nrm, inv, sums_in, gbo, gbi, cw, ns, gamma,
-                        out, gtok, both, results, offs, cgp, sums)
-    else:
-        finish_item(n, s, first, last_part, meta, tok, cot, branch, ag, nrm, inv, sums_in, gbo, gbi, cw, ns, gamma,
-                    out, gtok, both, results, offs, cgp, sums)
-
-
-def finish_item(n, s, first, last_part, meta, tok, cot, branch, ag, nrm, inv, sums_in, gbo, gbi, cw, ns, gamma,
-                out, gtok, both, results, offs, cgp, sums):
+def norm_grad_kernel(n, meta, tok, cot, branch, ag, nrm, inv, gbo, gbi, cw, ns, gamma,
+                     out, out_own, cgp, small_keep, small_send, offs, sums, sems):
+    s = pl.program_id(0)
     frames, width = tok.shape[1], tok.shape[2]
     taps, rates = cw.shape[0], ns.shape[0]
     half = taps // 2
     wq = width // LANES
     h = gbi.shape[1] // 2
 
-    @pl.when(s == first)
+    def place(j):
+        return pltpu.make_async_copy(out_own.at[j], out.at[meta[0] * n + j], sems.at[j])
+
+    @pl.when(s == 0)
     def _():
         place_items(n, meta, offs)
-        sums[...] = sums_in[...] if last_part else jnp.zeros_like(sums)
-        cgp[...] = jnp.zeros_like(cgp)
+        sums[...] = jnp.zeros_like(sums)
 
     item = meta[0] * n + s
     count = meta[2 + item]
@@ -406,14 +388,13 @@
     off = offs[s]
     scale = pick(ns, group)
     gam = as_row(gamma)
-    w = cw[...].astype(F32)
     zero = jnp.zeros((8, LANES), F32)
     steps = pl.cdiv(count, WIDE_CHUNK)
 
     def step(i, accs):
         r0 = pl.multiple_of(i * WIDE_CHUNK, WIDE_CHUNK)
         here = pl.ds(r0, WIDE_CHUNK)
-        live = (lax.broadcasted_iota(jnp.int32, (WIDE_CHUNK, 1), 0) + r0) < count
+        live = (lax.broadcasted_iota(jnp.int32, (WIDE_CHUNK, LANES), 0) + r0) < count
         src = pl.ds(pl.multiple_of(off + r0, 16), WIDE_CHUNK)
         new = []
         ngs, nrs = [], []
@@ -421,9 +402,7 @@
             a_ls, a_sc, a_sh = accs[3 * q:3 * q + 3]
             br = jnp.where(live, branch[src, lane(q)], 0.0)
             tk = jnp.where(live, tok[0, here, lane(q)].astype(F32), 0.0)
-            value = (tk + gam[:, lane(q)] * br).astype(BF)
-            both[0, 0, here, lane(q)] = value
-            out[0, here, lane(q)] = value
+            out_own[s, here, lane(q)] = (tk + gam[:, lane(q)] * br).astype(BF)
             g = jnp.where(live, ag[src, lane(q)], 0.0)
             nr = nrm[src, lane(q)].astype(F32)
             new += [a_ls + fold(cot[0, here, lane(q)].astype(F32) * br), a_sc + fold(g * nr), a_sh + fold(g)]
@@ -435,7 +414,7 @@
         istd = inv[src, :]
         for q in range(wq):
             cg = istd * (ngs[q] - m1 - nrs[q] * m2)
-            cgp[q, pl.ds(pl.multiple_of(r0 + PAD, 8), WIDE_CHUNK), :] = jnp.where(live, cg, 0.0)
+            cgp[s, q, pl.ds(pl.multiple_of(r0 + PAD, 8), WIDE_CHUNK), :] = jnp.where(live, cg, 0.0)
         return tuple(new)
 
     accs = lax.fori_loop(0, steps, step, (zero,) * (3 * wq))
@@ -446,46 +425,36 @@
 
     def clear(i, _):
         r0 = pl.multiple_of(i * WIDE_CHUNK, WIDE_CHUNK)
-        here = pl.ds(r0, WIDE_CHUNK)
-        for ref in (both.at[0, 0], both.at[1, 0], out.at[0], gtok.at[0]):
-            ref[here, :] = jnp.zeros((WIDE_CHUNK, width), ref.dtype)
+        out_own[s, pl.ds(r0, WIDE_CHUNK), :] = jnp.zeros((WIDE_CHUNK, width), BF)
         for q in range(wq):
-            cgp[q, pl.ds(pl.multiple_of(r0 + PAD, 8), WIDE_CHUNK), :] = jnp.zeros((WIDE_CHUNK, LANES), F32)
+            cgp[s, q, pl.ds(pl.multiple_of(r0 + PAD, 8), WIDE_CHUNK), :] = jnp.zeros((WIDE_CHUNK, LANES), F32)
         return 0
 
     lax.fori_loop(steps, frames // WIDE_CHUNK, clear, 0)
-
+    place(s).start()
     for q in range(wq):
-        wl = w[:, lane(q)]
+        cgp[s, q, :PAD, :] = jnp.zeros((PAD, LANES), F32)
+        cgp[s, q, PAD + frames:, :] = jnp.zeros((cgp.shape[2] - PAD - frames, LANES), F32)
 
         def conv_step(i, accs):
             r0 = pl.multiple_of(i * WIDE_CHUNK, WIDE_CHUNK)
             here = pl.ds(r0, WIDE_CHUNK)
-            live = (lax.broadcasted_iota(jnp.int32, (WIDE_CHUNK, 1), 0) + r0) < count
+            live = (lax.broadcasted_iota(jnp.int32, (WIDE_CHUNK, LANES), 0) + r0) < count
             tk = jnp.where(live, tok[0, here, lane(q)].astype(F32), 0.0)
-            total = cot[0, here, lane(q)].astype(F32)
             new = []
             for k in range(taps):
-                sh = cgp[q, pl.ds(r0 + (PAD + half - k), WIDE_CHUNK), :]
-                total = total + wl[k:k + 1] * sh
+                sh = cgp[s, q, pl.ds(r0 + (PAD + half - k), WIDE_CHUNK), :]
                 new.append(accs[k] + fold(tk * sh))
                 if k == half:
                     new_bias = accs[taps] + fold(sh)
-            total = jnp.where(live, total, 0.0).astype(BF)
-            both[1, 0, here, lane(q)] = total
-            gtok[0, here, lane(q)] = total.astype(F32)
             return tuple(new) + (new_bias,)
 
         accs = lax.fori_loop(0, steps, conv_step, (zero,) * (taps + 1))
         for k in range(taps + 1):
             sums[k, :, lane(q)] += accs[k]
 
-    @pl.when(pl.program_id(0) == pl.num_programs(0) - 1)
-    def _():
-        if not last_part:
-            results[0][...] = sums[...]
-            return
-        small_keep, small_send = results
+    @pl.when(s == n - 1)
+    def _():
         last = taps + 2 + 2 * rates
         rows = [jnp.sum(sums[i], axis=0, keepdims=True) for i in range(last)]
         rows.append(jnp.sum(gbo[...], axis=0, keepdims=True))
@@ -495,87 +464,167 @@
         for side, dst in ((0, small_keep), (1, small_send)):
             tail = [jnp.concatenate([gb[:, side * h:(side + 1) * h], fill], axis=1)]
             dst[...] = jnp.concatenate(rows + tail + spare, axis=0)
-
-
-def finish(meta, tok, cot, branch, ag, nrm, inv, sums, gbo, gbi, cw, ns, gamma, first, size, other=None, into=()):
+        for j in range(n):
+            place(j).wait()
+
+
+def norm_grad(meta, tok, cot, branch, ag, nrm, inv, gbo, gbi, cw, ns, gamma):
     items, frames, width = tok.shape
     n = items // 2
-    last_part = first + size == n
     wq = width // LANES
     taps, rates = cw.shape[0], ns.shape[0]
     n_small = -(-(taps + 4 + 2 * rates) // 8) * 8
-    sums_shape = (taps + 2 + 2 * rates, 8, width)
-    item = pl.BlockSpec((1, frames, width), lambda s, p, c: (c[0] * n + first + s, 0, 0))
-    mine = pl.BlockSpec((2, 1, frames, width), lambda s, p, c: (0, s, 0, 0))
-    dst = pl.BlockSpec((1, frames, width), lambda s, p, c: ((c[0] ^ p) * n + first * (1 - p) + s, 0, 0))
-    more = [(n_small, width)] * 2 if last_part else [sums_shape]
-    if sums is None:
-        sums = gbo
-    fixed = [meta, tok, cot, branch, ag, nrm, inv, sums, gbo, gbi, cw, ns, gamma]
-    extra = [mine] + [pl.BlockSpec(memory_space=pl.ANY)] * 2 if last_part else []
+    item = pl.BlockSpec((1, frames, width), lambda s, c: (c[0] * n + s, 0, 0))
     return pl.pallas_call(
-        functools.partial(finish_kernel, n, first, last_part),
+        functools.partial(norm_grad_kernel, n),
         grid_spec=pltpu.PrefetchScalarGridSpec(
-            num_scalar_prefetch=1, grid=(size, 2 if last_part else 1),
-            in_specs=[item, item] + [vmem()] * 7 + [whole(v.shape) for v in (cw, ns, gamma)] + extra,
-            out_specs=[dst, dst, mine] + [vmem()] * len(more),
+            num_scalar_prefetch=1, grid=(n,),
+            in_specs=[item, item] + [vmem()] * 6 + [whole(v.shape) for v in (cw, ns, gamma)],
+            out_specs=[hbm()] + [vmem()] * 4,
             scratch_shapes=[pltpu.SMEM((n + 2,), jnp.int32),
-                            pltpu.VMEM((wq, frames + 4 * PAD, LANES), F32),
-                            pltpu.VMEM(sums_shape, F32)]),
-        out_shape=[struct((items, frames, width), BF), struct((items, frames, width), F32),
-                   struct((2, size, frames, width), BF)] + [struct(v, F32) for v in more],
-        input_output_aliases={14: 0, 15: 1} if last_part else {},
+                            pltpu.VMEM((taps + 2 + 2 * rates, 8, width), F32),
+                            pltpu.SemaphoreType.DMA((n,))]),
+        out_shape=[struct((items, frames, width), BF), struct((n, frames, width), BF),
+                   struct((n, wq, frames + 4 * PAD, LANES), F32)] + [struct((n_small, width), F32)] * 2,
         compiler_params=params(), cost_estimate=cost(40000000),
-    )(*fixed, *((other,) + tuple(into) if last_part else ()))
-
-
-def merge_kernel(meta, other, out_in, gtok_in, out, gtok):
-    out[...] = other[0]
-    gtok[...] = other[1].astype(F32)
-
-
-def merge(meta, other, into, n, first, step=2):
-    _, size, frames, width = other.shape
-    src = pl.BlockSpec((2, step, frames, width), lambda s, c: (0, s, 0, 0))
-    dst = pl.BlockSpec((step, frames, width), lambda s, c: (((1 - c[0]) * n + first) // step + s, 0, 0))
+    )(meta, tok, cot, branch, ag, nrm, inv, gbo, gbi, cw, ns, gamma)
+
+
+def token_grad_kernel(n, meta, cot, cgp, cw, other, out_in, out, gtok, gtok_own, stage, sems, out_sem):
+    s = pl.program_id(0)
+    frames, width = cot.shape[1], cot.shape[2]
+    taps = cw.shape[0]
+    half = taps // 2
+    wq = width // LANES
+    count = meta[2 + meta[0] * n + s]
+    w = cw[...].astype(F32)
+    steps = pl.cdiv(count, CHUNK)
+    other_copy = pltpu.make_async_copy(other, out.at[pl.ds((1 - meta[0]) * n, n)], out_sem)
+
+    def place(j):
+        return pltpu.make_async_copy(stage.at[j], gtok.at[meta[0] * n + j], sems.at[j])
+
+    @pl.when(s == 0)
+    def _():
+        other_copy.start()
+
+    for q in range(wq):
+        wl = w[:, lane(q)]
+
+        def conv_step(i, _):
+            r0 = pl.multiple_of(i * CHUNK, CHUNK)
+            here = pl.ds(r0, CHUNK)
+            live = (lax.broadcasted_iota(jnp.int32, (CHUNK, LANES), 0) + r0) < count
+            total = cot[0, here, lane(q)].astype(F32)
+            for k in range(taps):
+                total = total + wl[k:k + 1] * cgp[s, q, pl.ds(r0 + (PAD + half - k), CHUNK), :]
+            total = jnp.where(live, total, 0.0).astype(BF)
+            gtok_own[s, here, lane(q)] = total
+            stage[s, here, lane(q)] = total.astype(F32)
+            return 0
+
+        lax.fori_loop(0, steps, conv_step, 0)
+
+    def clear(i, _):
+        here = pl.ds(pl.multiple_of(i * CHUNK, CHUNK), CHUNK)
+        gtok_own[s, here, :] = jnp.zeros((CHUNK, width), BF)
+        stage[s, here, :] = jnp.zeros((CHUNK, width), F32)
+        return 0
+
+    lax.fori_loop(steps, frames // CHUNK, clear, 0)
+    place(s).start()
+
+    @pl.when(s == n - 1)
+    def _():
+        other_copy.wait()
+        for j in range(n):
+            place(j).wait()
+
+
+def token_grad(meta, cot, cgp, cw, other, out):
+    items, frames, width = cot.shape
+    n = items // 2
+    item = pl.BlockSpec((1, frames, width), lambda s, c: (c[0] * n + s, 0, 0))
     return pl.pallas_call(
-        merge_kernel,
+        functools.partial(token_grad_kernel, n),
         grid_spec=pltpu.PrefetchScalarGridSpec(
-            num_scalar_prefetch=1, grid=(size // step,),
-            in_specs=[src] + [pl.BlockSpec(memory_space=pl.ANY)] * 2, out_specs=[dst, dst]),
-        out_shape=[struct(v.shape, v.dtype) for v in into],
-        input_output_aliases={2: 0, 3: 1},
+            num_scalar_prefetch=1, grid=(n,),
+            in_specs=[item, vmem(), whole(cw.shape), hbm(), hbm()], out_specs=[hbm(), hbm(), vmem()],
+            scratch_shapes=[pltpu.VMEM((n, frames, width), F32), pltpu.SemaphoreType.DMA((n,)), pltpu.SemaphoreType.DMA]),
+        out_shape=[struct(out.shape, BF), struct(out.shape, F32), struct((n, frames, width), BF)],
+        input_output_aliases={5: 0},
+        compiler_params=params(), cost_estimate=cost(40000000),
+    )(meta, cot, cgp, cw, other, out)
+
+
+def merge_kernel(n, meta, other, gtok_in, gtok, stage, sems):
+    copies = [pltpu.make_async_copy(stage.at[j], gtok.at[(1 - meta[0]) * n + j], sems.at[j]) for j in range(n)]
+    for j in range(n):
+        stage[j] = other[j].astype(F32)
+        copies[j].start()
+    for c in copies:
+        c.wait()
+
+
+def merge(meta, other, gtok):
+    n = other.shape[0]
+    return pl.pallas_call(
+        functools.partial(merge_kernel, n),
+        in_specs=[smem(), vmem(), hbm()], out_specs=hbm(), out_shape=struct(gtok.shape, F32),
+        scratch_shapes=[pltpu.VMEM(other.shape, F32), pltpu.SemaphoreType.DMA((n,))],
+        input_output_aliases={2: 0},
         compiler_params=params(), cost_estimate=cost(20000000),
-    )(meta, other, *into)
-
-
-def shard_kernel(stay, *refs):
+    )(meta, other, gtok)
+
+
+def put_small(small, dst, base):
+    high = small.astype(BF)
+    low = (small - high.astype(F32)).astype(BF)
+    rows = small.shape[0]
+    dst[base:base + rows, :] = high
+    dst[base + rows:base + 2 * rows, :] = low
+
+
+def get_small(src, base):
+    rows = (src.shape[0] - base) // 2
+    return src[base:base + rows, :].astype(F32) + src[base + rows:base + 2 * rows, :].astype(F32)
+
+
+def message_kernel(stay, keep, recv, *refs):
     pieces, out = refs[:-1], refs[-1]
-    total = stay[:out.shape[0], :]
+    m = pieces[0].shape[0]
+    total = stay[:m, :]
     for piece in pieces:
         total = total + piece[...].astype(F32)
-    out[...] = total.astype(BF)
-
-
-def make_shard(stay, pieces):
-    return pl.pallas_call(shard_kernel, in_specs=[vmem()] * (1 + len(pieces)), out_specs=vmem(),
-                          out_shape=struct(pieces[0].shape, BF), compiler_params=params())(stay, *pieces)
-
-
-def relay_kernel(*refs):
+    out[:m, :] = total.astype(BF)
+    small = keep[...] + recv[...]
+    put_small(jnp.concatenate([small[:, lane(q)] for q in range(small.shape[1] // LANES)], axis=0), out, m)
+
+
+def make_message(stay, keep, recv, pieces):
+    rows = pieces[0].shape[0] + 2 * keep.size // LANES
+    return pl.pallas_call(message_kernel, in_specs=[vmem()] * (3 + len(pieces)), out_specs=vmem(),
+                          out_shape=struct((rows, LANES), BF), compiler_params=params())(stay, keep, recv, *pieces)
+
+
+def relay_kernel(m, *refs):
     sources, out = refs[:-1], refs[-1]
-    m = sources[0].shape[0]
+    sums = []
     for d, src in enumerate(sources):
-        out[d * m:(d + 1) * m, :] = src[...]
-
-
-def relay(sources):
-    m = sources[0].shape[0]
-    return pl.pallas_call(relay_kernel, in_specs=[vmem()] * len(sources), out_specs=vmem(),
-                          out_shape=struct((len(sources) * m, LANES), BF), compiler_params=params())(*sources)
-
-
-def unpack_kernel(dp, taps, rates, meta, near, far, small, gcw, gcb, gns, gnsh, gwi, gbi, gwo, gbo, gls, full):
+        out[d * m:(d + 1) * m, :] = src[:m, :]
+        sums.append(get_small(src, m))
+    while len(sums) > 1:
+        sums = [a + b for a, b in zip(sums[::2], sums[1::2])]
+    put_small(sums[0], out, len(sources) * m)
+
+
+def relay(m, sources):
+    rows = len(sources) * m + sources[0].shape[0] - m
+    return pl.pallas_call(functools.partial(relay_kernel, m), in_specs=[vmem()] * len(sources), out_specs=vmem(),
+                          out_shape=struct((rows, LANES), BF), compiler_params=params())(*sources)
+
+
+def unpack_kernel(dp, taps, rates, meta, near, far, gcw, gcb, gns, gnsh, gwi, gbi, gwo, gbo, gls, full):
     h, width = gwo.shape
     wq, hq = width // LANES, h // LANES
     m = full.shape[0] // dp
@@ -588,6 +637,9 @@
     base = wq * h
     for q in range(hq):
         gwi[:, lane(q)] = full[base + q * width:base + (q + 1) * width, :]
+    small = get_small(near, dp // 2 * m) + get_small(far, dp // 2 * m)
+    rows = small.shape[0] // wq
+    small = jnp.concatenate([small[q * rows:(q + 1) * rows] for q in range(wq)], axis=1)
     gcw[...] = small[:taps]
     gcb[...] = small[taps]
     gls[...] = small[taps + 1]
@@ -598,13 +650,13 @@
     gbi[...] = small[at + 1, :h]
 
 
-def unpack(meta, near, far, small, dp, taps, rates, width, h):
+def unpack(meta, near, far, dp, taps, rates, width, h):
     shapes = [(taps, width), (width,), (rates, width), (rates, width), (width, h), (h,), (h, width), (width,), (width,)]
     return pl.pallas_call(
-        functools.partial(unpack_kernel, dp, taps, rates), in_specs=[smem(), vmem(), vmem(), vmem()],
+        functools.partial(unpack_kernel, dp, taps, rates), in_specs=[smem(), vmem(), vmem()],
         out_shape=[struct(s, F32) for s in shapes],
         scratch_shapes=[pltpu.VMEM((2 * width * h // LANES, LANES), F32)],
-        compiler_params=params())(meta, near, far, small)
+        compiler_params=params())(meta, near, far)
 
 
 def swap(x, step):
@@ -643,31 +695,20 @@
     stay = (stay + arrived.astype(F32)).reshape(dp // 2, -1, LANES)
     pieces = [across(stay[d].astype(BF), 2 * d) for d in range(1, dp // 2)]
 
-    def finish_part(sums, branch, first, *more):
-        return finish(meta, tokens, cotangent, branch, ag, nrm, inv, sums, gbo, gbi, conv_weight, norm_scale,
-                      layer_scale, first, n // 2, *more)
-
-    *parts, both, sums = finish_part(None, branch, 0)
-    pieces, sums, branch, both = lax.optimization_barrier((pieces, sums, branch, both))
-    other = swap(both, 1)
-    shard = make_shard(stay.reshape(-1, LANES), pieces)
-    near = [shard] + [across(shard, 2 * d) for d in range(1, dp // 2)]
-    *parts, both, small_keep, small_send = finish_part(sums, branch, n // 2, other, parts)
-    near, small_send, both = lax.optimization_barrier((near, small_send, both))
+    out, out_own, cgp, small_keep, small_send = norm_grad(
+        meta, tokens, cotangent, branch, ag, nrm, inv, gbo, gbi, conv_weight, norm_scale, layer_scale)
+    pieces, small_send, out_own, cgp = lax.optimization_barrier((pieces, small_send, out_own, cgp))
     small_got = swap(small_send, 1)
-    small_got, both = lax.optimization_barrier((small_got, both))
-    near = relay(near)
+    small_got, out_own = lax.optimization_barrier((small_got, out_own))
+    message = make_message(stay.reshape(-1, LANES), small_keep, small_got, pieces)
+    near = [message] + [across(message, 2 * d) for d in range(1, dp // 2)]
+    out, gtok, gtok_own = token_grad(meta, cotangent, cgp, conv_weight, swap(out_own, 1), out)
+    near, gtok_own = lax.optimization_barrier((near, gtok_own))
+    near = relay(pieces[0].shape[0], near)
     far = across(near, 1)
-    small = small_keep + small_got
-    got = across(small, 2)
-    out, gtok = merge(meta, swap(both, 1), parts, n, n // 2)
-    got, out, gtok = lax.optimization_barrier((got, out, gtok))
-    small = small + got
-    for i in range(2, dp.bit_length() - 1):
-        small = small + across(small, 1 << i)
-    small = small + across(small, 1)
-    far, out, gtok = lax.optimization_barrier((far, out, gtok))
-    gcw, gcb, gns, gnsh, gwi, gbi, gwo, gbo, gls = unpack(meta, near, far, small, dp, taps, rates, width, h)
+    gtok = merge(meta, swap(gtok_own, 1), gtok)
+    far, gtok = lax.optimization_barrier((far, gtok))
+    gcw, gcb, gns, gnsh, gwi, gbi, gwo, gbo, gls = unpack(meta, near, far, dp, taps, rates, width, h)
     return (out, gtok, gcw, gcb, gns, gnsh, gwi, gbi, gwo, gbo, gls)
 
 

time: 88 us -> 85.1 us (0.967)
  Pallas kernels: 55.9 us -> 53.8 us
    pallas_call x5, Pallas kernels: 23.2 us -> 21.3 us  [the longest x1 10.3 us: norm_grad(): pl.pallas_call(functools.partial(norm_grad_kernel, n), grid_spec=pltpu.Pr...]
    ppermute x11 -> x8, waiting for transfers between devices: 7.59 us -> 8.33 us  [across(): return lax.ppermute(x, 'dp', [(i, i ^ step) for i in range(size)])]
    ppermute x11 -> x8, starting transfers between devices: 12.8 us -> 12.5 us  [across(): return lax.ppermute(x, 'dp', [(i, i ^ step) for i in range(size)])]
  transfers between devices with their start and end apart: 18 -> 15, of which waited for: 6 -> 6; matrix products, arithmetic and copies ran while one was open for 1% -> 1% of each run, Pallas kernels for 60% -> 59%
where the time goes in v3:
time: 85.1 us; the launch traced here: 85.3 us
  Pallas kernels  53.8 us (63%)
  starting transfers between devices  15.8 us (19%)
  waiting for transfers between devices  14 us (16%)
    pallas_call x1, Pallas kernels, front(): pl.pallas_call(functools.partial(front_kernel, n), grid_spec=pltpu.Prefet...  16.8 us
    ppermute x8, starting transfers between devices, across(): return lax.ppermute(x, 'dp', [(i, i ^ step) for i in range(size)])  12.5 us
    pallas_call x1, Pallas kernels, mix(): pl.pallas_call(functools.partial(mix_kernel, n), in_specs=[smem()] + [vme...  11.8 us
    pallas_call x1, Pallas kernels, norm_grad(): pl.pallas_call(functools.partial(norm_grad_kernel, n), grid_spec=pltpu.Pr...  10.3 us
    ppermute x8, waiting for transfers between devices, across(): return lax.ppermute(x, 'dp', [(i, i ^ step) for i in range(size)])  8.33 us
    pallas_call x1, Pallas kernels, token_grad(): pl.pallas_call(functools.partial(token_grad_kernel, n), grid_spec=pltpu.P...  8.28 us
    ppermute x7, waiting for transfers between devices, swap(): return lax.ppermute(x, 'tp', [(i, i ^ step) for i in range(size)])  5.65 us
    ppermute x7, starting transfers between devices, swap(): return lax.ppermute(x, 'tp', [(i, i ^ step) for i in range(size)])  3.39 us
  transfers between devices with their start and end apart: 15, of which 6 were waited for; matrix products, arithmetic and copies ran while one was open for 1% of the time, Pallas kernels for 59%

profile of v3, /device:TPU:0, one launch (start us, length us, event | category | flops | bytes accessed | tf_op | source)
XLA Modules:
  0.0 85.3 jit_solution(15429786531109526590)
XLA Ops:
  0.6 1.3 %shard_map.212.buf_a = bf16[3088,128]{1,0:T(8,128)(2,1)S(1)} custom-call(bf16[512,384]{1,0:T(8,128)(2,1)} %wi.1, bf16[384]{0:T(512)(128)(2,1)} %bi.1, bf16[384,512]{1,0:T(8,128)(2,1)} %wo.1), custom_call_target="tpu_custom_call" | custom-call | tf_op jit(solution)/shard_map/pallas_call | solution.py:111
  1.9 0.5 collective-permute-start
  2.4 2.6 %collective-permute-start.3 = (bf16[3088,128]{1,0:T(8,128)(2,1)S(1)}, bf16[3088,128]{1,0:T(8,128)(2,1)S(1)}, u32[]{:S(2)}, u32[]{:S(2)}) collective-permute-start(bf16[3088,128]{1,0:T(8,128)(2,1)S(1)} %shard_map.212.buf_a), channel_id=1, source_target_pairs={{0,2},{1,3},{2,0},{3,1},{4,6},{5,7},{6,4},{7,5},{8,10},{9,11},{10,... | collective-permute-start | bytes 2371592 | tf_op jit(solution)/shard_map/ppermute | solution.py:664
  5.0 0.7 pad_add_fusion.meta
  5.8 0.0 collective-permute-done.buf_b
  5.8 16.8 %shard_map.213 = (bf16[2304,512]{1,0:T(8,128)(2,1)S(1)}, bf16[2304,512]{1,0:T(8,128)(2,1)S(1)}, bf16[2304,512]{1,0:T(8,128)(2,1)S(1)}, f32[2304,128]{1,0:T(8,128...) custom-call(s32[34]{0:T(128)S(1)} %pad_add_fusion.meta, ...), custom_call_target="tpu_custom_call" | custom-call | tf_op jit(solution)/shard_map/pallas_call | solution.py:291
  22.6 0.1 collective-permute-start.1
  22.7 0.6 collective-permute-done.3.buf_c
  23.2 0.0 collective-permute-start.4
  23.2 1.7 %collective-permute-done.1.recv = bf16[3072,128]{1,0:T(8,128)(2,1)S(1)} collective-permute-done((bf16[3072,128]{1,0:T(8,128)(2,1)S(1)}, bf16[3072,128]{1,0:T(8,128)(2,1)S(1)}, u32[]{:S(2)}, u32[]{:S(2)}) %collective-permute-start.1) | collective-permute-done | bytes 786464 | tf_op jit(solution)/shard_map/ppermute | solution.py:664
  24.9 0.7 shard_map.214
  25.6 1.6 %collective-permute-start.2 = (bf16[1536,128]{1,0:T(8,128)(2,1)S(1)}, bf16[1536,128]{1,0:T(8,128)(2,1)S(1)}, u32[]{:S(2)}, u32[]{:S(2)}) collective-permute-start(bf16[1536,128]{1,0:T(8,128)(2,1)S(1)} %get-tuple-element.64), channel_id=1, source_target_pairs={{0,4},{4,0},{8,12},{12,8},{16,20},{20,16},{24,28},{28,24},{1,5},{5... | collective-permute-start | bytes 1179656 | tf_op jit(solution)/shard_map/ppermute | solution.py:669
  27.3 0.0 collective-permute-done.4.buf_d
  27.3 11.8 %shard_map.215 = (f32[2304,512]{1,0:T(8,128)S(1)}, f32[2304,512]{1,0:T(8,128)S(1)}) custom-call(s32[34]{0:T(128)S(1)} %pad_add_fusion.meta, bf16[2304,512]{1,0:T(8,128)(2,1)S(1)} %get-tuple-element.65.ad, bf16[2304,512]{1,0:T(8,128)(2,1)S(1)} %get-tuple-element.66.low, bf16[2304,768]{1,0:T(8,128)(2,1)S(1)} %get-tuple-element.67.act, ...), custom_call_target="tpu_custom_call" | custom-call | tf_op jit(solution)/shard_map/pallas_call | solution.py:355
  39.1 0.0 collective-permute-done.2
  39.1 0.1 fusion
  39.2 3.5 %collective-permute-start.7 = (bf16[384,128]{1,0:T(8,128)(2,1)S(1)}, bf16[384,128]{1,0:T(8,128)(2,1)S(1)}, u32[]{:S(2)}, u32[]{:S(2)}) collective-permute-start(bf16[384,128]{1,0:T(8,128)(2,1)S(1)} %get-tuple-element.113), channel_id=1, source_target_pairs={{0,24},{4,28},{8,16},{12,20},{16,8},{20,12},{24,0},{28,4},{1,25},{... | collective-permute-start | bytes 294920 | tf_op jit(solution)/shard_map/ppermute | solution.py:669
  42.7 0.7 collective-permute-start.6
  43.4 0.3 collective-permute-start.5
  43.7 10.3 %shard_map.216 = (bf16[16,256,512]{2,1,0:T(8,128)(2,1)}, bf16[8,256,512]{2,1,0:T(8,128)(2,1)S(1)}, f32[8,4,288,128]{3,2,1,0:T(8,128)S(1)}, f32[16,512]{1,0:T(8,128)S(1)}, f32[16,512]{1,0:T(8,128)S(1)}) custom-call(s32[34]{0:T(128)S(1)} %pad_add_fusion.meta, bf16[16,256,512]{2,1,0:T(8,128)(2,1)} %tok.3, bf16[16,256,512]{2,1,0:T(8,128)(2,1)} %cot.5, ...), custom_call_target="tpu_custom_call" | custom-call | bytes 40000000 | tf_op jit(solution)/shard_map/pallas_call | solution.py:478
  54.0 0.0 collective-permute-done.7.refs_2_
  54.0 0.0 collective-permute-done.6.refs_1_
  54.0 0.0 collective-permute-done.5.refs_0_
  54.0 0.1 collective-permute-start.8
  54.1 1.2 %collective-permute-done.8.recv = f32[16,512]{1,0:T(8,128)S(1)} collective-permute-done((f32[16,512]{1,0:T(8,128)S(1)}, f32[16,512]{1,0:T(8,128)S(1)}, u32[]{:S(2)}, u32[]{:S(2)}) %collective-permute-start.8) | collective-permute-done | bytes 32800 | tf_op jit(solution)/shard_map/ppermute | solution.py:664
  55.3 0.2 collective-permute-start.9
  55.5 0.1 shard_map.218.refs_0_
  55.5 3.5 %collective-permute-start.12 = (bf16[512,128]{1,0:T(8,128)(2,1)S(1)}, bf16[512,128]{1,0:T(8,128)(2,1)S(1)}, u32[]{:S(2)}, u32[]{:S(2)}) collective-permute-start(bf16[512,128]{1,0:T(8,128)(2,1)S(1)} %shard_map.218.refs_0_), channel_id=1, source_target_pairs={{0,24},{4,28},{8,16},{12,20},{16,8},{20,12},{24,0},{28,4},{1,25},{... | collective-permute-start | bytes 393224 | tf_op jit(solution)/shard_map/ppermute | solution.py:669
  59.0 0.0 collective-permute-start.11
  59.0 1.0 %collective-permute-start.10 = (bf16[512,128]{1,0:T(8,128)(2,1)S(1)}, bf16[512,128]{1,0:T(8,128)(2,1)S(1)}, u32[]{:S(2)}, u32[]{:S(2)}) collective-permute-start(bf16[512,128]{1,0:T(8,128)(2,1)S(1)} %shard_map.218.refs_0_), channel_id=1, source_target_pairs={{0,8},{4,12},{8,0},{12,4},{16,24},{20,28},{24,16},{28,20},{1,9},{5... | collective-permute-start | bytes 393224 | tf_op jit(solution)/shard_map/ppermute | solution.py:669
  60.0 0.0 collective-permute-done.9.other
  60.0 8.3 %shard_map.217 = (bf16[16,256,512]{2,1,0:T(8,128)(2,1)}, f32[16,256,512]{2,1,0:T(8,128)}, bf16[8,256,512]{2,1,0:T(8,128)(2,1)S(1)}) custom-call(s32[34]{0:T(128)S(1)} %pad_add_fusion.meta, bf16[16,256,512]{2,1,0:T(8,128)(2,1)} %cot.5, f32[8,4,288,128]{3,2,1,0:T(8,128)S(1)} %get-tuple-element.82.cgp, ...), custom_call_target="tpu_custom_call", output_to_operand_aliasing={{0}: (5, {})} | custom-call | bytes 40000000 | tf_op jit(solution)/shard_map/pallas_call | solution.py:548
  68.3 0.0 collective-permute-done.12.refs_3_
  68.3 2.7 %collective-permute-done.11.refs_2_ = bf16[512,128]{1,0:T(8,128)(2,1)S(1)} collective-permute-done((bf16[512,128]{1,0:T(8,128)(2,1)S(1)}, bf16[512,128]{1,0:T(8,128)(2,1)S(1)}, u32[]{:S(2)}, u32[]{:S(2)}) %collective-permute-start.11) | collective-permute-done | bytes 131104 | tf_op jit(solution)/shard_map/ppermute | solution.py:669
  70.9 0.0 collective-permute-done.10.refs_1_
  70.9 0.0 collective-permute-start.14
  71.0 1.9 %collective-permute-start.13 = (bf16[1664,128]{1,0:T(8,128)(2,1)S(1)}, bf16[1664,128]{1,0:T(8,128)(2,1)S(1)}, u32[]{:S(2)}, u32[]{:S(2)}) collective-permute-start(bf16[1664,128]{1,0:T(8,128)(2,1)S(1)} %shard_map.219.near), channel_id=1, source_target_pairs={{0,4},{4,0},{8,12},{12,8},{16,20},{20,16},{24,28},{28,24},{1,5},{5... | collective-permute-start | bytes 1277960 | tf_op jit(solution)/shard_map/ppermute | solution.py:669
  72.9 2.2 %collective-permute-done.14.other = bf16[8,256,512]{2,1,0:T(8,128)(2,1)S(1)} collective-permute-done((bf16[8,256,512]{2,1,0:T(8,128)(2,1)S(1)}, bf16[8,256,512]{2,1,0:T(8,128)(2,1)S(1)}, u32[]{:S(2)}, u32[]{:S(2)}) %collective-permute-start.14) | collective-permute-done | bytes 2097184 | tf_op jit(solution)/shard_map/ppermute | solution.py:664
  75.1 2.6 %shard_map.220 = f32[16,256,512]{2,1,0:T(8,128)} custom-call(s32[34]{0:T(128)S(1)} %pad_add_fusion.meta, bf16[8,256,512]{2,1,0:T(8,128)(2,1)S(1)} %collective-permute-done.14.other, f32[16,256,512]{2,1,0:T(8,128)} %get-tuple-element.99.gtok_in), custom_call_target="tpu_custom_call", output_to_operand_aliasing={{}: (2, {})} | custom-call | bytes 20000000 | tf_op jit(solution)/shard_map/pallas_call | solution.py:571
  77.8 5.7 %collective-permute-done.13.far = bf16[1664,128]{1,0:T(8,128)(2,1)S(1)} collective-permute-done((bf16[1664,128]{1,0:T(8,128)(2,1)S(1)}, bf16[1664,128]{1,0:T(8,128)(2,1)S(1)}, u32[]{:S(2)}, u32[]{:S(2)}) %collective-permute-start.13) | collective-permute-done | bytes 426016 | tf_op jit(solution)/shard_map/ppermute | solution.py:669
  83.4 1.9 %shard_map.221 = (f32[7,512]{1,0:T(8,128)}, f32[512]{0:T(512)}, f32[2,512]{1,0:T(2,128)}, f32[2,512]{1,0:T(2,128)}, f32[512,384]{1,0:T(8,128)}, /*index=5*/f32[3...) custom-call(s32[34]{0:T(128)S(1)} %pad_add_fusion.meta, bf16[1664,128]{1,0:T(8,128)(2,1)S(1)} %shard_map.219.near, ...), custom_call_target="tpu_custom_call" | custom-call | tf_op jit(solution)/shard_map/pallas_call | solution.py:655
  (2 shorter events, 0.1 us)
Async XLA Ops:
  1.9 3.8 %collective-permute-start = (bf16[3088,128]{1,0:T(8,128)(2,1)S(1)}, bf16[3088,128]{1,0:T(8,128)(2,1)S(1)}, u32[]{:S(2)}, u32[]{:S(2)}) collective-permute-start(bf16[3088,128]{1,0:T(8,128)(2,1)S(1)} %shard_map.212.buf_a), channel_id=1, source_target_pairs={{0,1},{1,0},{2,3},{3,2},{4,5},{5,4},{6,7},{7,6},{8,9},{9,8},{10,11... | collective-permute-start | bytes 2371592 | tf_op jit(solution)/shard_map/ppermute | solution.py:664
  2.4 20.8 %collective-permute-start.3 = (bf16[3088,128]{1,0:T(8,128)(2,1)S(1)}, bf16[3088,128]{1,0:T(8,128)(2,1)S(1)}, u32[]{:S(2)}, u32[]{:S(2)}) collective-permute-start(bf16[3088,128]{1,0:T(8,128)(2,1)S(1)} %shard_map.212.buf_a), channel_id=1, source_target_pairs={{0,2},{1,3},{2,0},{3,1},{4,6},{5,7},{6,4},{7,5},{8,10},{9,11},{10,... | collective-permute-start | bytes 2371592 | tf_op jit(solution)/shard_map/ppermute | solution.py:664
  22.6 2.4 %collective-permute-start.1 = (bf16[3072,128]{1,0:T(8,128)(2,1)S(1)}, bf16[3072,128]{1,0:T(8,128)(2,1)S(1)}, u32[]{:S(2)}, u32[]{:S(2)}) collective-permute-start(bf16[3072,128]{1,0:T(8,128)(2,1)S(1)} %get-tuple-element.62), channel_id=1, source_target_pairs={{0,1},{1,0},{2,3},{3,2},{4,5},{5,4},{6,7},{7,6},{8,9},{9,8},{10,11... | collective-permute-start | bytes 2359304 | tf_op jit(solution)/shard_map/ppermute | solution.py:664
  23.2 4.0 %collective-permute-start.4 = (bf16[3088,128]{1,0:T(8,128)(2,1)S(1)}, bf16[3088,128]{1,0:T(8,128)(2,1)S(1)}, u32[]{:S(2)}, u32[]{:S(2)}) collective-permute-start(bf16[3088,128]{1,0:T(8,128)(2,1)S(1)} %collective-permute-done.3.buf_c), channel_id=1, source_target_pairs={{0,1},{1,0},{2,3},{3,2},{4,5},{5,4},{6,7},{7,6},{8,9},{9,8},{10,11... | collective-permute-start | bytes 2371592 | tf_op jit(solution)/shard_map/ppermute | solution.py:664
  25.6 13.4 %collective-permute-start.2 = (bf16[1536,128]{1,0:T(8,128)(2,1)S(1)}, bf16[1536,128]{1,0:T(8,128)(2,1)S(1)}, u32[]{:S(2)}, u32[]{:S(2)}) collective-permute-start(bf16[1536,128]{1,0:T(8,128)(2,1)S(1)} %get-tuple-element.64), channel_id=1, source_target_pairs={{0,4},{4,0},{8,12},{12,8},{16,20},{20,16},{24,28},{28,24},{1,5},{5... | collective-permute-start | bytes 1179656 | tf_op jit(solution)/shard_map/ppermute | solution.py:669
  39.2 14.8 %collective-permute-start.7 = (bf16[384,128]{1,0:T(8,128)(2,1)S(1)}, bf16[384,128]{1,0:T(8,128)(2,1)S(1)}, u32[]{:S(2)}, u32[]{:S(2)}) collective-permute-start(bf16[384,128]{1,0:T(8,128)(2,1)S(1)} %get-tuple-element.113), channel_id=1, source_target_pairs={{0,24},{4,28},{8,16},{12,20},{16,8},{20,12},{24,0},{28,4},{1,25},{... | collective-permute-start | bytes 294920 | tf_op jit(solution)/shard_map/ppermute | solution.py:669
  42.7 11.3 %collective-permute-start.6 = (bf16[384,128]{1,0:T(8,128)(2,1)S(1)}, bf16[384,128]{1,0:T(8,128)(2,1)S(1)}, u32[]{:S(2)}, u32[]{:S(2)}) collective-permute-start(bf16[384,128]{1,0:T(8,128)(2,1)S(1)} %get-tuple-element.114), channel_id=1, source_target_pairs={{0,16},{4,20},{8,24},{12,28},{16,0},{20,4},{24,8},{28,12},{1,17},{... | collective-permute-start | bytes 294920 | tf_op jit(solution)/shard_map/ppermute | solution.py:669
  43.4 10.6 %collective-permute-start.5 = (bf16[384,128]{1,0:T(8,128)(2,1)S(1)}, bf16[384,128]{1,0:T(8,128)(2,1)S(1)}, u32[]{:S(2)}, u32[]{:S(2)}) collective-permute-start(bf16[384,128]{1,0:T(8,128)(2,1)S(1)} %get-tuple-element.115), channel_id=1, source_target_pairs={{0,8},{4,12},{8,0},{12,4},{16,24},{20,28},{24,16},{28,20},{1,9},{5... | collective-permute-start | bytes 294920 | tf_op jit(solution)/shard_map/ppermute | solution.py:669
  54.0 1.3 %collective-permute-start.8 = (f32[16,512]{1,0:T(8,128)S(1)}, f32[16,512]{1,0:T(8,128)S(1)}, u32[]{:S(2)}, u32[]{:S(2)}) collective-permute-start(f32[16,512]{1,0:T(8,128)S(1)} %get-tuple-element.83), channel_id=1, source_target_pairs={{0,1},{1,0},{2,3},{3,2},{4,5},{5,4},{6,7},{7,6},{8,9},{9,8},{10,11... | collective-permute-start | bytes 98312 | tf_op jit(solution)/shard_map/ppermute | solution.py:664
  55.3 4.7 %collective-permute-start.9 = (bf16[8,256,512]{2,1,0:T(8,128)(2,1)S(1)}, bf16[8,256,512]{2,1,0:T(8,128)(2,1)S(1)}, u32[]{:S(2)}, u32[]{:S(2)}) collective-permute-start(bf16[8,256,512]{2,1,0:T(8,128)(2,1)S(1)} %get-tuple-element.85), channel_id=1, source_target_pairs={{0,1},{1,0},{2,3},{3,2},{4,5},{5,4},{6,7},{7,6},{8,9},{9,8},{10,11... | collective-permute-start | bytes 6291464 | tf_op jit(solution)/shard_map/ppermute | solution.py:664
  55.5 12.7 %collective-permute-start.12 = (bf16[512,128]{1,0:T(8,128)(2,1)S(1)}, bf16[512,128]{1,0:T(8,128)(2,1)S(1)}, u32[]{:S(2)}, u32[]{:S(2)}) collective-permute-start(bf16[512,128]{1,0:T(8,128)(2,1)S(1)} %shard_map.218.refs_0_), channel_id=1, source_target_pairs={{0,24},{4,28},{8,16},{12,20},{16,8},{20,12},{24,0},{28,4},{1,25},{... | collective-permute-start | bytes 393224 | tf_op jit(solution)/shard_map/ppermute | solution.py:669
  59.0 11.9 %collective-permute-start.11 = (bf16[512,128]{1,0:T(8,128)(2,1)S(1)}, bf16[512,128]{1,0:T(8,128)(2,1)S(1)}, u32[]{:S(2)}, u32[]{:S(2)}) collective-permute-start(bf16[512,128]{1,0:T(8,128)(2,1)S(1)} %shard_map.218.refs_0_), channel_id=1, source_target_pairs={{0,16},{4,20},{8,24},{12,28},{16,0},{20,4},{24,8},{28,12},{1,17},{... | collective-permute-start | bytes 393224 | tf_op jit(solution)/shard_map/ppermute | solution.py:669
  59.0 11.9 %collective-permute-start.10 = (bf16[512,128]{1,0:T(8,128)(2,1)S(1)}, bf16[512,128]{1,0:T(8,128)(2,1)S(1)}, u32[]{:S(2)}, u32[]{:S(2)}) collective-permute-start(bf16[512,128]{1,0:T(8,128)(2,1)S(1)} %shard_map.218.refs_0_), channel_id=1, source_target_pairs={{0,8},{4,12},{8,0},{12,4},{16,24},{20,28},{24,16},{28,20},{1,9},{5... | collective-permute-start | bytes 393224 | tf_op jit(solution)/shard_map/ppermute | solution.py:669
  70.9 4.2 %collective-permute-start.14 = (bf16[8,256,512]{2,1,0:T(8,128)(2,1)S(1)}, bf16[8,256,512]{2,1,0:T(8,128)(2,1)S(1)}, u32[]{:S(2)}, u32[]{:S(2)}) collective-permute-start(bf16[8,256,512]{2,1,0:T(8,128)(2,1)S(1)} %get-tuple-element.98), channel_id=1, source_target_pairs={{0,1},{1,0},{2,3},{3,2},{4,5},{5,4},{6,7},{7,6},{8,9},{9,8},{10,11... | collective-permute-start | bytes 6291464 | tf_op jit(solution)/shard_map/ppermute | solution.py:664
  71.0 12.4 %collective-permute-start.13 = (bf16[1664,128]{1,0:T(8,128)(2,1)S(1)}, bf16[1664,128]{1,0:T(8,128)(2,1)S(1)}, u32[]{:S(2)}, u32[]{:S(2)}) collective-permute-start(bf16[1664,128]{1,0:T(8,128)(2,1)S(1)} %shard_map.219.near), channel_id=1, source_target_pairs={{0,4},{4,0},{8,12},{12,8},{16,20},{20,16},{24,28},{28,24},{1,5},{5... | collective-permute-start | bytes 1277960 | tf_op jit(solution)/shard_map/ppermute | solution.py:669

commit v4 on v3

--- a/solution.py
+++ b/solution.py
@@ -92,9 +92,12 @@
     offs[n + 1] = (end + TILE - 1) // TILE
 
 
-def pack_kernel(wi, bi, wo, out):
+def pack_kernel(n, wi, bi, wo, counts, groups, out, meta, counts_s, groups_s, sems):
     width, h = wi.shape
     hq, wq = h // LANES, width // LANES
+    copies = [pltpu.make_async_copy(counts, counts_s, sems.at[0]), pltpu.make_async_copy(groups, groups_s, sems.at[1])]
+    for c in copies:
+        c.start()
     for q in range(hq):
         out[q * width:(q + 1) * width, :] = wi[:, lane(q)]
     base = hq * width
@@ -104,12 +107,25 @@
     bias = bi[...].astype(F32).reshape(1, h)
     rows = [bias[:, lane(q)] for q in range(hq)] + [jnp.zeros((1, LANES), F32)] * (16 - hq)
     out[base:base + 16, :] = jnp.concatenate(rows, axis=0).astype(BF)
-
-
-def pack(wi, bi, wo):
+    meta[0] = lax.axis_index("tp") & 1
+    meta[1] = lax.axis_index("dp")
+    for c in copies:
+        c.wait()
+    for j in range(2 * n):
+        meta[2 + j] = counts_s[j]
+        meta[2 + 2 * n + j] = groups_s[j]
+
+
+def pack(wi, bi, wo, counts, groups):
     rows = 2 * wi.size // LANES + 16
-    return pl.pallas_call(pack_kernel, out_shape=struct((rows, LANES), BF),
-                          compiler_params=params())(wi, bi, wo)
+    items = counts.shape[0]
+    return pl.pallas_call(
+        functools.partial(pack_kernel, items // 2),
+        in_specs=[whole(wi.shape), whole(bi.shape), whole(wo.shape), hbm(), hbm()],
+        out_specs=[whole((rows, LANES)), smem()],
+        out_shape=[struct((rows, LANES), BF), struct((2 + 2 * items,), jnp.int32)],
+        scratch_shapes=[pltpu.SMEM((items,), jnp.int32), pltpu.SMEM((items,), jnp.int32), pltpu.SemaphoreType.DMA((2,))],
+        compiler_params=params())(wi, bi, wo, counts, groups)
 
 
 def weight_copies(buf, side, win, wout, bias, sems):
@@ -577,67 +593,61 @@
     )(meta, other, gtok)
 
 
-def put_small(small, dst, base):
-    high = small.astype(BF)
-    low = (small - high.astype(F32)).astype(BF)
-    rows = small.shape[0]
-    dst[base:base + rows, :] = high
-    dst[base + rows:base + 2 * rows, :] = low
-
-
-def get_small(src, base):
-    rows = (src.shape[0] - base) // 2
-    return src[base:base + rows, :].astype(F32) + src[base + rows:base + 2 * rows, :].astype(F32)
-
-
 def message_kernel(stay, keep, recv, *refs):
-    pieces, out = refs[:-1], refs[-1]
+    pieces, (out, mine) = refs[:-2], refs[-2:]
     m = pieces[0].shape[0]
     total = stay[:m, :]
     for piece in pieces:
         total = total + piece[...].astype(F32)
     out[:m, :] = total.astype(BF)
-    small = keep[...] + recv[...]
-    put_small(jnp.concatenate([small[:, lane(q)] for q in range(small.shape[1] // LANES)], axis=0), out, m)
+    mine[...] = total.astype(BF)
+    small = (keep[...] + recv[...]).astype(BF)
+    rows = small.shape[0]
+    for q in range(small.shape[1] // LANES):
+        out[m + q * rows:m + (q + 1) * rows, :] = small[:, lane(q)]
 
 
 def make_message(stay, keep, recv, pieces):
-    rows = pieces[0].shape[0] + 2 * keep.size // LANES
-    return pl.pallas_call(message_kernel, in_specs=[vmem()] * (3 + len(pieces)), out_specs=vmem(),
-                          out_shape=struct((rows, LANES), BF), compiler_params=params())(stay, keep, recv, *pieces)
+    rows = pieces[0].shape[0] + keep.size // LANES
+    return pl.pallas_call(message_kernel, in_specs=[vmem()] * (3 + len(pieces)), out_specs=[vmem(), vmem()],
+                          out_shape=[struct((rows, LANES), BF), struct(pieces[0].shape, BF)],
+                          compiler_params=params())(stay, keep, recv, *pieces)
 
 
 def relay_kernel(m, *refs):
     sources, out = refs[:-1], refs[-1]
     sums = []
     for d, src in enumerate(sources):
-        out[d * m:(d + 1) * m, :] = src[:m, :]
-        sums.append(get_small(src, m))
+        if d > 0:
+            out[(d - 1) * m:d * m, :] = src[:m, :]
+        sums.append(src[m:, :].astype(F32))
     while len(sums) > 1:
         sums = [a + b for a, b in zip(sums[::2], sums[1::2])]
-    put_small(sums[0], out, len(sources) * m)
+    out[(len(sources) - 1) * m:, :] = sums[0].astype(BF)
 
 
 def relay(m, sources):
-    rows = len(sources) * m + sources[0].shape[0] - m
+    rows = (len(sources) - 1) * m + sources[0].shape[0] - m
     return pl.pallas_call(functools.partial(relay_kernel, m), in_specs=[vmem()] * len(sources), out_specs=vmem(),
                           out_shape=struct((rows, LANES), BF), compiler_params=params())(*sources)
 
 
-def unpack_kernel(dp, taps, rates, meta, near, far, gcw, gcb, gns, gnsh, gwi, gbi, gwo, gbo, gls, full):
+def unpack_kernel(dp, taps, rates, meta, mine, theirs, near, far, gcw, gcb, gns, gnsh, gwi, gbi, gwo, gbo, gls, full):
     h, width = gwo.shape
     wq, hq = width // LANES, h // LANES
     m = full.shape[0] // dp
-    for odd, mess in ((0, near), (1, far)):
+    for odd, first, others in ((0, mine, near), (1, theirs, far)):
         for d in range(dp // 2):
+            piece = others[(d - 1) * m:d * m, :] if d else first[:m, :]
             at = pl.multiple_of((meta[1] ^ (2 * d + odd)) * m, m)
-            full[pl.ds(at, m), :] = mess[d * m:(d + 1) * m, :].astype(F32)
+            full[pl.ds(at, m), :] = piece.astype(F32)
     for q in range(wq):
         gwo[:, lane(q)] = full[q * h:(q + 1) * h, :]
     base = wq * h
     for q in range(hq):
         gwi[:, lane(q)] = full[base + q * width:base + (q + 1) * width, :]
-    small = get_small(near, dp // 2 * m) + get_small(far, dp // 2 * m)
+    behind = (dp // 2 - 1) * m
+    small = near[behind:, :].astype(F32) + far[behind:, :].astype(F32)
     rows = small.shape[0] // wq
     small = jnp.concatenate([small[q * rows:(q + 1) * rows] for q in range(wq)], axis=1)
     gcw[...] = small[:taps]
@@ -650,13 +660,13 @@
     gbi[...] = small[at + 1, :h]
 
 
-def unpack(meta, near, far, dp, taps, rates, width, h):
+def unpack(meta, mine, theirs, near, far, dp, taps, rates, width, h):
     shapes = [(taps, width), (width,), (rates, width), (rates, width), (width, h), (h,), (h, width), (width,), (width,)]
     return pl.pallas_call(
-        functools.partial(unpack_kernel, dp, taps, rates), in_specs=[smem(), vmem(), vmem()],
+        functools.partial(unpack_kernel, dp, taps, rates), in_specs=[smem()] + [vmem()] * 4,
         out_shape=[struct(s, F32) for s in shapes],
         scratch_shapes=[pltpu.VMEM((2 * width * h // LANES, LANES), F32)],
-        compiler_params=params())(meta, near, far)
+        compiler_params=params())(meta, mine, theirs, near, far)
 
 
 def swap(x, step):
@@ -674,15 +684,12 @@
     width, h = weight_in.shape
     n = tokens.shape[0] // 2
     (tokens, cotangent, conv_weight, conv_bias, norm_scale, norm_shift, weight_in, bias_in, weight_out, bias_out,
-     layer_scale) = [pltpu.with_memory_space_constraint(v, pltpu.HBM) for v in (
+     layer_scale, frame_counts, rate_groups) = [pltpu.with_memory_space_constraint(v, pltpu.HBM) for v in (
          tokens, cotangent, conv_weight, conv_bias, norm_scale, norm_shift, weight_in, bias_in, weight_out, bias_out,
-         layer_scale)]
+         layer_scale, frame_counts, rate_groups)]
     taps, rates = conv_weight.shape[0], norm_scale.shape[0]
     dp = lax.axis_size("dp")
-    place = jnp.stack([lax.axis_index("tp") & 1, lax.axis_index("dp")]).astype(jnp.int32)
-    meta = jnp.concatenate([place, frame_counts, rate_groups])
-
-    buf_a = pack(weight_in, bias_in, weight_out)
+    buf_a, meta = pack(weight_in, bias_in, weight_out, frame_counts, rate_groups)
     buf_b = swap(buf_a, 1)
     buf_c = swap(buf_a, 2)
     buf_d = swap(buf_c, 1)
@@ -700,15 +707,17 @@
     pieces, small_send, out_own, cgp = lax.optimization_barrier((pieces, small_send, out_own, cgp))
     small_got = swap(small_send, 1)
     small_got, out_own = lax.optimization_barrier((small_got, out_own))
-    message = make_message(stay.reshape(-1, LANES), small_keep, small_got, pieces)
+    message, mine = make_message(stay.reshape(-1, LANES), small_keep, small_got, pieces)
+    m = pieces[0].shape[0]
     near = [message] + [across(message, 2 * d) for d in range(1, dp // 2)]
+    theirs = across(mine, 1)
     out, gtok, gtok_own = token_grad(meta, cotangent, cgp, conv_weight, swap(out_own, 1), out)
-    near, gtok_own = lax.optimization_barrier((near, gtok_own))
-    near = relay(pieces[0].shape[0], near)
+    near, theirs, gtok_own = lax.optimization_barrier((near, theirs, gtok_own))
+    near = relay(m, near)
     far = across(near, 1)
     gtok = merge(meta, swap(gtok_own, 1), gtok)
     far, gtok = lax.optimization_barrier((far, gtok))
-    gcw, gcb, gns, gnsh, gwi, gbi, gwo, gbo, gls = unpack(meta, near, far, dp, taps, rates, width, h)
+    gcw, gcb, gns, gnsh, gwi, gbi, gwo, gbo, gls = unpack(meta, mine, theirs, near, far, dp, taps, rates, width, h)
     return (out, gtok, gcw, gcb, gns, gnsh, gwi, gbi, gwo, gbo, gls)
 
 

time: 85.1 us -> 82.4 us (0.968)
  waiting for transfers between devices: 14 us -> 9.31 us
  Pallas kernels: 53.8 us -> 55.3 us
    ppermute x8 -> x9, waiting for transfers between devices: 8.33 us -> 3.08 us  [across(): return lax.ppermute(x, 'dp', [(i, i ^ step) for i in range(size)])]
    pallas_call x1, Pallas kernels: 1.28 us -> 2.43 us  [pack(): pl.pallas_call(functools.partial(pack_kernel, items // 2), in_specs=[whol...]
    ppermute x8 -> x9, starting transfers between devices: 12.5 us -> 12.9 us  [across(): return lax.ppermute(x, 'dp', [(i, i ^ step) for i in range(size)])]
  transfers between devices with their start and end apart: 15 -> 16, of which waited for: 6 -> 5; matrix products, arithmetic and copies ran while one was open for 1% -> 0% of each run, Pallas kernels for 59% -> 62%
where the time goes in v4:
time: 82.4 us; the launch traced here: 82.1 us
  Pallas kernels  55.3 us (67%)
  starting transfers between devices  16.5 us (20%)
  waiting for transfers between devices  9.31 us (11%)
    pallas_call x1, Pallas kernels, front(): pl.pallas_call(functools.partial(front_kernel, n), grid_spec=pltpu.Prefet...  17.1 us
    ppermute x9, starting transfers between devices, across(): return lax.ppermute(x, 'dp', [(i, i ^ step) for i in range(size)])  12.9 us
    pallas_call x1, Pallas kernels, mix(): pl.pallas_call(functools.partial(mix_kernel, n), in_specs=[smem()] + [vme...  11.8 us
    pallas_call x1, Pallas kernels, norm_grad(): pl.pallas_call(functools.partial(norm_grad_kernel, n), grid_spec=pltpu.Pr...  10.3 us
    pallas_call x1, Pallas kernels, token_grad(): pl.pallas_call(functools.partial(token_grad_kernel, n), grid_spec=pltpu.P...  8.33 us
    ppermute x7, waiting for transfers between devices, swap(): return lax.ppermute(x, 'tp', [(i, i ^ step) for i in range(size)])  6.23 us
    ppermute x7, starting transfers between devices, swap(): return lax.ppermute(x, 'tp', [(i, i ^ step) for i in range(size)])  3.62 us
    ppermute x9, waiting for transfers between devices, across(): return lax.ppermute(x, 'dp', [(i, i ^ step) for i in range(size)])  3.08 us
  transfers between devices with their start and end apart: 16, of which 5 were waited for; matrix products, arithmetic and copies ran while one was open for 0% of the time, Pallas kernels for 62%

profile of v4, /device:TPU:0, one launch (start us, length us, event | category | flops | bytes accessed | tf_op | source)
XLA Modules:
  0.0 82.1 jit_solution(17080248180389140777)
XLA Ops:
  0.6 2.4 %shard_map.212 = (bf16[3088,128]{1,0:T(8,128)(2,1)S(1)}, s32[34]{0:T(128)S(1)}) custom-call(bf16[512,384]{1,0:T(8,128)(2,1)} %wi.1, bf16[384]{0:T(512)(128)(2,1)} %bi.1, bf16[384,512]{1,0:T(8,128)(2,1)} %wo.1, s32[16]{0:T(128)} %counts.1, s32[16]{0:T(128)} %groups.1), custom_call_target="tpu_custom_call" | custom-call | tf_op jit(solution)/shard_map/pallas_call | solution.py:122
  3.1 0.5 collective-permute-start
  3.6 2.6 %collective-permute-start.3 = (bf16[3088,128]{1,0:T(8,128)(2,1)S(1)}, bf16[3088,128]{1,0:T(8,128)(2,1)S(1)}, u32[]{:S(2)}, u32[]{:S(2)}) collective-permute-start(bf16[3088,128]{1,0:T(8,128)(2,1)S(1)} %get-tuple-element.67.buf_a), channel_id=1, source_target_pairs={{0,2},{1,3},{2,0},{3,1},{4,6},{5,7},{6,4},{7,5},{8,10},{9,11},{10,... | collective-permute-start | bytes 2371592 | tf_op jit(solution)/shard_map/ppermute | solution.py:674
  6.2 0.0 collective-permute-done.buf_b
  6.2 17.1 %shard_map.213 = (bf16[2304,512]{1,0:T(8,128)(2,1)S(1)}, bf16[2304,512]{1,0:T(8,128)(2,1)S(1)}, bf16[2304,512]{1,0:T(8,128)(2,1)S(1)}, f32[2304,128]{1,0:T(8,128...) custom-call(s32[34]{0:T(128)S(1)} %get-tuple-element.66.meta, ...), custom_call_target="tpu_custom_call" | custom-call | tf_op jit(solution)/shard_map/pallas_call | solution.py:307
  23.3 0.2 collective-permute-start.1
  23.5 0.9 %collective-permute-done.3.buf_c = bf16[3088,128]{1,0:T(8,128)(2,1)S(1)} collective-permute-done((bf16[3088,128]{1,0:T(8,128)(2,1)S(1)}, bf16[3088,128]{1,0:T(8,128)(2,1)S(1)}, u32[]{:S(2)}, u32[]{:S(2)}) %collective-permute-start.3) | collective-permute-done | bytes 790560 | tf_op jit(solution)/shard_map/ppermute | solution.py:674
  24.4 0.0 collective-permute-start.4
  24.4 1.3 %collective-permute-done.1.recv = bf16[3072,128]{1,0:T(8,128)(2,1)S(1)} collective-permute-done((bf16[3072,128]{1,0:T(8,128)(2,1)S(1)}, bf16[3072,128]{1,0:T(8,128)(2,1)S(1)}, u32[]{:S(2)}, u32[]{:S(2)}) %collective-permute-start.1) | collective-permute-done | bytes 786464 | tf_op jit(solution)/shard_map/ppermute | solution.py:674
  25.6 0.7 shard_map.214
  26.3 2.1 %collective-permute-start.2 = (bf16[1536,128]{1,0:T(8,128)(2,1)S(1)}, bf16[1536,128]{1,0:T(8,128)(2,1)S(1)}, u32[]{:S(2)}, u32[]{:S(2)}) collective-permute-start(bf16[1536,128]{1,0:T(8,128)(2,1)S(1)} %get-tuple-element.71), channel_id=1, source_target_pairs={{0,4},{4,0},{8,12},{12,8},{16,20},{20,16},{24,28},{28,24},{1,5},{5... | collective-permute-start | bytes 1179656 | tf_op jit(solution)/shard_map/ppermute | solution.py:679
  28.4 0.0 collective-permute-done.4.buf_d
  28.4 11.8 %shard_map.215 = (f32[2304,512]{1,0:T(8,128)S(1)}, f32[2304,512]{1,0:T(8,128)S(1)}) custom-call(s32[34]{0:T(128)S(1)} %get-tuple-element.66.meta, bf16[2304,512]{1,0:T(8,128)(2,1)S(1)} %get-tuple-element.72.ad, bf16[2304,512]{1,0:T(8,128)(2,1)S(1)} %get-tuple-element.73.low, bf16[2304,768]{1,0:T(8,128)(2,1)S(1)} %get-tuple-element.74.act, ...), custom_call_target="tpu_custom_call" | custom-call | tf_op jit(solution)/shard_map/pallas_call | solution.py:371
  40.2 0.0 collective-permute-done.2
  40.2 0.1 fusion
  40.3 2.6 %collective-permute-start.7 = (bf16[384,128]{1,0:T(8,128)(2,1)S(1)}, bf16[384,128]{1,0:T(8,128)(2,1)S(1)}, u32[]{:S(2)}, u32[]{:S(2)}) collective-permute-start(bf16[384,128]{1,0:T(8,128)(2,1)S(1)} %get-tuple-element.123), channel_id=1, source_target_pairs={{0,24},{4,28},{8,16},{12,20},{16,8},{20,12},{24,0},{28,4},{1,25},{... | collective-permute-start | bytes 294920 | tf_op jit(solution)/shard_map/ppermute | solution.py:679
  43.0 0.5 collective-permute-start.6
  43.5 1.3 %collective-permute-start.5 = (bf16[384,128]{1,0:T(8,128)(2,1)S(1)}, bf16[384,128]{1,0:T(8,128)(2,1)S(1)}, u32[]{:S(2)}, u32[]{:S(2)}) collective-permute-start(bf16[384,128]{1,0:T(8,128)(2,1)S(1)} %get-tuple-element.125), channel_id=1, source_target_pairs={{0,8},{4,12},{8,0},{12,4},{16,24},{20,28},{24,16},{28,20},{1,9},{5... | collective-permute-start | bytes 294920 | tf_op jit(solution)/shard_map/ppermute | solution.py:679
  44.8 10.3 %shard_map.216 = (bf16[16,256,512]{2,1,0:T(8,128)(2,1)}, bf16[8,256,512]{2,1,0:T(8,128)(2,1)S(1)}, f32[8,4,288,128]{3,2,1,0:T(8,128)S(1)}, f32[16,512]{1,0:T(8,128)S(1)}, f32[16,512]{1,0:T(8,128)S(1)}) custom-call(s32[34]{0:T(128)S(1)} %get-tuple-element.66.meta, bf16[16,256,512]{2,1,0:T(8,128)(2,1)} %tok.3, bf16[16,256,512]{2,1,0:T(8,128)(2,1)} %cot.5, ...), custom_call_target="tpu_custom_call" | custom-call | bytes 40000000 | tf_op jit(solution)/shard_map/pallas_call | solution.py:494
  55.1 0.0 collective-permute-done.7.refs_2_
  55.1 0.0 collective-permute-done.6.refs_1_
  55.1 0.0 collective-permute-done.5.refs_0_
  55.2 0.1 collective-permute-start.8
  55.2 1.2 %collective-permute-done.8.recv = f32[16,512]{1,0:T(8,128)S(1)} collective-permute-done((f32[16,512]{1,0:T(8,128)S(1)}, f32[16,512]{1,0:T(8,128)S(1)}, u32[]{:S(2)}, u32[]{:S(2)}) %collective-permute-start.8) | collective-permute-done | bytes 32800 | tf_op jit(solution)/shard_map/ppermute | solution.py:674
  56.4 0.2 collective-permute-start.9
  56.6 3.0 %collective-permute-start.12 = (bf16[448,128]{1,0:T(8,128)(2,1)S(1)}, bf16[448,128]{1,0:T(8,128)(2,1)S(1)}, u32[]{:S(2)}, u32[]{:S(2)}) collective-permute-start(bf16[448,128]{1,0:T(8,128)(2,1)S(1)} %get-tuple-element.103.refs_0_), channel_id=1, source_target_pairs={{0,24},{4,28},{8,16},{12,20},{16,8},{20,12},{24,0},{28,4},{1,25},{... | collective-permute-start | bytes 344072 | tf_op jit(solution)/shard_map/ppermute | solution.py:679
  59.6 0.0 collective-permute-start.11
  59.7 1.5 %collective-permute-start.10 = (bf16[448,128]{1,0:T(8,128)(2,1)S(1)}, bf16[448,128]{1,0:T(8,128)(2,1)S(1)}, u32[]{:S(2)}, u32[]{:S(2)}) collective-permute-start(bf16[448,128]{1,0:T(8,128)(2,1)S(1)} %get-tuple-element.103.refs_0_), channel_id=1, source_target_pairs={{0,8},{4,12},{8,0},{12,4},{16,24},{20,28},{24,16},{28,20},{1,9},{5... | collective-permute-start | bytes 344072 | tf_op jit(solution)/shard_map/ppermute | solution.py:679
  61.1 0.7 collective-permute-start.13
  61.8 0.0 collective-permute-done.9.other
  61.8 8.3 %shard_map.217 = (bf16[16,256,512]{2,1,0:T(8,128)(2,1)}, f32[16,256,512]{2,1,0:T(8,128)}, bf16[8,256,512]{2,1,0:T(8,128)(2,1)S(1)}) custom-call(s32[34]{0:T(128)S(1)} %get-tuple-element.66.meta, bf16[16,256,512]{2,1,0:T(8,128)(2,1)} %cot.5, f32[8,4,288,128]{3,2,1,0:T(8,128)S(1)} %get-tuple-element.89.cgp, ...), custom_call_target="tpu_custom_call", output_to_operand_aliasing={{0}: (5, {})} | custom-call | bytes 40000000 | tf_op jit(solution)/shard_map/pallas_call | solution.py:564
  70.2 0.0 collective-permute-done.13.theirs
  70.2 0.0 collective-permute-done.12.refs_3_
  70.2 0.0 collective-permute-done.11.refs_2_
  70.2 0.0 collective-permute-done.10.refs_1_
  70.2 0.1 collective-permute-start.15
  70.3 1.2 %collective-permute-start.14 = (bf16[1216,128]{1,0:T(8,128)(2,1)S(1)}, bf16[1216,128]{1,0:T(8,128)(2,1)S(1)}, u32[]{:S(2)}, u32[]{:S(2)}) collective-permute-start(bf16[1216,128]{1,0:T(8,128)(2,1)S(1)} %shard_map.219.near), channel_id=1, source_target_pairs={{0,4},{4,0},{8,12},{12,8},{16,20},{20,16},{24,28},{28,24},{1,5},{5... | collective-permute-start | bytes 933896 | tf_op jit(solution)/shard_map/ppermute | solution.py:679
  71.5 2.9 %collective-permute-done.15.other = bf16[8,256,512]{2,1,0:T(8,128)(2,1)S(1)} collective-permute-done((bf16[8,256,512]{2,1,0:T(8,128)(2,1)S(1)}, bf16[8,256,512]{2,1,0:T(8,128)(2,1)S(1)}, u32[]{:S(2)}, u32[]{:S(2)}) %collective-permute-start.15) | collective-permute-done | bytes 2097184 | tf_op jit(solution)/shard_map/ppermute | solution.py:674
  74.4 2.6 %shard_map.220 = f32[16,256,512]{2,1,0:T(8,128)} custom-call(s32[34]{0:T(128)S(1)} %get-tuple-element.66.meta, bf16[8,256,512]{2,1,0:T(8,128)(2,1)S(1)} %collective-permute-done.15.other, f32[16,256,512]{2,1,0:T(8,128)} %get-tuple-element.108.gtok_in), custom_call_target="tpu_custom_call", output_to_operand_aliasing={{}: (2, {})} | custom-call | bytes 20000000 | tf_op jit(solution)/shard_map/pallas_call | solution.py:587
  77.1 3.1 %collective-permute-done.14.far = bf16[1216,128]{1,0:T(8,128)(2,1)S(1)} collective-permute-done((bf16[1216,128]{1,0:T(8,128)(2,1)S(1)}, bf16[1216,128]{1,0:T(8,128)(2,1)S(1)}, u32[]{:S(2)}, u32[]{:S(2)}) %collective-permute-start.14) | collective-permute-done | bytes 311328 | tf_op jit(solution)/shard_map/ppermute | solution.py:679
  80.2 1.9 %shard_map.221 = (f32[7,512]{1,0:T(8,128)}, f32[512]{0:T(512)}, f32[2,512]{1,0:T(2,128)}, f32[2,512]{1,0:T(2,128)}, f32[512,384]{1,0:T(8,128)}, /*index=5*/f32[3...) custom-call(s32[34]{0:T(128)S(1)} %get-tuple-element.66.meta, bf16[384,128]{1,0:T(8,128)(2,1)S(1)} %get-tuple-element.101.mine, ...), custom_call_target="tpu_custom_call" | custom-call | tf_op jit(solution)/shard_map/pallas_call | solution.py:665
  (3 shorter events, 0.1 us)
Async XLA Ops:
  3.1 3.1 %collective-permute-start = (bf16[3088,128]{1,0:T(8,128)(2,1)S(1)}, bf16[3088,128]{1,0:T(8,128)(2,1)S(1)}, u32[]{:S(2)}, u32[]{:S(2)}) collective-permute-start(bf16[3088,128]{1,0:T(8,128)(2,1)S(1)} %get-tuple-element.67.buf_a), channel_id=1, source_target_pairs={{0,1},{1,0},{2,3},{3,2},{4,5},{5,4},{6,7},{7,6},{8,9},{9,8},{10,11... | collective-permute-start | bytes 2371592 | tf_op jit(solution)/shard_map/ppermute | solution.py:674
  3.6 20.8 %collective-permute-start.3 = (bf16[3088,128]{1,0:T(8,128)(2,1)S(1)}, bf16[3088,128]{1,0:T(8,128)(2,1)S(1)}, u32[]{:S(2)}, u32[]{:S(2)}) collective-permute-start(bf16[3088,128]{1,0:T(8,128)(2,1)S(1)} %get-tuple-element.67.buf_a), channel_id=1, source_target_pairs={{0,2},{1,3},{2,0},{3,1},{4,6},{5,7},{6,4},{7,5},{8,10},{9,11},{10,... | collective-permute-start | bytes 2371592 | tf_op jit(solution)/shard_map/ppermute | solution.py:674
  23.3 2.4 %collective-permute-start.1 = (bf16[3072,128]{1,0:T(8,128)(2,1)S(1)}, bf16[3072,128]{1,0:T(8,128)(2,1)S(1)}, u32[]{:S(2)}, u32[]{:S(2)}) collective-permute-start(bf16[3072,128]{1,0:T(8,128)(2,1)S(1)} %get-tuple-element.69), channel_id=1, source_target_pairs={{0,1},{1,0},{2,3},{3,2},{4,5},{5,4},{6,7},{7,6},{8,9},{9,8},{10,11... | collective-permute-start | bytes 2359304 | tf_op jit(solution)/shard_map/ppermute | solution.py:674
  24.4 4.0 %collective-permute-start.4 = (bf16[3088,128]{1,0:T(8,128)(2,1)S(1)}, bf16[3088,128]{1,0:T(8,128)(2,1)S(1)}, u32[]{:S(2)}, u32[]{:S(2)}) collective-permute-start(bf16[3088,128]{1,0:T(8,128)(2,1)S(1)} %collective-permute-done.3.buf_c), channel_id=1, source_target_pairs={{0,1},{1,0},{2,3},{3,2},{4,5},{5,4},{6,7},{7,6},{8,9},{9,8},{10,11... | collective-permute-start | bytes 2371592 | tf_op jit(solution)/shard_map/ppermute | solution.py:674
  26.3 13.9 %collective-permute-start.2 = (bf16[1536,128]{1,0:T(8,128)(2,1)S(1)}, bf16[1536,128]{1,0:T(8,128)(2,1)S(1)}, u32[]{:S(2)}, u32[]{:S(2)}) collective-permute-start(bf16[1536,128]{1,0:T(8,128)(2,1)S(1)} %get-tuple-element.71), channel_id=1, source_target_pairs={{0,4},{4,0},{8,12},{12,8},{16,20},{20,16},{24,28},{28,24},{1,5},{5... | collective-permute-start | bytes 1179656 | tf_op jit(solution)/shard_map/ppermute | solution.py:679
  40.3 14.8 %collective-permute-start.7 = (bf16[384,128]{1,0:T(8,128)(2,1)S(1)}, bf16[384,128]{1,0:T(8,128)(2,1)S(1)}, u32[]{:S(2)}, u32[]{:S(2)}) collective-permute-start(bf16[384,128]{1,0:T(8,128)(2,1)S(1)} %get-tuple-element.123), channel_id=1, source_target_pairs={{0,24},{4,28},{8,16},{12,20},{16,8},{20,12},{24,0},{28,4},{1,25},{... | collective-permute-start | bytes 294920 | tf_op jit(solution)/shard_map/ppermute | solution.py:679
  43.0 12.2 %collective-permute-start.6 = (bf16[384,128]{1,0:T(8,128)(2,1)S(1)}, bf16[384,128]{1,0:T(8,128)(2,1)S(1)}, u32[]{:S(2)}, u32[]{:S(2)}) collective-permute-start(bf16[384,128]{1,0:T(8,128)(2,1)S(1)} %get-tuple-element.124), channel_id=1, source_target_pairs={{0,16},{4,20},{8,24},{12,28},{16,0},{20,4},{24,8},{28,12},{1,17},{... | collective-permute-start | bytes 294920 | tf_op jit(solution)/shard_map/ppermute | solution.py:679
  43.5 11.7 %collective-permute-start.5 = (bf16[384,128]{1,0:T(8,128)(2,1)S(1)}, bf16[384,128]{1,0:T(8,128)(2,1)S(1)}, u32[]{:S(2)}, u32[]{:S(2)}) collective-permute-start(bf16[384,128]{1,0:T(8,128)(2,1)S(1)} %get-tuple-element.125), channel_id=1, source_target_pairs={{0,8},{4,12},{8,0},{12,4},{16,24},{20,28},{24,16},{28,20},{1,9},{5... | collective-permute-start | bytes 294920 | tf_op jit(solution)/shard_map/ppermute | solution.py:679
  55.2 1.3 %collective-permute-start.8 = (f32[16,512]{1,0:T(8,128)S(1)}, f32[16,512]{1,0:T(8,128)S(1)}, u32[]{:S(2)}, u32[]{:S(2)}) collective-permute-start(f32[16,512]{1,0:T(8,128)S(1)} %get-tuple-element.90), channel_id=1, source_target_pairs={{0,1},{1,0},{2,3},{3,2},{4,5},{5,4},{6,7},{7,6},{8,9},{9,8},{10,11... | collective-permute-start | bytes 98312 | tf_op jit(solution)/shard_map/ppermute | solution.py:674
  56.4 5.4 %collective-permute-start.9 = (bf16[8,256,512]{2,1,0:T(8,128)(2,1)S(1)}, bf16[8,256,512]{2,1,0:T(8,128)(2,1)S(1)}, u32[]{:S(2)}, u32[]{:S(2)}) collective-permute-start(bf16[8,256,512]{2,1,0:T(8,128)(2,1)S(1)} %get-tuple-element.92), channel_id=1, source_target_pairs={{0,1},{1,0},{2,3},{3,2},{4,5},{5,4},{6,7},{7,6},{8,9},{9,8},{10,11... | collective-permute-start | bytes 6291464 | tf_op jit(solution)/shard_map/ppermute | solution.py:674
  56.6 13.5 %collective-permute-start.12 = (bf16[448,128]{1,0:T(8,128)(2,1)S(1)}, bf16[448,128]{1,0:T(8,128)(2,1)S(1)}, u32[]{:S(2)}, u32[]{:S(2)}) collective-permute-start(bf16[448,128]{1,0:T(8,128)(2,1)S(1)} %get-tuple-element.103.refs_0_), channel_id=1, source_target_pairs={{0,24},{4,28},{8,16},{12,20},{16,8},{20,12},{24,0},{28,4},{1,25},{... | collective-permute-start | bytes 344072 | tf_op jit(solution)/shard_map/ppermute | solution.py:679
  59.6 10.5 %collective-permute-start.11 = (bf16[448,128]{1,0:T(8,128)(2,1)S(1)}, bf16[448,128]{1,0:T(8,128)(2,1)S(1)}, u32[]{:S(2)}, u32[]{:S(2)}) collective-permute-start(bf16[448,128]{1,0:T(8,128)(2,1)S(1)} %get-tuple-element.103.refs_0_), channel_id=1, source_target_pairs={{0,16},{4,20},{8,24},{12,28},{16,0},{20,4},{24,8},{28,12},{1,17},{... | collective-permute-start | bytes 344072 | tf_op jit(solution)/shard_map/ppermute | solution.py:679
  59.7 10.6 %collective-permute-start.10 = (bf16[448,128]{1,0:T(8,128)(2,1)S(1)}, bf16[448,128]{1,0:T(8,128)(2,1)S(1)}, u32[]{:S(2)}, u32[]{:S(2)}) collective-permute-start(bf16[448,128]{1,0:T(8,128)(2,1)S(1)} %get-tuple-element.103.refs_0_), channel_id=1, source_target_pairs={{0,8},{4,12},{8,0},{12,4},{16,24},{20,28},{24,16},{28,20},{1,9},{5... | collective-permute-start | bytes 344072 | tf_op jit(solution)/shard_map/ppermute | solution.py:679
  61.1 9.1 %collective-permute-start.13 = (bf16[384,128]{1,0:T(8,128)(2,1)S(1)}, bf16[384,128]{1,0:T(8,128)(2,1)S(1)}, u32[]{:S(2)}, u32[]{:S(2)}) collective-permute-start(bf16[384,128]{1,0:T(8,128)(2,1)S(1)} %get-tuple-element.101.mine), channel_id=1, source_target_pairs={{0,4},{4,0},{8,12},{12,8},{16,20},{20,16},{24,28},{28,24},{1,5},{5... | collective-permute-start | bytes 294920 | tf_op jit(solution)/shard_map/ppermute | solution.py:679
  70.2 4.2 %collective-permute-start.15 = (bf16[8,256,512]{2,1,0:T(8,128)(2,1)S(1)}, bf16[8,256,512]{2,1,0:T(8,128)(2,1)S(1)}, u32[]{:S(2)}, u32[]{:S(2)}) collective-permute-start(bf16[8,256,512]{2,1,0:T(8,128)(2,1)S(1)} %get-tuple-element.107), channel_id=1, source_target_pairs={{0,1},{1,0},{2,3},{3,2},{4,5},{5,4},{6,7},{7,6},{8,9},{9,8},{10,11... | collective-permute-start | bytes 6291464 | tf_op jit(solution)/shard_map/ppermute | solution.py:674
  70.3 9.8 %collective-permute-start.14 = (bf16[1216,128]{1,0:T(8,128)(2,1)S(1)}, bf16[1216,128]{1,0:T(8,128)(2,1)S(1)}, u32[]{:S(2)}, u32[]{:S(2)}) collective-permute-start(bf16[1216,128]{1,0:T(8,128)(2,1)S(1)} %shard_map.219.near), channel_id=1, source_target_pairs={{0,4},{4,0},{8,12},{12,8},{16,20},{20,16},{24,28},{28,24},{1,5},{5... | collective-permute-start | bytes 933896 | tf_op jit(solution)/shard_map/ppermute | solution.py:679

commit v5 on v4

--- a/solution.py
+++ b/solution.py
@@ -92,12 +92,9 @@
     offs[n + 1] = (end + TILE - 1) // TILE
 
 
-def pack_kernel(n, wi, bi, wo, counts, groups, out, meta, counts_s, groups_s, sems):
+def pack_kernel(wi, bi, wo, out):
     width, h = wi.shape
     hq, wq = h // LANES, width // LANES
-    copies = [pltpu.make_async_copy(counts, counts_s, sems.at[0]), pltpu.make_async_copy(groups, groups_s, sems.at[1])]
-    for c in copies:
-        c.start()
     for q in range(hq):
         out[q * width:(q + 1) * width, :] = wi[:, lane(q)]
     base = hq * width
@@ -107,25 +104,12 @@
     bias = bi[...].astype(F32).reshape(1, h)
     rows = [bias[:, lane(q)] for q in range(hq)] + [jnp.zeros((1, LANES), F32)] * (16 - hq)
     out[base:base + 16, :] = jnp.concatenate(rows, axis=0).astype(BF)
-    meta[0] = lax.axis_index("tp") & 1
-    meta[1] = lax.axis_index("dp")
-    for c in copies:
-        c.wait()
-    for j in range(2 * n):
-        meta[2 + j] = counts_s[j]
-        meta[2 + 2 * n + j] = groups_s[j]
-
-
-def pack(wi, bi, wo, counts, groups):
+
+
+def pack(wi, bi, wo):
     rows = 2 * wi.size // LANES + 16
-    items = counts.shape[0]
-    return pl.pallas_call(
-        functools.partial(pack_kernel, items // 2),
-        in_specs=[whole(wi.shape), whole(bi.shape), whole(wo.shape), hbm(), hbm()],
-        out_specs=[whole((rows, LANES)), smem()],
-        out_shape=[struct((rows, LANES), BF), struct((2 + 2 * items,), jnp.int32)],
-        scratch_shapes=[pltpu.SMEM((items,), jnp.int32), pltpu.SMEM((items,), jnp.int32), pltpu.SemaphoreType.DMA((2,))],
-        compiler_params=params())(wi, bi, wo, counts, groups)
+    return pl.pallas_call(pack_kernel, out_shape=struct((rows, LANES), BF),
+                          compiler_params=params())(wi, bi, wo)
 
 
 def weight_copies(buf, side, win, wout, bias, sems):
@@ -150,21 +134,36 @@
             row[:, lane(at)] = bias[side, q:q + 1, :].astype(F32)
 
 
-def front_kernel(n, meta, tok, cot, cw, cb, ns, nsh, gamma, buf_a, buf_b,
-                 ad, nrm, low, inv, act, pre, win, wout, keep, send, gbo, gbi,
-                 offs, pad, ad_s, nrm_s, low_s, inv_s, bias, bias_row, dwo, dwi, sems):
+def front_kernel(n, meta, tok_hbm, cot_hbm, cw, cb, ns, nsh, gamma, bout, buf_a, buf_b,
+                 ad, nrm, low, inv, act, pre, win, wout, keep, send, gbo, gbi, tok, cot, consts,
+                 offs, pad, ad_s, nrm_s, low_s, inv_s, bias, bias_row, dwo, dwi, sems, item_sems):
     s = pl.program_id(0)
     frames, width = tok.shape[1], tok.shape[2]
-    taps = cw.shape[0]
+    taps, rates = cw.shape[0], ns.shape[0]
     half = taps // 2
     wq = width // LANES
     h = win.shape[1] // 2
     copies = weight_copies(buf_a, 0, win, wout, bias, sems) + weight_copies(buf_b, 1, win, wout, bias, sems)
 
+    def fetch(j):
+        at = meta[0] * n + j
+        return [pltpu.make_async_copy(src.at[at], dst.at[j], item_sems.at[i, j])
+                for i, (src, dst) in enumerate(((tok_hbm, tok), (cot_hbm, cot)))]
+
     @pl.when(s == 0)
     def _():
+        for c in fetch(0) + fetch(1):
+            c.start()
         for c in copies:
             c.start()
+        for j in range(2, n):
+            for c in fetch(j):
+                c.start()
+        consts[...] = jnp.zeros_like(consts)
+        consts[:taps, :] = cw[...].astype(F32)
+        consts[taps:taps + 1, :] = as_row(gamma)
+        consts[taps + 1:taps + 2, :] = as_row(bout)
+        consts[taps + 2:taps + 2 + rates, :] = ns[...].astype(F32)
         place_items(n, meta, offs)
         offs[n + 2] = 0
         gbo[...] = jnp.zeros_like(gbo)
@@ -188,6 +187,8 @@
         dwi[...] = jnp.zeros_like(dwi)
         gbi[...] = jnp.zeros_like(gbi)
 
+    for c in fetch(s):
+        c.wait()
     item = meta[0] * n + s
     count = meta[2 + item]
     group = meta[2 + 2 * n + item]
@@ -195,7 +196,7 @@
     def setup():
         rows = lax.broadcasted_iota(jnp.int32, (frames, LANES), 0)
         for q in range(wq):
-            pad[q, PAD:PAD + frames, :] = jnp.where(rows < count, tok[0, :, lane(q)].astype(F32), 0.0)
+            pad[q, PAD:PAD + frames, :] = jnp.where(rows < count, tok[s, :, lane(q)].astype(F32), 0.0)
         return pick(ns, group), pick(nsh, group), as_row(gamma), as_row(cb), cw[...].astype(F32)
 
     def conv_step(i, acc, consts):
@@ -220,7 +221,7 @@
             normed = cents[q] * istd
             ad_s[here, lane(q)] = (normed * scale[:, lane(q)] + shift[:, lane(q)]).astype(BF)
             nrm_s[here, lane(q)] = normed.astype(BF)
-            back = jnp.where(live, cot[0, here, lane(q)].astype(F32), 0.0) * gam[:, lane(q)]
+            back = jnp.where(live, cot[s, here, lane(q)].astype(F32), 0.0) * gam[:, lane(q)]
             low_s[here, lane(q)] = back.astype(BF)
             new.append(acc[q] + fold(back))
         return tuple(new)
@@ -297,31 +298,32 @@
                 dst[base + q * width:base + (q + 1) * width, :] = dwi[:, lane(side * (h // LANES) + q)].astype(dst.dtype)
 
 
-def front(meta, tok, cot, cw, cb, ns, nsh, gamma, buf_a, buf_b, h):
+def front(meta, tok, cot, cw, cb, ns, nsh, gamma, bout, buf_a, buf_b, h):
     items, frames, width = tok.shape
     n = items // 2
     rows = n * frames + TILE
     packed = 2 * width * h // LANES
     wq, hq = width // LANES, h // LANES
-    item = pl.BlockSpec((1, frames, width), lambda s, c: (c[0] * n + s, 0, 0))
+    n_consts = -(-(cw.shape[0] + 2 + ns.shape[0]) // 8) * 8
     return pl.pallas_call(
         functools.partial(front_kernel, n),
         grid_spec=pltpu.PrefetchScalarGridSpec(
             num_scalar_prefetch=1, grid=(n,),
-            in_specs=[item, item] + [whole(v.shape) for v in (cw, cb, ns, nsh, gamma)] + [hbm()] * 2,
-            out_specs=[vmem()] * 12,
+            in_specs=[hbm()] * 2 + [whole(v.shape) for v in (cw, cb, ns, nsh, gamma, bout)] + [hbm()] * 2,
+            out_specs=[vmem()] * 15,
             scratch_shapes=[pltpu.SMEM((n + 3,), jnp.int32),
                             pltpu.VMEM((wq, frames + 4 * PAD, LANES), F32),
                             pltpu.VMEM((frames, width), BF), pltpu.VMEM((frames, width), BF),
                             pltpu.VMEM((frames, width), BF), pltpu.VMEM((frames, LANES), F32),
                             pltpu.VMEM((2, 16, LANES), BF), pltpu.VMEM((1, 2 * h), F32),
                             pltpu.VMEM((2 * h, width), F32), pltpu.VMEM((width, 2 * h), F32),
-                            pltpu.SemaphoreType.DMA((2, hq + wq + 1))]),
+                            pltpu.SemaphoreType.DMA((2, hq + wq + 1)), pltpu.SemaphoreType.DMA((2, n))]),
         out_shape=[struct((rows, width), BF)] * 3 + [struct((rows, LANES), F32)]
         + [struct((rows, 2 * h), BF)] * 2 + [struct((width, 2 * h), BF), struct((2 * h, width), BF)]
-        + [struct((packed, LANES), F32), struct((packed, LANES), BF), struct((8, width), F32), struct((8, 2 * h), F32)],
+        + [struct((packed, LANES), F32), struct((packed, LANES), BF), struct((8, width), F32), struct((8, 2 * h), F32)]
+        + [struct((n, frames, width), BF)] * 2 + [struct((n_consts, width), F32)],
         compiler_params=params(), cost_estimate=cost(0),
-    )(meta, tok, cot, cw, cb, ns, nsh, gamma, buf_a, buf_b)
+    )(meta, tok, cot, cw, cb, ns, nsh, gamma, bout, buf_a, buf_b)
 
 
 def combine_kernel(dp, meta, keep, recv, stay, leave):
@@ -342,7 +344,7 @@
         compiler_params=params())(meta, keep, recv)
 
 
-def mix_kernel(n, meta, ad, low, act, pre, win1, wout1, bout, buf_c, buf_d, branch, ag,
+def mix_kernel(n, taps, meta, ad, low, act, pre, win1, wout1, consts, buf_c, buf_d, branch, ag,
                offs, win2, wout2, bias, bias_row, sems):
     copies = weight_copies(buf_c, 0, win2, wout2, bias, sems) + weight_copies(buf_d, 1, win2, wout2, bias, sems)
     for c in copies:
@@ -357,20 +359,20 @@
         a, b = ad[at, :], low[at, :]
         activation, slope = gelu_parts(dot(a, win2[...]) + bias_row[...])
         grad = dot_t(b, wout2[...]) * slope
-        branch[at, :] = (dot(act[at, :], wout1[...]) + dot(activation.astype(BF), wout2[...])) + as_row(bout)
+        branch[at, :] = (dot(act[at, :], wout1[...]) + dot(activation.astype(BF), wout2[...])) + consts[taps + 1:taps + 2, :]
         ag[at, :] = dot_t(pre[at, :], win1[...]) + dot_t(grad.astype(BF), win2[...])
         return 0
 
     lax.fori_loop(0, offs[n + 1], tile, 0)
 
 
-def mix(meta, ad, low, act, pre, win, wout, bout, buf_c, buf_d, n):
+def mix(meta, ad, low, act, pre, win, wout, consts, buf_c, buf_d, n, taps):
     rows, width = ad.shape
     h = act.shape[1] // 2
     wq, hq = width // LANES, h // LANES
     return pl.pallas_call(
-        functools.partial(mix_kernel, n),
-        in_specs=[smem()] + [vmem()] * 6 + [whole(bout.shape)] + [hbm()] * 2,
+        functools.partial(mix_kernel, n, taps),
+        in_specs=[smem()] + [vmem()] * 7 + [hbm()] * 2,
         out_specs=[vmem(), vmem()],
         scratch_shapes=[pltpu.SMEM((n + 2,), jnp.int32),
                         pltpu.VMEM((width, 2 * h), BF), pltpu.VMEM((2 * h, width), BF),
@@ -378,14 +380,13 @@
                         pltpu.SemaphoreType.DMA((2, hq + wq + 1))],
         out_shape=[struct((rows, width), F32)] * 2,
         compiler_params=params(), cost_estimate=cost(0),
-    )(meta, ad, low, act, pre, win, wout, bout, buf_c, buf_d)
-
-
-def norm_grad_kernel(n, meta, tok, cot, branch, ag, nrm, inv, gbo, gbi, cw, ns, gamma,
+    )(meta, ad, low, act, pre, win, wout, consts, buf_c, buf_d)
+
+
+def norm_grad_kernel(n, taps, rates, meta, tok, cot, branch, ag, nrm, inv, gbo, gbi, consts,
                      out, out_own, cgp, small_keep, small_send, offs, sums, sems):
     s = pl.program_id(0)
     frames, width = tok.shape[1], tok.shape[2]
-    taps, rates = cw.shape[0], ns.shape[0]
     half = taps // 2
     wq = width // LANES
     h = gbi.shape[1] // 2
@@ -402,8 +403,8 @@
     count = meta[2 + item]
     group = meta[2 + 2 * n + item]
     off = offs[s]
-    scale = pick(ns, group)
-    gam = as_row(gamma)
+    scale = pick(consts.at[taps + 2:taps + 2 + rates], group)
+    gam = consts[taps:taps + 1, :]
     zero = jnp.zeros((8, LANES), F32)
     steps = pl.cdiv(count, WIDE_CHUNK)
 
@@ -417,11 +418,11 @@
         for q in range(wq):
             a_ls, a_sc, a_sh = accs[3 * q:3 * q + 3]
             br = jnp.where(live, branch[src, lane(q)], 0.0)
-            tk = jnp.where(live, tok[0, here, lane(q)].astype(F32), 0.0)
+            tk = jnp.where(live, tok[s, here, lane(q)].astype(F32), 0.0)
             out_own[s, here, lane(q)] = (tk + gam[:, lane(q)] * br).astype(BF)
             g = jnp.where(live, ag[src, lane(q)], 0.0)
             nr = nrm[src, lane(q)].astype(F32)
-            new += [a_ls + fold(cot[0, here, lane(q)].astype(F32) * br), a_sc + fold(g * nr), a_sh + fold(g)]
+            new += [a_ls + fold(cot[s, here, lane(q)].astype(F32) * br), a_sc + fold(g * nr), a_sh + fold(g)]
             ngs.append(g * scale[:, lane(q)])
             nrs.append(nr)
         cross = [a * b for a, b in zip(ngs, nrs)]
@@ -456,7 +457,7 @@
             r0 = pl.multiple_of(i * WIDE_CHUNK, WIDE_CHUNK)
             here = pl.ds(r0, WIDE_CHUNK)
             live = (lax.broadcasted_iota(jnp.int32, (WIDE_CHUNK, LANES), 0) + r0) < count
-            tk = jnp.where(live, tok[0, here, lane(q)].astype(F32), 0.0)
+            tk = jnp.where(live, tok[s, here, lane(q)].astype(F32), 0.0)
             new = []
             for k in range(taps):
                 sh = cgp[s, q, pl.ds(r0 + (PAD + half - k), WIDE_CHUNK), :]
@@ -484,36 +485,29 @@
             place(j).wait()
 
 
-def norm_grad(meta, tok, cot, branch, ag, nrm, inv, gbo, gbi, cw, ns, gamma):
-    items, frames, width = tok.shape
-    n = items // 2
+def norm_grad(meta, tok, cot, branch, ag, nrm, inv, gbo, gbi, consts, taps, rates):
+    n, frames, width = tok.shape
     wq = width // LANES
-    taps, rates = cw.shape[0], ns.shape[0]
     n_small = -(-(taps + 4 + 2 * rates) // 8) * 8
-    item = pl.BlockSpec((1, frames, width), lambda s, c: (c[0] * n + s, 0, 0))
     return pl.pallas_call(
-        functools.partial(norm_grad_kernel, n),
-        grid_spec=pltpu.PrefetchScalarGridSpec(
-            num_scalar_prefetch=1, grid=(n,),
-            in_specs=[item, item] + [vmem()] * 6 + [whole(v.shape) for v in (cw, ns, gamma)],
-            out_specs=[hbm()] + [vmem()] * 4,
-            scratch_shapes=[pltpu.SMEM((n + 2,), jnp.int32),
-                            pltpu.VMEM((taps + 2 + 2 * rates, 8, width), F32),
-                            pltpu.SemaphoreType.DMA((n,))]),
-        out_shape=[struct((items, frames, width), BF), struct((n, frames, width), BF),
+        functools.partial(norm_grad_kernel, n, taps, rates), grid=(n,),
+        in_specs=[smem()] + [vmem()] * 9, out_specs=[hbm()] + [vmem()] * 4,
+        scratch_shapes=[pltpu.SMEM((n + 2,), jnp.int32),
+                        pltpu.VMEM((taps + 2 + 2 * rates, 8, width), F32),
+                        pltpu.SemaphoreType.DMA((n,))],
+        out_shape=[struct((2 * n, frames, width), BF), struct((n, frames, width), BF),
                    struct((n, wq, frames + 4 * PAD, LANES), F32)] + [struct((n_small, width), F32)] * 2,
         compiler_params=params(), cost_estimate=cost(40000000),
-    )(meta, tok, cot, branch, ag, nrm, inv, gbo, gbi, cw, ns, gamma)
-
-
-def token_grad_kernel(n, meta, cot, cgp, cw, other, out_in, out, gtok, gtok_own, stage, sems, out_sem):
+    )(meta, tok, cot, branch, ag, nrm, inv, gbo, gbi, consts)
+
+
+def token_grad_kernel(n, taps, meta, cot, cgp, consts, other, out_in, out, gtok, gtok_own, stage, sems, out_sem):
     s = pl.program_id(0)
     frames, width = cot.shape[1], cot.shape[2]
-    taps = cw.shape[0]
     half = taps // 2
     wq = width // LANES
     count = meta[2 + meta[0] * n + s]
-    w = cw[...].astype(F32)
+    w = consts[:taps, :]
     steps = pl.cdiv(count, CHUNK)
     other_copy = pltpu.make_async_copy(other, out.at[pl.ds((1 - meta[0]) * n, n)], out_sem)
 
@@ -524,22 +518,20 @@
     def _():
         other_copy.start()
 
-    for q in range(wq):
-        wl = w[:, lane(q)]
-
-        def conv_step(i, _):
-            r0 = pl.multiple_of(i * CHUNK, CHUNK)
-            here = pl.ds(r0, CHUNK)
-            live = (lax.broadcasted_iota(jnp.int32, (CHUNK, LANES), 0) + r0) < count
-            total = cot[0, here, lane(q)].astype(F32)
+    def conv_step(i, _):
+        r0 = pl.multiple_of(i * CHUNK, CHUNK)
+        here = pl.ds(r0, CHUNK)
+        live = (lax.broadcasted_iota(jnp.int32, (CHUNK, LANES), 0) + r0) < count
+        for q in range(wq):
+            total = cot[s, here, lane(q)].astype(F32)
             for k in range(taps):
-                total = total + wl[k:k + 1] * cgp[s, q, pl.ds(r0 + (PAD + half - k), CHUNK), :]
+                total = total + w[k:k + 1, lane(q)] * cgp[s, q, pl.ds(r0 + (PAD + half - k), CHUNK), :]
             total = jnp.where(live, total, 0.0).astype(BF)
             gtok_own[s, here, lane(q)] = total
             stage[s, here, lane(q)] = total.astype(F32)
-            return 0
-
-        lax.fori_loop(0, steps, conv_step, 0)
+        return 0
+
+    lax.fori_loop(0, steps, conv_step, 0)
 
     def clear(i, _):
         here = pl.ds(pl.multiple_of(i * CHUNK, CHUNK), CHUNK)
@@ -557,20 +549,16 @@
             place(j).wait()
 
 
-def token_grad(meta, cot, cgp, cw, other, out):
-    items, frames, width = cot.shape
-    n = items // 2
-    item = pl.BlockSpec((1, frames, width), lambda s, c: (c[0] * n + s, 0, 0))
+def token_grad(meta, cot, cgp, consts, other, out, taps):
+    n, frames, width = cot.shape
     return pl.pallas_call(
-        functools.partial(token_grad_kernel, n),
-        grid_spec=pltpu.PrefetchScalarGridSpec(
-            num_scalar_prefetch=1, grid=(n,),
-            in_specs=[item, vmem(), whole(cw.shape), hbm(), hbm()], out_specs=[hbm(), hbm(), vmem()],
-            scratch_shapes=[pltpu.VMEM((n, frames, width), F32), pltpu.SemaphoreType.DMA((n,)), pltpu.SemaphoreType.DMA]),
+        functools.partial(token_grad_kernel, n, taps), grid=(n,),
+        in_specs=[smem()] + [vmem()] * 3 + [hbm()] * 2, out_specs=[hbm(), hbm(), vmem()],
+        scratch_shapes=[pltpu.VMEM((n, frames, width), F32), pltpu.SemaphoreType.DMA((n,)), pltpu.SemaphoreType.DMA],
         out_shape=[struct(out.shape, BF), struct(out.shape, F32), struct((n, frames, width), BF)],
         input_output_aliases={5: 0},
         compiler_params=params(), cost_estimate=cost(40000000),
-    )(meta, cot, cgp, cw, other, out)
+    )(meta, cot, cgp, consts, other, out)
 
 
 def merge_kernel(n, meta, other, gtok_in, gtok, stage, sems):
@@ -684,26 +672,29 @@
     width, h = weight_in.shape
     n = tokens.shape[0] // 2
     (tokens, cotangent, conv_weight, conv_bias, norm_scale, norm_shift, weight_in, bias_in, weight_out, bias_out,
-     layer_scale, frame_counts, rate_groups) = [pltpu.with_memory_space_constraint(v, pltpu.HBM) for v in (
+     layer_scale) = [pltpu.with_memory_space_constraint(v, pltpu.HBM) for v in (
          tokens, cotangent, conv_weight, conv_bias, norm_scale, norm_shift, weight_in, bias_in, weight_out, bias_out,
-         layer_scale, frame_counts, rate_groups)]
+         layer_scale)]
     taps, rates = conv_weight.shape[0], norm_scale.shape[0]
     dp = lax.axis_size("dp")
-    buf_a, meta = pack(weight_in, bias_in, weight_out, frame_counts, rate_groups)
+    place = jnp.stack([lax.axis_index("tp") & 1, lax.axis_index("dp")]).astype(jnp.int32)
+    meta = jnp.concatenate([place, frame_counts, rate_groups])
+
+    buf_a = pack(weight_in, bias_in, weight_out)
     buf_b = swap(buf_a, 1)
     buf_c = swap(buf_a, 2)
     buf_d = swap(buf_c, 1)
-    ad, nrm, low, inv, act, pre, win, wout, keep, send, gbo, gbi = front(
-        meta, tokens, cotangent, conv_weight, conv_bias, norm_scale, norm_shift, layer_scale, buf_a, buf_b, h)
+    ad, nrm, low, inv, act, pre, win, wout, keep, send, gbo, gbi, tok, cot, consts = front(
+        meta, tokens, cotangent, conv_weight, conv_bias, norm_scale, norm_shift, layer_scale, bias_out, buf_a, buf_b, h)
     stay, leave = combine(meta, keep, swap(send, 1), dp)
     arrived = across(leave, 1)
-    branch, ag = mix(meta, ad, low, act, pre, win, wout, bias_out, buf_c, buf_d, n)
+    branch, ag = mix(meta, ad, low, act, pre, win, wout, consts, buf_c, buf_d, n, taps)
     arrived, branch = lax.optimization_barrier((arrived, branch))
     stay = (stay + arrived.astype(F32)).reshape(dp // 2, -1, LANES)
     pieces = [across(stay[d].astype(BF), 2 * d) for d in range(1, dp // 2)]
 
     out, out_own, cgp, small_keep, small_send = norm_grad(
-        meta, tokens, cotangent, branch, ag, nrm, inv, gbo, gbi, conv_weight, norm_scale, layer_scale)
+        meta, tok, cot, branch, ag, nrm, inv, gbo, gbi, consts, taps, rates)
     pieces, small_send, out_own, cgp = lax.optimization_barrier((pieces, small_send, out_own, cgp))
     small_got = swap(small_send, 1)
     small_got, out_own = lax.optimization_barrier((small_got, out_own))
@@ -711,7 +702,7 @@
     m = pieces[0].shape[0]
     near = [message] + [across(message, 2 * d) for d in range(1, dp // 2)]
     theirs = across(mine, 1)
-    out, gtok, gtok_own = token_grad(meta, cotangent, cgp, conv_weight, swap(out_own, 1), out)
+    out, gtok, gtok_own = token_grad(meta, cot, cgp, consts, swap(out_own, 1), out, taps)
     near, theirs, gtok_own = lax.optimization_barrier((near, theirs, gtok_own))
     near = relay(m, near)
     far = across(near, 1)

time: 82.4 us -> 80.9 us (0.982)
  Pallas kernels: 55.3 us -> 46.3 us
  waiting for transfers between devices: 9.31 us -> 14.2 us
  starting transfers between devices: 16.5 us -> 18.4 us
    pallas_call x4, Pallas kernels: 32.9 us -> 24.6 us  [the longest x1 10.1 us: mix(): pl.pallas_call(functools.partial(mix_kernel, n, taps), in_specs=[smem()]...]
    ppermute x9, waiting for transfers between devices: 3.08 us -> 7.39 us  [across(): return lax.ppermute(x, 'dp', [(i, i ^ step) for i in range(size)])]
    ppermute x9, starting transfers between devices: 12.9 us -> 14.7 us  [across(): return lax.ppermute(x, 'dp', [(i, i ^ step) for i in range(size)])]
  transfers between devices with their start and end apart: 16 -> 16, of which waited for: 5 -> 6; matrix products, arithmetic and copies ran while one was open for 0% -> 1% of each run, Pallas kernels for 62% -> 53%
where the time goes in v5:
time: 80.9 us; the launch traced here: 80.6 us
  Pallas kernels  46.3 us (57%)
  starting transfers between devices  18.4 us (23%)
  waiting for transfers between devices  14.2 us (18%)
  other arithmetic  0.85 us (1%)
    pallas_call x1, Pallas kernels, front(): pl.pallas_call(functools.partial(front_kernel, n), grid_spec=pltpu.Prefet...  16.3 us
    ppermute x9, starting transfers between devices, across(): return lax.ppermute(x, 'dp', [(i, i ^ step) for i in range(size)])  14.7 us
    pallas_call x1, Pallas kernels, mix(): pl.pallas_call(functools.partial(mix_kernel, n, taps), in_specs=[smem()]...  10.1 us
    pallas_call x1, Pallas kernels, norm_grad(): pl.pallas_call(functools.partial(norm_grad_kernel, n, taps, rates), grid=...  8.68 us
    ppermute x9, waiting for transfers between devices, across(): return lax.ppermute(x, 'dp', [(i, i ^ step) for i in range(size)])  7.39 us
    ppermute x7, waiting for transfers between devices, swap(): return lax.ppermute(x, 'tp', [(i, i ^ step) for i in range(size)])  6.82 us
    pallas_call x1, Pallas kernels, token_grad(): pl.pallas_call(functools.partial(token_grad_kernel, n, taps), grid=(n,),...  4.51 us
    ppermute x7, starting transfers between devices, swap(): return lax.ppermute(x, 'tp', [(i, i ^ step) for i in range(size)])  3.75 us
  transfers between devices with their start and end apart: 16, of which 6 were waited for; matrix products, arithmetic and copies ran while one was open for 1% of the time, Pallas kernels for 53%

profile of v5, /device:TPU:0, one launch (start us, length us, event | category | flops | bytes accessed | tf_op | source)
XLA Modules:
  0.0 80.6 jit_solution(16185132426527999710)
XLA Ops:
  0.6 1.3 %shard_map.212.buf_a = bf16[3088,128]{1,0:T(8,128)(2,1)S(1)} custom-call(bf16[512,384]{1,0:T(8,128)(2,1)} %wi.1, bf16[384]{0:T(512)(128)(2,1)} %bi.1, bf16[384,512]{1,0:T(8,128)(2,1)} %wo.1), custom_call_target="tpu_custom_call" | custom-call | tf_op jit(solution)/shard_map/pallas_call | solution.py:111
  1.9 0.5 collective-permute-start
  2.4 2.6 %collective-permute-start.3 = (bf16[3088,128]{1,0:T(8,128)(2,1)S(1)}, bf16[3088,128]{1,0:T(8,128)(2,1)S(1)}, u32[]{:S(2)}, u32[]{:S(2)}) collective-permute-start(bf16[3088,128]{1,0:T(8,128)(2,1)S(1)} %shard_map.212.buf_a), channel_id=1, source_target_pairs={{0,2},{1,3},{2,0},{3,1},{4,6},{5,7},{6,4},{7,5},{8,10},{9,11},{10,... | collective-permute-start | bytes 2371592 | tf_op jit(solution)/shard_map/ppermute | solution.py:662
  5.0 0.7 pad_add_fusion.meta
  5.8 0.0 collective-permute-done.buf_b
  5.8 16.3 %shard_map.213 = (bf16[2304,512]{1,0:T(8,128)(2,1)S(1)}, bf16[2304,512]{1,0:T(8,128)(2,1)S(1)}, bf16[2304,512]{1,0:T(8,128)(2,1)S(1)}, f32[2304,128]{1,0:T(8,128...) custom-call(s32[34]{0:T(128)S(1)} %pad_add_fusion.meta, ...), custom_call_target="tpu_custom_call" | custom-call | tf_op jit(solution)/shard_map/pallas_call | solution.py:308
  22.1 0.4 collective-permute-start.1
  22.5 0.7 collective-permute-done.3.buf_c
  23.2 0.0 collective-permute-start.4
  23.2 1.2 %collective-permute-done.1.recv = bf16[3072,128]{1,0:T(8,128)(2,1)S(1)} collective-permute-done((bf16[3072,128]{1,0:T(8,128)(2,1)S(1)}, bf16[3072,128]{1,0:T(8,128)(2,1)S(1)}, u32[]{:S(2)}, u32[]{:S(2)}) %collective-permute-start.1) | collective-permute-done | bytes 786464 | tf_op jit(solution)/shard_map/ppermute | solution.py:662
  24.4 0.7 shard_map.214
  25.1 3.2 %collective-permute-start.2 = (bf16[1536,128]{1,0:T(8,128)(2,1)S(1)}, bf16[1536,128]{1,0:T(8,128)(2,1)S(1)}, u32[]{:S(2)}, u32[]{:S(2)}) collective-permute-start(bf16[1536,128]{1,0:T(8,128)(2,1)S(1)} %get-tuple-element.71), channel_id=1, source_target_pairs={{0,4},{4,0},{8,12},{12,8},{16,20},{20,16},{24,28},{28,24},{1,5},{5... | collective-permute-start | bytes 1179656 | tf_op jit(solution)/shard_map/ppermute | solution.py:667
  28.4 0.0 collective-permute-done.4.buf_d
  28.4 10.1 %shard_map.215 = (f32[2304,512]{1,0:T(8,128)S(1)}, f32[2304,512]{1,0:T(8,128)S(1)}) custom-call(s32[34]{0:T(128)S(1)} %pad_add_fusion.meta, bf16[2304,512]{1,0:T(8,128)(2,1)S(1)} %get-tuple-element.72.ad, bf16[2304,512]{1,0:T(8,128)(2,1)S(1)} %get-tuple-element.73.low, bf16[2304,768]{1,0:T(8,128)(2,1)S(1)} %get-tuple-element.74.act, ...), custom_call_target="tpu_custom_call" | custom-call | tf_op jit(solution)/shard_map/pallas_call | solution.py:373
  38.5 0.0 collective-permute-done.2
  38.6 0.1 fusion
  38.7 5.1 %collective-permute-start.7 = (bf16[384,128]{1,0:T(8,128)(2,1)S(1)}, bf16[384,128]{1,0:T(8,128)(2,1)S(1)}, u32[]{:S(2)}, u32[]{:S(2)}) collective-permute-start(bf16[384,128]{1,0:T(8,128)(2,1)S(1)} %get-tuple-element.125), channel_id=1, source_target_pairs={{0,24},{4,28},{8,16},{12,20},{16,8},{20,12},{24,0},{28,4},{1,25},{... | collective-permute-start | bytes 294920 | tf_op jit(solution)/shard_map/ppermute | solution.py:667
  43.8 0.0 collective-permute-start.6
  43.8 0.6 collective-permute-start.5
  44.5 8.7 %shard_map.216 = (bf16[16,256,512]{2,1,0:T(8,128)(2,1)}, bf16[8,256,512]{2,1,0:T(8,128)(2,1)S(1)}, f32[8,4,288,128]{3,2,1,0:T(8,128)S(1)}, f32[16,512]{1,0:T(8,128)S(1)}, f32[16,512]{1,0:T(8,128)S(1)}) custom-call(s32[34]{0:T(128)S(1)} %pad_add_fusion.meta, bf16[8,256,512]{2,1,0:T(8,128)(2,1)S(1)} %get-tuple-element.81.tok, ...), custom_call_target="tpu_custom_call" | custom-call | bytes 40000000 | tf_op jit(solution)/shard_map/pallas_call | solution.py:492
  53.1 0.0 collective-permute-done.7.refs_2_
  53.2 0.0 collective-permute-done.6.refs_1_
  53.2 0.0 collective-permute-done.5.refs_0_
  53.2 0.1 collective-permute-start.8
  53.3 1.2 %collective-permute-done.8.recv = f32[16,512]{1,0:T(8,128)S(1)} collective-permute-done((f32[16,512]{1,0:T(8,128)S(1)}, f32[16,512]{1,0:T(8,128)S(1)}, u32[]{:S(2)}, u32[]{:S(2)}) %collective-permute-start.8) | collective-permute-done | bytes 32800 | tf_op jit(solution)/shard_map/ppermute | solution.py:662
  54.5 0.2 collective-permute-start.9
  54.7 4.3 %collective-permute-start.12 = (bf16[448,128]{1,0:T(8,128)(2,1)S(1)}, bf16[448,128]{1,0:T(8,128)(2,1)S(1)}, u32[]{:S(2)}, u32[]{:S(2)}) collective-permute-start(bf16[448,128]{1,0:T(8,128)(2,1)S(1)} %get-tuple-element.105.refs_0_), channel_id=1, source_target_pairs={{0,24},{4,28},{8,16},{12,20},{16,8},{20,12},{24,0},{28,4},{1,25},{... | collective-permute-start | bytes 344072 | tf_op jit(solution)/shard_map/ppermute | solution.py:667
  58.9 0.0 collective-permute-start.11
  58.9 0.6 collective-permute-start.10
  59.6 0.4 collective-permute-start.13
  59.9 0.0 collective-permute-done.9.other
  59.9 4.5 %shard_map.217 = (bf16[16,256,512]{2,1,0:T(8,128)(2,1)}, f32[16,256,512]{2,1,0:T(8,128)}, bf16[8,256,512]{2,1,0:T(8,128)(2,1)S(1)}) custom-call(s32[34]{0:T(128)S(1)} %pad_add_fusion.meta, bf16[8,256,512]{2,1,0:T(8,128)(2,1)S(1)} %get-tuple-element.67.cot, f32[8,4,288,128]{3,2,1,0:T(8,128)S(1)} %get-tuple-element.91.cgp, ...), custom_call_target="tpu_custom_call", output_to_operand_aliasing={{0}: (5, {})} | custom-call | bytes 40000000 | tf_op jit(solution)/shard_map/pallas_call | solution.py:554
  64.4 0.0 collective-permute-done.13.theirs
  64.5 0.0 collective-permute-done.12.refs_3_
  64.5 4.3 %collective-permute-done.11.refs_2_ = bf16[448,128]{1,0:T(8,128)(2,1)S(1)} collective-permute-done((bf16[448,128]{1,0:T(8,128)(2,1)S(1)}, bf16[448,128]{1,0:T(8,128)(2,1)S(1)}, u32[]{:S(2)}, u32[]{:S(2)}) %collective-permute-start.11) | collective-permute-done | bytes 114720 | tf_op jit(solution)/shard_map/ppermute | solution.py:667
  68.8 0.0 collective-permute-done.10.refs_1_
  68.8 0.0 collective-permute-start.15
  68.8 0.4 collective-permute-start.14
  69.2 3.7 %collective-permute-done.15.other = bf16[8,256,512]{2,1,0:T(8,128)(2,1)S(1)} collective-permute-done((bf16[8,256,512]{2,1,0:T(8,128)(2,1)S(1)}, bf16[8,256,512]{2,1,0:T(8,128)(2,1)S(1)}, u32[]{:S(2)}, u32[]{:S(2)}) %collective-permute-start.15) | collective-permute-done | bytes 2097184 | tf_op jit(solution)/shard_map/ppermute | solution.py:662
  72.9 2.6 %shard_map.220 = f32[16,256,512]{2,1,0:T(8,128)} custom-call(s32[34]{0:T(128)S(1)} %pad_add_fusion.meta, bf16[8,256,512]{2,1,0:T(8,128)(2,1)S(1)} %collective-permute-done.15.other, f32[16,256,512]{2,1,0:T(8,128)} %get-tuple-element.110.gtok_in), custom_call_target="tpu_custom_call", output_to_operand_aliasing={{}: (2, {})} | custom-call | bytes 20000000 | tf_op jit(solution)/shard_map/pallas_call | solution.py:575
  75.6 3.1 %collective-permute-done.14.far = bf16[1216,128]{1,0:T(8,128)(2,1)S(1)} collective-permute-done((bf16[1216,128]{1,0:T(8,128)(2,1)S(1)}, bf16[1216,128]{1,0:T(8,128)(2,1)S(1)}, u32[]{:S(2)}, u32[]{:S(2)}) %collective-permute-start.14) | collective-permute-done | bytes 311328 | tf_op jit(solution)/shard_map/ppermute | solution.py:667
  78.7 1.9 %shard_map.221 = (f32[7,512]{1,0:T(8,128)}, f32[512]{0:T(512)}, f32[2,512]{1,0:T(2,128)}, f32[2,512]{1,0:T(2,128)}, f32[512,384]{1,0:T(8,128)}, /*index=5*/f32[3...) custom-call(s32[34]{0:T(128)S(1)} %pad_add_fusion.meta, bf16[384,128]{1,0:T(8,128)(2,1)S(1)} %get-tuple-element.103.mine, ...), custom_call_target="tpu_custom_call" | custom-call | tf_op jit(solution)/shard_map/pallas_call | solution.py:653
  (3 shorter events, 0.1 us)
Async XLA Ops:
  1.9 3.8 %collective-permute-start = (bf16[3088,128]{1,0:T(8,128)(2,1)S(1)}, bf16[3088,128]{1,0:T(8,128)(2,1)S(1)}, u32[]{:S(2)}, u32[]{:S(2)}) collective-permute-start(bf16[3088,128]{1,0:T(8,128)(2,1)S(1)} %shard_map.212.buf_a), channel_id=1, source_target_pairs={{0,1},{1,0},{2,3},{3,2},{4,5},{5,4},{6,7},{7,6},{8,9},{9,8},{10,11... | collective-permute-start | bytes 2371592 | tf_op jit(solution)/shard_map/ppermute | solution.py:662
  2.4 20.8 %collective-permute-start.3 = (bf16[3088,128]{1,0:T(8,128)(2,1)S(1)}, bf16[3088,128]{1,0:T(8,128)(2,1)S(1)}, u32[]{:S(2)}, u32[]{:S(2)}) collective-permute-start(bf16[3088,128]{1,0:T(8,128)(2,1)S(1)} %shard_map.212.buf_a), channel_id=1, source_target_pairs={{0,2},{1,3},{2,0},{3,1},{4,6},{5,7},{6,4},{7,5},{8,10},{9,11},{10,... | collective-permute-start | bytes 2371592 | tf_op jit(solution)/shard_map/ppermute | solution.py:662
  22.1 2.4 %collective-permute-start.1 = (bf16[3072,128]{1,0:T(8,128)(2,1)S(1)}, bf16[3072,128]{1,0:T(8,128)(2,1)S(1)}, u32[]{:S(2)}, u32[]{:S(2)}) collective-permute-start(bf16[3072,128]{1,0:T(8,128)(2,1)S(1)} %get-tuple-element.69), channel_id=1, source_target_pairs={{0,1},{1,0},{2,3},{3,2},{4,5},{5,4},{6,7},{7,6},{8,9},{9,8},{10,11... | collective-permute-start | bytes 2359304 | tf_op jit(solution)/shard_map/ppermute | solution.py:662
  23.2 5.2 %collective-permute-start.4 = (bf16[3088,128]{1,0:T(8,128)(2,1)S(1)}, bf16[3088,128]{1,0:T(8,128)(2,1)S(1)}, u32[]{:S(2)}, u32[]{:S(2)}) collective-permute-start(bf16[3088,128]{1,0:T(8,128)(2,1)S(1)} %collective-permute-done.3.buf_c), channel_id=1, source_target_pairs={{0,1},{1,0},{2,3},{3,2},{4,5},{5,4},{6,7},{7,6},{8,9},{9,8},{10,11... | collective-permute-start | bytes 2371592 | tf_op jit(solution)/shard_map/ppermute | solution.py:662
  25.1 13.4 %collective-permute-start.2 = (bf16[1536,128]{1,0:T(8,128)(2,1)S(1)}, bf16[1536,128]{1,0:T(8,128)(2,1)S(1)}, u32[]{:S(2)}, u32[]{:S(2)}) collective-permute-start(bf16[1536,128]{1,0:T(8,128)(2,1)S(1)} %get-tuple-element.71), channel_id=1, source_target_pairs={{0,4},{4,0},{8,12},{12,8},{16,20},{20,16},{24,28},{28,24},{1,5},{5... | collective-permute-start | bytes 1179656 | tf_op jit(solution)/shard_map/ppermute | solution.py:667
  38.7 14.5 %collective-permute-start.7 = (bf16[384,128]{1,0:T(8,128)(2,1)S(1)}, bf16[384,128]{1,0:T(8,128)(2,1)S(1)}, u32[]{:S(2)}, u32[]{:S(2)}) collective-permute-start(bf16[384,128]{1,0:T(8,128)(2,1)S(1)} %get-tuple-element.125), channel_id=1, source_target_pairs={{0,24},{4,28},{8,16},{12,20},{16,8},{20,12},{24,0},{28,4},{1,25},{... | collective-permute-start | bytes 294920 | tf_op jit(solution)/shard_map/ppermute | solution.py:667
  43.8 9.3 %collective-permute-start.6 = (bf16[384,128]{1,0:T(8,128)(2,1)S(1)}, bf16[384,128]{1,0:T(8,128)(2,1)S(1)}, u32[]{:S(2)}, u32[]{:S(2)}) collective-permute-start(bf16[384,128]{1,0:T(8,128)(2,1)S(1)} %get-tuple-element.126), channel_id=1, source_target_pairs={{0,16},{4,20},{8,24},{12,28},{16,0},{20,4},{24,8},{28,12},{1,17},{... | collective-permute-start | bytes 294920 | tf_op jit(solution)/shard_map/ppermute | solution.py:667
  43.8 9.3 %collective-permute-start.5 = (bf16[384,128]{1,0:T(8,128)(2,1)S(1)}, bf16[384,128]{1,0:T(8,128)(2,1)S(1)}, u32[]{:S(2)}, u32[]{:S(2)}) collective-permute-start(bf16[384,128]{1,0:T(8,128)(2,1)S(1)} %get-tuple-element.127), channel_id=1, source_target_pairs={{0,8},{4,12},{8,0},{12,4},{16,24},{20,28},{24,16},{28,20},{1,9},{5... | collective-permute-start | bytes 294920 | tf_op jit(solution)/shard_map/ppermute | solution.py:667
  53.2 1.3 %collective-permute-start.8 = (f32[16,512]{1,0:T(8,128)S(1)}, f32[16,512]{1,0:T(8,128)S(1)}, u32[]{:S(2)}, u32[]{:S(2)}) collective-permute-start(f32[16,512]{1,0:T(8,128)S(1)} %get-tuple-element.92), channel_id=1, source_target_pairs={{0,1},{1,0},{2,3},{3,2},{4,5},{5,4},{6,7},{7,6},{8,9},{9,8},{10,11... | collective-permute-start | bytes 98312 | tf_op jit(solution)/shard_map/ppermute | solution.py:662
  54.5 5.5 %collective-permute-start.9 = (bf16[8,256,512]{2,1,0:T(8,128)(2,1)S(1)}, bf16[8,256,512]{2,1,0:T(8,128)(2,1)S(1)}, u32[]{:S(2)}, u32[]{:S(2)}) collective-permute-start(bf16[8,256,512]{2,1,0:T(8,128)(2,1)S(1)} %get-tuple-element.94), channel_id=1, source_target_pairs={{0,1},{1,0},{2,3},{3,2},{4,5},{5,4},{6,7},{7,6},{8,9},{9,8},{10,11... | collective-permute-start | bytes 6291464 | tf_op jit(solution)/shard_map/ppermute | solution.py:662
  54.7 9.8 %collective-permute-start.12 = (bf16[448,128]{1,0:T(8,128)(2,1)S(1)}, bf16[448,128]{1,0:T(8,128)(2,1)S(1)}, u32[]{:S(2)}, u32[]{:S(2)}) collective-permute-start(bf16[448,128]{1,0:T(8,128)(2,1)S(1)} %get-tuple-element.105.refs_0_), channel_id=1, source_target_pairs={{0,24},{4,28},{8,16},{12,20},{16,8},{20,12},{24,0},{28,4},{1,25},{... | collective-permute-start | bytes 344072 | tf_op jit(solution)/shard_map/ppermute | solution.py:667
  58.9 9.8 %collective-permute-start.11 = (bf16[448,128]{1,0:T(8,128)(2,1)S(1)}, bf16[448,128]{1,0:T(8,128)(2,1)S(1)}, u32[]{:S(2)}, u32[]{:S(2)}) collective-permute-start(bf16[448,128]{1,0:T(8,128)(2,1)S(1)} %get-tuple-element.105.refs_0_), channel_id=1, source_target_pairs={{0,16},{4,20},{8,24},{12,28},{16,0},{20,4},{24,8},{28,12},{1,17},{... | collective-permute-start | bytes 344072 | tf_op jit(solution)/shard_map/ppermute | solution.py:667
  58.9 9.8 %collective-permute-start.10 = (bf16[448,128]{1,0:T(8,128)(2,1)S(1)}, bf16[448,128]{1,0:T(8,128)(2,1)S(1)}, u32[]{:S(2)}, u32[]{:S(2)}) collective-permute-start(bf16[448,128]{1,0:T(8,128)(2,1)S(1)} %get-tuple-element.105.refs_0_), channel_id=1, source_target_pairs={{0,8},{4,12},{8,0},{12,4},{16,24},{20,28},{24,16},{28,20},{1,9},{5... | collective-permute-start | bytes 344072 | tf_op jit(solution)/shard_map/ppermute | solution.py:667
  59.6 4.9 %collective-permute-start.13 = (bf16[384,128]{1,0:T(8,128)(2,1)S(1)}, bf16[384,128]{1,0:T(8,128)(2,1)S(1)}, u32[]{:S(2)}, u32[]{:S(2)}) collective-permute-start(bf16[384,128]{1,0:T(8,128)(2,1)S(1)} %get-tuple-element.103.mine), channel_id=1, source_target_pairs={{0,4},{4,0},{8,12},{12,8},{16,20},{20,16},{24,28},{28,24},{1,5},{5... | collective-permute-start | bytes 294920 | tf_op jit(solution)/shard_map/ppermute | solution.py:667
  68.8 4.2 %collective-permute-start.15 = (bf16[8,256,512]{2,1,0:T(8,128)(2,1)S(1)}, bf16[8,256,512]{2,1,0:T(8,128)(2,1)S(1)}, u32[]{:S(2)}, u32[]{:S(2)}) collective-permute-start(bf16[8,256,512]{2,1,0:T(8,128)(2,1)S(1)} %get-tuple-element.109), channel_id=1, source_target_pairs={{0,1},{1,0},{2,3},{3,2},{4,5},{5,4},{6,7},{7,6},{8,9},{9,8},{10,11... | collective-permute-start | bytes 6291464 | tf_op jit(solution)/shard_map/ppermute | solution.py:662
  68.8 9.8 %collective-permute-start.14 = (bf16[1216,128]{1,0:T(8,128)(2,1)S(1)}, bf16[1216,128]{1,0:T(8,128)(2,1)S(1)}, u32[]{:S(2)}, u32[]{:S(2)}) collective-permute-start(bf16[1216,128]{1,0:T(8,128)(2,1)S(1)} %shard_map.219.near), channel_id=1, source_target_pairs={{0,4},{4,0},{8,12},{12,8},{16,20},{20,16},{24,28},{28,24},{1,5},{5... | collective-permute-start | bytes 933896 | tf_op jit(solution)/shard_map/ppermute | solution.py:667

commit v6 on v5

--- a/solution.py
+++ b/solution.py
@@ -134,9 +134,9 @@
             row[:, lane(at)] = bias[side, q:q + 1, :].astype(F32)
 
 
-def front_kernel(n, meta, tok_hbm, cot_hbm, cw, cb, ns, nsh, gamma, bout, buf_a, buf_b,
-                 ad, nrm, low, inv, act, pre, win, wout, keep, send, gbo, gbi, tok, cot, consts,
-                 offs, pad, ad_s, nrm_s, low_s, inv_s, bias, bias_row, dwo, dwi, sems, item_sems):
+def front_kernel(n, counts_hbm, groups_hbm, tok_hbm, cot_hbm, cw, cb, ns, nsh, gamma, bout, buf_a, buf_b,
+                 ad, nrm, low, inv, act, pre, win, wout, keep, send, gbo, gbi, tok, cot, consts, meta,
+                 offs, counts_s, groups_s, pad, ad_s, nrm_s, low_s, inv_s, bias, bias_row, dwo, dwi, sems, item_sems, meta_sems):
     s = pl.program_id(0)
     frames, width = tok.shape[1], tok.shape[2]
     taps, rates = cw.shape[0], ns.shape[0]
@@ -146,13 +146,15 @@
     copies = weight_copies(buf_a, 0, win, wout, bias, sems) + weight_copies(buf_b, 1, win, wout, bias, sems)
 
     def fetch(j):
-        at = meta[0] * n + j
+        at = (lax.axis_index("tp") & 1) * n + j
         return [pltpu.make_async_copy(src.at[at], dst.at[j], item_sems.at[i, j])
                 for i, (src, dst) in enumerate(((tok_hbm, tok), (cot_hbm, cot)))]
 
     @pl.when(s == 0)
     def _():
-        for c in fetch(0) + fetch(1):
+        tables = [pltpu.make_async_copy(counts_hbm, counts_s, meta_sems.at[0]),
+                  pltpu.make_async_copy(groups_hbm, groups_s, meta_sems.at[1])]
+        for c in tables + fetch(0) + fetch(1):
             c.start()
         for c in copies:
             c.start()
@@ -164,10 +166,17 @@
         consts[taps:taps + 1, :] = as_row(gamma)
         consts[taps + 1:taps + 2, :] = as_row(bout)
         consts[taps + 2:taps + 2 + rates, :] = ns[...].astype(F32)
-        place_items(n, meta, offs)
         offs[n + 2] = 0
         gbo[...] = jnp.zeros_like(gbo)
         pad[...] = jnp.zeros_like(pad)
+        meta[0] = lax.axis_index("tp") & 1
+        meta[1] = lax.axis_index("dp")
+        for c in tables:
+            c.wait()
+        for j in range(2 * n):
+            meta[2 + j] = counts_s[j]
+            meta[2 + 2 * n + j] = groups_s[j]
+        place_items(n, meta, offs)
 
     def flush(j):
         dst = pl.ds(pl.multiple_of(offs[j], 16), frames)
@@ -276,7 +285,10 @@
     @pl.when(jnp.logical_not(ready))
     def _():
         consts = setup()
-        add_gbo(lax.fori_loop(0, pl.cdiv(count, CHUNK), lambda i, acc: conv_step(i, acc, consts), none))
+        state = none
+        for i in range(frames // CHUNK):
+            state = conv_step(i, state, consts)
+        add_gbo(state)
 
     @pl.when(s == n - 1)
     def _():
@@ -298,7 +310,7 @@
                 dst[base + q * width:base + (q + 1) * width, :] = dwi[:, lane(side * (h // LANES) + q)].astype(dst.dtype)
 
 
-def front(meta, tok, cot, cw, cb, ns, nsh, gamma, bout, buf_a, buf_b, h):
+def front(counts, groups, tok, cot, cw, cb, ns, nsh, gamma, bout, buf_a, buf_b, h):
     items, frames, width = tok.shape
     n = items // 2
     rows = n * frames + TILE
@@ -307,23 +319,24 @@
     n_consts = -(-(cw.shape[0] + 2 + ns.shape[0]) // 8) * 8
     return pl.pallas_call(
         functools.partial(front_kernel, n),
-        grid_spec=pltpu.PrefetchScalarGridSpec(
-            num_scalar_prefetch=1, grid=(n,),
-            in_specs=[hbm()] * 2 + [whole(v.shape) for v in (cw, cb, ns, nsh, gamma, bout)] + [hbm()] * 2,
-            out_specs=[vmem()] * 15,
-            scratch_shapes=[pltpu.SMEM((n + 3,), jnp.int32),
+        grid_spec=pl.GridSpec(
+            grid=(n,),
+            in_specs=[hbm()] * 4 + [whole(v.shape) for v in (cw, cb, ns, nsh, gamma, bout)] + [hbm()] * 2,
+            out_specs=[vmem()] * 15 + [smem()],
+            scratch_shapes=[pltpu.SMEM((n + 3,), jnp.int32), pltpu.SMEM((items,), jnp.int32), pltpu.SMEM((items,), jnp.int32),
                             pltpu.VMEM((wq, frames + 4 * PAD, LANES), F32),
                             pltpu.VMEM((frames, width), BF), pltpu.VMEM((frames, width), BF),
                             pltpu.VMEM((frames, width), BF), pltpu.VMEM((frames, LANES), F32),
                             pltpu.VMEM((2, 16, LANES), BF), pltpu.VMEM((1, 2 * h), F32),
                             pltpu.VMEM((2 * h, width), F32), pltpu.VMEM((width, 2 * h), F32),
-                            pltpu.SemaphoreType.DMA((2, hq + wq + 1)), pltpu.SemaphoreType.DMA((2, n))]),
+                            pltpu.SemaphoreType.DMA((2, hq + wq + 1)), pltpu.SemaphoreType.DMA((2, n)),
+                            pltpu.SemaphoreType.DMA((2,))]),
         out_shape=[struct((rows, width), BF)] * 3 + [struct((rows, LANES), F32)]
         + [struct((rows, 2 * h), BF)] * 2 + [struct((width, 2 * h), BF), struct((2 * h, width), BF)]
         + [struct((packed, LANES), F32), struct((packed, LANES), BF), struct((8, width), F32), struct((8, 2 * h), F32)]
-        + [struct((n, frames, width), BF)] * 2 + [struct((n_consts, width), F32)],
+        + [struct((n, frames, width), BF)] * 2 + [struct((n_consts, width), F32), struct((2 + 2 * items,), jnp.int32)],
         compiler_params=params(), cost_estimate=cost(0),
-    )(meta, tok, cot, cw, cb, ns, nsh, gamma, bout, buf_a, buf_b)
+    )(counts, groups, tok, cot, cw, cb, ns, nsh, gamma, bout, buf_a, buf_b)
 
 
 def combine_kernel(dp, meta, keep, recv, stay, leave):
@@ -384,16 +397,13 @@
 
 
 def norm_grad_kernel(n, taps, rates, meta, tok, cot, branch, ag, nrm, inv, gbo, gbi, consts,
-                     out, out_own, cgp, small_keep, small_send, offs, sums, sems):
+                     cgp, small_keep, small_send, offs, sums):
     s = pl.program_id(0)
     frames, width = tok.shape[1], tok.shape[2]
     half = taps // 2
     wq = width // LANES
     h = gbi.shape[1] // 2
 
-    def place(j):
-        return pltpu.make_async_copy(out_own.at[j], out.at[meta[0] * n + j], sems.at[j])
-
     @pl.when(s == 0)
     def _():
         place_items(n, meta, offs)
@@ -404,7 +414,6 @@
     group = meta[2 + 2 * n + item]
     off = offs[s]
     scale = pick(consts.at[taps + 2:taps + 2 + rates], group)
-    gam = consts[taps:taps + 1, :]
     zero = jnp.zeros((8, LANES), F32)
     steps = pl.cdiv(count, WIDE_CHUNK)
 
@@ -418,8 +427,6 @@
         for q in range(wq):
             a_ls, a_sc, a_sh = accs[3 * q:3 * q + 3]
             br = jnp.where(live, branch[src, lane(q)], 0.0)
-            tk = jnp.where(live, tok[s, here, lane(q)].astype(F32), 0.0)
-            out_own[s, here, lane(q)] = (tk + gam[:, lane(q)] * br).astype(BF)
             g = jnp.where(live, ag[src, lane(q)], 0.0)
             nr = nrm[src, lane(q)].astype(F32)
             new += [a_ls + fold(cot[s, here, lane(q)].astype(F32) * br), a_sc + fold(g * nr), a_sh + fold(g)]
@@ -442,13 +449,11 @@
 
     def clear(i, _):
         r0 = pl.multiple_of(i * WIDE_CHUNK, WIDE_CHUNK)
-        out_own[s, pl.ds(r0, WIDE_CHUNK), :] = jnp.zeros((WIDE_CHUNK, width), BF)
         for q in range(wq):
             cgp[s, q, pl.ds(pl.multiple_of(r0 + PAD, 8), WIDE_CHUNK), :] = jnp.zeros((WIDE_CHUNK, LANES), F32)
         return 0
 
     lax.fori_loop(steps, frames // WIDE_CHUNK, clear, 0)
-    place(s).start()
     for q in range(wq):
         cgp[s, q, :PAD, :] = jnp.zeros((PAD, LANES), F32)
         cgp[s, q, PAD + frames:, :] = jnp.zeros((cgp.shape[2] - PAD - frames, LANES), F32)
@@ -481,8 +486,6 @@
         for side, dst in ((0, small_keep), (1, small_send)):
             tail = [jnp.concatenate([gb[:, side * h:(side + 1) * h], fill], axis=1)]
             dst[...] = jnp.concatenate(rows + tail + spare, axis=0)
-        for j in range(n):
-            place(j).wait()
 
 
 def norm_grad(meta, tok, cot, branch, ag, nrm, inv, gbo, gbi, consts, taps, rates):
@@ -491,17 +494,55 @@
     n_small = -(-(taps + 4 + 2 * rates) // 8) * 8
     return pl.pallas_call(
         functools.partial(norm_grad_kernel, n, taps, rates), grid=(n,),
-        in_specs=[smem()] + [vmem()] * 9, out_specs=[hbm()] + [vmem()] * 4,
+        in_specs=[smem()] + [vmem()] * 9, out_specs=[vmem()] * 3,
         scratch_shapes=[pltpu.SMEM((n + 2,), jnp.int32),
-                        pltpu.VMEM((taps + 2 + 2 * rates, 8, width), F32),
-                        pltpu.SemaphoreType.DMA((n,))],
-        out_shape=[struct((2 * n, frames, width), BF), struct((n, frames, width), BF),
-                   struct((n, wq, frames + 4 * PAD, LANES), F32)] + [struct((n_small, width), F32)] * 2,
+                        pltpu.VMEM((taps + 2 + 2 * rates, 8, width), F32)],
+        out_shape=[struct((n, wq, frames + 4 * PAD, LANES), F32)] + [struct((n_small, width), F32)] * 2,
         compiler_params=params(), cost_estimate=cost(40000000),
     )(meta, tok, cot, branch, ag, nrm, inv, gbo, gbi, consts)
 
 
-def token_grad_kernel(n, taps, meta, cot, cgp, consts, other, out_in, out, gtok, gtok_own, stage, sems, out_sem):
+def block_out_kernel(n, taps, meta, tok, branch, consts, out, own, offs, sems):
+    s = pl.program_id(0)
+    frames, width = tok.shape[1], tok.shape[2]
+
+    def place(j):
+        return pltpu.make_async_copy(own.at[j], out.at[meta[0] * n + j], sems.at[j])
+
+    @pl.when(s == 0)
+    def _():
+        place_items(n, meta, offs)
+
+    count = meta[2 + meta[0] * n + s]
+    off = offs[s]
+    gam = consts[taps:taps + 1, :]
+    for i in range(frames // CHUNK):
+        here = pl.ds(i * CHUNK, CHUNK)
+        live = (lax.broadcasted_iota(jnp.int32, (CHUNK, LANES), 0) + i * CHUNK) < count
+        src = pl.ds(pl.multiple_of(off + i * CHUNK, 16), CHUNK)
+        for q in range(width // LANES):
+            value = tok[s, here, lane(q)].astype(F32) + gam[:, lane(q)] * branch[src, lane(q)]
+            own[s, here, lane(q)] = jnp.where(live, value, 0.0).astype(BF)
+    place(s).start()
+
+    @pl.when(s == n - 1)
+    def _():
+        for j in range(n):
+            place(j).wait()
+
+
+def block_out(meta, tok, branch, consts, taps):
+    n, frames, width = tok.shape
+    return pl.pallas_call(
+        functools.partial(block_out_kernel, n, taps), grid=(n,),
+        in_specs=[smem()] + [vmem()] * 3, out_specs=[hbm(), vmem()],
+        scratch_shapes=[pltpu.SMEM((n + 2,), jnp.int32), pltpu.SemaphoreType.DMA((n,))],
+        out_shape=[struct((2 * n, frames, width), BF), struct((n, frames, width), BF)],
+        compiler_params=params(), cost_estimate=cost(40000000),
+    )(meta, tok, branch, consts)
+
+
+def token_grad_kernel(n, taps, meta, cot, cgp, consts, gtok, gtok_own, stage, sems):
     s = pl.program_id(0)
     frames, width = cot.shape[1], cot.shape[2]
     half = taps // 2
@@ -509,14 +550,9 @@
     count = meta[2 + meta[0] * n + s]
     w = consts[:taps, :]
     steps = pl.cdiv(count, CHUNK)
-    other_copy = pltpu.make_async_copy(other, out.at[pl.ds((1 - meta[0]) * n, n)], out_sem)
 
     def place(j):
         return pltpu.make_async_copy(stage.at[j], gtok.at[meta[0] * n + j], sems.at[j])
-
-    @pl.when(s == 0)
-    def _():
-        other_copy.start()
 
     def conv_step(i, _):
         r0 = pl.multiple_of(i * CHUNK, CHUNK)
@@ -544,41 +580,44 @@
 
     @pl.when(s == n - 1)
     def _():
-        other_copy.wait()
         for j in range(n):
             place(j).wait()
 
 
-def token_grad(meta, cot, cgp, consts, other, out, taps):
+def token_grad(meta, cot, cgp, consts, taps):
     n, frames, width = cot.shape
     return pl.pallas_call(
         functools.partial(token_grad_kernel, n, taps), grid=(n,),
-        in_specs=[smem()] + [vmem()] * 3 + [hbm()] * 2, out_specs=[hbm(), hbm(), vmem()],
-        scratch_shapes=[pltpu.VMEM((n, frames, width), F32), pltpu.SemaphoreType.DMA((n,)), pltpu.SemaphoreType.DMA],
-        out_shape=[struct(out.shape, BF), struct(out.shape, F32), struct((n, frames, width), BF)],
-        input_output_aliases={5: 0},
+        in_specs=[smem()] + [vmem()] * 3, out_specs=[hbm(), vmem()],
+        scratch_shapes=[pltpu.VMEM((n, frames, width), F32), pltpu.SemaphoreType.DMA((n,))],
+        out_shape=[struct((2 * n, frames, width), F32), struct((n, frames, width), BF)],
         compiler_params=params(), cost_estimate=cost(40000000),
-    )(meta, cot, cgp, consts, other, out)
-
-
-def merge_kernel(n, meta, other, gtok_in, gtok, stage, sems):
-    copies = [pltpu.make_async_copy(stage.at[j], gtok.at[(1 - meta[0]) * n + j], sems.at[j]) for j in range(n)]
+    )(meta, cot, cgp, consts)
+
+
+def merge_kernel(n, meta, out_b, gtok_b, out_in, gtok_in, out, gtok, stage, sems, out_sem):
+    first = (1 - meta[0]) * n
+    whole_copy = pltpu.make_async_copy(out_b, out.at[pl.ds(first, n)], out_sem)
+    whole_copy.start()
+    copies = [pltpu.make_async_copy(stage.at[j], gtok.at[first + j], sems.at[j]) for j in range(n)]
     for j in range(n):
-        stage[j] = other[j].astype(F32)
+        stage[j] = gtok_b[j].astype(F32)
         copies[j].start()
+    whole_copy.wait()
     for c in copies:
         c.wait()
 
 
-def merge(meta, other, gtok):
-    n = other.shape[0]
+def merge(meta, out_b, gtok_b, out, gtok):
+    n = out_b.shape[0]
     return pl.pallas_call(
         functools.partial(merge_kernel, n),
-        in_specs=[smem(), vmem(), hbm()], out_specs=hbm(), out_shape=struct(gtok.shape, F32),
-        scratch_shapes=[pltpu.VMEM(other.shape, F32), pltpu.SemaphoreType.DMA((n,))],
-        input_output_aliases={2: 0},
+        in_specs=[smem(), hbm(), vmem(), hbm(), hbm()], out_specs=[hbm(), hbm()],
+        out_shape=[struct(out.shape, BF), struct(gtok.shape, F32)],
+        scratch_shapes=[pltpu.VMEM(gtok_b.shape, F32), pltpu.SemaphoreType.DMA((n,)), pltpu.SemaphoreType.DMA],
+        input_output_aliases={3: 0, 4: 1},
         compiler_params=params(), cost_estimate=cost(20000000),
-    )(meta, other, gtok)
+    )(meta, out_b, gtok_b, out, gtok)
 
 
 def message_kernel(stay, keep, recv, *refs):
@@ -672,20 +711,17 @@
     width, h = weight_in.shape
     n = tokens.shape[0] // 2
     (tokens, cotangent, conv_weight, conv_bias, norm_scale, norm_shift, weight_in, bias_in, weight_out, bias_out,
-     layer_scale) = [pltpu.with_memory_space_constraint(v, pltpu.HBM) for v in (
+     layer_scale, frame_counts, rate_groups) = [pltpu.with_memory_space_constraint(v, pltpu.HBM) for v in (
          tokens, cotangent, conv_weight, conv_bias, norm_scale, norm_shift, weight_in, bias_in, weight_out, bias_out,
-         layer_scale)]
+         layer_scale, frame_counts, rate_groups)]
     taps, rates = conv_weight.shape[0], norm_scale.shape[0]
     dp = lax.axis_size("dp")
-    place = jnp.stack([lax.axis_index("tp") & 1, lax.axis_index("dp")]).astype(jnp.int32)
-    meta = jnp.concatenate([place, frame_counts, rate_groups])
-
     buf_a = pack(weight_in, bias_in, weight_out)
     buf_b = swap(buf_a, 1)
     buf_c = swap(buf_a, 2)
     buf_d = swap(buf_c, 1)
-    ad, nrm, low, inv, act, pre, win, wout, keep, send, gbo, gbi, tok, cot, consts = front(
-        meta, tokens, cotangent, conv_weight, conv_bias, norm_scale, norm_shift, layer_scale, bias_out, buf_a, buf_b, h)
+    ad, nrm, low, inv, act, pre, win, wout, keep, send, gbo, gbi, tok, cot, consts, meta = front(
+        frame_counts, rate_groups, tokens, cotangent, conv_weight, conv_bias, norm_scale, norm_shift, layer_scale, bias_out, buf_a, buf_b, h)
     stay, leave = combine(meta, keep, swap(send, 1), dp)
     arrived = across(leave, 1)
     branch, ag = mix(meta, ad, low, act, pre, win, wout, consts, buf_c, buf_d, n, taps)
@@ -693,20 +729,21 @@
     stay = (stay + arrived.astype(F32)).reshape(dp // 2, -1, LANES)
     pieces = [across(stay[d].astype(BF), 2 * d) for d in range(1, dp // 2)]
 
-    out, out_own, cgp, small_keep, small_send = norm_grad(
-        meta, tok, cot, branch, ag, nrm, inv, gbo, gbi, consts, taps, rates)
-    pieces, small_send, out_own, cgp = lax.optimization_barrier((pieces, small_send, out_own, cgp))
+    cgp, small_keep, small_send = norm_grad(meta, tok, cot, branch, ag, nrm, inv, gbo, gbi, consts, taps, rates)
+    pieces, small_send, cgp, branch = lax.optimization_barrier((pieces, small_send, cgp, branch))
     small_got = swap(small_send, 1)
-    small_got, out_own = lax.optimization_barrier((small_got, out_own))
     message, mine = make_message(stay.reshape(-1, LANES), small_keep, small_got, pieces)
     m = pieces[0].shape[0]
     near = [message] + [across(message, 2 * d) for d in range(1, dp // 2)]
     theirs = across(mine, 1)
-    out, gtok, gtok_own = token_grad(meta, cot, cgp, consts, swap(out_own, 1), out, taps)
+    out, out_own = block_out(meta, tok, branch, consts, taps)
+    cgp, out, out_own = lax.optimization_barrier((cgp, out, out_own))
+    out_b = swap(out_own, 1)
+    gtok, gtok_own = token_grad(meta, cot, cgp, consts, taps)
     near, theirs, gtok_own = lax.optimization_barrier((near, theirs, gtok_own))
     near = relay(m, near)
     far = across(near, 1)
-    gtok = merge(meta, swap(gtok_own, 1), gtok)
+    out, gtok = merge(meta, out_b, swap(gtok_own, 1), out, gtok)
     far, gtok = lax.optimization_barrier((far, gtok))
     gcw, gcb, gns, gnsh, gwi, gbi, gwo, gbo, gls = unpack(meta, mine, theirs, near, far, dp, taps, rates, width, h)
     return (out, gtok, gcw, gcb, gns, gnsh, gwi, gbi, gwo, gbo, gls)

time: 80.9 us -> 78.1 us (0.965)
  waiting for transfers between devices: 14.2 us -> 10.9 us
  Pallas kernels: 46.3 us -> 48.6 us
  starting transfers between devices: 18.4 us -> 17.5 us
    pallas_call x2 -> x3, Pallas kernels: 19 us -> 22.1 us  [the longest x1 16.2 us: front(): pl.pallas_call(functools.partial(front_kernel, n), grid_spec=pl.GridSpec(...]
    ppermute x9, waiting for transfers between devices: 7.39 us -> 4.34 us  [across(): return lax.ppermute(x, 'dp', [(i, i ^ step) for i in range(size)])]
  transfers between devices with their start and end apart: 16 -> 16, of which waited for: 6 -> 7; matrix products, arithmetic and copies ran while one was open for 1% -> 0% of each run, Pallas kernels for 53% -> 58%
where the time goes in v6:
time: 78.1 us; the launch traced here: 77.9 us
  Pallas kernels  48.6 us (62%)
  starting transfers between devices  17.5 us (22%)
  waiting for transfers between devices  10.9 us (14%)
    pallas_call x1, Pallas kernels, front(): pl.pallas_call(functools.partial(front_kernel, n), grid_spec=pl.GridSpec(...  16.2 us
    ppermute x9, starting transfers between devices, across(): return lax.ppermute(x, 'dp', [(i, i ^ step) for i in range(size)])  14.1 us
    pallas_call x1, Pallas kernels, mix(): pl.pallas_call(functools.partial(mix_kernel, n, taps), in_specs=[smem()]...  10.1 us
    pallas_call x1, Pallas kernels, norm_grad(): pl.pallas_call(functools.partial(norm_grad_kernel, n, taps, rates), grid=...  8.09 us
    ppermute x7, waiting for transfers between devices, swap(): return lax.ppermute(x, 'tp', [(i, i ^ step) for i in range(size)])  6.56 us
    pallas_call x1, Pallas kernels, token_grad(): pl.pallas_call(functools.partial(token_grad_kernel, n, taps), grid=(n,),...  4.42 us
    ppermute x9, waiting for transfers between devices, across(): return lax.ppermute(x, 'dp', [(i, i ^ step) for i in range(size)])  4.34 us
    ppermute x7, starting transfers between devices, swap(): return lax.ppermute(x, 'tp', [(i, i ^ step) for i in range(size)])  3.39 us
  transfers between devices with their start and end apart: 16, of which 7 were waited for; matrix products, arithmetic and copies ran while one was open for 0% of the time, Pallas kernels for 58%

profile of v6, /device:TPU:0, one launch (start us, length us, event | category | flops | bytes accessed | tf_op | source)
XLA Modules:
  0.0 77.9 jit_solution(12774582450922710593)
XLA Ops:
  0.6 1.3 %shard_map.212.buf_a = bf16[3088,128]{1,0:T(8,128)(2,1)S(1)} custom-call(bf16[512,384]{1,0:T(8,128)(2,1)} %wi.1, bf16[384]{0:T(512)(128)(2,1)} %bi.1, bf16[384,512]{1,0:T(8,128)(2,1)} %wo.1), custom_call_target="tpu_custom_call" | custom-call | tf_op jit(solution)/shard_map/pallas_call | solution.py:111
  1.9 0.5 collective-permute-start
  2.4 2.6 %collective-permute-start.3 = (bf16[3088,128]{1,0:T(8,128)(2,1)S(1)}, bf16[3088,128]{1,0:T(8,128)(2,1)S(1)}, u32[]{:S(2)}, u32[]{:S(2)}) collective-permute-start(bf16[3088,128]{1,0:T(8,128)(2,1)S(1)} %shard_map.212.buf_a), channel_id=1, source_target_pairs={{0,2},{1,3},{2,0},{3,1},{4,6},{5,7},{6,4},{7,5},{8,10},{9,11},{10,... | collective-permute-start | bytes 2371592 | tf_op jit(solution)/shard_map/ppermute | solution.py:701
  5.0 0.0 collective-permute-done.buf_b
  5.0 16.2 %shard_map.213 = (bf16[2304,512]{1,0:T(8,128)(2,1)S(1)}, bf16[2304,512]{1,0:T(8,128)(2,1)S(1)}, bf16[2304,512]{1,0:T(8,128)(2,1)S(1)}, f32[2304,128]{1,0:T(8,128...) custom-call(s32[16]{0:T(128)} %counts_hbm.1, ...), custom_call_target="tpu_custom_call" | custom-call | tf_op jit(solution)/shard_map/pallas_call | solution.py:320
  21.3 0.2 collective-permute-start.1
  21.5 1.7 %collective-permute-done.3.buf_c = bf16[3088,128]{1,0:T(8,128)(2,1)S(1)} collective-permute-done((bf16[3088,128]{1,0:T(8,128)(2,1)S(1)}, bf16[3088,128]{1,0:T(8,128)(2,1)S(1)}, u32[]{:S(2)}, u32[]{:S(2)}) %collective-permute-start.3) | collective-permute-done | bytes 790560 | tf_op jit(solution)/shard_map/ppermute | solution.py:701
  23.2 0.0 collective-permute-start.4
  23.2 0.4 collective-permute-done.1.recv
  23.6 0.7 shard_map.214
  24.3 3.2 %collective-permute-start.2 = (bf16[1536,128]{1,0:T(8,128)(2,1)S(1)}, bf16[1536,128]{1,0:T(8,128)(2,1)S(1)}, u32[]{:S(2)}, u32[]{:S(2)}) collective-permute-start(bf16[1536,128]{1,0:T(8,128)(2,1)S(1)} %get-tuple-element.74), channel_id=1, source_target_pairs={{0,4},{4,0},{8,12},{12,8},{16,20},{20,16},{24,28},{28,24},{1,5},{5... | collective-permute-start | bytes 1179656 | tf_op jit(solution)/shard_map/ppermute | solution.py:706
  27.4 0.0 collective-permute-done.4.buf_d
  27.4 10.1 %shard_map.215 = (f32[2304,512]{1,0:T(8,128)S(1)}, f32[2304,512]{1,0:T(8,128)S(1)}) custom-call(s32[34]{0:T(128)S(1)} %get-tuple-element.70.meta, bf16[2304,512]{1,0:T(8,128)(2,1)S(1)} %get-tuple-element.75.ad, bf16[2304,512]{1,0:T(8,128)(2,1)S(1)} %get-tuple-element.76.low, bf16[2304,768]{1,0:T(8,128)(2,1)S(1)} %get-tuple-element.77.act, ...), custom_call_target="tpu_custom_call" | custom-call | tf_op jit(solution)/shard_map/pallas_call | solution.py:386
  37.6 0.0 collective-permute-done.2
  37.6 0.1 fusion
  37.7 3.7 %collective-permute-start.7 = (bf16[384,128]{1,0:T(8,128)(2,1)S(1)}, bf16[384,128]{1,0:T(8,128)(2,1)S(1)}, u32[]{:S(2)}, u32[]{:S(2)}) collective-permute-start(bf16[384,128]{1,0:T(8,128)(2,1)S(1)} %get-tuple-element.131), channel_id=1, source_target_pairs={{0,24},{4,28},{8,16},{12,20},{16,8},{20,12},{24,0},{28,4},{1,25},{... | collective-permute-start | bytes 294920 | tf_op jit(solution)/shard_map/ppermute | solution.py:706
  41.4 1.2 %collective-permute-start.6 = (bf16[384,128]{1,0:T(8,128)(2,1)S(1)}, bf16[384,128]{1,0:T(8,128)(2,1)S(1)}, u32[]{:S(2)}, u32[]{:S(2)}) collective-permute-start(bf16[384,128]{1,0:T(8,128)(2,1)S(1)} %get-tuple-element.132), channel_id=1, source_target_pairs={{0,16},{4,20},{8,24},{12,28},{16,0},{20,4},{24,8},{28,12},{1,17},{... | collective-permute-start | bytes 294920 | tf_op jit(solution)/shard_map/ppermute | solution.py:706
  42.6 0.1 collective-permute-start.5
  42.7 8.1 %shard_map.216 = (f32[8,4,288,128]{3,2,1,0:T(8,128)S(1)}, f32[16,512]{1,0:T(8,128)S(1)}, f32[16,512]{1,0:T(8,128)S(1)}) custom-call(s32[34]{0:T(128)S(1)} %get-tuple-element.70.meta, bf16[8,256,512]{2,1,0:T(8,128)(2,1)S(1)} %get-tuple-element.84.tok, bf16[8,256,512]{2,1,0:T(8,128)(2,1)S(1)} %get-tuple-element.85.cot, ...), custom_call_target="tpu_custom_call" | custom-call | bytes 40000000 | tf_op jit(solution)/shard_map/pallas_call | solution.py:495
  50.8 0.0 collective-permute-done.7.refs_2_
  50.8 0.6 collective-permute-done.6.refs_1_
  51.4 0.0 collective-permute-done.5.refs_0_
  51.4 0.0 collective-permute-start.9
  51.4 1.2 %collective-permute-done.9.recv = f32[16,512]{1,0:T(8,128)S(1)} collective-permute-done((f32[16,512]{1,0:T(8,128)S(1)}, f32[16,512]{1,0:T(8,128)S(1)}, u32[]{:S(2)}, u32[]{:S(2)}) %collective-permute-start.9) | collective-permute-done | bytes 32800 | tf_op jit(solution)/shard_map/ppermute | solution.py:701
  52.7 3.0 %collective-permute-start.12 = (bf16[448,128]{1,0:T(8,128)(2,1)S(1)}, bf16[448,128]{1,0:T(8,128)(2,1)S(1)}, u32[]{:S(2)}, u32[]{:S(2)}) collective-permute-start(bf16[448,128]{1,0:T(8,128)(2,1)S(1)} %get-tuple-element.112.refs_0_), channel_id=1, source_target_pairs={{0,24},{4,28},{8,16},{12,20},{16,8},{20,12},{24,0},{28,4},{1,25},{... | collective-permute-start | bytes 344072 | tf_op jit(solution)/shard_map/ppermute | solution.py:706
  55.7 0.0 collective-permute-start.11
  55.7 1.4 %collective-permute-start.10 = (bf16[448,128]{1,0:T(8,128)(2,1)S(1)}, bf16[448,128]{1,0:T(8,128)(2,1)S(1)}, u32[]{:S(2)}, u32[]{:S(2)}) collective-permute-start(bf16[448,128]{1,0:T(8,128)(2,1)S(1)} %get-tuple-element.112.refs_0_), channel_id=1, source_target_pairs={{0,8},{4,12},{8,0},{12,4},{16,24},{20,28},{24,16},{28,20},{1,9},{5... | collective-permute-start | bytes 344072 | tf_op jit(solution)/shard_map/ppermute | solution.py:706
  57.2 0.7 collective-permute-start.13
  57.8 2.5 %shard_map.217 = (bf16[16,256,512]{2,1,0:T(8,128)(2,1)}, bf16[8,256,512]{2,1,0:T(8,128)(2,1)S(1)}) custom-call(s32[34]{0:T(128)S(1)} %get-tuple-element.70.meta, bf16[8,256,512]{2,1,0:T(8,128)(2,1)S(1)} %get-tuple-element.84.tok, f32[2304,512]{1,0:T(8,128)S(1)} %get-tuple-element.95.branch, f32[16,512]{1,0:T(8,128)S(1)} %get-tuple-element.81.consts), custom_call_target="tpu_custom_call" | custom-call | bytes 40000000 | tf_op jit(solution)/shard_map/pallas_call | solution.py:536
  60.4 0.1 collective-permute-start.8
  60.4 4.4 %shard_map.219 = (f32[16,256,512]{2,1,0:T(8,128)}, bf16[8,256,512]{2,1,0:T(8,128)(2,1)S(1)}) custom-call(s32[34]{0:T(128)S(1)} %get-tuple-element.70.meta, bf16[8,256,512]{2,1,0:T(8,128)(2,1)S(1)} %get-tuple-element.85.cot, f32[8,4,288,128]{3,2,1,0:T(8,128)S(1)} %get-tuple-element.106.cgp, f32[16,512]{1,0:T(8,128)S(1)} %get-tuple-element.81.consts), custom_call_target="tpu_custom_call" | custom-call | bytes 40000000 | tf_op jit(solution)/shard_map/pallas_call | solution.py:589
  64.9 0.0 collective-permute-done.13.theirs
  64.9 0.0 collective-permute-done.12.refs_3_
  64.9 1.3 %collective-permute-done.11.refs_2_ = bf16[448,128]{1,0:T(8,128)(2,1)S(1)} collective-permute-done((bf16[448,128]{1,0:T(8,128)(2,1)S(1)}, bf16[448,128]{1,0:T(8,128)(2,1)S(1)}, u32[]{:S(2)}, u32[]{:S(2)}) %collective-permute-start.11) | collective-permute-done | bytes 114720 | tf_op jit(solution)/shard_map/ppermute | solution.py:706
  66.2 0.0 collective-permute-done.10.refs_1_
  66.2 0.0 collective-permute-start.14
  66.2 0.9 %collective-permute-start.15 = (bf16[1216,128]{1,0:T(8,128)(2,1)S(1)}, bf16[1216,128]{1,0:T(8,128)(2,1)S(1)}, u32[]{:S(2)}, u32[]{:S(2)}) collective-permute-start(bf16[1216,128]{1,0:T(8,128)(2,1)S(1)} %shard_map.221.near), channel_id=1, source_target_pairs={{0,4},{4,0},{8,12},{12,8},{16,20},{20,16},{24,28},{28,24},{1,5},{5... | collective-permute-start | bytes 933896 | tf_op jit(solution)/shard_map/ppermute | solution.py:706
  67.1 0.0 collective-permute-done.8.out_b
  67.1 3.2 %collective-permute-done.14.gtok_b = bf16[8,256,512]{2,1,0:T(8,128)(2,1)S(1)} collective-permute-done((bf16[8,256,512]{2,1,0:T(8,128)(2,1)S(1)}, bf16[8,256,512]{2,1,0:T(8,128)(2,1)S(1)}, u32[]{:S(2)}, u32[]{:S(2)}) %collective-permute-start.14) | collective-permute-done | bytes 2097184 | tf_op jit(solution)/shard_map/ppermute | solution.py:701
  70.3 3.3 %shard_map.220 = (bf16[16,256,512]{2,1,0:T(8,128)(2,1)}, f32[16,256,512]{2,1,0:T(8,128)}) custom-call(s32[34]{0:T(128)S(1)} %get-tuple-element.70.meta, bf16[8,256,512]{2,1,0:T(8,128)(2,1)S(1)} %collective-permute-done.8.out_b, bf16[8,256,512]{2,1,0:T(8,128)(2,1)S(1)} %collective-permute-done.14.gtok_b, ...), custom_call_target="tpu_custom_call", output_to_operand_aliasing={{0}: (3, {}), {1}: (4, {})} | custom-call | bytes 20000000 | tf_op jit(solution)/shard_map/pallas_call | solution.py:613
  73.6 2.4 %collective-permute-done.15.far = bf16[1216,128]{1,0:T(8,128)(2,1)S(1)} collective-permute-done((bf16[1216,128]{1,0:T(8,128)(2,1)S(1)}, bf16[1216,128]{1,0:T(8,128)(2,1)S(1)}, u32[]{:S(2)}, u32[]{:S(2)}) %collective-permute-start.15) | collective-permute-done | bytes 311328 | tf_op jit(solution)/shard_map/ppermute | solution.py:706
  76.0 1.9 %shard_map.222 = (f32[7,512]{1,0:T(8,128)}, f32[512]{0:T(512)}, f32[2,512]{1,0:T(2,128)}, f32[2,512]{1,0:T(2,128)}, f32[512,384]{1,0:T(8,128)}, /*index=5*/f32[3...) custom-call(s32[34]{0:T(128)S(1)} %get-tuple-element.70.meta, bf16[384,128]{1,0:T(8,128)(2,1)S(1)} %get-tuple-element.105.mine, ...), custom_call_target="tpu_custom_call" | custom-call | tf_op jit(solution)/shard_map/pallas_call | solution.py:692
  (3 shorter events, 0.1 us)
Async XLA Ops:
  1.9 3.1 %collective-permute-start = (bf16[3088,128]{1,0:T(8,128)(2,1)S(1)}, bf16[3088,128]{1,0:T(8,128)(2,1)S(1)}, u32[]{:S(2)}, u32[]{:S(2)}) collective-permute-start(bf16[3088,128]{1,0:T(8,128)(2,1)S(1)} %shard_map.212.buf_a), channel_id=1, source_target_pairs={{0,1},{1,0},{2,3},{3,2},{4,5},{5,4},{6,7},{7,6},{8,9},{9,8},{10,11... | collective-permute-start | bytes 2371592 | tf_op jit(solution)/shard_map/ppermute | solution.py:701
  2.4 20.8 %collective-permute-start.3 = (bf16[3088,128]{1,0:T(8,128)(2,1)S(1)}, bf16[3088,128]{1,0:T(8,128)(2,1)S(1)}, u32[]{:S(2)}, u32[]{:S(2)}) collective-permute-start(bf16[3088,128]{1,0:T(8,128)(2,1)S(1)} %shard_map.212.buf_a), channel_id=1, source_target_pairs={{0,2},{1,3},{2,0},{3,1},{4,6},{5,7},{6,4},{7,5},{8,10},{9,11},{10,... | collective-permute-start | bytes 2371592 | tf_op jit(solution)/shard_map/ppermute | solution.py:701
  21.3 2.4 %collective-permute-start.1 = (bf16[3072,128]{1,0:T(8,128)(2,1)S(1)}, bf16[3072,128]{1,0:T(8,128)(2,1)S(1)}, u32[]{:S(2)}, u32[]{:S(2)}) collective-permute-start(bf16[3072,128]{1,0:T(8,128)(2,1)S(1)} %get-tuple-element.72), channel_id=1, source_target_pairs={{0,1},{1,0},{2,3},{3,2},{4,5},{5,4},{6,7},{7,6},{8,9},{9,8},{10,11... | collective-permute-start | bytes 2359304 | tf_op jit(solution)/shard_map/ppermute | solution.py:701
  23.2 4.2 %collective-permute-start.4 = (bf16[3088,128]{1,0:T(8,128)(2,1)S(1)}, bf16[3088,128]{1,0:T(8,128)(2,1)S(1)}, u32[]{:S(2)}, u32[]{:S(2)}) collective-permute-start(bf16[3088,128]{1,0:T(8,128)(2,1)S(1)} %collective-permute-done.3.buf_c), channel_id=1, source_target_pairs={{0,1},{1,0},{2,3},{3,2},{4,5},{5,4},{6,7},{7,6},{8,9},{9,8},{10,11... | collective-permute-start | bytes 2371592 | tf_op jit(solution)/shard_map/ppermute | solution.py:701
  24.3 13.3 %collective-permute-start.2 = (bf16[1536,128]{1,0:T(8,128)(2,1)S(1)}, bf16[1536,128]{1,0:T(8,128)(2,1)S(1)}, u32[]{:S(2)}, u32[]{:S(2)}) collective-permute-start(bf16[1536,128]{1,0:T(8,128)(2,1)S(1)} %get-tuple-element.74), channel_id=1, source_target_pairs={{0,4},{4,0},{8,12},{12,8},{16,20},{20,16},{24,28},{28,24},{1,5},{5... | collective-permute-start | bytes 1179656 | tf_op jit(solution)/shard_map/ppermute | solution.py:706
  37.7 13.1 %collective-permute-start.7 = (bf16[384,128]{1,0:T(8,128)(2,1)S(1)}, bf16[384,128]{1,0:T(8,128)(2,1)S(1)}, u32[]{:S(2)}, u32[]{:S(2)}) collective-permute-start(bf16[384,128]{1,0:T(8,128)(2,1)S(1)} %get-tuple-element.131), channel_id=1, source_target_pairs={{0,24},{4,28},{8,16},{12,20},{16,8},{20,12},{24,0},{28,4},{1,25},{... | collective-permute-start | bytes 294920 | tf_op jit(solution)/shard_map/ppermute | solution.py:706
  41.4 10.0 %collective-permute-start.6 = (bf16[384,128]{1,0:T(8,128)(2,1)S(1)}, bf16[384,128]{1,0:T(8,128)(2,1)S(1)}, u32[]{:S(2)}, u32[]{:S(2)}) collective-permute-start(bf16[384,128]{1,0:T(8,128)(2,1)S(1)} %get-tuple-element.132), channel_id=1, source_target_pairs={{0,16},{4,20},{8,24},{12,28},{16,0},{20,4},{24,8},{28,12},{1,17},{... | collective-permute-start | bytes 294920 | tf_op jit(solution)/shard_map/ppermute | solution.py:706
  42.6 8.8 %collective-permute-start.5 = (bf16[384,128]{1,0:T(8,128)(2,1)S(1)}, bf16[384,128]{1,0:T(8,128)(2,1)S(1)}, u32[]{:S(2)}, u32[]{:S(2)}) collective-permute-start(bf16[384,128]{1,0:T(8,128)(2,1)S(1)} %get-tuple-element.133), channel_id=1, source_target_pairs={{0,8},{4,12},{8,0},{12,4},{16,24},{20,28},{24,16},{28,20},{1,9},{5... | collective-permute-start | bytes 294920 | tf_op jit(solution)/shard_map/ppermute | solution.py:706
  51.4 1.2 %collective-permute-start.9 = (f32[16,512]{1,0:T(8,128)S(1)}, f32[16,512]{1,0:T(8,128)S(1)}, u32[]{:S(2)}, u32[]{:S(2)}) collective-permute-start(f32[16,512]{1,0:T(8,128)S(1)} %get-tuple-element.100), channel_id=1, source_target_pairs={{0,1},{1,0},{2,3},{3,2},{4,5},{5,4},{6,7},{7,6},{8,9},{9,8},{10,11... | collective-permute-start | bytes 98312 | tf_op jit(solution)/shard_map/ppermute | solution.py:701
  52.7 12.2 %collective-permute-start.12 = (bf16[448,128]{1,0:T(8,128)(2,1)S(1)}, bf16[448,128]{1,0:T(8,128)(2,1)S(1)}, u32[]{:S(2)}, u32[]{:S(2)}) collective-permute-start(bf16[448,128]{1,0:T(8,128)(2,1)S(1)} %get-tuple-element.112.refs_0_), channel_id=1, source_target_pairs={{0,24},{4,28},{8,16},{12,20},{16,8},{20,12},{24,0},{28,4},{1,25},{... | collective-permute-start | bytes 344072 | tf_op jit(solution)/shard_map/ppermute | solution.py:706
  55.7 10.4 %collective-permute-start.11 = (bf16[448,128]{1,0:T(8,128)(2,1)S(1)}, bf16[448,128]{1,0:T(8,128)(2,1)S(1)}, u32[]{:S(2)}, u32[]{:S(2)}) collective-permute-start(bf16[448,128]{1,0:T(8,128)(2,1)S(1)} %get-tuple-element.112.refs_0_), channel_id=1, source_target_pairs={{0,16},{4,20},{8,24},{12,28},{16,0},{20,4},{24,8},{28,12},{1,17},{... | collective-permute-start | bytes 344072 | tf_op jit(solution)/shard_map/ppermute | solution.py:706
  55.7 10.4 %collective-permute-start.10 = (bf16[448,128]{1,0:T(8,128)(2,1)S(1)}, bf16[448,128]{1,0:T(8,128)(2,1)S(1)}, u32[]{:S(2)}, u32[]{:S(2)}) collective-permute-start(bf16[448,128]{1,0:T(8,128)(2,1)S(1)} %get-tuple-element.112.refs_0_), channel_id=1, source_target_pairs={{0,8},{4,12},{8,0},{12,4},{16,24},{20,28},{24,16},{28,20},{1,9},{5... | collective-permute-start | bytes 344072 | tf_op jit(solution)/shard_map/ppermute | solution.py:706
  57.2 7.7 %collective-permute-start.13 = (bf16[384,128]{1,0:T(8,128)(2,1)S(1)}, bf16[384,128]{1,0:T(8,128)(2,1)S(1)}, u32[]{:S(2)}, u32[]{:S(2)}) collective-permute-start(bf16[384,128]{1,0:T(8,128)(2,1)S(1)} %get-tuple-element.105.mine), channel_id=1, source_target_pairs={{0,4},{4,0},{8,12},{12,8},{16,20},{20,16},{24,28},{28,24},{1,5},{5... | collective-permute-start | bytes 294920 | tf_op jit(solution)/shard_map/ppermute | solution.py:706
  60.4 6.7 %collective-permute-start.8 = (bf16[8,256,512]{2,1,0:T(8,128)(2,1)S(1)}, bf16[8,256,512]{2,1,0:T(8,128)(2,1)S(1)}, u32[]{:S(2)}, u32[]{:S(2)}) collective-permute-start(bf16[8,256,512]{2,1,0:T(8,128)(2,1)S(1)} %get-tuple-element.98), channel_id=1, source_target_pairs={{0,1},{1,0},{2,3},{3,2},{4,5},{5,4},{6,7},{7,6},{8,9},{9,8},{10,11... | collective-permute-start | bytes 6291464 | tf_op jit(solution)/shard_map/ppermute | solution.py:701
  66.2 4.2 %collective-permute-start.14 = (bf16[8,256,512]{2,1,0:T(8,128)(2,1)S(1)}, bf16[8,256,512]{2,1,0:T(8,128)(2,1)S(1)}, u32[]{:S(2)}, u32[]{:S(2)}) collective-permute-start(bf16[8,256,512]{2,1,0:T(8,128)(2,1)S(1)} %get-tuple-element.108), channel_id=1, source_target_pairs={{0,1},{1,0},{2,3},{3,2},{4,5},{5,4},{6,7},{7,6},{8,9},{9,8},{10,11... | collective-permute-start | bytes 6291464 | tf_op jit(solution)/shard_map/ppermute | solution.py:701
  66.2 9.8 %collective-permute-start.15 = (bf16[1216,128]{1,0:T(8,128)(2,1)S(1)}, bf16[1216,128]{1,0:T(8,128)(2,1)S(1)}, u32[]{:S(2)}, u32[]{:S(2)}) collective-permute-start(bf16[1216,128]{1,0:T(8,128)(2,1)S(1)} %shard_map.221.near), channel_id=1, source_target_pairs={{0,4},{4,0},{8,12},{12,8},{16,20},{20,16},{24,28},{28,24},{1,5},{5... | collective-permute-start | bytes 933896 | tf_op jit(solution)/shard_map/ppermute | solution.py:706

commit v7 on v6

--- a/solution.py
+++ b/solution.py
@@ -595,29 +595,43 @@
     )(meta, cot, cgp, consts)
 
 
-def merge_kernel(n, meta, out_b, gtok_b, out_in, gtok_in, out, gtok, stage, sems, out_sem):
-    first = (1 - meta[0]) * n
-    whole_copy = pltpu.make_async_copy(out_b, out.at[pl.ds(first, n)], out_sem)
-    whole_copy.start()
-    copies = [pltpu.make_async_copy(stage.at[j], gtok.at[first + j], sems.at[j]) for j in range(n)]
+def merge_gtok_kernel(n, meta, other, gtok_in, gtok, stage, sems):
+    copies = [pltpu.make_async_copy(stage.at[j], gtok.at[(1 - meta[0]) * n + j], sems.at[j]) for j in range(n)]
     for j in range(n):
-        stage[j] = gtok_b[j].astype(F32)
+        stage[j] = other[j].astype(F32)
         copies[j].start()
-    whole_copy.wait()
     for c in copies:
         c.wait()
 
 
-def merge(meta, out_b, gtok_b, out, gtok):
-    n = out_b.shape[0]
-    return pl.pallas_call(
-        functools.partial(merge_kernel, n),
-        in_specs=[smem(), hbm(), vmem(), hbm(), hbm()], out_specs=[hbm(), hbm()],
-        out_shape=[struct(out.shape, BF), struct(gtok.shape, F32)],
-        scratch_shapes=[pltpu.VMEM(gtok_b.shape, F32), pltpu.SemaphoreType.DMA((n,)), pltpu.SemaphoreType.DMA],
-        input_output_aliases={3: 0, 4: 1},
+def merge_gtok(meta, other, gtok):
+    n = other.shape[0]
+    return pl.pallas_call(
+        functools.partial(merge_gtok_kernel, n),
+        in_specs=[smem(), vmem(), hbm()], out_specs=hbm(), out_shape=struct(gtok.shape, F32),
+        scratch_shapes=[pltpu.VMEM(other.shape, F32), pltpu.SemaphoreType.DMA((n,))],
+        input_output_aliases={2: 0},
         compiler_params=params(), cost_estimate=cost(20000000),
-    )(meta, out_b, gtok_b, out, gtok)
+    )(meta, other, gtok)
+
+
+def merge_out_kernel(n, meta, other, out_in, out, sems):
+    copies = [pltpu.make_async_copy(other.at[j], out.at[(1 - meta[0]) * n + j], sems.at[j]) for j in range(n)]
+    for c in copies:
+        c.start()
+    for c in copies:
+        c.wait()
+
+
+def merge_out(meta, other, out):
+    n = other.shape[0]
+    return pl.pallas_call(
+        functools.partial(merge_out_kernel, n),
+        in_specs=[smem(), vmem(), hbm()], out_specs=hbm(), out_shape=struct(out.shape, BF),
+        scratch_shapes=[pltpu.SemaphoreType.DMA((n,))],
+        input_output_aliases={2: 0},
+        compiler_params=params(), cost_estimate=cost(10000000),
+    )(meta, other, out)
 
 
 def message_kernel(stay, keep, recv, *refs):
@@ -645,27 +659,27 @@
     sources, out = refs[:-1], refs[-1]
     sums = []
     for d, src in enumerate(sources):
-        if d > 0:
-            out[(d - 1) * m:d * m, :] = src[:m, :]
+        if d > 1:
+            out[(d - 2) * m:(d - 1) * m, :] = src[:m, :]
         sums.append(src[m:, :].astype(F32))
     while len(sums) > 1:
         sums = [a + b for a, b in zip(sums[::2], sums[1::2])]
-    out[(len(sources) - 1) * m:, :] = sums[0].astype(BF)
+    out[(len(sources) - 2) * m:, :] = sums[0].astype(BF)
 
 
 def relay(m, sources):
-    rows = (len(sources) - 1) * m + sources[0].shape[0] - m
+    rows = (len(sources) - 2) * m + sources[0].shape[0] - m
     return pl.pallas_call(functools.partial(relay_kernel, m), in_specs=[vmem()] * len(sources), out_specs=vmem(),
                           out_shape=struct((rows, LANES), BF), compiler_params=params())(*sources)
 
 
-def unpack_kernel(dp, taps, rates, meta, mine, theirs, near, far, gcw, gcb, gns, gnsh, gwi, gbi, gwo, gbo, gls, full):
+def unpack_kernel(dp, taps, rates, meta, mine, theirs, near_1, far_1, near, far, gcw, gcb, gns, gnsh, gwi, gbi, gwo, gbo, gls, full):
     h, width = gwo.shape
     wq, hq = width // LANES, h // LANES
     m = full.shape[0] // dp
-    for odd, first, others in ((0, mine, near), (1, theirs, far)):
+    for odd, early, others in ((0, (mine, near_1), near), (1, (theirs, far_1), far)):
         for d in range(dp // 2):
-            piece = others[(d - 1) * m:d * m, :] if d else first[:m, :]
+            piece = others[(d - 2) * m:(d - 1) * m, :] if d > 1 else early[d][:m, :]
             at = pl.multiple_of((meta[1] ^ (2 * d + odd)) * m, m)
             full[pl.ds(at, m), :] = piece.astype(F32)
     for q in range(wq):
@@ -673,7 +687,7 @@
     base = wq * h
     for q in range(hq):
         gwi[:, lane(q)] = full[base + q * width:base + (q + 1) * width, :]
-    behind = (dp // 2 - 1) * m
+    behind = (dp // 2 - 2) * m
     small = near[behind:, :].astype(F32) + far[behind:, :].astype(F32)
     rows = small.shape[0] // wq
     small = jnp.concatenate([small[q * rows:(q + 1) * rows] for q in range(wq)], axis=1)
@@ -687,13 +701,13 @@
     gbi[...] = small[at + 1, :h]
 
 
-def unpack(meta, mine, theirs, near, far, dp, taps, rates, width, h):
+def unpack(meta, mine, theirs, near_1, far_1, near, far, dp, taps, rates, width, h):
     shapes = [(taps, width), (width,), (rates, width), (rates, width), (width, h), (h,), (h, width), (width,), (width,)]
     return pl.pallas_call(
-        functools.partial(unpack_kernel, dp, taps, rates), in_specs=[smem()] + [vmem()] * 4,
+        functools.partial(unpack_kernel, dp, taps, rates), in_specs=[smem()] + [vmem()] * 6,
         out_shape=[struct(s, F32) for s in shapes],
         scratch_shapes=[pltpu.VMEM((2 * width * h // LANES, LANES), F32)],
-        compiler_params=params())(meta, mine, theirs, near, far)
+        compiler_params=params())(meta, mine, theirs, near_1, far_1, near, far)
 
 
 def swap(x, step):
@@ -736,16 +750,19 @@
     m = pieces[0].shape[0]
     near = [message] + [across(message, 2 * d) for d in range(1, dp // 2)]
     theirs = across(mine, 1)
+    far_1 = across(message, 3)
+    gtok, gtok_own = token_grad(meta, cot, cgp, consts, taps)
+    gtok_own, branch = lax.optimization_barrier((gtok_own, branch))
     out, out_own = block_out(meta, tok, branch, consts, taps)
-    cgp, out, out_own = lax.optimization_barrier((cgp, out, out_own))
-    out_b = swap(out_own, 1)
-    gtok, gtok_own = token_grad(meta, cot, cgp, consts, taps)
-    near, theirs, gtok_own = lax.optimization_barrier((near, theirs, gtok_own))
-    near = relay(m, near)
-    far = across(near, 1)
-    out, gtok = merge(meta, out_b, swap(gtok_own, 1), out, gtok)
-    far, gtok = lax.optimization_barrier((far, gtok))
-    gcw, gcb, gns, gnsh, gwi, gbi, gwo, gbo, gls = unpack(meta, mine, theirs, near, far, dp, taps, rates, width, h)
+    near, theirs, far_1, out_own = lax.optimization_barrier((near, theirs, far_1, out_own))
+    late = relay(m, near)
+    far = across(late, 1)
+    gtok = merge_gtok(meta, swap(gtok_own, 1), gtok)
+    out_b, gtok = lax.optimization_barrier((swap(out_own, 1), gtok))
+    out = merge_out(meta, out_b, out)
+    far, out, gtok = lax.optimization_barrier((far, out, gtok))
+    gcw, gcb, gns, gnsh, gwi, gbi, gwo, gbo, gls = unpack(meta, mine, theirs, near[1], far_1, late, far, dp, taps, rates,
+                                                          width, h)
     return (out, gtok, gcw, gcb, gns, gnsh, gwi, gbi, gwo, gbo, gls)
 
 

time: 78.1 us -> 78.7 us (level)
  waiting for transfers between devices: 10.9 us -> 5.92 us
  Pallas kernels: 48.6 us -> 52.5 us
  starting transfers between devices: 17.5 us -> 18.9 us
    ppermute x9 -> x10, waiting for transfers between devices: 4.34 us -> 0.09 us  [across(): return lax.ppermute(x, 'dp', [(i, i ^ step) for i in range(size)])]
    pallas_call x1, Pallas kernels: 10.1 us -> 11.6 us  [mix(): pl.pallas_call(functools.partial(mix_kernel, n, taps), in_specs=[smem()]...]
    pallas_call x1 -> x2, Pallas kernels: 3.27 us -> 4.56 us  [the longest x1 2.64 us: merge_gtok(): pl.pallas_call(functools.partial(merge_gtok_kernel, n), in_specs=[smem(),...]
    pallas_call x1, Pallas kernels: 16.2 us -> 17.3 us  [front(): pl.pallas_call(functools.partial(front_kernel, n), grid_spec=pl.GridSpec(...]
    ppermute x9 -> x10, starting transfers between devices: 14.1 us -> 15.1 us  [across(): return lax.ppermute(x, 'dp', [(i, i ^ step) for i in range(size)])]
  transfers between devices with their start and end apart: 16 -> 17, of which waited for: 7 -> 6; matrix products, arithmetic and copies ran while one was open for 0% -> 0% of each run, Pallas kernels for 58% -> 63%
where the time goes in v7:
time: 78.7 us; the launch traced here: 78.3 us
  Pallas kernels  52.5 us (67%)
  starting transfers between devices  18.9 us (24%)
  waiting for transfers between devices  5.92 us (8%)
  between operations  0.83 us (1%)
    pallas_call x1, Pallas kernels, front(): pl.pallas_call(functools.partial(front_kernel, n), grid_spec=pl.GridSpec(...  17.3 us
    ppermute x10, starting transfers between devices, across(): return lax.ppermute(x, 'dp', [(i, i ^ step) for i in range(size)])  15.1 us
    pallas_call x1, Pallas kernels, mix(): pl.pallas_call(functools.partial(mix_kernel, n, taps), in_specs=[smem()]...  11.6 us
    pallas_call x1, Pallas kernels, norm_grad(): pl.pallas_call(functools.partial(norm_grad_kernel, n, taps, rates), grid=...  8.09 us
    ppermute x7, waiting for transfers between devices, swap(): return lax.ppermute(x, 'tp', [(i, i ^ step) for i in range(size)])  5.83 us
    pallas_call x1, Pallas kernels, token_grad(): pl.pallas_call(functools.partial(token_grad_kernel, n, taps), grid=(n,),...  4.41 us
    ppermute x7, starting transfers between devices, swap(): return lax.ppermute(x, 'tp', [(i, i ^ step) for i in range(size)])  3.79 us
    pallas_call x1, Pallas kernels, merge_gtok(): pl.pallas_call(functools.partial(merge_gtok_kernel, n), in_specs=[smem(),...  2.64 us
  transfers between devices with their start and end apart: 17, of which 6 were waited for; matrix products, arithmetic and copies ran while one was open for 0% of the time, Pallas kernels for 63%

profile of v7, /device:TPU:0, one launch (start us, length us, event | category | flops | bytes accessed | tf_op | source)
XLA Modules:
  0.0 78.3 jit_solution(13363923461104807445)
XLA Ops:
  0.6 1.3 %shard_map.212.buf_a = bf16[3088,128]{1,0:T(8,128)(2,1)S(1)} custom-call(bf16[512,384]{1,0:T(8,128)(2,1)} %wi.1, bf16[384]{0:T(512)(128)(2,1)} %bi.1, bf16[384,512]{1,0:T(8,128)(2,1)} %wo.1), custom_call_target="tpu_custom_call" | custom-call | tf_op jit(solution)/shard_map/pallas_call | solution.py:111
  1.9 0.5 collective-permute-start
  2.4 2.6 %collective-permute-start.3 = (bf16[3088,128]{1,0:T(8,128)(2,1)S(1)}, bf16[3088,128]{1,0:T(8,128)(2,1)S(1)}, u32[]{:S(2)}, u32[]{:S(2)}) collective-permute-start(bf16[3088,128]{1,0:T(8,128)(2,1)S(1)} %shard_map.212.buf_a), channel_id=1, source_target_pairs={{0,2},{1,3},{2,0},{3,1},{4,6},{5,7},{6,4},{7,5},{8,10},{9,11},{10,... | collective-permute-start | bytes 2371592 | tf_op jit(solution)/shard_map/ppermute | solution.py:715
  5.0 0.0 collective-permute-done.buf_b
  5.0 17.3 %shard_map.213 = (bf16[2304,512]{1,0:T(8,128)(2,1)S(1)}, bf16[2304,512]{1,0:T(8,128)(2,1)S(1)}, bf16[2304,512]{1,0:T(8,128)(2,1)S(1)}, f32[2304,128]{1,0:T(8,128...) custom-call(s32[16]{0:T(128)} %counts_hbm.1, ...), custom_call_target="tpu_custom_call" | custom-call | tf_op jit(solution)/shard_map/pallas_call | solution.py:320
  22.3 0.1 collective-permute-start.1
  22.4 0.8 %collective-permute-done.3.buf_c = bf16[3088,128]{1,0:T(8,128)(2,1)S(1)} collective-permute-done((bf16[3088,128]{1,0:T(8,128)(2,1)S(1)}, bf16[3088,128]{1,0:T(8,128)(2,1)S(1)}, u32[]{:S(2)}, u32[]{:S(2)}) %collective-permute-start.3) | collective-permute-done | bytes 790560 | tf_op jit(solution)/shard_map/ppermute | solution.py:715
  23.2 0.0 collective-permute-start.4
  23.2 1.5 %collective-permute-done.1.recv = bf16[3072,128]{1,0:T(8,128)(2,1)S(1)} collective-permute-done((bf16[3072,128]{1,0:T(8,128)(2,1)S(1)}, bf16[3072,128]{1,0:T(8,128)(2,1)S(1)}, u32[]{:S(2)}, u32[]{:S(2)}) %collective-permute-start.1) | collective-permute-done | bytes 786464 | tf_op jit(solution)/shard_map/ppermute | solution.py:715
  24.7 0.7 shard_map.214
  25.4 2.3 %collective-permute-start.2 = (bf16[1536,128]{1,0:T(8,128)(2,1)S(1)}, bf16[1536,128]{1,0:T(8,128)(2,1)S(1)}, u32[]{:S(2)}, u32[]{:S(2)}) collective-permute-start(bf16[1536,128]{1,0:T(8,128)(2,1)S(1)} %get-tuple-element.75), channel_id=1, source_target_pairs={{0,4},{4,0},{8,12},{12,8},{16,20},{20,16},{24,28},{28,24},{1,5},{5... | collective-permute-start | bytes 1179656 | tf_op jit(solution)/shard_map/ppermute | solution.py:720
  27.7 0.0 collective-permute-done.4.buf_d
  27.7 11.6 %shard_map.215 = (f32[2304,512]{1,0:T(8,128)S(1)}, f32[2304,512]{1,0:T(8,128)S(1)}) custom-call(s32[34]{0:T(128)S(1)} %get-tuple-element.71.meta, bf16[2304,512]{1,0:T(8,128)(2,1)S(1)} %get-tuple-element.76.ad, bf16[2304,512]{1,0:T(8,128)(2,1)S(1)} %get-tuple-element.77.low, bf16[2304,768]{1,0:T(8,128)(2,1)S(1)} %get-tuple-element.78.act, ...), custom_call_target="tpu_custom_call" | custom-call | tf_op jit(solution)/shard_map/pallas_call | solution.py:386
  39.3 0.0 collective-permute-done.2
  39.3 0.1 fusion
  39.5 3.3 %collective-permute-start.7 = (bf16[384,128]{1,0:T(8,128)(2,1)S(1)}, bf16[384,128]{1,0:T(8,128)(2,1)S(1)}, u32[]{:S(2)}, u32[]{:S(2)}) collective-permute-start(bf16[384,128]{1,0:T(8,128)(2,1)S(1)} %get-tuple-element.133), channel_id=1, source_target_pairs={{0,24},{4,28},{8,16},{12,20},{16,8},{20,12},{24,0},{28,4},{1,25},{... | collective-permute-start | bytes 294920 | tf_op jit(solution)/shard_map/ppermute | solution.py:720
  42.8 0.0 collective-permute-start.6
  42.8 1.1 %collective-permute-start.5 = (bf16[384,128]{1,0:T(8,128)(2,1)S(1)}, bf16[384,128]{1,0:T(8,128)(2,1)S(1)}, u32[]{:S(2)}, u32[]{:S(2)}) collective-permute-start(bf16[384,128]{1,0:T(8,128)(2,1)S(1)} %get-tuple-element.135), channel_id=1, source_target_pairs={{0,8},{4,12},{8,0},{12,4},{16,24},{20,28},{24,16},{28,20},{1,9},{5... | collective-permute-start | bytes 294920 | tf_op jit(solution)/shard_map/ppermute | solution.py:720
  43.9 8.1 %shard_map.216 = (f32[8,4,288,128]{3,2,1,0:T(8,128)S(1)}, f32[16,512]{1,0:T(8,128)S(1)}, f32[16,512]{1,0:T(8,128)S(1)}) custom-call(s32[34]{0:T(128)S(1)} %get-tuple-element.71.meta, bf16[8,256,512]{2,1,0:T(8,128)(2,1)S(1)} %get-tuple-element.85.tok, bf16[8,256,512]{2,1,0:T(8,128)(2,1)S(1)} %get-tuple-element.86.cot, ...), custom_call_target="tpu_custom_call" | custom-call | bytes 40000000 | tf_op jit(solution)/shard_map/pallas_call | solution.py:495
  52.0 0.0 collective-permute-done.7.refs_2_
  52.0 0.0 collective-permute-done.6.refs_1_
  52.0 0.0 collective-permute-done.5.refs_0_
  52.1 0.1 collective-permute-start.8
  52.1 1.2 %collective-permute-done.8.recv = f32[16,512]{1,0:T(8,128)S(1)} collective-permute-done((f32[16,512]{1,0:T(8,128)S(1)}, f32[16,512]{1,0:T(8,128)S(1)}, u32[]{:S(2)}, u32[]{:S(2)}) %collective-permute-start.8) | collective-permute-done | bytes 32800 | tf_op jit(solution)/shard_map/ppermute | solution.py:715
  53.3 0.1 shard_map.217
  53.4 0.2 collective-permute-start.13
  53.6 3.2 %collective-permute-start.11 = (bf16[448,128]{1,0:T(8,128)(2,1)S(1)}, bf16[448,128]{1,0:T(8,128)(2,1)S(1)}, u32[]{:S(2)}, u32[]{:S(2)}) collective-permute-start(bf16[448,128]{1,0:T(8,128)(2,1)S(1)} %get-tuple-element.107.refs_0_), channel_id=1, source_target_pairs={{0,24},{4,28},{8,16},{12,20},{16,8},{20,12},{24,0},{28,4},{1,25},{... | collective-permute-start | bytes 344072 | tf_op jit(solution)/shard_map/ppermute | solution.py:720
  56.8 0.0 collective-permute-start.10
  56.8 1.2 %collective-permute-start.9 = (bf16[448,128]{1,0:T(8,128)(2,1)S(1)}, bf16[448,128]{1,0:T(8,128)(2,1)S(1)}, u32[]{:S(2)}, u32[]{:S(2)}) collective-permute-start(bf16[448,128]{1,0:T(8,128)(2,1)S(1)} %get-tuple-element.107.refs_0_), channel_id=1, source_target_pairs={{0,8},{4,12},{8,0},{12,4},{16,24},{20,28},{24,16},{28,20},{1,9},{5... | collective-permute-start | bytes 344072 | tf_op jit(solution)/shard_map/ppermute | solution.py:720
  58.0 2.2 %collective-permute-start.12 = (bf16[384,128]{1,0:T(8,128)(2,1)S(1)}, bf16[384,128]{1,0:T(8,128)(2,1)S(1)}, u32[]{:S(2)}, u32[]{:S(2)}) collective-permute-start(bf16[384,128]{1,0:T(8,128)(2,1)S(1)} %get-tuple-element.101.mine), channel_id=1, source_target_pairs={{0,4},{4,0},{8,12},{12,8},{16,20},{20,16},{24,28},{28,24},{1,5},{5... | collective-permute-start | bytes 294920 | tf_op jit(solution)/shard_map/ppermute | solution.py:720
  60.2 4.4 %shard_map.218 = (f32[16,256,512]{2,1,0:T(8,128)}, bf16[8,256,512]{2,1,0:T(8,128)(2,1)S(1)}) custom-call(s32[34]{0:T(128)S(1)} %get-tuple-element.71.meta, bf16[8,256,512]{2,1,0:T(8,128)(2,1)S(1)} %get-tuple-element.86.cot, f32[8,4,288,128]{3,2,1,0:T(8,128)S(1)} %get-tuple-element.102.cgp, f32[16,512]{1,0:T(8,128)S(1)} %get-tuple-element.82.consts), custom_call_target="tpu_custom_call" | custom-call | bytes 40000000 | tf_op jit(solution)/shard_map/pallas_call | solution.py:589
  64.6 2.6 %shard_map.219 = (bf16[16,256,512]{2,1,0:T(8,128)(2,1)}, bf16[8,256,512]{2,1,0:T(8,128)(2,1)S(1)}) custom-call(s32[34]{0:T(128)S(1)} %get-tuple-element.71.meta, bf16[8,256,512]{2,1,0:T(8,128)(2,1)S(1)} %get-tuple-element.85.tok, f32[2304,512]{1,0:T(8,128)S(1)} %get-tuple-element.105.branch, f32[16,512]{1,0:T(8,128)S(1)} %get-tuple-element.82.consts), custom_call_target="tpu_custom_call" | custom-call | bytes 40000000 | tf_op jit(solution)/shard_map/pallas_call | solution.py:536
  67.2 0.0 collective-permute-done.12.theirs
  67.2 0.1 collective-permute-start.16
  67.3 0.0 collective-permute-done.13.far_1
  67.3 0.0 collective-permute-done.11.refs_3_
  67.3 0.1 collective-permute-done.10.refs_2_
  67.4 0.0 collective-permute-done.9.refs_1_.near_1
  67.4 0.5 collective-permute-start.15
  67.9 1.5 %collective-permute-start.14 = (bf16[832,128]{1,0:T(8,128)(2,1)S(1)}, bf16[832,128]{1,0:T(8,128)(2,1)S(1)}, u32[]{:S(2)}, u32[]{:S(2)}) collective-permute-start(bf16[832,128]{1,0:T(8,128)(2,1)S(1)} %shard_map.220.near), channel_id=1, source_target_pairs={{0,4},{4,0},{8,12},{12,8},{16,20},{20,16},{24,28},{28,24},{1,5},{5... | collective-permute-start | bytes 638984 | tf_op jit(solution)/shard_map/ppermute | solution.py:720
  69.4 2.0 %collective-permute-done.16.other = bf16[8,256,512]{2,1,0:T(8,128)(2,1)S(1)} collective-permute-done((bf16[8,256,512]{2,1,0:T(8,128)(2,1)S(1)}, bf16[8,256,512]{2,1,0:T(8,128)(2,1)S(1)}, u32[]{:S(2)}, u32[]{:S(2)}) %collective-permute-start.16) | collective-permute-done | bytes 2097184 | tf_op jit(solution)/shard_map/ppermute | solution.py:715
  71.4 2.6 %shard_map.221 = f32[16,256,512]{2,1,0:T(8,128)} custom-call(s32[34]{0:T(128)S(1)} %get-tuple-element.71.meta, bf16[8,256,512]{2,1,0:T(8,128)(2,1)S(1)} %collective-permute-done.16.other, f32[16,256,512]{2,1,0:T(8,128)} %get-tuple-element.113.gtok_in), custom_call_target="tpu_custom_call", output_to_operand_aliasing={{}: (2, {})} | custom-call | bytes 20000000 | tf_op jit(solution)/shard_map/pallas_call | solution.py:609
  74.1 0.3 collective-permute-done.15.other
  74.4 1.9 %shard_map.222 = bf16[16,256,512]{2,1,0:T(8,128)(2,1)} custom-call(s32[34]{0:T(128)S(1)} %get-tuple-element.71.meta, bf16[8,256,512]{2,1,0:T(8,128)(2,1)S(1)} %collective-permute-done.15.other, bf16[16,256,512]{2,1,0:T(8,128)(2,1)} %get-tuple-element.115.out_in), custom_call_target="tpu_custom_call", output_to_operand_aliasing={{}: (2, {})} | custom-call | bytes 10000000 | tf_op jit(solution)/shard_map/pallas_call | solution.py:628
  76.3 0.0 collective-permute-done.14.far
  76.4 1.9 %shard_map.223 = (f32[7,512]{1,0:T(8,128)}, f32[512]{0:T(512)}, f32[2,512]{1,0:T(2,128)}, f32[2,512]{1,0:T(2,128)}, f32[512,384]{1,0:T(8,128)}, /*index=5*/f32[3...) custom-call(s32[34]{0:T(128)S(1)} %get-tuple-element.71.meta, bf16[384,128]{1,0:T(8,128)(2,1)S(1)} %get-tuple-element.101.mine, ...), custom_call_target="tpu_custom_call" | custom-call | tf_op jit(solution)/shard_map/pallas_call | solution.py:706
  (2 shorter events, 0.0 us)
Async XLA Ops:
  1.9 3.1 %collective-permute-start = (bf16[3088,128]{1,0:T(8,128)(2,1)S(1)}, bf16[3088,128]{1,0:T(8,128)(2,1)S(1)}, u32[]{:S(2)}, u32[]{:S(2)}) collective-permute-start(bf16[3088,128]{1,0:T(8,128)(2,1)S(1)} %shard_map.212.buf_a), channel_id=1, source_target_pairs={{0,1},{1,0},{2,3},{3,2},{4,5},{5,4},{6,7},{7,6},{8,9},{9,8},{10,11... | collective-permute-start | bytes 2371592 | tf_op jit(solution)/shard_map/ppermute | solution.py:715
  2.4 20.8 %collective-permute-start.3 = (bf16[3088,128]{1,0:T(8,128)(2,1)S(1)}, bf16[3088,128]{1,0:T(8,128)(2,1)S(1)}, u32[]{:S(2)}, u32[]{:S(2)}) collective-permute-start(bf16[3088,128]{1,0:T(8,128)(2,1)S(1)} %shard_map.212.buf_a), channel_id=1, source_target_pairs={{0,2},{1,3},{2,0},{3,1},{4,6},{5,7},{6,4},{7,5},{8,10},{9,11},{10,... | collective-permute-start | bytes 2371592 | tf_op jit(solution)/shard_map/ppermute | solution.py:715
  22.3 2.4 %collective-permute-start.1 = (bf16[3072,128]{1,0:T(8,128)(2,1)S(1)}, bf16[3072,128]{1,0:T(8,128)(2,1)S(1)}, u32[]{:S(2)}, u32[]{:S(2)}) collective-permute-start(bf16[3072,128]{1,0:T(8,128)(2,1)S(1)} %get-tuple-element.73), channel_id=1, source_target_pairs={{0,1},{1,0},{2,3},{3,2},{4,5},{5,4},{6,7},{7,6},{8,9},{9,8},{10,11... | collective-permute-start | bytes 2359304 | tf_op jit(solution)/shard_map/ppermute | solution.py:715
  23.2 4.4 %collective-permute-start.4 = (bf16[3088,128]{1,0:T(8,128)(2,1)S(1)}, bf16[3088,128]{1,0:T(8,128)(2,1)S(1)}, u32[]{:S(2)}, u32[]{:S(2)}) collective-permute-start(bf16[3088,128]{1,0:T(8,128)(2,1)S(1)} %collective-permute-done.3.buf_c), channel_id=1, source_target_pairs={{0,1},{1,0},{2,3},{3,2},{4,5},{5,4},{6,7},{7,6},{8,9},{9,8},{10,11... | collective-permute-start | bytes 2371592 | tf_op jit(solution)/shard_map/ppermute | solution.py:715
  25.4 14.0 %collective-permute-start.2 = (bf16[1536,128]{1,0:T(8,128)(2,1)S(1)}, bf16[1536,128]{1,0:T(8,128)(2,1)S(1)}, u32[]{:S(2)}, u32[]{:S(2)}) collective-permute-start(bf16[1536,128]{1,0:T(8,128)(2,1)S(1)} %get-tuple-element.75), channel_id=1, source_target_pairs={{0,4},{4,0},{8,12},{12,8},{16,20},{20,16},{24,28},{28,24},{1,5},{5... | collective-permute-start | bytes 1179656 | tf_op jit(solution)/shard_map/ppermute | solution.py:720
  39.5 12.6 %collective-permute-start.7 = (bf16[384,128]{1,0:T(8,128)(2,1)S(1)}, bf16[384,128]{1,0:T(8,128)(2,1)S(1)}, u32[]{:S(2)}, u32[]{:S(2)}) collective-permute-start(bf16[384,128]{1,0:T(8,128)(2,1)S(1)} %get-tuple-element.133), channel_id=1, source_target_pairs={{0,24},{4,28},{8,16},{12,20},{16,8},{20,12},{24,0},{28,4},{1,25},{... | collective-permute-start | bytes 294920 | tf_op jit(solution)/shard_map/ppermute | solution.py:720
  42.8 9.2 %collective-permute-start.6 = (bf16[384,128]{1,0:T(8,128)(2,1)S(1)}, bf16[384,128]{1,0:T(8,128)(2,1)S(1)}, u32[]{:S(2)}, u32[]{:S(2)}) collective-permute-start(bf16[384,128]{1,0:T(8,128)(2,1)S(1)} %get-tuple-element.134), channel_id=1, source_target_pairs={{0,16},{4,20},{8,24},{12,28},{16,0},{20,4},{24,8},{28,12},{1,17},{... | collective-permute-start | bytes 294920 | tf_op jit(solution)/shard_map/ppermute | solution.py:720
  42.8 9.2 %collective-permute-start.5 = (bf16[384,128]{1,0:T(8,128)(2,1)S(1)}, bf16[384,128]{1,0:T(8,128)(2,1)S(1)}, u32[]{:S(2)}, u32[]{:S(2)}) collective-permute-start(bf16[384,128]{1,0:T(8,128)(2,1)S(1)} %get-tuple-element.135), channel_id=1, source_target_pairs={{0,8},{4,12},{8,0},{12,4},{16,24},{20,28},{24,16},{28,20},{1,9},{5... | collective-permute-start | bytes 294920 | tf_op jit(solution)/shard_map/ppermute | solution.py:720
  52.1 1.3 %collective-permute-start.8 = (f32[16,512]{1,0:T(8,128)S(1)}, f32[16,512]{1,0:T(8,128)S(1)}, u32[]{:S(2)}, u32[]{:S(2)}) collective-permute-start(f32[16,512]{1,0:T(8,128)S(1)} %get-tuple-element.96), channel_id=1, source_target_pairs={{0,1},{1,0},{2,3},{3,2},{4,5},{5,4},{6,7},{7,6},{8,9},{9,8},{10,11... | collective-permute-start | bytes 98312 | tf_op jit(solution)/shard_map/ppermute | solution.py:715
  53.4 13.9 %collective-permute-start.13 = (bf16[448,128]{1,0:T(8,128)(2,1)S(1)}, bf16[448,128]{1,0:T(8,128)(2,1)S(1)}, u32[]{:S(2)}, u32[]{:S(2)}) collective-permute-start(bf16[448,128]{1,0:T(8,128)(2,1)S(1)} %get-tuple-element.107.refs_0_), channel_id=1, source_target_pairs={{0,12},{4,8},{8,4},{12,0},{16,28},{20,24},{24,20},{28,16},{1,13},{... | collective-permute-start | bytes 344072 | tf_op jit(solution)/shard_map/ppermute | solution.py:720
  53.6 13.7 %collective-permute-start.11 = (bf16[448,128]{1,0:T(8,128)(2,1)S(1)}, bf16[448,128]{1,0:T(8,128)(2,1)S(1)}, u32[]{:S(2)}, u32[]{:S(2)}) collective-permute-start(bf16[448,128]{1,0:T(8,128)(2,1)S(1)} %get-tuple-element.107.refs_0_), channel_id=1, source_target_pairs={{0,24},{4,28},{8,16},{12,20},{16,8},{20,12},{24,0},{28,4},{1,25},{... | collective-permute-start | bytes 344072 | tf_op jit(solution)/shard_map/ppermute | solution.py:720
  56.8 10.6 %collective-permute-start.10 = (bf16[448,128]{1,0:T(8,128)(2,1)S(1)}, bf16[448,128]{1,0:T(8,128)(2,1)S(1)}, u32[]{:S(2)}, u32[]{:S(2)}) collective-permute-start(bf16[448,128]{1,0:T(8,128)(2,1)S(1)} %get-tuple-element.107.refs_0_), channel_id=1, source_target_pairs={{0,16},{4,20},{8,24},{12,28},{16,0},{20,4},{24,8},{28,12},{1,17},{... | collective-permute-start | bytes 344072 | tf_op jit(solution)/shard_map/ppermute | solution.py:720
  56.8 10.6 %collective-permute-start.9 = (bf16[448,128]{1,0:T(8,128)(2,1)S(1)}, bf16[448,128]{1,0:T(8,128)(2,1)S(1)}, u32[]{:S(2)}, u32[]{:S(2)}) collective-permute-start(bf16[448,128]{1,0:T(8,128)(2,1)S(1)} %get-tuple-element.107.refs_0_), channel_id=1, source_target_pairs={{0,8},{4,12},{8,0},{12,4},{16,24},{20,28},{24,16},{28,20},{1,9},{5... | collective-permute-start | bytes 344072 | tf_op jit(solution)/shard_map/ppermute | solution.py:720
  58.0 9.2 %collective-permute-start.12 = (bf16[384,128]{1,0:T(8,128)(2,1)S(1)}, bf16[384,128]{1,0:T(8,128)(2,1)S(1)}, u32[]{:S(2)}, u32[]{:S(2)}) collective-permute-start(bf16[384,128]{1,0:T(8,128)(2,1)S(1)} %get-tuple-element.101.mine), channel_id=1, source_target_pairs={{0,4},{4,0},{8,12},{12,8},{16,20},{20,16},{24,28},{28,24},{1,5},{5... | collective-permute-start | bytes 294920 | tf_op jit(solution)/shard_map/ppermute | solution.py:720
  67.2 4.2 %collective-permute-start.16 = (bf16[8,256,512]{2,1,0:T(8,128)(2,1)S(1)}, bf16[8,256,512]{2,1,0:T(8,128)(2,1)S(1)}, u32[]{:S(2)}, u32[]{:S(2)}) collective-permute-start(bf16[8,256,512]{2,1,0:T(8,128)(2,1)S(1)} %get-tuple-element.112), channel_id=1, source_target_pairs={{0,1},{1,0},{2,3},{3,2},{4,5},{5,4},{6,7},{7,6},{8,9},{9,8},{10,11... | collective-permute-start | bytes 6291464 | tf_op jit(solution)/shard_map/ppermute | solution.py:715
  67.4 7.1 %collective-permute-start.15 = (bf16[8,256,512]{2,1,0:T(8,128)(2,1)S(1)}, bf16[8,256,512]{2,1,0:T(8,128)(2,1)S(1)}, u32[]{:S(2)}, u32[]{:S(2)}) collective-permute-start(bf16[8,256,512]{2,1,0:T(8,128)(2,1)S(1)} %get-tuple-element.111), channel_id=1, source_target_pairs={{0,1},{1,0},{2,3},{3,2},{4,5},{5,4},{6,7},{7,6},{8,9},{9,8},{10,11... | collective-permute-start | bytes 6291464 | tf_op jit(solution)/shard_map/ppermute | solution.py:715
  67.9 8.5 %collective-permute-start.14 = (bf16[832,128]{1,0:T(8,128)(2,1)S(1)}, bf16[832,128]{1,0:T(8,128)(2,1)S(1)}, u32[]{:S(2)}, u32[]{:S(2)}) collective-permute-start(bf16[832,128]{1,0:T(8,128)(2,1)S(1)} %shard_map.220.near), channel_id=1, source_target_pairs={{0,4},{4,0},{8,12},{12,8},{16,20},{20,16},{24,28},{28,24},{1,5},{5... | collective-permute-start | bytes 638984 | tf_op jit(solution)/shard_map/ppermute | solution.py:720

commit v8 on v7

--- a/solution.py
+++ b/solution.py
@@ -13,7 +13,6 @@
 LANES = 128
 PAD = 8
 CHUNK = 64
-WIDE_CHUNK = 128
 VMEM_LIMIT = 12 * 1024 * 1024
 
 
@@ -169,6 +168,8 @@
         offs[n + 2] = 0
         gbo[...] = jnp.zeros_like(gbo)
         pad[...] = jnp.zeros_like(pad)
+        for stage in (ad_s, nrm_s, low_s, inv_s):
+            stage[...] = jnp.zeros_like(stage)
         meta[0] = lax.axis_index("tp") & 1
         meta[1] = lax.axis_index("dp")
         for c in tables:
@@ -265,8 +266,7 @@
     ready = offs[s] >= (done + 1) * TILE
     none = (jnp.zeros((8, LANES), F32),) * wq
 
-    @pl.when(ready)
-    def _():
+    def conv_with(chunks, with_tile):
         consts = setup()
         state = [none]
 
@@ -276,19 +276,23 @@
                     state[0] = conv_step(i, state[0], consts)
             return run
 
-        count_c = frames // CHUNK
-        cuts = [count_c * k // 4 for k in range(5)]
-        tile(done, [part(cuts[k], cuts[k + 1]) for k in range(4)])
+        cuts = [chunks * k // 4 for k in range(5)]
+        parts = [part(cuts[k], cuts[k + 1]) for k in range(4)]
+        if with_tile:
+            tile(done, parts)
+        else:
+            for run in parts:
+                run()
         add_gbo(state[0])
-        offs[n + 2] = done + 1
-
-    @pl.when(jnp.logical_not(ready))
-    def _():
-        consts = setup()
-        state = none
-        for i in range(frames // CHUNK):
-            state = conv_step(i, state, consts)
-        add_gbo(state)
+        if with_tile:
+            offs[n + 2] = done + 1
+
+    all_chunks = frames // CHUNK
+    short = count <= (all_chunks - 1) * CHUNK
+    for with_tile in (True, False):
+        for chunks in (all_chunks - 1, all_chunks):
+            fits = short if chunks < all_chunks else jnp.logical_not(short)
+            pl.when((ready == with_tile) & fits)(functools.partial(conv_with, chunks, with_tile))
 
     @pl.when(s == n - 1)
     def _():
@@ -363,20 +367,30 @@
     for c in copies:
         c.start()
     place_items(n, meta, offs)
+
+    def own(at):
+        return dot(act[at, :], wout1[...]), dot_t(pre[at, :], win1[...])
+
+    def rest(at, own_branch, own_ag):
+        a, b = ad[at, :], low[at, :]
+        activation, slope = gelu_parts(dot(a, win2[...]) + bias_row[...])
+        grad = dot_t(b, wout2[...]) * slope
+        branch[at, :] = (own_branch + dot(activation.astype(BF), wout2[...])) + consts[taps + 1:taps + 2, :]
+        ag[at, :] = own_ag + dot_t(grad.astype(BF), win2[...])
+
+    first = pl.ds(0, TILE)
+    branch[first, :], ag[first, :] = own(first)
     for c in copies:
         c.wait()
     spread_bias(bias, bias_row)
+    rest(first, branch[first, :], ag[first, :])
 
     def tile(t, _):
         at = pl.ds(pl.multiple_of(t * TILE, TILE), TILE)
-        a, b = ad[at, :], low[at, :]
-        activation, slope = gelu_parts(dot(a, win2[...]) + bias_row[...])
-        grad = dot_t(b, wout2[...]) * slope
-        branch[at, :] = (dot(act[at, :], wout1[...]) + dot(activation.astype(BF), wout2[...])) + consts[taps + 1:taps + 2, :]
-        ag[at, :] = dot_t(pre[at, :], win1[...]) + dot_t(grad.astype(BF), win2[...])
+        rest(at, *own(at))
         return 0
 
-    lax.fori_loop(0, offs[n + 1], tile, 0)
+    lax.fori_loop(1, offs[n + 1], tile, 0)
 
 
 def mix(meta, ad, low, act, pre, win, wout, consts, buf_c, buf_d, n, taps):
@@ -415,13 +429,13 @@
     off = offs[s]
     scale = pick(consts.at[taps + 2:taps + 2 + rates], group)
     zero = jnp.zeros((8, LANES), F32)
-    steps = pl.cdiv(count, WIDE_CHUNK)
-
-    def step(i, accs):
-        r0 = pl.multiple_of(i * WIDE_CHUNK, WIDE_CHUNK)
-        here = pl.ds(r0, WIDE_CHUNK)
-        live = (lax.broadcasted_iota(jnp.int32, (WIDE_CHUNK, LANES), 0) + r0) < count
-        src = pl.ds(pl.multiple_of(off + r0, 16), WIDE_CHUNK)
+    steps = pl.cdiv(count, CHUNK)
+    wide = steps // 2
+
+    def step(r0, size, accs):
+        here = pl.ds(r0, size)
+        live = (lax.broadcasted_iota(jnp.int32, (size, LANES), 0) + r0) < count
+        src = pl.ds(pl.multiple_of(off + r0, 16), size)
         new = []
         ngs, nrs = [], []
         for q in range(wq):
@@ -438,42 +452,53 @@
         istd = inv[src, :]
         for q in range(wq):
             cg = istd * (ngs[q] - m1 - nrs[q] * m2)
-            cgp[s, q, pl.ds(pl.multiple_of(r0 + PAD, 8), WIDE_CHUNK), :] = jnp.where(live, cg, 0.0)
+            cgp[s, q, pl.ds(pl.multiple_of(r0 + PAD, 8), size), :] = jnp.where(live, cg, 0.0)
         return tuple(new)
 
-    accs = lax.fori_loop(0, steps, step, (zero,) * (3 * wq))
-    for q in range(wq):
-        sums[taps + 1, :, lane(q)] += accs[3 * q]
-        sums[taps + 2 + group, :, lane(q)] += accs[3 * q + 1]
-        sums[taps + 2 + rates + group, :, lane(q)] += accs[3 * q + 2]
+    def both_sizes(run, width_of_state, add):
+        add(lax.fori_loop(0, wide, lambda i, accs: run(pl.multiple_of(i * 2 * CHUNK, 2 * CHUNK), 2 * CHUNK, accs),
+                          (zero,) * width_of_state))
+
+        @pl.when(steps > 2 * wide)
+        def _():
+            add(run(pl.multiple_of(wide * 2 * CHUNK, 2 * CHUNK), CHUNK, (zero,) * width_of_state))
+
+    def add_norm(accs):
+        for q in range(wq):
+            sums[taps + 1, :, lane(q)] += accs[3 * q]
+            sums[taps + 2 + group, :, lane(q)] += accs[3 * q + 1]
+            sums[taps + 2 + rates + group, :, lane(q)] += accs[3 * q + 2]
+
+    both_sizes(step, 3 * wq, add_norm)
 
     def clear(i, _):
-        r0 = pl.multiple_of(i * WIDE_CHUNK, WIDE_CHUNK)
-        for q in range(wq):
-            cgp[s, q, pl.ds(pl.multiple_of(r0 + PAD, 8), WIDE_CHUNK), :] = jnp.zeros((WIDE_CHUNK, LANES), F32)
+        r0 = pl.multiple_of(i * CHUNK, CHUNK)
+        for q in range(wq):
+            cgp[s, q, pl.ds(pl.multiple_of(r0 + PAD, 8), CHUNK), :] = jnp.zeros((CHUNK, LANES), F32)
         return 0
 
-    lax.fori_loop(steps, frames // WIDE_CHUNK, clear, 0)
+    lax.fori_loop(steps, frames // CHUNK, clear, 0)
     for q in range(wq):
         cgp[s, q, :PAD, :] = jnp.zeros((PAD, LANES), F32)
         cgp[s, q, PAD + frames:, :] = jnp.zeros((cgp.shape[2] - PAD - frames, LANES), F32)
 
-        def conv_step(i, accs):
-            r0 = pl.multiple_of(i * WIDE_CHUNK, WIDE_CHUNK)
-            here = pl.ds(r0, WIDE_CHUNK)
-            live = (lax.broadcasted_iota(jnp.int32, (WIDE_CHUNK, LANES), 0) + r0) < count
+        def conv_step(r0, size, accs):
+            here = pl.ds(r0, size)
+            live = (lax.broadcasted_iota(jnp.int32, (size, LANES), 0) + r0) < count
             tk = jnp.where(live, tok[s, here, lane(q)].astype(F32), 0.0)
             new = []
             for k in range(taps):
-                sh = cgp[s, q, pl.ds(r0 + (PAD + half - k), WIDE_CHUNK), :]
+                sh = cgp[s, q, pl.ds(r0 + (PAD + half - k), size), :]
                 new.append(accs[k] + fold(tk * sh))
                 if k == half:
                     new_bias = accs[taps] + fold(sh)
             return tuple(new) + (new_bias,)
 
-        accs = lax.fori_loop(0, steps, conv_step, (zero,) * (taps + 1))
-        for k in range(taps + 1):
-            sums[k, :, lane(q)] += accs[k]
+        def add_conv(accs):
+            for k in range(taps + 1):
+                sums[k, :, lane(q)] += accs[k]
+
+        both_sizes(conv_step, taps + 1, add_conv)
 
     @pl.when(s == n - 1)
     def _():

time: 78.7 us -> 78.1 us (level)
  Pallas kernels: 52.5 us -> 48.3 us
  waiting for transfers between devices: 5.92 us -> 8.23 us
  starting transfers between devices: 18.9 us -> 20.9 us
    ppermute x10, starting transfers between devices: 15.1 us -> 17.4 us  [across(): return lax.ppermute(x, 'dp', [(i, i ^ step) for i in range(size)])]
    ppermute x10, waiting for transfers between devices: 0.09 us -> 2.03 us  [across(): return lax.ppermute(x, 'dp', [(i, i ^ step) for i in range(size)])]
    pallas_call x1, Pallas kernels: 17.3 us -> 15.5 us  [front(): pl.pallas_call(functools.partial(front_kernel, n), grid_spec=pl.GridSpec(...]
    pallas_call x1, Pallas kernels: 11.6 us -> 10.3 us  [mix(): pl.pallas_call(functools.partial(mix_kernel, n, taps), in_specs=[smem()]...]
    pallas_call x1, Pallas kernels: 8.09 us -> 7.14 us  [norm_grad(): pl.pallas_call(functools.partial(norm_grad_kernel, n, taps, rates), grid=...]
  transfers between devices with their start and end apart: 17 -> 17, of which waited for: 6 -> 6; matrix products, arithmetic and copies ran while one was open for 0% -> 0% of each run, Pallas kernels for 63% -> 58%
where the time goes in v8:
time: 78.1 us; the launch traced here: 78.4 us
  Pallas kernels  48.3 us (62%)
  starting transfers between devices  20.9 us (27%)
  waiting for transfers between devices  8.23 us (11%)
  between operations  0.82 us (1%)
    ppermute x10, starting transfers between devices, across(): return lax.ppermute(x, 'dp', [(i, i ^ step) for i in range(size)])  17.4 us
    pallas_call x1, Pallas kernels, front(): pl.pallas_call(functools.partial(front_kernel, n), grid_spec=pl.GridSpec(...  15.5 us
    pallas_call x1, Pallas kernels, mix(): pl.pallas_call(functools.partial(mix_kernel, n, taps), in_specs=[smem()]...  10.3 us
    pallas_call x1, Pallas kernels, norm_grad(): pl.pallas_call(functools.partial(norm_grad_kernel, n, taps, rates), grid=...  7.14 us
    ppermute x7, waiting for transfers between devices, swap(): return lax.ppermute(x, 'tp', [(i, i ^ step) for i in range(size)])  6.2 us
    pallas_call x1, Pallas kernels, token_grad(): pl.pallas_call(functools.partial(token_grad_kernel, n, taps), grid=(n,),...  4.33 us
    ppermute x7, starting transfers between devices, swap(): return lax.ppermute(x, 'tp', [(i, i ^ step) for i in range(size)])  3.47 us
    pallas_call x1, Pallas kernels, merge_gtok(): pl.pallas_call(functools.partial(merge_gtok_kernel, n), in_specs=[smem(),...  2.64 us
  transfers between devices with their start and end apart: 17, of which 6 were waited for; matrix products, arithmetic and copies ran while one was open for 0% of the time, Pallas kernels for 58%

profile of v8, /device:TPU:0, one launch (start us, length us, event | category | flops | bytes accessed | tf_op | source)
XLA Modules:
  0.0 78.4 jit_solution(13394263927212378015)
XLA Ops:
  0.6 1.3 %shard_map.212.buf_a = bf16[3088,128]{1,0:T(8,128)(2,1)S(1)} custom-call(bf16[512,384]{1,0:T(8,128)(2,1)} %wi.1, bf16[384]{0:T(512)(128)(2,1)} %bi.1, bf16[384,512]{1,0:T(8,128)(2,1)} %wo.1), custom_call_target="tpu_custom_call" | custom-call | tf_op jit(solution)/shard_map/pallas_call | solution.py:110
  1.9 0.5 collective-permute-start
  2.4 2.6 %collective-permute-start.3 = (bf16[3088,128]{1,0:T(8,128)(2,1)S(1)}, bf16[3088,128]{1,0:T(8,128)(2,1)S(1)}, u32[]{:S(2)}, u32[]{:S(2)}) collective-permute-start(bf16[3088,128]{1,0:T(8,128)(2,1)S(1)} %shard_map.212.buf_a), channel_id=1, source_target_pairs={{0,2},{1,3},{2,0},{3,1},{4,6},{5,7},{6,4},{7,5},{8,10},{9,11},{10,... | collective-permute-start | bytes 2371592 | tf_op jit(solution)/shard_map/ppermute | solution.py:740
  5.0 0.0 collective-permute-done.buf_b
  5.0 15.5 %shard_map.213 = (bf16[2304,512]{1,0:T(8,128)(2,1)S(1)}, bf16[2304,512]{1,0:T(8,128)(2,1)S(1)}, bf16[2304,512]{1,0:T(8,128)(2,1)S(1)}, f32[2304,128]{1,0:T(8,128...) custom-call(s32[16]{0:T(128)} %counts_hbm.1, ...), custom_call_target="tpu_custom_call" | custom-call | tf_op jit(solution)/shard_map/pallas_call | solution.py:324
  20.5 0.2 collective-permute-start.1
  20.8 2.4 %collective-permute-done.3.buf_c = bf16[3088,128]{1,0:T(8,128)(2,1)S(1)} collective-permute-done((bf16[3088,128]{1,0:T(8,128)(2,1)S(1)}, bf16[3088,128]{1,0:T(8,128)(2,1)S(1)}, u32[]{:S(2)}, u32[]{:S(2)}) %collective-permute-start.3) | collective-permute-done | bytes 790560 | tf_op jit(solution)/shard_map/ppermute | solution.py:740
  23.2 0.0 collective-permute-start.4
  23.2 0.0 collective-permute-done.1.recv
  23.2 0.7 shard_map.214
  23.9 2.3 %collective-permute-start.2 = (bf16[1536,128]{1,0:T(8,128)(2,1)S(1)}, bf16[1536,128]{1,0:T(8,128)(2,1)S(1)}, u32[]{:S(2)}, u32[]{:S(2)}) collective-permute-start(bf16[1536,128]{1,0:T(8,128)(2,1)S(1)} %get-tuple-element.75), channel_id=1, source_target_pairs={{0,4},{4,0},{8,12},{12,8},{16,20},{20,16},{24,28},{28,24},{1,5},{5... | collective-permute-start | bytes 1179656 | tf_op jit(solution)/shard_map/ppermute | solution.py:745
  26.2 0.0 collective-permute-done.4.buf_d
  26.2 10.3 %shard_map.215 = (f32[2304,512]{1,0:T(8,128)S(1)}, f32[2304,512]{1,0:T(8,128)S(1)}) custom-call(s32[34]{0:T(128)S(1)} %get-tuple-element.71.meta, bf16[2304,512]{1,0:T(8,128)(2,1)S(1)} %get-tuple-element.76.ad, bf16[2304,512]{1,0:T(8,128)(2,1)S(1)} %get-tuple-element.77.low, bf16[2304,768]{1,0:T(8,128)(2,1)S(1)} %get-tuple-element.78.act, ...), custom_call_target="tpu_custom_call" | custom-call | tf_op jit(solution)/shard_map/pallas_call | solution.py:400
  36.5 0.0 collective-permute-done.2
  36.5 0.1 fusion
  36.6 3.9 %collective-permute-start.7 = (bf16[384,128]{1,0:T(8,128)(2,1)S(1)}, bf16[384,128]{1,0:T(8,128)(2,1)S(1)}, u32[]{:S(2)}, u32[]{:S(2)}) collective-permute-start(bf16[384,128]{1,0:T(8,128)(2,1)S(1)} %get-tuple-element.133), channel_id=1, source_target_pairs={{0,24},{4,28},{8,16},{12,20},{16,8},{20,12},{24,0},{28,4},{1,25},{... | collective-permute-start | bytes 294920 | tf_op jit(solution)/shard_map/ppermute | solution.py:745
  40.6 2.7 %collective-permute-start.6 = (bf16[384,128]{1,0:T(8,128)(2,1)S(1)}, bf16[384,128]{1,0:T(8,128)(2,1)S(1)}, u32[]{:S(2)}, u32[]{:S(2)}) collective-permute-start(bf16[384,128]{1,0:T(8,128)(2,1)S(1)} %get-tuple-element.134), channel_id=1, source_target_pairs={{0,16},{4,20},{8,24},{12,28},{16,0},{20,4},{24,8},{28,12},{1,17},{... | collective-permute-start | bytes 294920 | tf_op jit(solution)/shard_map/ppermute | solution.py:745
  43.2 0.5 collective-permute-start.5
  43.7 7.1 %shard_map.216 = (f32[8,4,288,128]{3,2,1,0:T(8,128)S(1)}, f32[16,512]{1,0:T(8,128)S(1)}, f32[16,512]{1,0:T(8,128)S(1)}) custom-call(s32[34]{0:T(128)S(1)} %get-tuple-element.71.meta, bf16[8,256,512]{2,1,0:T(8,128)(2,1)S(1)} %get-tuple-element.85.tok, bf16[8,256,512]{2,1,0:T(8,128)(2,1)S(1)} %get-tuple-element.86.cot, ...), custom_call_target="tpu_custom_call" | custom-call | bytes 40000000 | tf_op jit(solution)/shard_map/pallas_call | solution.py:520
  50.9 0.0 collective-permute-done.7.refs_2_
  50.9 0.0 collective-permute-done.6.refs_1_
  50.9 0.0 collective-permute-done.5.refs_0_
  50.9 0.1 collective-permute-start.8
  51.0 1.2 %collective-permute-done.8.recv = f32[16,512]{1,0:T(8,128)S(1)} collective-permute-done((f32[16,512]{1,0:T(8,128)S(1)}, f32[16,512]{1,0:T(8,128)S(1)}, u32[]{:S(2)}, u32[]{:S(2)}) %collective-permute-start.8) | collective-permute-done | bytes 32800 | tf_op jit(solution)/shard_map/ppermute | solution.py:740
  52.2 0.1 shard_map.217
  52.2 2.6 %collective-permute-start.13 = (bf16[448,128]{1,0:T(8,128)(2,1)S(1)}, bf16[448,128]{1,0:T(8,128)(2,1)S(1)}, u32[]{:S(2)}, u32[]{:S(2)}) collective-permute-start(bf16[448,128]{1,0:T(8,128)(2,1)S(1)} %get-tuple-element.107.refs_0_), channel_id=1, source_target_pairs={{0,12},{4,8},{8,4},{12,0},{16,28},{20,24},{24,20},{28,16},{1,13},{... | collective-permute-start | bytes 344072 | tf_op jit(solution)/shard_map/ppermute | solution.py:745
  54.8 3.4 %collective-permute-start.11 = (bf16[448,128]{1,0:T(8,128)(2,1)S(1)}, bf16[448,128]{1,0:T(8,128)(2,1)S(1)}, u32[]{:S(2)}, u32[]{:S(2)}) collective-permute-start(bf16[448,128]{1,0:T(8,128)(2,1)S(1)} %get-tuple-element.107.refs_0_), channel_id=1, source_target_pairs={{0,24},{4,28},{8,16},{12,20},{16,8},{20,12},{24,0},{28,4},{1,25},{... | collective-permute-start | bytes 344072 | tf_op jit(solution)/shard_map/ppermute | solution.py:745
  58.3 0.0 collective-permute-start.10
  58.3 1.0 %collective-permute-start.9 = (bf16[448,128]{1,0:T(8,128)(2,1)S(1)}, bf16[448,128]{1,0:T(8,128)(2,1)S(1)}, u32[]{:S(2)}, u32[]{:S(2)}) collective-permute-start(bf16[448,128]{1,0:T(8,128)(2,1)S(1)} %get-tuple-element.107.refs_0_), channel_id=1, source_target_pairs={{0,8},{4,12},{8,0},{12,4},{16,24},{20,28},{24,16},{28,20},{1,9},{5... | collective-permute-start | bytes 344072 | tf_op jit(solution)/shard_map/ppermute | solution.py:745
  59.2 0.8 %collective-permute-start.12 = (bf16[384,128]{1,0:T(8,128)(2,1)S(1)}, bf16[384,128]{1,0:T(8,128)(2,1)S(1)}, u32[]{:S(2)}, u32[]{:S(2)}) collective-permute-start(bf16[384,128]{1,0:T(8,128)(2,1)S(1)} %get-tuple-element.101.mine), channel_id=1, source_target_pairs={{0,4},{4,0},{8,12},{12,8},{16,20},{20,16},{24,28},{28,24},{1,5},{5... | collective-permute-start | bytes 294920 | tf_op jit(solution)/shard_map/ppermute | solution.py:745
  60.1 4.3 %shard_map.218 = (f32[16,256,512]{2,1,0:T(8,128)}, bf16[8,256,512]{2,1,0:T(8,128)(2,1)S(1)}) custom-call(s32[34]{0:T(128)S(1)} %get-tuple-element.71.meta, bf16[8,256,512]{2,1,0:T(8,128)(2,1)S(1)} %get-tuple-element.86.cot, f32[8,4,288,128]{3,2,1,0:T(8,128)S(1)} %get-tuple-element.102.cgp, f32[16,512]{1,0:T(8,128)S(1)} %get-tuple-element.82.consts), custom_call_target="tpu_custom_call" | custom-call | bytes 40000000 | tf_op jit(solution)/shard_map/pallas_call | solution.py:614
  64.4 2.6 %shard_map.219 = (bf16[16,256,512]{2,1,0:T(8,128)(2,1)}, bf16[8,256,512]{2,1,0:T(8,128)(2,1)S(1)}) custom-call(s32[34]{0:T(128)S(1)} %get-tuple-element.71.meta, bf16[8,256,512]{2,1,0:T(8,128)(2,1)S(1)} %get-tuple-element.85.tok, f32[2304,512]{1,0:T(8,128)S(1)} %get-tuple-element.105.branch, f32[16,512]{1,0:T(8,128)S(1)} %get-tuple-element.82.consts), custom_call_target="tpu_custom_call" | custom-call | bytes 40000000 | tf_op jit(solution)/shard_map/pallas_call | solution.py:561
  67.0 0.0 collective-permute-done.12.theirs
  67.0 0.1 collective-permute-start.16
  67.1 0.0 collective-permute-done.13.far_1
  67.1 0.0 collective-permute-done.11.refs_3_
  67.1 1.6 %collective-permute-done.10.refs_2_ = bf16[448,128]{1,0:T(8,128)(2,1)S(1)} collective-permute-done((bf16[448,128]{1,0:T(8,128)(2,1)S(1)}, bf16[448,128]{1,0:T(8,128)(2,1)S(1)}, u32[]{:S(2)}, u32[]{:S(2)}) %collective-permute-start.10) | collective-permute-done | bytes 114720 | tf_op jit(solution)/shard_map/ppermute | solution.py:745
  68.7 0.0 collective-permute-done.9.refs_1_.near_1
  68.7 0.0 collective-permute-start.15
  68.8 0.2 collective-permute-start.14
  69.0 2.2 %collective-permute-done.16.other = bf16[8,256,512]{2,1,0:T(8,128)(2,1)S(1)} collective-permute-done((bf16[8,256,512]{2,1,0:T(8,128)(2,1)S(1)}, bf16[8,256,512]{2,1,0:T(8,128)(2,1)S(1)}, u32[]{:S(2)}, u32[]{:S(2)}) %collective-permute-start.16) | collective-permute-done | bytes 2097184 | tf_op jit(solution)/shard_map/ppermute | solution.py:740
  71.2 2.6 %shard_map.221 = f32[16,256,512]{2,1,0:T(8,128)} custom-call(s32[34]{0:T(128)S(1)} %get-tuple-element.71.meta, bf16[8,256,512]{2,1,0:T(8,128)(2,1)S(1)} %collective-permute-done.16.other, f32[16,256,512]{2,1,0:T(8,128)} %get-tuple-element.113.gtok_in), custom_call_target="tpu_custom_call", output_to_operand_aliasing={{}: (2, {})} | custom-call | bytes 20000000 | tf_op jit(solution)/shard_map/pallas_call | solution.py:634
  73.9 0.3 collective-permute-done.15.other
  74.2 1.9 %shard_map.222 = bf16[16,256,512]{2,1,0:T(8,128)(2,1)} custom-call(s32[34]{0:T(128)S(1)} %get-tuple-element.71.meta, bf16[8,256,512]{2,1,0:T(8,128)(2,1)S(1)} %collective-permute-done.15.other, bf16[16,256,512]{2,1,0:T(8,128)(2,1)} %get-tuple-element.115.out_in), custom_call_target="tpu_custom_call", output_to_operand_aliasing={{}: (2, {})} | custom-call | bytes 10000000 | tf_op jit(solution)/shard_map/pallas_call | solution.py:653
  76.1 0.4 collective-permute-done.14.far
  76.5 1.9 %shard_map.223 = (f32[7,512]{1,0:T(8,128)}, f32[512]{0:T(512)}, f32[2,512]{1,0:T(2,128)}, f32[2,512]{1,0:T(2,128)}, f32[512,384]{1,0:T(8,128)}, /*index=5*/f32[3...) custom-call(s32[34]{0:T(128)S(1)} %get-tuple-element.71.meta, bf16[384,128]{1,0:T(8,128)(2,1)S(1)} %get-tuple-element.101.mine, ...), custom_call_target="tpu_custom_call" | custom-call | tf_op jit(solution)/shard_map/pallas_call | solution.py:731
  (2 shorter events, 0.0 us)
Async XLA Ops:
  1.9 3.1 %collective-permute-start = (bf16[3088,128]{1,0:T(8,128)(2,1)S(1)}, bf16[3088,128]{1,0:T(8,128)(2,1)S(1)}, u32[]{:S(2)}, u32[]{:S(2)}) collective-permute-start(bf16[3088,128]{1,0:T(8,128)(2,1)S(1)} %shard_map.212.buf_a), channel_id=1, source_target_pairs={{0,1},{1,0},{2,3},{3,2},{4,5},{5,4},{6,7},{7,6},{8,9},{9,8},{10,11... | collective-permute-start | bytes 2371592 | tf_op jit(solution)/shard_map/ppermute | solution.py:740
  2.4 20.8 %collective-permute-start.3 = (bf16[3088,128]{1,0:T(8,128)(2,1)S(1)}, bf16[3088,128]{1,0:T(8,128)(2,1)S(1)}, u32[]{:S(2)}, u32[]{:S(2)}) collective-permute-start(bf16[3088,128]{1,0:T(8,128)(2,1)S(1)} %shard_map.212.buf_a), channel_id=1, source_target_pairs={{0,2},{1,3},{2,0},{3,1},{4,6},{5,7},{6,4},{7,5},{8,10},{9,11},{10,... | collective-permute-start | bytes 2371592 | tf_op jit(solution)/shard_map/ppermute | solution.py:740
  20.5 2.7 %collective-permute-start.1 = (bf16[3072,128]{1,0:T(8,128)(2,1)S(1)}, bf16[3072,128]{1,0:T(8,128)(2,1)S(1)}, u32[]{:S(2)}, u32[]{:S(2)}) collective-permute-start(bf16[3072,128]{1,0:T(8,128)(2,1)S(1)} %get-tuple-element.73), channel_id=1, source_target_pairs={{0,1},{1,0},{2,3},{3,2},{4,5},{5,4},{6,7},{7,6},{8,9},{9,8},{10,11... | collective-permute-start | bytes 2359304 | tf_op jit(solution)/shard_map/ppermute | solution.py:740
  23.2 2.9 %collective-permute-start.4 = (bf16[3088,128]{1,0:T(8,128)(2,1)S(1)}, bf16[3088,128]{1,0:T(8,128)(2,1)S(1)}, u32[]{:S(2)}, u32[]{:S(2)}) collective-permute-start(bf16[3088,128]{1,0:T(8,128)(2,1)S(1)} %collective-permute-done.3.buf_c), channel_id=1, source_target_pairs={{0,1},{1,0},{2,3},{3,2},{4,5},{5,4},{6,7},{7,6},{8,9},{9,8},{10,11... | collective-permute-start | bytes 2371592 | tf_op jit(solution)/shard_map/ppermute | solution.py:740
  23.9 12.6 %collective-permute-start.2 = (bf16[1536,128]{1,0:T(8,128)(2,1)S(1)}, bf16[1536,128]{1,0:T(8,128)(2,1)S(1)}, u32[]{:S(2)}, u32[]{:S(2)}) collective-permute-start(bf16[1536,128]{1,0:T(8,128)(2,1)S(1)} %get-tuple-element.75), channel_id=1, source_target_pairs={{0,4},{4,0},{8,12},{12,8},{16,20},{20,16},{24,28},{28,24},{1,5},{5... | collective-permute-start | bytes 1179656 | tf_op jit(solution)/shard_map/ppermute | solution.py:745
  36.6 14.2 %collective-permute-start.7 = (bf16[384,128]{1,0:T(8,128)(2,1)S(1)}, bf16[384,128]{1,0:T(8,128)(2,1)S(1)}, u32[]{:S(2)}, u32[]{:S(2)}) collective-permute-start(bf16[384,128]{1,0:T(8,128)(2,1)S(1)} %get-tuple-element.133), channel_id=1, source_target_pairs={{0,24},{4,28},{8,16},{12,20},{16,8},{20,12},{24,0},{28,4},{1,25},{... | collective-permute-start | bytes 294920 | tf_op jit(solution)/shard_map/ppermute | solution.py:745
  40.6 10.3 %collective-permute-start.6 = (bf16[384,128]{1,0:T(8,128)(2,1)S(1)}, bf16[384,128]{1,0:T(8,128)(2,1)S(1)}, u32[]{:S(2)}, u32[]{:S(2)}) collective-permute-start(bf16[384,128]{1,0:T(8,128)(2,1)S(1)} %get-tuple-element.134), channel_id=1, source_target_pairs={{0,16},{4,20},{8,24},{12,28},{16,0},{20,4},{24,8},{28,12},{1,17},{... | collective-permute-start | bytes 294920 | tf_op jit(solution)/shard_map/ppermute | solution.py:745
  43.2 7.7 %collective-permute-start.5 = (bf16[384,128]{1,0:T(8,128)(2,1)S(1)}, bf16[384,128]{1,0:T(8,128)(2,1)S(1)}, u32[]{:S(2)}, u32[]{:S(2)}) collective-permute-start(bf16[384,128]{1,0:T(8,128)(2,1)S(1)} %get-tuple-element.135), channel_id=1, source_target_pairs={{0,8},{4,12},{8,0},{12,4},{16,24},{20,28},{24,16},{28,20},{1,9},{5... | collective-permute-start | bytes 294920 | tf_op jit(solution)/shard_map/ppermute | solution.py:745
  50.9 1.3 %collective-permute-start.8 = (f32[16,512]{1,0:T(8,128)S(1)}, f32[16,512]{1,0:T(8,128)S(1)}, u32[]{:S(2)}, u32[]{:S(2)}) collective-permute-start(f32[16,512]{1,0:T(8,128)S(1)} %get-tuple-element.96), channel_id=1, source_target_pairs={{0,1},{1,0},{2,3},{3,2},{4,5},{5,4},{6,7},{7,6},{8,9},{9,8},{10,11... | collective-permute-start | bytes 98312 | tf_op jit(solution)/shard_map/ppermute | solution.py:740
  52.2 14.8 %collective-permute-start.13 = (bf16[448,128]{1,0:T(8,128)(2,1)S(1)}, bf16[448,128]{1,0:T(8,128)(2,1)S(1)}, u32[]{:S(2)}, u32[]{:S(2)}) collective-permute-start(bf16[448,128]{1,0:T(8,128)(2,1)S(1)} %get-tuple-element.107.refs_0_), channel_id=1, source_target_pairs={{0,12},{4,8},{8,4},{12,0},{16,28},{20,24},{24,20},{28,16},{1,13},{... | collective-permute-start | bytes 344072 | tf_op jit(solution)/shard_map/ppermute | solution.py:745
  54.8 12.2 %collective-permute-start.11 = (bf16[448,128]{1,0:T(8,128)(2,1)S(1)}, bf16[448,128]{1,0:T(8,128)(2,1)S(1)}, u32[]{:S(2)}, u32[]{:S(2)}) collective-permute-start(bf16[448,128]{1,0:T(8,128)(2,1)S(1)} %get-tuple-element.107.refs_0_), channel_id=1, source_target_pairs={{0,24},{4,28},{8,16},{12,20},{16,8},{20,12},{24,0},{28,4},{1,25},{... | collective-permute-start | bytes 344072 | tf_op jit(solution)/shard_map/ppermute | solution.py:745
  58.3 10.5 %collective-permute-start.10 = (bf16[448,128]{1,0:T(8,128)(2,1)S(1)}, bf16[448,128]{1,0:T(8,128)(2,1)S(1)}, u32[]{:S(2)}, u32[]{:S(2)}) collective-permute-start(bf16[448,128]{1,0:T(8,128)(2,1)S(1)} %get-tuple-element.107.refs_0_), channel_id=1, source_target_pairs={{0,16},{4,20},{8,24},{12,28},{16,0},{20,4},{24,8},{28,12},{1,17},{... | collective-permute-start | bytes 344072 | tf_op jit(solution)/shard_map/ppermute | solution.py:745
  58.3 10.5 %collective-permute-start.9 = (bf16[448,128]{1,0:T(8,128)(2,1)S(1)}, bf16[448,128]{1,0:T(8,128)(2,1)S(1)}, u32[]{:S(2)}, u32[]{:S(2)}) collective-permute-start(bf16[448,128]{1,0:T(8,128)(2,1)S(1)} %get-tuple-element.107.refs_0_), channel_id=1, source_target_pairs={{0,8},{4,12},{8,0},{12,4},{16,24},{20,28},{24,16},{28,20},{1,9},{5... | collective-permute-start | bytes 344072 | tf_op jit(solution)/shard_map/ppermute | solution.py:745
  59.2 7.8 %collective-permute-start.12 = (bf16[384,128]{1,0:T(8,128)(2,1)S(1)}, bf16[384,128]{1,0:T(8,128)(2,1)S(1)}, u32[]{:S(2)}, u32[]{:S(2)}) collective-permute-start(bf16[384,128]{1,0:T(8,128)(2,1)S(1)} %get-tuple-element.101.mine), channel_id=1, source_target_pairs={{0,4},{4,0},{8,12},{12,8},{16,20},{20,16},{24,28},{28,24},{1,5},{5... | collective-permute-start | bytes 294920 | tf_op jit(solution)/shard_map/ppermute | solution.py:745
  67.0 4.2 %collective-permute-start.16 = (bf16[8,256,512]{2,1,0:T(8,128)(2,1)S(1)}, bf16[8,256,512]{2,1,0:T(8,128)(2,1)S(1)}, u32[]{:S(2)}, u32[]{:S(2)}) collective-permute-start(bf16[8,256,512]{2,1,0:T(8,128)(2,1)S(1)} %get-tuple-element.112), channel_id=1, source_target_pairs={{0,1},{1,0},{2,3},{3,2},{4,5},{5,4},{6,7},{7,6},{8,9},{9,8},{10,11... | collective-permute-start | bytes 6291464 | tf_op jit(solution)/shard_map/ppermute | solution.py:740
  68.7 5.5 %collective-permute-start.15 = (bf16[8,256,512]{2,1,0:T(8,128)(2,1)S(1)}, bf16[8,256,512]{2,1,0:T(8,128)(2,1)S(1)}, u32[]{:S(2)}, u32[]{:S(2)}) collective-permute-start(bf16[8,256,512]{2,1,0:T(8,128)(2,1)S(1)} %get-tuple-element.111), channel_id=1, source_target_pairs={{0,1},{1,0},{2,3},{3,2},{4,5},{5,4},{6,7},{7,6},{8,9},{9,8},{10,11... | collective-permute-start | bytes 6291464 | tf_op jit(solution)/shard_map/ppermute | solution.py:740
  68.8 7.7 %collective-permute-start.14 = (bf16[832,128]{1,0:T(8,128)(2,1)S(1)}, bf16[832,128]{1,0:T(8,128)(2,1)S(1)}, u32[]{:S(2)}, u32[]{:S(2)}) collective-permute-start(bf16[832,128]{1,0:T(8,128)(2,1)S(1)} %shard_map.220.near), channel_id=1, source_target_pairs={{0,4},{4,0},{8,12},{12,8},{16,20},{20,16},{24,28},{28,24},{1,5},{5... | collective-permute-start | bytes 638984 | tf_op jit(solution)/shard_map/ppermute | solution.py:745

commit v9 on v8

--- a/solution.py
+++ b/solution.py
@@ -134,8 +134,8 @@
 
 
 def front_kernel(n, counts_hbm, groups_hbm, tok_hbm, cot_hbm, cw, cb, ns, nsh, gamma, bout, buf_a, buf_b,
-                 ad, nrm, low, inv, act, pre, win, wout, keep, send, gbo, gbi, tok, cot, consts, meta,
-                 offs, counts_s, groups_s, pad, ad_s, nrm_s, low_s, inv_s, bias, bias_row, dwo, dwi, sems, item_sems, meta_sems):
+                 ad, nrm, low, inv, act, pre, win, wout, keep, send, gbo, gbi, tok, cot, consts, tokp, meta,
+                 offs, counts_s, groups_s, pad, ad_s, nrm_s, low_s, inv_s, bias, bias_row, dwo, dwi, sems, item_sems, meta_sems, packed_sem):
     s = pl.program_id(0)
     frames, width = tok.shape[1], tok.shape[2]
     taps, rates = cw.shape[0], ns.shape[0]
@@ -199,6 +199,21 @@
 
     for c in fetch(s):
         c.wait()
+
+    def fetch_packed(j):
+        dst = pl.ds(pl.multiple_of(offs[j], 16), frames)
+        return pltpu.make_async_copy(tok_hbm.at[(lax.axis_index("tp") & 1) * n + j], tokp.at[dst, :], packed_sem)
+
+    @pl.when(s > 0)
+    def _():
+        fetch_packed(s - 1).wait()
+
+    fetch_packed(s).start()
+
+    @pl.when(s == n - 1)
+    def _():
+        fetch_packed(s).wait()
+
     item = meta[0] * n + s
     count = meta[2 + item]
     group = meta[2 + 2 * n + item]
@@ -326,7 +341,7 @@
         grid_spec=pl.GridSpec(
             grid=(n,),
             in_specs=[hbm()] * 4 + [whole(v.shape) for v in (cw, cb, ns, nsh, gamma, bout)] + [hbm()] * 2,
-            out_specs=[vmem()] * 15 + [smem()],
+            out_specs=[vmem()] * 16 + [smem()],
             scratch_shapes=[pltpu.SMEM((n + 3,), jnp.int32), pltpu.SMEM((items,), jnp.int32), pltpu.SMEM((items,), jnp.int32),
                             pltpu.VMEM((wq, frames + 4 * PAD, LANES), F32),
                             pltpu.VMEM((frames, width), BF), pltpu.VMEM((frames, width), BF),
@@ -334,11 +349,11 @@
                             pltpu.VMEM((2, 16, LANES), BF), pltpu.VMEM((1, 2 * h), F32),
                             pltpu.VMEM((2 * h, width), F32), pltpu.VMEM((width, 2 * h), F32),
                             pltpu.SemaphoreType.DMA((2, hq + wq + 1)), pltpu.SemaphoreType.DMA((2, n)),
-                            pltpu.SemaphoreType.DMA((2,))]),
+                            pltpu.SemaphoreType.DMA((2,)), pltpu.SemaphoreType.DMA]),
         out_shape=[struct((rows, width), BF)] * 3 + [struct((rows, LANES), F32)]
         + [struct((rows, 2 * h), BF)] * 2 + [struct((width, 2 * h), BF), struct((2 * h, width), BF)]
         + [struct((packed, LANES), F32), struct((packed, LANES), BF), struct((8, width), F32), struct((8, 2 * h), F32)]
-        + [struct((n, frames, width), BF)] * 2 + [struct((n_consts, width), F32), struct((2 + 2 * items,), jnp.int32)],
+        + [struct((n, frames, width), BF)] * 2 + [struct((n_consts, width), F32), struct((rows, width), BF), struct((2 + 2 * items,), jnp.int32)],
         compiler_params=params(), cost_estimate=cost(0),
     )(counts, groups, tok, cot, cw, cb, ns, nsh, gamma, bout, buf_a, buf_b)
 
@@ -361,7 +376,7 @@
         compiler_params=params())(meta, keep, recv)
 
 
-def mix_kernel(n, taps, meta, ad, low, act, pre, win1, wout1, consts, buf_c, buf_d, branch, ag,
+def mix_kernel(n, taps, meta, ad, low, act, pre, win1, wout1, consts, tokp, buf_c, buf_d, branch, ag, out,
                offs, win2, wout2, bias, bias_row, sems):
     copies = weight_copies(buf_c, 0, win2, wout2, bias, sems) + weight_copies(buf_d, 1, win2, wout2, bias, sems)
     for c in copies:
@@ -375,7 +390,9 @@
         a, b = ad[at, :], low[at, :]
         activation, slope = gelu_parts(dot(a, win2[...]) + bias_row[...])
         grad = dot_t(b, wout2[...]) * slope
-        branch[at, :] = (own_branch + dot(activation.astype(BF), wout2[...])) + consts[taps + 1:taps + 2, :]
+        value = (own_branch + dot(activation.astype(BF), wout2[...])) + consts[taps + 1:taps + 2, :]
+        branch[at, :] = value
+        out[at, :] = (tokp[at, :].astype(F32) + consts[taps:taps + 1, :] * value).astype(BF)
         ag[at, :] = own_ag + dot_t(grad.astype(BF), win2[...])
 
     first = pl.ds(0, TILE)
@@ -393,21 +410,21 @@
     lax.fori_loop(1, offs[n + 1], tile, 0)
 
 
-def mix(meta, ad, low, act, pre, win, wout, consts, buf_c, buf_d, n, taps):
+def mix(meta, ad, low, act, pre, win, wout, consts, tokp, buf_c, buf_d, n, taps):
     rows, width = ad.shape
     h = act.shape[1] // 2
     wq, hq = width // LANES, h // LANES
     return pl.pallas_call(
         functools.partial(mix_kernel, n, taps),
-        in_specs=[smem()] + [vmem()] * 7 + [hbm()] * 2,
-        out_specs=[vmem(), vmem()],
+        in_specs=[smem()] + [vmem()] * 8 + [hbm()] * 2,
+        out_specs=[vmem()] * 3,
         scratch_shapes=[pltpu.SMEM((n + 2,), jnp.int32),
                         pltpu.VMEM((width, 2 * h), BF), pltpu.VMEM((2 * h, width), BF),
                         pltpu.VMEM((2, 16, LANES), BF), pltpu.VMEM((1, 2 * h), F32),
                         pltpu.SemaphoreType.DMA((2, hq + wq + 1))],
-        out_shape=[struct((rows, width), F32)] * 2,
+        out_shape=[struct((rows, width), F32)] * 2 + [struct((rows, width), BF)],
         compiler_params=params(), cost_estimate=cost(0),
-    )(meta, ad, low, act, pre, win, wout, consts, buf_c, buf_d)
+    )(meta, ad, low, act, pre, win, wout, consts, tokp, buf_c, buf_d)
 
 
 def norm_grad_kernel(n, taps, rates, meta, tok, cot, branch, ag, nrm, inv, gbo, gbi, consts,
@@ -527,44 +544,35 @@
     )(meta, tok, cot, branch, ag, nrm, inv, gbo, gbi, consts)
 
 
-def block_out_kernel(n, taps, meta, tok, branch, consts, out, own, offs, sems):
-    s = pl.program_id(0)
-    frames, width = tok.shape[1], tok.shape[2]
-
-    def place(j):
-        return pltpu.make_async_copy(own.at[j], out.at[meta[0] * n + j], sems.at[j])
-
-    @pl.when(s == 0)
-    def _():
-        place_items(n, meta, offs)
-
-    count = meta[2 + meta[0] * n + s]
-    off = offs[s]
-    gam = consts[taps:taps + 1, :]
-    for i in range(frames // CHUNK):
-        here = pl.ds(i * CHUNK, CHUNK)
-        live = (lax.broadcasted_iota(jnp.int32, (CHUNK, LANES), 0) + i * CHUNK) < count
-        src = pl.ds(pl.multiple_of(off + i * CHUNK, 16), CHUNK)
-        for q in range(width // LANES):
-            value = tok[s, here, lane(q)].astype(F32) + gam[:, lane(q)] * branch[src, lane(q)]
-            own[s, here, lane(q)] = jnp.where(live, value, 0.0).astype(BF)
-    place(s).start()
-
-    @pl.when(s == n - 1)
-    def _():
+def place_out_kernel(n, meta, own, other, out, stage, sems):
+    frames, width = stage.shape[1], stage.shape[2]
+    copies = []
+    for side, src in ((0, own), (1, other)):
+        first = (meta[0] ^ side) * n
+        off = jnp.int32(0)
         for j in range(n):
-            place(j).wait()
-
-
-def block_out(meta, tok, branch, consts, taps):
-    n, frames, width = tok.shape
+            count = meta[2 + first + j]
+            for i in range(frames // CHUNK):
+                live = (lax.broadcasted_iota(jnp.int32, (CHUNK, LANES), 0) + i * CHUNK) < count
+                rows = pl.ds(pl.multiple_of(off + i * CHUNK, 16), CHUNK)
+                for q in range(width // LANES):
+                    value = jnp.where(live, src[rows, lane(q)].astype(F32), 0.0)
+                    stage[side * n + j, i * CHUNK:(i + 1) * CHUNK, lane(q)] = value.astype(BF)
+            copies.append(pltpu.make_async_copy(stage.at[side * n + j], out.at[first + j], sems.at[side * n + j]))
+            copies[-1].start()
+            off = off + ((count + 15) & -16)
+    for c in copies:
+        c.wait()
+
+
+def place_out(meta, own, other, n, frames):
+    width = own.shape[1]
     return pl.pallas_call(
-        functools.partial(block_out_kernel, n, taps), grid=(n,),
-        in_specs=[smem()] + [vmem()] * 3, out_specs=[hbm(), vmem()],
-        scratch_shapes=[pltpu.SMEM((n + 2,), jnp.int32), pltpu.SemaphoreType.DMA((n,))],
-        out_shape=[struct((2 * n, frames, width), BF), struct((n, frames, width), BF)],
+        functools.partial(place_out_kernel, n),
+        in_specs=[smem(), vmem(), vmem()], out_specs=hbm(), out_shape=struct((2 * n, frames, width), BF),
+        scratch_shapes=[pltpu.VMEM((2 * n, frames, width), BF), pltpu.SemaphoreType.DMA((2 * n,))],
         compiler_params=params(), cost_estimate=cost(40000000),
-    )(meta, tok, branch, consts)
+    )(meta, own, other)
 
 
 def token_grad_kernel(n, taps, meta, cot, cgp, consts, gtok, gtok_own, stage, sems):
@@ -638,25 +646,6 @@
         input_output_aliases={2: 0},
         compiler_params=params(), cost_estimate=cost(20000000),
     )(meta, other, gtok)
-
-
-def merge_out_kernel(n, meta, other, out_in, out, sems):
-    copies = [pltpu.make_async_copy(other.at[j], out.at[(1 - meta[0]) * n + j], sems.at[j]) for j in range(n)]
-    for c in copies:
-        c.start()
-    for c in copies:
-        c.wait()
-
-
-def merge_out(meta, other, out):
-    n = other.shape[0]
-    return pl.pallas_call(
-        functools.partial(merge_out_kernel, n),
-        in_specs=[smem(), vmem(), hbm()], out_specs=hbm(), out_shape=struct(out.shape, BF),
-        scratch_shapes=[pltpu.SemaphoreType.DMA((n,))],
-        input_output_aliases={2: 0},
-        compiler_params=params(), cost_estimate=cost(10000000),
-    )(meta, other, out)
 
 
 def message_kernel(stay, keep, recv, *refs):
@@ -759,33 +748,33 @@
     buf_b = swap(buf_a, 1)
     buf_c = swap(buf_a, 2)
     buf_d = swap(buf_c, 1)
-    ad, nrm, low, inv, act, pre, win, wout, keep, send, gbo, gbi, tok, cot, consts, meta = front(
+    ad, nrm, low, inv, act, pre, win, wout, keep, send, gbo, gbi, tok, cot, consts, tokp, meta = front(
         frame_counts, rate_groups, tokens, cotangent, conv_weight, conv_bias, norm_scale, norm_shift, layer_scale, bias_out, buf_a, buf_b, h)
     stay, leave = combine(meta, keep, swap(send, 1), dp)
     arrived = across(leave, 1)
-    branch, ag = mix(meta, ad, low, act, pre, win, wout, consts, buf_c, buf_d, n, taps)
-    arrived, branch = lax.optimization_barrier((arrived, branch))
+    branch, ag, out_own = mix(meta, ad, low, act, pre, win, wout, consts, tokp, buf_c, buf_d, n, taps)
+    arrived, branch, out_own = lax.optimization_barrier((arrived, branch, out_own))
+    out_b = swap(out_own, 1)
     stay = (stay + arrived.astype(F32)).reshape(dp // 2, -1, LANES)
     pieces = [across(stay[d].astype(BF), 2 * d) for d in range(1, dp // 2)]
 
     cgp, small_keep, small_send = norm_grad(meta, tok, cot, branch, ag, nrm, inv, gbo, gbi, consts, taps, rates)
-    pieces, small_send, cgp, branch = lax.optimization_barrier((pieces, small_send, cgp, branch))
+    pieces, small_send, cgp, out_b = lax.optimization_barrier((pieces, small_send, cgp, out_b))
     small_got = swap(small_send, 1)
     message, mine = make_message(stay.reshape(-1, LANES), small_keep, small_got, pieces)
+    message, mine, out_b = lax.optimization_barrier((message, mine, out_b))
     m = pieces[0].shape[0]
     near = [message] + [across(message, 2 * d) for d in range(1, dp // 2)]
     theirs = across(mine, 1)
     far_1 = across(message, 3)
+    out = place_out(meta, out_own, out_b, n, tokens.shape[1])
+    cgp, out = lax.optimization_barrier((cgp, out))
     gtok, gtok_own = token_grad(meta, cot, cgp, consts, taps)
-    gtok_own, branch = lax.optimization_barrier((gtok_own, branch))
-    out, out_own = block_out(meta, tok, branch, consts, taps)
-    near, theirs, far_1, out_own = lax.optimization_barrier((near, theirs, far_1, out_own))
+    near, theirs, far_1, gtok_own = lax.optimization_barrier((near, theirs, far_1, gtok_own))
     late = relay(m, near)
     far = across(late, 1)
     gtok = merge_gtok(meta, swap(gtok_own, 1), gtok)
-    out_b, gtok = lax.optimization_barrier((swap(out_own, 1), gtok))
-    out = merge_out(meta, out_b, out)
-    far, out, gtok = lax.optimization_barrier((far, out, gtok))
+    far, gtok = lax.optimization_barrier((far, gtok))
     gcw, gcb, gns, gnsh, gwi, gbi, gwo, gbo, gls = unpack(meta, mine, theirs, near[1], far_1, late, far, dp, taps, rates,
                                                           width, h)
     return (out, gtok, gcw, gcb, gns, gnsh, gwi, gbi, gwo, gbo, gls)

time: 78.1 us -> 79.3 us (1.015); the launches traced: 78.4 us -> 78.7 us
    pallas_call x2 -> x1, Pallas kernels: 4.47 us -> 2.73 us  [place_out(): pl.pallas_call(functools.partial(place_out_kernel, n), in_specs=[smem(),...]
    pallas_call x1, Pallas kernels: 15.5 us -> 17.1 us  [front(): pl.pallas_call(functools.partial(front_kernel, n), grid_spec=pl.GridSpec(...]
where the time goes in v9:
time: 79.3 us; the launch traced here: 78.7 us
  Pallas kernels  48.8 us (62%)
  starting transfers between devices  21.3 us (27%)
  waiting for transfers between devices  7.6 us (10%)
  between operations  0.82 us (1%)
    ppermute x10, starting transfers between devices, across(): return lax.ppermute(x, 'dp', [(i, i ^ step) for i in range(size)])  18 us
    pallas_call x1, Pallas kernels, front(): pl.pallas_call(functools.partial(front_kernel, n), grid_spec=pl.GridSpec(...  17.1 us
    pallas_call x1, Pallas kernels, mix(): pl.pallas_call(functools.partial(mix_kernel, n, taps), in_specs=[smem()]...  10.4 us
    pallas_call x1, Pallas kernels, norm_grad(): pl.pallas_call(functools.partial(norm_grad_kernel, n, taps, rates), grid=...  7.54 us
    ppermute x7, waiting for transfers between devices, swap(): return lax.ppermute(x, 'tp', [(i, i ^ step) for i in range(size)])  6.07 us
    pallas_call x1, Pallas kernels, token_grad(): pl.pallas_call(functools.partial(token_grad_kernel, n, taps), grid=(n,),...  4.51 us
    ppermute x7, starting transfers between devices, swap(): return lax.ppermute(x, 'tp', [(i, i ^ step) for i in range(size)])  3.3 us
    pallas_call x1, Pallas kernels, place_out(): pl.pallas_call(functools.partial(place_out_kernel, n), in_specs=[smem(),...  2.73 us
  transfers between devices with their start and end apart: 17, of which 6 were waited for; matrix products, arithmetic and copies ran while one was open for 0% of the time, Pallas kernels for 58%

profile of v9, /device:TPU:0, one launch (start us, length us, event | category | flops | bytes accessed | tf_op | source)
XLA Modules:
  0.0 78.7 jit_solution(8981509971041625086)
XLA Ops:
  0.6 1.3 %shard_map.212.buf_a = bf16[3088,128]{1,0:T(8,128)(2,1)S(1)} custom-call(bf16[512,384]{1,0:T(8,128)(2,1)} %wi.1, bf16[384]{0:T(512)(128)(2,1)} %bi.1, bf16[384,512]{1,0:T(8,128)(2,1)} %wo.1), custom_call_target="tpu_custom_call" | custom-call | tf_op jit(solution)/shard_map/pallas_call | solution.py:110
  1.9 0.5 collective-permute-start
  2.4 2.6 %collective-permute-start.3 = (bf16[3088,128]{1,0:T(8,128)(2,1)S(1)}, bf16[3088,128]{1,0:T(8,128)(2,1)S(1)}, u32[]{:S(2)}, u32[]{:S(2)}) collective-permute-start(bf16[3088,128]{1,0:T(8,128)(2,1)S(1)} %shard_map.212.buf_a), channel_id=1, source_target_pairs={{0,2},{1,3},{2,0},{3,1},{4,6},{5,7},{6,4},{7,5},{8,10},{9,11},{10,... | collective-permute-start | bytes 2371592 | tf_op jit(solution)/shard_map/ppermute | solution.py:729
  5.0 0.0 collective-permute-done.buf_b
  5.0 17.1 %shard_map.213 = (bf16[2304,512]{1,0:T(8,128)(2,1)S(1)}, bf16[2304,512]{1,0:T(8,128)(2,1)S(1)}, bf16[2304,512]{1,0:T(8,128)(2,1)S(1)}, f32[2304,128]{1,0:T(8,128...) custom-call(s32[16]{0:T(128)} %counts_hbm.1, ...), custom_call_target="tpu_custom_call" | custom-call | tf_op jit(solution)/shard_map/pallas_call | solution.py:339
  22.1 0.1 collective-permute-start.1
  22.2 1.0 %collective-permute-done.3.buf_c = bf16[3088,128]{1,0:T(8,128)(2,1)S(1)} collective-permute-done((bf16[3088,128]{1,0:T(8,128)(2,1)S(1)}, bf16[3088,128]{1,0:T(8,128)(2,1)S(1)}, u32[]{:S(2)}, u32[]{:S(2)}) %collective-permute-start.3) | collective-permute-done | bytes 790560 | tf_op jit(solution)/shard_map/ppermute | solution.py:729
  23.2 0.0 collective-permute-start.4
  23.2 1.3 %collective-permute-done.1.recv = bf16[3072,128]{1,0:T(8,128)(2,1)S(1)} collective-permute-done((bf16[3072,128]{1,0:T(8,128)(2,1)S(1)}, bf16[3072,128]{1,0:T(8,128)(2,1)S(1)}, u32[]{:S(2)}, u32[]{:S(2)}) %collective-permute-start.1) | collective-permute-done | bytes 786464 | tf_op jit(solution)/shard_map/ppermute | solution.py:729
  24.5 0.7 shard_map.214
  25.2 3.2 %collective-permute-start.2 = (bf16[1536,128]{1,0:T(8,128)(2,1)S(1)}, bf16[1536,128]{1,0:T(8,128)(2,1)S(1)}, u32[]{:S(2)}, u32[]{:S(2)}) collective-permute-start(bf16[1536,128]{1,0:T(8,128)(2,1)S(1)} %get-tuple-element.76), channel_id=1, source_target_pairs={{0,4},{4,0},{8,12},{12,8},{16,20},{20,16},{24,28},{28,24},{1,5},{5... | collective-permute-start | bytes 1179656 | tf_op jit(solution)/shard_map/ppermute | solution.py:734
  28.4 0.0 collective-permute-done.4.buf_d
  28.4 10.4 %shard_map.215 = (f32[2304,512]{1,0:T(8,128)S(1)}, f32[2304,512]{1,0:T(8,128)S(1)}, bf16[2304,512]{1,0:T(8,128)(2,1)S(1)}) custom-call(s32[34]{0:T(128)S(1)} %get-tuple-element.72.meta, bf16[2304,512]{1,0:T(8,128)(2,1)S(1)} %get-tuple-element.77.ad, bf16[2304,512]{1,0:T(8,128)(2,1)S(1)} %get-tuple-element.78.low, ...), custom_call_target="tpu_custom_call" | custom-call | tf_op jit(solution)/shard_map/pallas_call | solution.py:417
  38.7 0.0 collective-permute-done.2
  38.8 0.1 collective-permute-start.8
  38.8 0.1 fusion
  39.0 5.5 %collective-permute-start.7 = (bf16[384,128]{1,0:T(8,128)(2,1)S(1)}, bf16[384,128]{1,0:T(8,128)(2,1)S(1)}, u32[]{:S(2)}, u32[]{:S(2)}) collective-permute-start(bf16[384,128]{1,0:T(8,128)(2,1)S(1)} %get-tuple-element.135), channel_id=1, source_target_pairs={{0,24},{4,28},{8,16},{12,20},{16,8},{20,12},{24,0},{28,4},{1,25},{... | collective-permute-start | bytes 294920 | tf_op jit(solution)/shard_map/ppermute | solution.py:734
  44.5 0.0 collective-permute-start.6
  44.5 0.6 collective-permute-start.5
  45.1 7.5 %shard_map.216 = (f32[8,4,288,128]{3,2,1,0:T(8,128)S(1)}, f32[16,512]{1,0:T(8,128)S(1)}, f32[16,512]{1,0:T(8,128)S(1)}) custom-call(s32[34]{0:T(128)S(1)} %get-tuple-element.72.meta, bf16[8,256,512]{2,1,0:T(8,128)(2,1)S(1)} %get-tuple-element.88.tok, bf16[8,256,512]{2,1,0:T(8,128)(2,1)S(1)} %get-tuple-element.89.cot, ...), custom_call_target="tpu_custom_call" | custom-call | bytes 40000000 | tf_op jit(solution)/shard_map/pallas_call | solution.py:537
  52.7 0.0 collective-permute-done.7.refs_2_
  52.7 0.0 collective-permute-done.6.refs_1_
  52.7 0.0 collective-permute-done.5.refs_0_
  52.7 0.0 collective-permute-done.8.other
  52.7 0.1 collective-permute-start.9
  52.8 1.2 %collective-permute-done.9.recv = f32[16,512]{1,0:T(8,128)S(1)} collective-permute-done((f32[16,512]{1,0:T(8,128)S(1)}, f32[16,512]{1,0:T(8,128)S(1)}, u32[]{:S(2)}, u32[]{:S(2)}) %collective-permute-start.9) | collective-permute-done | bytes 32800 | tf_op jit(solution)/shard_map/ppermute | solution.py:729
  54.0 0.1 shard_map.217
  54.1 1.1 %collective-permute-start.14 = (bf16[448,128]{1,0:T(8,128)(2,1)S(1)}, bf16[448,128]{1,0:T(8,128)(2,1)S(1)}, u32[]{:S(2)}, u32[]{:S(2)}) collective-permute-start(bf16[448,128]{1,0:T(8,128)(2,1)S(1)} %get-tuple-element.114.refs_0_), channel_id=1, source_target_pairs={{0,12},{4,8},{8,4},{12,0},{16,28},{20,24},{24,20},{28,16},{1,13},{... | collective-permute-start | bytes 344072 | tf_op jit(solution)/shard_map/ppermute | solution.py:734
  55.2 2.8 %collective-permute-start.12 = (bf16[448,128]{1,0:T(8,128)(2,1)S(1)}, bf16[448,128]{1,0:T(8,128)(2,1)S(1)}, u32[]{:S(2)}, u32[]{:S(2)}) collective-permute-start(bf16[448,128]{1,0:T(8,128)(2,1)S(1)} %get-tuple-element.114.refs_0_), channel_id=1, source_target_pairs={{0,24},{4,28},{8,16},{12,20},{16,8},{20,12},{24,0},{28,4},{1,25},{... | collective-permute-start | bytes 344072 | tf_op jit(solution)/shard_map/ppermute | solution.py:734
  57.9 0.5 collective-permute-start.11
  58.4 1.1 %collective-permute-start.10 = (bf16[448,128]{1,0:T(8,128)(2,1)S(1)}, bf16[448,128]{1,0:T(8,128)(2,1)S(1)}, u32[]{:S(2)}, u32[]{:S(2)}) collective-permute-start(bf16[448,128]{1,0:T(8,128)(2,1)S(1)} %get-tuple-element.114.refs_0_), channel_id=1, source_target_pairs={{0,8},{4,12},{8,0},{12,4},{16,24},{20,28},{24,16},{28,20},{1,9},{5... | collective-permute-start | bytes 344072 | tf_op jit(solution)/shard_map/ppermute | solution.py:734
  59.6 1.6 %collective-permute-start.13 = (bf16[384,128]{1,0:T(8,128)(2,1)S(1)}, bf16[384,128]{1,0:T(8,128)(2,1)S(1)}, u32[]{:S(2)}, u32[]{:S(2)}) collective-permute-start(bf16[384,128]{1,0:T(8,128)(2,1)S(1)} %get-tuple-element.111.mine), channel_id=1, source_target_pairs={{0,4},{4,0},{8,12},{12,8},{16,20},{20,16},{24,28},{28,24},{1,5},{5... | collective-permute-start | bytes 294920 | tf_op jit(solution)/shard_map/ppermute | solution.py:734
  61.1 2.7 %shard_map.218 = bf16[16,256,512]{2,1,0:T(8,128)(2,1)} custom-call(s32[34]{0:T(128)S(1)} %get-tuple-element.72.meta, bf16[2304,512]{1,0:T(8,128)(2,1)S(1)} %get-tuple-element.98.own, bf16[2304,512]{1,0:T(8,128)(2,1)S(1)} %collective-permute-done.8.other), custom_call_target="tpu_custom_call" | custom-call | bytes 40000000 | tf_op jit(solution)/shard_map/pallas_call | solution.py:570
  63.9 4.5 %shard_map.219 = (f32[16,256,512]{2,1,0:T(8,128)}, bf16[8,256,512]{2,1,0:T(8,128)(2,1)S(1)}) custom-call(s32[34]{0:T(128)S(1)} %get-tuple-element.72.meta, bf16[8,256,512]{2,1,0:T(8,128)(2,1)S(1)} %get-tuple-element.89.cot, f32[8,4,288,128]{3,2,1,0:T(8,128)S(1)} %get-tuple-element.112.cgp, f32[16,512]{1,0:T(8,128)S(1)} %get-tuple-element.83.consts), custom_call_target="tpu_custom_call" | custom-call | bytes 40000000 | tf_op jit(solution)/shard_map/pallas_call | solution.py:622
  68.4 0.0 collective-permute-done.13.theirs
  68.4 0.0 collective-permute-done.14.far_1
  68.4 0.0 collective-permute-done.12.refs_3_
  68.4 0.6 collective-permute-done.11.refs_2_
  69.0 0.0 collective-permute-done.10.refs_1_.near_1
  69.0 0.0 collective-permute-start.16
  69.0 1.5 %collective-permute-start.15 = (bf16[832,128]{1,0:T(8,128)(2,1)S(1)}, bf16[832,128]{1,0:T(8,128)(2,1)S(1)}, u32[]{:S(2)}, u32[]{:S(2)}) collective-permute-start(bf16[832,128]{1,0:T(8,128)(2,1)S(1)} %shard_map.220.near), channel_id=1, source_target_pairs={{0,4},{4,0},{8,12},{12,8},{16,20},{20,16},{24,28},{28,24},{1,5},{5... | collective-permute-start | bytes 638984 | tf_op jit(solution)/shard_map/ppermute | solution.py:734
  70.6 2.6 %collective-permute-done.16.other = bf16[8,256,512]{2,1,0:T(8,128)(2,1)S(1)} collective-permute-done((bf16[8,256,512]{2,1,0:T(8,128)(2,1)S(1)}, bf16[8,256,512]{2,1,0:T(8,128)(2,1)S(1)}, u32[]{:S(2)}, u32[]{:S(2)}) %collective-permute-start.16) | collective-permute-done | bytes 2097184 | tf_op jit(solution)/shard_map/ppermute | solution.py:729
  73.2 2.6 %shard_map.221 = f32[16,256,512]{2,1,0:T(8,128)} custom-call(s32[34]{0:T(128)S(1)} %get-tuple-element.72.meta, bf16[8,256,512]{2,1,0:T(8,128)(2,1)S(1)} %collective-permute-done.16.other, f32[16,256,512]{2,1,0:T(8,128)} %get-tuple-element.119.gtok_in), custom_call_target="tpu_custom_call", output_to_operand_aliasing={{}: (2, {})} | custom-call | bytes 20000000 | tf_op jit(solution)/shard_map/pallas_call | solution.py:642
  75.8 1.0 %collective-permute-done.15.far = bf16[832,128]{1,0:T(8,128)(2,1)S(1)} collective-permute-done((bf16[832,128]{1,0:T(8,128)(2,1)S(1)}, bf16[832,128]{1,0:T(8,128)(2,1)S(1)}, u32[]{:S(2)}, u32[]{:S(2)}) %collective-permute-start.15) | collective-permute-done | bytes 213024 | tf_op jit(solution)/shard_map/ppermute | solution.py:734
  76.8 1.9 %shard_map.222 = (f32[7,512]{1,0:T(8,128)}, f32[512]{0:T(512)}, f32[2,512]{1,0:T(2,128)}, f32[2,512]{1,0:T(2,128)}, f32[512,384]{1,0:T(8,128)}, /*index=5*/f32[3...) custom-call(s32[34]{0:T(128)S(1)} %get-tuple-element.72.meta, bf16[384,128]{1,0:T(8,128)(2,1)S(1)} %get-tuple-element.111.mine, ...), custom_call_target="tpu_custom_call" | custom-call | tf_op jit(solution)/shard_map/pallas_call | solution.py:720
  (2 shorter events, 0.0 us)
Async XLA Ops:
  1.9 3.1 %collective-permute-start = (bf16[3088,128]{1,0:T(8,128)(2,1)S(1)}, bf16[3088,128]{1,0:T(8,128)(2,1)S(1)}, u32[]{:S(2)}, u32[]{:S(2)}) collective-permute-start(bf16[3088,128]{1,0:T(8,128)(2,1)S(1)} %shard_map.212.buf_a), channel_id=1, source_target_pairs={{0,1},{1,0},{2,3},{3,2},{4,5},{5,4},{6,7},{7,6},{8,9},{9,8},{10,11... | collective-permute-start | bytes 2371592 | tf_op jit(solution)/shard_map/ppermute | solution.py:729
  2.4 20.8 %collective-permute-start.3 = (bf16[3088,128]{1,0:T(8,128)(2,1)S(1)}, bf16[3088,128]{1,0:T(8,128)(2,1)S(1)}, u32[]{:S(2)}, u32[]{:S(2)}) collective-permute-start(bf16[3088,128]{1,0:T(8,128)(2,1)S(1)} %shard_map.212.buf_a), channel_id=1, source_target_pairs={{0,2},{1,3},{2,0},{3,1},{4,6},{5,7},{6,4},{7,5},{8,10},{9,11},{10,... | collective-permute-start | bytes 2371592 | tf_op jit(solution)/shard_map/ppermute | solution.py:729
  22.1 2.4 %collective-permute-start.1 = (bf16[3072,128]{1,0:T(8,128)(2,1)S(1)}, bf16[3072,128]{1,0:T(8,128)(2,1)S(1)}, u32[]{:S(2)}, u32[]{:S(2)}) collective-permute-start(bf16[3072,128]{1,0:T(8,128)(2,1)S(1)} %get-tuple-element.74), channel_id=1, source_target_pairs={{0,1},{1,0},{2,3},{3,2},{4,5},{5,4},{6,7},{7,6},{8,9},{9,8},{10,11... | collective-permute-start | bytes 2359304 | tf_op jit(solution)/shard_map/ppermute | solution.py:729
  23.2 5.1 %collective-permute-start.4 = (bf16[3088,128]{1,0:T(8,128)(2,1)S(1)}, bf16[3088,128]{1,0:T(8,128)(2,1)S(1)}, u32[]{:S(2)}, u32[]{:S(2)}) collective-permute-start(bf16[3088,128]{1,0:T(8,128)(2,1)S(1)} %collective-permute-done.3.buf_c), channel_id=1, source_target_pairs={{0,1},{1,0},{2,3},{3,2},{4,5},{5,4},{6,7},{7,6},{8,9},{9,8},{10,11... | collective-permute-start | bytes 2371592 | tf_op jit(solution)/shard_map/ppermute | solution.py:729
  25.2 13.6 %collective-permute-start.2 = (bf16[1536,128]{1,0:T(8,128)(2,1)S(1)}, bf16[1536,128]{1,0:T(8,128)(2,1)S(1)}, u32[]{:S(2)}, u32[]{:S(2)}) collective-permute-start(bf16[1536,128]{1,0:T(8,128)(2,1)S(1)} %get-tuple-element.76), channel_id=1, source_target_pairs={{0,4},{4,0},{8,12},{12,8},{16,20},{20,16},{24,28},{28,24},{1,5},{5... | collective-permute-start | bytes 1179656 | tf_op jit(solution)/shard_map/ppermute | solution.py:734
  38.8 14.0 %collective-permute-start.8 = (bf16[2304,512]{1,0:T(8,128)(2,1)S(1)}, bf16[2304,512]{1,0:T(8,128)(2,1)S(1)}, u32[]{:S(2)}, u32[]{:S(2)}) collective-permute-start(bf16[2304,512]{1,0:T(8,128)(2,1)S(1)} %get-tuple-element.98.own), channel_id=1, source_target_pairs={{0,1},{1,0},{2,3},{3,2},{4,5},{5,4},{6,7},{7,6},{8,9},{9,8},{10,11... | collective-permute-start | bytes 7077896 | tf_op jit(solution)/shard_map/ppermute | solution.py:729
  39.0 13.7 %collective-permute-start.7 = (bf16[384,128]{1,0:T(8,128)(2,1)S(1)}, bf16[384,128]{1,0:T(8,128)(2,1)S(1)}, u32[]{:S(2)}, u32[]{:S(2)}) collective-permute-start(bf16[384,128]{1,0:T(8,128)(2,1)S(1)} %get-tuple-element.135), channel_id=1, source_target_pairs={{0,24},{4,28},{8,16},{12,20},{16,8},{20,12},{24,0},{28,4},{1,25},{... | collective-permute-start | bytes 294920 | tf_op jit(solution)/shard_map/ppermute | solution.py:734
  44.5 8.2 %collective-permute-start.6 = (bf16[384,128]{1,0:T(8,128)(2,1)S(1)}, bf16[384,128]{1,0:T(8,128)(2,1)S(1)}, u32[]{:S(2)}, u32[]{:S(2)}) collective-permute-start(bf16[384,128]{1,0:T(8,128)(2,1)S(1)} %get-tuple-element.136), channel_id=1, source_target_pairs={{0,16},{4,20},{8,24},{12,28},{16,0},{20,4},{24,8},{28,12},{1,17},{... | collective-permute-start | bytes 294920 | tf_op jit(solution)/shard_map/ppermute | solution.py:734
  44.5 8.2 %collective-permute-start.5 = (bf16[384,128]{1,0:T(8,128)(2,1)S(1)}, bf16[384,128]{1,0:T(8,128)(2,1)S(1)}, u32[]{:S(2)}, u32[]{:S(2)}) collective-permute-start(bf16[384,128]{1,0:T(8,128)(2,1)S(1)} %get-tuple-element.137), channel_id=1, source_target_pairs={{0,8},{4,12},{8,0},{12,4},{16,24},{20,28},{24,16},{28,20},{1,9},{5... | collective-permute-start | bytes 294920 | tf_op jit(solution)/shard_map/ppermute | solution.py:734
  52.7 1.3 %collective-permute-start.9 = (f32[16,512]{1,0:T(8,128)S(1)}, f32[16,512]{1,0:T(8,128)S(1)}, u32[]{:S(2)}, u32[]{:S(2)}) collective-permute-start(f32[16,512]{1,0:T(8,128)S(1)} %get-tuple-element.101), channel_id=1, source_target_pairs={{0,1},{1,0},{2,3},{3,2},{4,5},{5,4},{6,7},{7,6},{8,9},{9,8},{10,11... | collective-permute-start | bytes 98312 | tf_op jit(solution)/shard_map/ppermute | solution.py:729
  54.1 14.4 %collective-permute-start.14 = (bf16[448,128]{1,0:T(8,128)(2,1)S(1)}, bf16[448,128]{1,0:T(8,128)(2,1)S(1)}, u32[]{:S(2)}, u32[]{:S(2)}) collective-permute-start(bf16[448,128]{1,0:T(8,128)(2,1)S(1)} %get-tuple-element.114.refs_0_), channel_id=1, source_target_pairs={{0,12},{4,8},{8,4},{12,0},{16,28},{20,24},{24,20},{28,16},{1,13},{... | collective-permute-start | bytes 344072 | tf_op jit(solution)/shard_map/ppermute | solution.py:734
  55.2 13.3 %collective-permute-start.12 = (bf16[448,128]{1,0:T(8,128)(2,1)S(1)}, bf16[448,128]{1,0:T(8,128)(2,1)S(1)}, u32[]{:S(2)}, u32[]{:S(2)}) collective-permute-start(bf16[448,128]{1,0:T(8,128)(2,1)S(1)} %get-tuple-element.114.refs_0_), channel_id=1, source_target_pairs={{0,24},{4,28},{8,16},{12,20},{16,8},{20,12},{24,0},{28,4},{1,25},{... | collective-permute-start | bytes 344072 | tf_op jit(solution)/shard_map/ppermute | solution.py:734
  57.9 11.0 %collective-permute-start.11 = (bf16[448,128]{1,0:T(8,128)(2,1)S(1)}, bf16[448,128]{1,0:T(8,128)(2,1)S(1)}, u32[]{:S(2)}, u32[]{:S(2)}) collective-permute-start(bf16[448,128]{1,0:T(8,128)(2,1)S(1)} %get-tuple-element.114.refs_0_), channel_id=1, source_target_pairs={{0,16},{4,20},{8,24},{12,28},{16,0},{20,4},{24,8},{28,12},{1,17},{... | collective-permute-start | bytes 344072 | tf_op jit(solution)/shard_map/ppermute | solution.py:734
  58.4 10.6 %collective-permute-start.10 = (bf16[448,128]{1,0:T(8,128)(2,1)S(1)}, bf16[448,128]{1,0:T(8,128)(2,1)S(1)}, u32[]{:S(2)}, u32[]{:S(2)}) collective-permute-start(bf16[448,128]{1,0:T(8,128)(2,1)S(1)} %get-tuple-element.114.refs_0_), channel_id=1, source_target_pairs={{0,8},{4,12},{8,0},{12,4},{16,24},{20,28},{24,16},{28,20},{1,9},{5... | collective-permute-start | bytes 344072 | tf_op jit(solution)/shard_map/ppermute | solution.py:734
  59.6 8.8 %collective-permute-start.13 = (bf16[384,128]{1,0:T(8,128)(2,1)S(1)}, bf16[384,128]{1,0:T(8,128)(2,1)S(1)}, u32[]{:S(2)}, u32[]{:S(2)}) collective-permute-start(bf16[384,128]{1,0:T(8,128)(2,1)S(1)} %get-tuple-element.111.mine), channel_id=1, source_target_pairs={{0,4},{4,0},{8,12},{12,8},{16,20},{20,16},{24,28},{28,24},{1,5},{5... | collective-permute-start | bytes 294920 | tf_op jit(solution)/shard_map/ppermute | solution.py:734
  69.0 4.2 %collective-permute-start.16 = (bf16[8,256,512]{2,1,0:T(8,128)(2,1)S(1)}, bf16[8,256,512]{2,1,0:T(8,128)(2,1)S(1)}, u32[]{:S(2)}, u32[]{:S(2)}) collective-permute-start(bf16[8,256,512]{2,1,0:T(8,128)(2,1)S(1)} %get-tuple-element.118), channel_id=1, source_target_pairs={{0,1},{1,0},{2,3},{3,2},{4,5},{5,4},{6,7},{7,6},{8,9},{9,8},{10,11... | collective-permute-start | bytes 6291464 | tf_op jit(solution)/shard_map/ppermute | solution.py:729
  69.0 7.7 %collective-permute-start.15 = (bf16[832,128]{1,0:T(8,128)(2,1)S(1)}, bf16[832,128]{1,0:T(8,128)(2,1)S(1)}, u32[]{:S(2)}, u32[]{:S(2)}) collective-permute-start(bf16[832,128]{1,0:T(8,128)(2,1)S(1)} %shard_map.220.near), channel_id=1, source_target_pairs={{0,4},{4,0},{8,12},{12,8},{16,20},{20,16},{24,28},{28,24},{1,5},{5... | collective-permute-start | bytes 638984 | tf_op jit(solution)/shard_map/ppermute | solution.py:734

commit v10 on v9

--- a/solution.py
+++ b/solution.py
@@ -204,15 +204,13 @@
         dst = pl.ds(pl.multiple_of(offs[j], 16), frames)
         return pltpu.make_async_copy(tok_hbm.at[(lax.axis_index("tp") & 1) * n + j], tokp.at[dst, :], packed_sem)
 
+    @pl.when(s > 1)
+    def _():
+        fetch_packed(s - 2).wait()
+
     @pl.when(s > 0)
     def _():
-        fetch_packed(s - 1).wait()
-
-    fetch_packed(s).start()
-
-    @pl.when(s == n - 1)
-    def _():
-        fetch_packed(s).wait()
+        fetch_packed(s - 1).start()
 
     item = meta[0] * n + s
     count = meta[2 + item]
@@ -316,11 +314,15 @@
         ad[end, :] = jnp.zeros((TILE, width), BF)
         low[end, :] = jnp.zeros((TILE, width), BF)
 
+        fetch_packed(n - 2).wait()
+        fetch_packed(n - 1).start()
+
         def rest(t, _):
             tile(t)
             return 0
 
         lax.fori_loop(offs[n + 2], offs[n + 1], rest, 0)
+        fetch_packed(n - 1).wait()
         for side, dst in ((0, keep), (1, send)):
             for q in range(wq):
                 dst[q * h:(q + 1) * h, :] = dwo[side * h:(side + 1) * h, lane(q)].astype(dst.dtype)

time: 79.3 us -> 78.2 us (0.986); the launches traced: 78.7 us -> 79.1 us
  starting transfers between devices: 21.3 us -> 16.7 us
  waiting for transfers between devices: 7.6 us -> 11.2 us
  Pallas kernels: 48.8 us -> 50.3 us
    ppermute x10, starting transfers between devices: 18 us -> 13.4 us  [across(): return lax.ppermute(x, 'dp', [(i, i ^ step) for i in range(size)])]
    ppermute x10, waiting for transfers between devices: 1.53 us -> 4.07 us  [across(): return lax.ppermute(x, 'dp', [(i, i ^ step) for i in range(size)])]
    pallas_call x1, Pallas kernels: 10.4 us -> 11.9 us  [mix(): pl.pallas_call(functools.partial(mix_kernel, n, taps), in_specs=[smem()]...]
    ppermute x7, waiting for transfers between devices: 6.07 us -> 7.08 us  [swap(): return lax.ppermute(x, 'tp', [(i, i ^ step) for i in range(size)])]
  transfers between devices with their start and end apart: 17 -> 17, of which waited for: 6 -> 7; matrix products, arithmetic and copies ran while one was open for 0% -> 0% of each run, Pallas kernels for 58% -> 59%
where the time goes in v10:
time: 78.2 us; the launch traced here: 79.1 us
  Pallas kernels  50.3 us (64%)
  starting transfers between devices  16.7 us (21%)
  waiting for transfers between devices  11.2 us (14%)
  between operations  0.79 us (1%)
    pallas_call x1, Pallas kernels, front(): pl.pallas_call(functools.partial(front_kernel, n), grid_spec=pl.GridSpec(...  17 us
    ppermute x10, starting transfers between devices, across(): return lax.ppermute(x, 'dp', [(i, i ^ step) for i in range(size)])  13.4 us
    pallas_call x1, Pallas kernels, mix(): pl.pallas_call(functools.partial(mix_kernel, n, taps), in_specs=[smem()]...  11.9 us
    pallas_call x1, Pallas kernels, norm_grad(): pl.pallas_call(functools.partial(norm_grad_kernel, n, taps, rates), grid=...  7.54 us
    ppermute x7, waiting for transfers between devices, swap(): return lax.ppermute(x, 'tp', [(i, i ^ step) for i in range(size)])  7.08 us
    pallas_call x1, Pallas kernels, token_grad(): pl.pallas_call(functools.partial(token_grad_kernel, n, taps), grid=(n,),...  4.51 us
    ppermute x10, waiting for transfers between devices, across(): return lax.ppermute(x, 'dp', [(i, i ^ step) for i in range(size)])  4.07 us
    ppermute x7, starting transfers between devices, swap(): return lax.ppermute(x, 'tp', [(i, i ^ step) for i in range(size)])  3.33 us
  transfers between devices with their start and end apart: 17, of which 7 were waited for; matrix products, arithmetic and copies ran while one was open for 0% of the time, Pallas kernels for 59%

profile of v10, /device:TPU:0, one launch (start us, length us, event | category | flops | bytes accessed | tf_op | source)
XLA Modules:
  0.0 79.1 jit_solution(7339309443469937405)
XLA Ops:
  0.6 1.3 %shard_map.212.buf_a = bf16[3088,128]{1,0:T(8,128)(2,1)S(1)} custom-call(bf16[512,384]{1,0:T(8,128)(2,1)} %wi.1, bf16[384]{0:T(512)(128)(2,1)} %bi.1, bf16[384,512]{1,0:T(8,128)(2,1)} %wo.1), custom_call_target="tpu_custom_call" | custom-call | tf_op jit(solution)/shard_map/pallas_call | solution.py:110
  1.9 0.5 collective-permute-start
  2.4 2.6 %collective-permute-start.3 = (bf16[3088,128]{1,0:T(8,128)(2,1)S(1)}, bf16[3088,128]{1,0:T(8,128)(2,1)S(1)}, u32[]{:S(2)}, u32[]{:S(2)}) collective-permute-start(bf16[3088,128]{1,0:T(8,128)(2,1)S(1)} %shard_map.212.buf_a), channel_id=1, source_target_pairs={{0,2},{1,3},{2,0},{3,1},{4,6},{5,7},{6,4},{7,5},{8,10},{9,11},{10,... | collective-permute-start | bytes 2371592 | tf_op jit(solution)/shard_map/ppermute | solution.py:731
  5.0 0.0 collective-permute-done.buf_b
  5.0 17.0 %shard_map.213 = (bf16[2304,512]{1,0:T(8,128)(2,1)S(1)}, bf16[2304,512]{1,0:T(8,128)(2,1)S(1)}, bf16[2304,512]{1,0:T(8,128)(2,1)S(1)}, f32[2304,128]{1,0:T(8,128...) custom-call(s32[16]{0:T(128)} %counts_hbm.1, ...), custom_call_target="tpu_custom_call" | custom-call | tf_op jit(solution)/shard_map/pallas_call | solution.py:341
  22.0 0.1 collective-permute-start.1
  22.1 1.1 %collective-permute-done.3.buf_c = bf16[3088,128]{1,0:T(8,128)(2,1)S(1)} collective-permute-done((bf16[3088,128]{1,0:T(8,128)(2,1)S(1)}, bf16[3088,128]{1,0:T(8,128)(2,1)S(1)}, u32[]{:S(2)}, u32[]{:S(2)}) %collective-permute-start.3) | collective-permute-done | bytes 790560 | tf_op jit(solution)/shard_map/ppermute | solution.py:731
  23.2 0.0 collective-permute-start.4
  23.2 1.2 %collective-permute-done.1.recv = bf16[3072,128]{1,0:T(8,128)(2,1)S(1)} collective-permute-done((bf16[3072,128]{1,0:T(8,128)(2,1)S(1)}, bf16[3072,128]{1,0:T(8,128)(2,1)S(1)}, u32[]{:S(2)}, u32[]{:S(2)}) %collective-permute-start.1) | collective-permute-done | bytes 786464 | tf_op jit(solution)/shard_map/ppermute | solution.py:731
  24.4 0.7 shard_map.214
  25.1 2.5 %collective-permute-start.2 = (bf16[1536,128]{1,0:T(8,128)(2,1)S(1)}, bf16[1536,128]{1,0:T(8,128)(2,1)S(1)}, u32[]{:S(2)}, u32[]{:S(2)}) collective-permute-start(bf16[1536,128]{1,0:T(8,128)(2,1)S(1)} %get-tuple-element.76), channel_id=1, source_target_pairs={{0,4},{4,0},{8,12},{12,8},{16,20},{20,16},{24,28},{28,24},{1,5},{5... | collective-permute-start | bytes 1179656 | tf_op jit(solution)/shard_map/ppermute | solution.py:736
  27.5 0.0 collective-permute-done.4.buf_d
  27.5 11.9 %shard_map.215 = (f32[2304,512]{1,0:T(8,128)S(1)}, f32[2304,512]{1,0:T(8,128)S(1)}, bf16[2304,512]{1,0:T(8,128)(2,1)S(1)}) custom-call(s32[34]{0:T(128)S(1)} %get-tuple-element.72.meta, bf16[2304,512]{1,0:T(8,128)(2,1)S(1)} %get-tuple-element.77.ad, bf16[2304,512]{1,0:T(8,128)(2,1)S(1)} %get-tuple-element.78.low, ...), custom_call_target="tpu_custom_call" | custom-call | tf_op jit(solution)/shard_map/pallas_call | solution.py:419
  39.4 0.0 collective-permute-done.2
  39.4 0.1 collective-permute-start.8
  39.5 0.1 fusion
  39.7 3.2 %collective-permute-start.7 = (bf16[384,128]{1,0:T(8,128)(2,1)S(1)}, bf16[384,128]{1,0:T(8,128)(2,1)S(1)}, u32[]{:S(2)}, u32[]{:S(2)}) collective-permute-start(bf16[384,128]{1,0:T(8,128)(2,1)S(1)} %get-tuple-element.135), channel_id=1, source_target_pairs={{0,24},{4,28},{8,16},{12,20},{16,8},{20,12},{24,0},{28,4},{1,25},{... | collective-permute-start | bytes 294920 | tf_op jit(solution)/shard_map/ppermute | solution.py:736
  42.9 0.6 collective-permute-start.6
  43.5 0.6 collective-permute-start.5
  44.1 7.5 %shard_map.216 = (f32[8,4,288,128]{3,2,1,0:T(8,128)S(1)}, f32[16,512]{1,0:T(8,128)S(1)}, f32[16,512]{1,0:T(8,128)S(1)}) custom-call(s32[34]{0:T(128)S(1)} %get-tuple-element.72.meta, bf16[8,256,512]{2,1,0:T(8,128)(2,1)S(1)} %get-tuple-element.88.tok, bf16[8,256,512]{2,1,0:T(8,128)(2,1)S(1)} %get-tuple-element.89.cot, ...), custom_call_target="tpu_custom_call" | custom-call | bytes 40000000 | tf_op jit(solution)/shard_map/pallas_call | solution.py:539
  51.7 0.0 collective-permute-done.7.refs_2_
  51.7 1.4 %collective-permute-done.6.refs_1_ = bf16[384,128]{1,0:T(8,128)(2,1)S(1)} collective-permute-done((bf16[384,128]{1,0:T(8,128)(2,1)S(1)}, bf16[384,128]{1,0:T(8,128)(2,1)S(1)}, u32[]{:S(2)}, u32[]{:S(2)}) %collective-permute-start.6) | collective-permute-done | bytes 98336 | tf_op jit(solution)/shard_map/ppermute | solution.py:736
  53.0 0.0 collective-permute-done.5.refs_0_
  53.1 0.0 collective-permute-done.8.other
  53.1 0.1 collective-permute-start.9
  53.2 1.1 %collective-permute-done.9.recv = f32[16,512]{1,0:T(8,128)S(1)} collective-permute-done((f32[16,512]{1,0:T(8,128)S(1)}, f32[16,512]{1,0:T(8,128)S(1)}, u32[]{:S(2)}, u32[]{:S(2)}) %collective-permute-start.9) | collective-permute-done | bytes 32800 | tf_op jit(solution)/shard_map/ppermute | solution.py:731
  54.3 0.1 shard_map.217
  54.3 1.5 %collective-permute-start.14 = (bf16[448,128]{1,0:T(8,128)(2,1)S(1)}, bf16[448,128]{1,0:T(8,128)(2,1)S(1)}, u32[]{:S(2)}, u32[]{:S(2)}) collective-permute-start(bf16[448,128]{1,0:T(8,128)(2,1)S(1)} %get-tuple-element.114.refs_0_), channel_id=1, source_target_pairs={{0,12},{4,8},{8,4},{12,0},{16,28},{20,24},{24,20},{28,16},{1,13},{... | collective-permute-start | bytes 344072 | tf_op jit(solution)/shard_map/ppermute | solution.py:736
  55.8 3.4 %collective-permute-start.12 = (bf16[448,128]{1,0:T(8,128)(2,1)S(1)}, bf16[448,128]{1,0:T(8,128)(2,1)S(1)}, u32[]{:S(2)}, u32[]{:S(2)}) collective-permute-start(bf16[448,128]{1,0:T(8,128)(2,1)S(1)} %get-tuple-element.114.refs_0_), channel_id=1, source_target_pairs={{0,24},{4,28},{8,16},{12,20},{16,8},{20,12},{24,0},{28,4},{1,25},{... | collective-permute-start | bytes 344072 | tf_op jit(solution)/shard_map/ppermute | solution.py:736
  59.2 0.0 collective-permute-start.11
  59.2 1.0 %collective-permute-start.10 = (bf16[448,128]{1,0:T(8,128)(2,1)S(1)}, bf16[448,128]{1,0:T(8,128)(2,1)S(1)}, u32[]{:S(2)}, u32[]{:S(2)}) collective-permute-start(bf16[448,128]{1,0:T(8,128)(2,1)S(1)} %get-tuple-element.114.refs_0_), channel_id=1, source_target_pairs={{0,8},{4,12},{8,0},{12,4},{16,24},{20,28},{24,16},{28,20},{1,9},{5... | collective-permute-start | bytes 344072 | tf_op jit(solution)/shard_map/ppermute | solution.py:736
  60.2 0.2 collective-permute-start.13
  60.4 2.7 %shard_map.218 = bf16[16,256,512]{2,1,0:T(8,128)(2,1)} custom-call(s32[34]{0:T(128)S(1)} %get-tuple-element.72.meta, bf16[2304,512]{1,0:T(8,128)(2,1)S(1)} %get-tuple-element.98.own, bf16[2304,512]{1,0:T(8,128)(2,1)S(1)} %collective-permute-done.8.other), custom_call_target="tpu_custom_call" | custom-call | bytes 40000000 | tf_op jit(solution)/shard_map/pallas_call | solution.py:572
  63.1 4.5 %shard_map.219 = (f32[16,256,512]{2,1,0:T(8,128)}, bf16[8,256,512]{2,1,0:T(8,128)(2,1)S(1)}) custom-call(s32[34]{0:T(128)S(1)} %get-tuple-element.72.meta, bf16[8,256,512]{2,1,0:T(8,128)(2,1)S(1)} %get-tuple-element.89.cot, f32[8,4,288,128]{3,2,1,0:T(8,128)S(1)} %get-tuple-element.112.cgp, f32[16,512]{1,0:T(8,128)S(1)} %get-tuple-element.83.consts), custom_call_target="tpu_custom_call" | custom-call | bytes 40000000 | tf_op jit(solution)/shard_map/pallas_call | solution.py:624
  67.6 0.0 collective-permute-done.13.theirs
  67.6 0.0 collective-permute-done.14.far_1
  67.7 0.0 collective-permute-done.12.refs_3_
  67.7 1.7 %collective-permute-done.11.refs_2_ = bf16[448,128]{1,0:T(8,128)(2,1)S(1)} collective-permute-done((bf16[448,128]{1,0:T(8,128)(2,1)S(1)}, bf16[448,128]{1,0:T(8,128)(2,1)S(1)}, u32[]{:S(2)}, u32[]{:S(2)}) %collective-permute-start.11) | collective-permute-done | bytes 114720 | tf_op jit(solution)/shard_map/ppermute | solution.py:736
  69.4 0.0 collective-permute-done.10.refs_1_.near_1
  69.4 0.0 collective-permute-start.16
  69.4 0.4 collective-permute-start.15
  69.9 3.7 %collective-permute-done.16.other = bf16[8,256,512]{2,1,0:T(8,128)(2,1)S(1)} collective-permute-done((bf16[8,256,512]{2,1,0:T(8,128)(2,1)S(1)}, bf16[8,256,512]{2,1,0:T(8,128)(2,1)S(1)}, u32[]{:S(2)}, u32[]{:S(2)}) %collective-permute-start.16) | collective-permute-done | bytes 2097184 | tf_op jit(solution)/shard_map/ppermute | solution.py:731
  73.6 2.6 %shard_map.221 = f32[16,256,512]{2,1,0:T(8,128)} custom-call(s32[34]{0:T(128)S(1)} %get-tuple-element.72.meta, bf16[8,256,512]{2,1,0:T(8,128)(2,1)S(1)} %collective-permute-done.16.other, f32[16,256,512]{2,1,0:T(8,128)} %get-tuple-element.119.gtok_in), custom_call_target="tpu_custom_call", output_to_operand_aliasing={{}: (2, {})} | custom-call | bytes 20000000 | tf_op jit(solution)/shard_map/pallas_call | solution.py:644
  76.2 1.0 %collective-permute-done.15.far = bf16[832,128]{1,0:T(8,128)(2,1)S(1)} collective-permute-done((bf16[832,128]{1,0:T(8,128)(2,1)S(1)}, bf16[832,128]{1,0:T(8,128)(2,1)S(1)}, u32[]{:S(2)}, u32[]{:S(2)}) %collective-permute-start.15) | collective-permute-done | bytes 213024 | tf_op jit(solution)/shard_map/ppermute | solution.py:736
  77.2 1.9 %shard_map.222 = (f32[7,512]{1,0:T(8,128)}, f32[512]{0:T(512)}, f32[2,512]{1,0:T(2,128)}, f32[2,512]{1,0:T(2,128)}, f32[512,384]{1,0:T(8,128)}, /*index=5*/f32[3...) custom-call(s32[34]{0:T(128)S(1)} %get-tuple-element.72.meta, bf16[384,128]{1,0:T(8,128)(2,1)S(1)} %get-tuple-element.111.mine, ...), custom_call_target="tpu_custom_call" | custom-call | tf_op jit(solution)/shard_map/pallas_call | solution.py:722
  (2 shorter events, 0.0 us)
Async XLA Ops:
  1.9 3.1 %collective-permute-start = (bf16[3088,128]{1,0:T(8,128)(2,1)S(1)}, bf16[3088,128]{1,0:T(8,128)(2,1)S(1)}, u32[]{:S(2)}, u32[]{:S(2)}) collective-permute-start(bf16[3088,128]{1,0:T(8,128)(2,1)S(1)} %shard_map.212.buf_a), channel_id=1, source_target_pairs={{0,1},{1,0},{2,3},{3,2},{4,5},{5,4},{6,7},{7,6},{8,9},{9,8},{10,11... | collective-permute-start | bytes 2371592 | tf_op jit(solution)/shard_map/ppermute | solution.py:731
  2.4 20.8 %collective-permute-start.3 = (bf16[3088,128]{1,0:T(8,128)(2,1)S(1)}, bf16[3088,128]{1,0:T(8,128)(2,1)S(1)}, u32[]{:S(2)}, u32[]{:S(2)}) collective-permute-start(bf16[3088,128]{1,0:T(8,128)(2,1)S(1)} %shard_map.212.buf_a), channel_id=1, source_target_pairs={{0,2},{1,3},{2,0},{3,1},{4,6},{5,7},{6,4},{7,5},{8,10},{9,11},{10,... | collective-permute-start | bytes 2371592 | tf_op jit(solution)/shard_map/ppermute | solution.py:731
  22.0 2.4 %collective-permute-start.1 = (bf16[3072,128]{1,0:T(8,128)(2,1)S(1)}, bf16[3072,128]{1,0:T(8,128)(2,1)S(1)}, u32[]{:S(2)}, u32[]{:S(2)}) collective-permute-start(bf16[3072,128]{1,0:T(8,128)(2,1)S(1)} %get-tuple-element.74), channel_id=1, source_target_pairs={{0,1},{1,0},{2,3},{3,2},{4,5},{5,4},{6,7},{7,6},{8,9},{9,8},{10,11... | collective-permute-start | bytes 2359304 | tf_op jit(solution)/shard_map/ppermute | solution.py:731
  23.2 4.3 %collective-permute-start.4 = (bf16[3088,128]{1,0:T(8,128)(2,1)S(1)}, bf16[3088,128]{1,0:T(8,128)(2,1)S(1)}, u32[]{:S(2)}, u32[]{:S(2)}) collective-permute-start(bf16[3088,128]{1,0:T(8,128)(2,1)S(1)} %collective-permute-done.3.buf_c), channel_id=1, source_target_pairs={{0,1},{1,0},{2,3},{3,2},{4,5},{5,4},{6,7},{7,6},{8,9},{9,8},{10,11... | collective-permute-start | bytes 2371592 | tf_op jit(solution)/shard_map/ppermute | solution.py:731
  25.1 14.4 %collective-permute-start.2 = (bf16[1536,128]{1,0:T(8,128)(2,1)S(1)}, bf16[1536,128]{1,0:T(8,128)(2,1)S(1)}, u32[]{:S(2)}, u32[]{:S(2)}) collective-permute-start(bf16[1536,128]{1,0:T(8,128)(2,1)S(1)} %get-tuple-element.76), channel_id=1, source_target_pairs={{0,4},{4,0},{8,12},{12,8},{16,20},{20,16},{24,28},{28,24},{1,5},{5... | collective-permute-start | bytes 1179656 | tf_op jit(solution)/shard_map/ppermute | solution.py:736
  39.4 13.6 %collective-permute-start.8 = (bf16[2304,512]{1,0:T(8,128)(2,1)S(1)}, bf16[2304,512]{1,0:T(8,128)(2,1)S(1)}, u32[]{:S(2)}, u32[]{:S(2)}) collective-permute-start(bf16[2304,512]{1,0:T(8,128)(2,1)S(1)} %get-tuple-element.98.own), channel_id=1, source_target_pairs={{0,1},{1,0},{2,3},{3,2},{4,5},{5,4},{6,7},{7,6},{8,9},{9,8},{10,11... | collective-permute-start | bytes 7077896 | tf_op jit(solution)/shard_map/ppermute | solution.py:731
  39.7 12.0 %collective-permute-start.7 = (bf16[384,128]{1,0:T(8,128)(2,1)S(1)}, bf16[384,128]{1,0:T(8,128)(2,1)S(1)}, u32[]{:S(2)}, u32[]{:S(2)}) collective-permute-start(bf16[384,128]{1,0:T(8,128)(2,1)S(1)} %get-tuple-element.135), channel_id=1, source_target_pairs={{0,24},{4,28},{8,16},{12,20},{16,8},{20,12},{24,0},{28,4},{1,25},{... | collective-permute-start | bytes 294920 | tf_op jit(solution)/shard_map/ppermute | solution.py:736
  42.9 10.2 %collective-permute-start.6 = (bf16[384,128]{1,0:T(8,128)(2,1)S(1)}, bf16[384,128]{1,0:T(8,128)(2,1)S(1)}, u32[]{:S(2)}, u32[]{:S(2)}) collective-permute-start(bf16[384,128]{1,0:T(8,128)(2,1)S(1)} %get-tuple-element.136), channel_id=1, source_target_pairs={{0,16},{4,20},{8,24},{12,28},{16,0},{20,4},{24,8},{28,12},{1,17},{... | collective-permute-start | bytes 294920 | tf_op jit(solution)/shard_map/ppermute | solution.py:736
  43.5 9.5 %collective-permute-start.5 = (bf16[384,128]{1,0:T(8,128)(2,1)S(1)}, bf16[384,128]{1,0:T(8,128)(2,1)S(1)}, u32[]{:S(2)}, u32[]{:S(2)}) collective-permute-start(bf16[384,128]{1,0:T(8,128)(2,1)S(1)} %get-tuple-element.137), channel_id=1, source_target_pairs={{0,8},{4,12},{8,0},{12,4},{16,24},{20,28},{24,16},{28,20},{1,9},{5... | collective-permute-start | bytes 294920 | tf_op jit(solution)/shard_map/ppermute | solution.py:736
  53.1 1.2 %collective-permute-start.9 = (f32[16,512]{1,0:T(8,128)S(1)}, f32[16,512]{1,0:T(8,128)S(1)}, u32[]{:S(2)}, u32[]{:S(2)}) collective-permute-start(f32[16,512]{1,0:T(8,128)S(1)} %get-tuple-element.101), channel_id=1, source_target_pairs={{0,1},{1,0},{2,3},{3,2},{4,5},{5,4},{6,7},{7,6},{8,9},{9,8},{10,11... | collective-permute-start | bytes 98312 | tf_op jit(solution)/shard_map/ppermute | solution.py:731
  54.3 13.3 %collective-permute-start.14 = (bf16[448,128]{1,0:T(8,128)(2,1)S(1)}, bf16[448,128]{1,0:T(8,128)(2,1)S(1)}, u32[]{:S(2)}, u32[]{:S(2)}) collective-permute-start(bf16[448,128]{1,0:T(8,128)(2,1)S(1)} %get-tuple-element.114.refs_0_), channel_id=1, source_target_pairs={{0,12},{4,8},{8,4},{12,0},{16,28},{20,24},{24,20},{28,16},{1,13},{... | collective-permute-start | bytes 344072 | tf_op jit(solution)/shard_map/ppermute | solution.py:736
  55.8 11.9 %collective-permute-start.12 = (bf16[448,128]{1,0:T(8,128)(2,1)S(1)}, bf16[448,128]{1,0:T(8,128)(2,1)S(1)}, u32[]{:S(2)}, u32[]{:S(2)}) collective-permute-start(bf16[448,128]{1,0:T(8,128)(2,1)S(1)} %get-tuple-element.114.refs_0_), channel_id=1, source_target_pairs={{0,24},{4,28},{8,16},{12,20},{16,8},{20,12},{24,0},{28,4},{1,25},{... | collective-permute-start | bytes 344072 | tf_op jit(solution)/shard_map/ppermute | solution.py:736
  59.2 10.2 %collective-permute-start.11 = (bf16[448,128]{1,0:T(8,128)(2,1)S(1)}, bf16[448,128]{1,0:T(8,128)(2,1)S(1)}, u32[]{:S(2)}, u32[]{:S(2)}) collective-permute-start(bf16[448,128]{1,0:T(8,128)(2,1)S(1)} %get-tuple-element.114.refs_0_), channel_id=1, source_target_pairs={{0,16},{4,20},{8,24},{12,28},{16,0},{20,4},{24,8},{28,12},{1,17},{... | collective-permute-start | bytes 344072 | tf_op jit(solution)/shard_map/ppermute | solution.py:736
  59.2 10.2 %collective-permute-start.10 = (bf16[448,128]{1,0:T(8,128)(2,1)S(1)}, bf16[448,128]{1,0:T(8,128)(2,1)S(1)}, u32[]{:S(2)}, u32[]{:S(2)}) collective-permute-start(bf16[448,128]{1,0:T(8,128)(2,1)S(1)} %get-tuple-element.114.refs_0_), channel_id=1, source_target_pairs={{0,8},{4,12},{8,0},{12,4},{16,24},{20,28},{24,16},{28,20},{1,9},{5... | collective-permute-start | bytes 344072 | tf_op jit(solution)/shard_map/ppermute | solution.py:736
  60.2 7.4 %collective-permute-start.13 = (bf16[384,128]{1,0:T(8,128)(2,1)S(1)}, bf16[384,128]{1,0:T(8,128)(2,1)S(1)}, u32[]{:S(2)}, u32[]{:S(2)}) collective-permute-start(bf16[384,128]{1,0:T(8,128)(2,1)S(1)} %get-tuple-element.111.mine), channel_id=1, source_target_pairs={{0,4},{4,0},{8,12},{12,8},{16,20},{20,16},{24,28},{28,24},{1,5},{5... | collective-permute-start | bytes 294920 | tf_op jit(solution)/shard_map/ppermute | solution.py:736
  69.4 4.2 %collective-permute-start.16 = (bf16[8,256,512]{2,1,0:T(8,128)(2,1)S(1)}, bf16[8,256,512]{2,1,0:T(8,128)(2,1)S(1)}, u32[]{:S(2)}, u32[]{:S(2)}) collective-permute-start(bf16[8,256,512]{2,1,0:T(8,128)(2,1)S(1)} %get-tuple-element.118), channel_id=1, source_target_pairs={{0,1},{1,0},{2,3},{3,2},{4,5},{5,4},{6,7},{7,6},{8,9},{9,8},{10,11... | collective-permute-start | bytes 6291464 | tf_op jit(solution)/shard_map/ppermute | solution.py:731
  69.4 7.7 %collective-permute-start.15 = (bf16[832,128]{1,0:T(8,128)(2,1)S(1)}, bf16[832,128]{1,0:T(8,128)(2,1)S(1)}, u32[]{:S(2)}, u32[]{:S(2)}) collective-permute-start(bf16[832,128]{1,0:T(8,128)(2,1)S(1)} %shard_map.220.near), channel_id=1, source_target_pairs={{0,4},{4,0},{8,12},{12,8},{16,20},{20,16},{24,28},{28,24},{1,5},{5... | collective-permute-start | bytes 638984 | tf_op jit(solution)/shard_map/ppermute | solution.py:736

commit v11 on v10

--- a/solution.py
+++ b/solution.py
@@ -202,7 +202,7 @@
 
     def fetch_packed(j):
         dst = pl.ds(pl.multiple_of(offs[j], 16), frames)
-        return pltpu.make_async_copy(tok_hbm.at[(lax.axis_index("tp") & 1) * n + j], tokp.at[dst, :], packed_sem)
+        return pltpu.make_async_copy(tok.at[j], tokp.at[dst, :], packed_sem)
 
     @pl.when(s > 1)
     def _():
@@ -404,12 +404,19 @@
     spread_bias(bias, bias_row)
     rest(first, branch[first, :], ag[first, :])
 
-    def tile(t, _):
-        at = pl.ds(pl.multiple_of(t * TILE, TILE), TILE)
+    def pair(t, _):
+        at = pl.ds(pl.multiple_of((2 * t + 1) * TILE, TILE), 2 * TILE)
         rest(at, *own(at))
         return 0
 
-    lax.fori_loop(1, offs[n + 1], tile, 0)
+    left = offs[n + 1] - 1
+    pairs = lax.shift_right_arithmetic(left, 1)
+    lax.fori_loop(0, pairs, pair, 0)
+
+    @pl.when(left > 2 * pairs)
+    def _():
+        at = pl.ds(pl.multiple_of(left * TILE, TILE), TILE)
+        rest(at, *own(at))
 
 
 def mix(meta, ad, low, act, pre, win, wout, consts, tokp, buf_c, buf_d, n, taps):

time: 78.2 us -> 76.6 us (0.980); the launches traced: 79.1 us -> 76.7 us
  waiting for transfers between devices: 11.2 us -> 7.79 us
  starting transfers between devices: 16.7 us -> 18.7 us
  Pallas kernels: 50.3 us -> 49.3 us
    ppermute x10, waiting for transfers between devices: 4.07 us -> 1.93 us  [across(): return lax.ppermute(x, 'dp', [(i, i ^ step) for i in range(size)])]
    ppermute x10, starting transfers between devices: 13.4 us -> 15.2 us  [across(): return lax.ppermute(x, 'dp', [(i, i ^ step) for i in range(size)])]
    ppermute x7, waiting for transfers between devices: 7.08 us -> 5.85 us  [swap(): return lax.ppermute(x, 'tp', [(i, i ^ step) for i in range(size)])]
    pallas_call x1, Pallas kernels: 11.9 us -> 11 us  [mix(): pl.pallas_call(functools.partial(mix_kernel, n, taps), in_specs=[smem()]...]
  transfers between devices with their start and end apart: 17 -> 17, of which waited for: 7 -> 7; matrix products, arithmetic and copies ran while one was open for 0% -> 0% of each run, Pallas kernels for 59% -> 60%
where the time goes in v11:
time: 76.6 us; the launch traced here: 76.7 us
  Pallas kernels  49.3 us (64%)
  starting transfers between devices  18.7 us (24%)
  waiting for transfers between devices  7.79 us (10%)
  between operations  0.78 us (1%)
    pallas_call x1, Pallas kernels, front(): pl.pallas_call(functools.partial(front_kernel, n), grid_spec=pl.GridSpec(...  17 us
    ppermute x10, starting transfers between devices, across(): return lax.ppermute(x, 'dp', [(i, i ^ step) for i in range(size)])  15.2 us
    pallas_call x1, Pallas kernels, mix(): pl.pallas_call(functools.partial(mix_kernel, n, taps), in_specs=[smem()]...  11 us
    pallas_call x1, Pallas kernels, norm_grad(): pl.pallas_call(functools.partial(norm_grad_kernel, n, taps, rates), grid=...  7.54 us
    ppermute x7, waiting for transfers between devices, swap(): return lax.ppermute(x, 'tp', [(i, i ^ step) for i in range(size)])  5.85 us
    pallas_call x1, Pallas kernels, token_grad(): pl.pallas_call(functools.partial(token_grad_kernel, n, taps), grid=(n,),...  4.51 us
    ppermute x7, starting transfers between devices, swap(): return lax.ppermute(x, 'tp', [(i, i ^ step) for i in range(size)])  3.46 us
    pallas_call x1, Pallas kernels, place_out(): pl.pallas_call(functools.partial(place_out_kernel, n), in_specs=[smem(),...  2.73 us
  transfers between devices with their start and end apart: 17, of which 7 were waited for; matrix products, arithmetic and copies ran while one was open for 0% of the time, Pallas kernels for 60%

profile of v11, /device:TPU:0, one launch (start us, length us, event | category | flops | bytes accessed | tf_op | source)
XLA Modules:
  0.0 76.7 jit_solution(13853352469229971024)
XLA Ops:
  0.6 1.3 %shard_map.212.buf_a = bf16[3088,128]{1,0:T(8,128)(2,1)S(1)} custom-call(bf16[512,384]{1,0:T(8,128)(2,1)} %wi.1, bf16[384]{0:T(512)(128)(2,1)} %bi.1, bf16[384,512]{1,0:T(8,128)(2,1)} %wo.1), custom_call_target="tpu_custom_call" | custom-call | tf_op jit(solution)/shard_map/pallas_call | solution.py:110
  1.9 0.5 collective-permute-start
  2.4 2.6 %collective-permute-start.3 = (bf16[3088,128]{1,0:T(8,128)(2,1)S(1)}, bf16[3088,128]{1,0:T(8,128)(2,1)S(1)}, u32[]{:S(2)}, u32[]{:S(2)}) collective-permute-start(bf16[3088,128]{1,0:T(8,128)(2,1)S(1)} %shard_map.212.buf_a), channel_id=1, source_target_pairs={{0,2},{1,3},{2,0},{3,1},{4,6},{5,7},{6,4},{7,5},{8,10},{9,11},{10,... | collective-permute-start | bytes 2371592 | tf_op jit(solution)/shard_map/ppermute | solution.py:738
  5.0 0.0 collective-permute-done.buf_b
  5.0 17.0 %shard_map.213 = (bf16[2304,512]{1,0:T(8,128)(2,1)S(1)}, bf16[2304,512]{1,0:T(8,128)(2,1)S(1)}, bf16[2304,512]{1,0:T(8,128)(2,1)S(1)}, f32[2304,128]{1,0:T(8,128...) custom-call(s32[16]{0:T(128)} %counts_hbm.1, ...), custom_call_target="tpu_custom_call" | custom-call | tf_op jit(solution)/shard_map/pallas_call | solution.py:341
  22.0 0.2 collective-permute-start.1
  22.2 1.0 %collective-permute-done.3.buf_c = bf16[3088,128]{1,0:T(8,128)(2,1)S(1)} collective-permute-done((bf16[3088,128]{1,0:T(8,128)(2,1)S(1)}, bf16[3088,128]{1,0:T(8,128)(2,1)S(1)}, u32[]{:S(2)}, u32[]{:S(2)}) %collective-permute-start.3) | collective-permute-done | bytes 790560 | tf_op jit(solution)/shard_map/ppermute | solution.py:738
  23.2 0.0 collective-permute-start.4
  23.2 1.1 %collective-permute-done.1.recv = bf16[3072,128]{1,0:T(8,128)(2,1)S(1)} collective-permute-done((bf16[3072,128]{1,0:T(8,128)(2,1)S(1)}, bf16[3072,128]{1,0:T(8,128)(2,1)S(1)}, u32[]{:S(2)}, u32[]{:S(2)}) %collective-permute-start.1) | collective-permute-done | bytes 786464 | tf_op jit(solution)/shard_map/ppermute | solution.py:738
  24.4 0.7 shard_map.214
  25.0 2.1 %collective-permute-start.2 = (bf16[1536,128]{1,0:T(8,128)(2,1)S(1)}, bf16[1536,128]{1,0:T(8,128)(2,1)S(1)}, u32[]{:S(2)}, u32[]{:S(2)}) collective-permute-start(bf16[1536,128]{1,0:T(8,128)(2,1)S(1)} %get-tuple-element.76), channel_id=1, source_target_pairs={{0,4},{4,0},{8,12},{12,8},{16,20},{20,16},{24,28},{28,24},{1,5},{5... | collective-permute-start | bytes 1179656 | tf_op jit(solution)/shard_map/ppermute | solution.py:743
  27.1 0.0 collective-permute-done.4.buf_d
  27.1 11.0 %shard_map.215 = (f32[2304,512]{1,0:T(8,128)S(1)}, f32[2304,512]{1,0:T(8,128)S(1)}, bf16[2304,512]{1,0:T(8,128)(2,1)S(1)}) custom-call(s32[34]{0:T(128)S(1)} %get-tuple-element.72.meta, bf16[2304,512]{1,0:T(8,128)(2,1)S(1)} %get-tuple-element.77.ad, bf16[2304,512]{1,0:T(8,128)(2,1)S(1)} %get-tuple-element.78.low, ...), custom_call_target="tpu_custom_call" | custom-call | tf_op jit(solution)/shard_map/pallas_call | solution.py:426
  38.1 0.0 collective-permute-done.2
  38.1 0.1 collective-permute-start.8
  38.3 0.1 fusion
  38.4 4.0 %collective-permute-start.7 = (bf16[384,128]{1,0:T(8,128)(2,1)S(1)}, bf16[384,128]{1,0:T(8,128)(2,1)S(1)}, u32[]{:S(2)}, u32[]{:S(2)}) collective-permute-start(bf16[384,128]{1,0:T(8,128)(2,1)S(1)} %get-tuple-element.135), channel_id=1, source_target_pairs={{0,24},{4,28},{8,16},{12,20},{16,8},{20,12},{24,0},{28,4},{1,25},{... | collective-permute-start | bytes 294920 | tf_op jit(solution)/shard_map/ppermute | solution.py:743
  42.4 0.0 collective-permute-start.6
  42.4 0.6 collective-permute-start.5
  43.1 7.5 %shard_map.216 = (f32[8,4,288,128]{3,2,1,0:T(8,128)S(1)}, f32[16,512]{1,0:T(8,128)S(1)}, f32[16,512]{1,0:T(8,128)S(1)}) custom-call(s32[34]{0:T(128)S(1)} %get-tuple-element.72.meta, bf16[8,256,512]{2,1,0:T(8,128)(2,1)S(1)} %get-tuple-element.88.tok, bf16[8,256,512]{2,1,0:T(8,128)(2,1)S(1)} %get-tuple-element.89.cot, ...), custom_call_target="tpu_custom_call" | custom-call | bytes 40000000 | tf_op jit(solution)/shard_map/pallas_call | solution.py:546
  50.6 0.0 collective-permute-done.7.refs_2_
  50.6 0.7 collective-permute-done.6.refs_1_
  51.3 0.0 collective-permute-done.5.refs_0_
  51.3 0.0 collective-permute-done.8.other
  51.3 0.0 collective-permute-start.9
  51.3 1.2 %collective-permute-done.9.recv = f32[16,512]{1,0:T(8,128)S(1)} collective-permute-done((f32[16,512]{1,0:T(8,128)S(1)}, f32[16,512]{1,0:T(8,128)S(1)}, u32[]{:S(2)}, u32[]{:S(2)}) %collective-permute-start.9) | collective-permute-done | bytes 32800 | tf_op jit(solution)/shard_map/ppermute | solution.py:738
  52.5 0.1 shard_map.217
  52.6 1.1 %collective-permute-start.14 = (bf16[448,128]{1,0:T(8,128)(2,1)S(1)}, bf16[448,128]{1,0:T(8,128)(2,1)S(1)}, u32[]{:S(2)}, u32[]{:S(2)}) collective-permute-start(bf16[448,128]{1,0:T(8,128)(2,1)S(1)} %get-tuple-element.114.refs_0_), channel_id=1, source_target_pairs={{0,12},{4,8},{8,4},{12,0},{16,28},{20,24},{24,20},{28,16},{1,13},{... | collective-permute-start | bytes 344072 | tf_op jit(solution)/shard_map/ppermute | solution.py:743
  53.7 2.5 %collective-permute-start.12 = (bf16[448,128]{1,0:T(8,128)(2,1)S(1)}, bf16[448,128]{1,0:T(8,128)(2,1)S(1)}, u32[]{:S(2)}, u32[]{:S(2)}) collective-permute-start(bf16[448,128]{1,0:T(8,128)(2,1)S(1)} %get-tuple-element.114.refs_0_), channel_id=1, source_target_pairs={{0,24},{4,28},{8,16},{12,20},{16,8},{20,12},{24,0},{28,4},{1,25},{... | collective-permute-start | bytes 344072 | tf_op jit(solution)/shard_map/ppermute | solution.py:743
  56.2 0.2 collective-permute-start.11
  56.4 1.6 %collective-permute-start.10 = (bf16[448,128]{1,0:T(8,128)(2,1)S(1)}, bf16[448,128]{1,0:T(8,128)(2,1)S(1)}, u32[]{:S(2)}, u32[]{:S(2)}) collective-permute-start(bf16[448,128]{1,0:T(8,128)(2,1)S(1)} %get-tuple-element.114.refs_0_), channel_id=1, source_target_pairs={{0,8},{4,12},{8,0},{12,4},{16,24},{20,28},{24,16},{28,20},{1,9},{5... | collective-permute-start | bytes 344072 | tf_op jit(solution)/shard_map/ppermute | solution.py:743
  58.1 1.4 %collective-permute-start.13 = (bf16[384,128]{1,0:T(8,128)(2,1)S(1)}, bf16[384,128]{1,0:T(8,128)(2,1)S(1)}, u32[]{:S(2)}, u32[]{:S(2)}) collective-permute-start(bf16[384,128]{1,0:T(8,128)(2,1)S(1)} %get-tuple-element.111.mine), channel_id=1, source_target_pairs={{0,4},{4,0},{8,12},{12,8},{16,20},{20,16},{24,28},{28,24},{1,5},{5... | collective-permute-start | bytes 294920 | tf_op jit(solution)/shard_map/ppermute | solution.py:743
  59.5 2.7 %shard_map.218 = bf16[16,256,512]{2,1,0:T(8,128)(2,1)} custom-call(s32[34]{0:T(128)S(1)} %get-tuple-element.72.meta, bf16[2304,512]{1,0:T(8,128)(2,1)S(1)} %get-tuple-element.98.own, bf16[2304,512]{1,0:T(8,128)(2,1)S(1)} %collective-permute-done.8.other), custom_call_target="tpu_custom_call" | custom-call | bytes 40000000 | tf_op jit(solution)/shard_map/pallas_call | solution.py:579
  62.2 4.5 %shard_map.219 = (f32[16,256,512]{2,1,0:T(8,128)}, bf16[8,256,512]{2,1,0:T(8,128)(2,1)S(1)}) custom-call(s32[34]{0:T(128)S(1)} %get-tuple-element.72.meta, bf16[8,256,512]{2,1,0:T(8,128)(2,1)S(1)} %get-tuple-element.89.cot, f32[8,4,288,128]{3,2,1,0:T(8,128)S(1)} %get-tuple-element.112.cgp, f32[16,512]{1,0:T(8,128)S(1)} %get-tuple-element.83.consts), custom_call_target="tpu_custom_call" | custom-call | bytes 40000000 | tf_op jit(solution)/shard_map/pallas_call | solution.py:631
  66.7 0.0 collective-permute-done.13.theirs
  66.7 0.0 collective-permute-done.14.far_1
  66.7 0.0 collective-permute-done.12.refs_3_
  66.7 0.3 collective-permute-done.11.refs_2_
  67.0 0.0 collective-permute-done.10.refs_1_.near_1
  67.0 0.0 collective-permute-start.16
  67.0 1.6 %collective-permute-start.15 = (bf16[832,128]{1,0:T(8,128)(2,1)S(1)}, bf16[832,128]{1,0:T(8,128)(2,1)S(1)}, u32[]{:S(2)}, u32[]{:S(2)}) collective-permute-start(bf16[832,128]{1,0:T(8,128)(2,1)S(1)} %shard_map.220.near), channel_id=1, source_target_pairs={{0,4},{4,0},{8,12},{12,8},{16,20},{20,16},{24,28},{28,24},{1,5},{5... | collective-permute-start | bytes 638984 | tf_op jit(solution)/shard_map/ppermute | solution.py:743
  68.6 2.5 %collective-permute-done.16.other = bf16[8,256,512]{2,1,0:T(8,128)(2,1)S(1)} collective-permute-done((bf16[8,256,512]{2,1,0:T(8,128)(2,1)S(1)}, bf16[8,256,512]{2,1,0:T(8,128)(2,1)S(1)}, u32[]{:S(2)}, u32[]{:S(2)}) %collective-permute-start.16) | collective-permute-done | bytes 2097184 | tf_op jit(solution)/shard_map/ppermute | solution.py:738
  71.2 2.6 %shard_map.221 = f32[16,256,512]{2,1,0:T(8,128)} custom-call(s32[34]{0:T(128)S(1)} %get-tuple-element.72.meta, bf16[8,256,512]{2,1,0:T(8,128)(2,1)S(1)} %collective-permute-done.16.other, f32[16,256,512]{2,1,0:T(8,128)} %get-tuple-element.119.gtok_in), custom_call_target="tpu_custom_call", output_to_operand_aliasing={{}: (2, {})} | custom-call | bytes 20000000 | tf_op jit(solution)/shard_map/pallas_call | solution.py:651
  73.8 1.0 %collective-permute-done.15.far = bf16[832,128]{1,0:T(8,128)(2,1)S(1)} collective-permute-done((bf16[832,128]{1,0:T(8,128)(2,1)S(1)}, bf16[832,128]{1,0:T(8,128)(2,1)S(1)}, u32[]{:S(2)}, u32[]{:S(2)}) %collective-permute-start.15) | collective-permute-done | bytes 213024 | tf_op jit(solution)/shard_map/ppermute | solution.py:743
  74.8 1.9 %shard_map.222 = (f32[7,512]{1,0:T(8,128)}, f32[512]{0:T(512)}, f32[2,512]{1,0:T(2,128)}, f32[2,512]{1,0:T(2,128)}, f32[512,384]{1,0:T(8,128)}, /*index=5*/f32[3...) custom-call(s32[34]{0:T(128)S(1)} %get-tuple-element.72.meta, bf16[384,128]{1,0:T(8,128)(2,1)S(1)} %get-tuple-element.111.mine, ...), custom_call_target="tpu_custom_call" | custom-call | tf_op jit(solution)/shard_map/pallas_call | solution.py:729
  (2 shorter events, 0.0 us)
Async XLA Ops:
  1.9 3.1 %collective-permute-start = (bf16[3088,128]{1,0:T(8,128)(2,1)S(1)}, bf16[3088,128]{1,0:T(8,128)(2,1)S(1)}, u32[]{:S(2)}, u32[]{:S(2)}) collective-permute-start(bf16[3088,128]{1,0:T(8,128)(2,1)S(1)} %shard_map.212.buf_a), channel_id=1, source_target_pairs={{0,1},{1,0},{2,3},{3,2},{4,5},{5,4},{6,7},{7,6},{8,9},{9,8},{10,11... | collective-permute-start | bytes 2371592 | tf_op jit(solution)/shard_map/ppermute | solution.py:738
  2.4 20.8 %collective-permute-start.3 = (bf16[3088,128]{1,0:T(8,128)(2,1)S(1)}, bf16[3088,128]{1,0:T(8,128)(2,1)S(1)}, u32[]{:S(2)}, u32[]{:S(2)}) collective-permute-start(bf16[3088,128]{1,0:T(8,128)(2,1)S(1)} %shard_map.212.buf_a), channel_id=1, source_target_pairs={{0,2},{1,3},{2,0},{3,1},{4,6},{5,7},{6,4},{7,5},{8,10},{9,11},{10,... | collective-permute-start | bytes 2371592 | tf_op jit(solution)/shard_map/ppermute | solution.py:738
  22.0 2.4 %collective-permute-start.1 = (bf16[3072,128]{1,0:T(8,128)(2,1)S(1)}, bf16[3072,128]{1,0:T(8,128)(2,1)S(1)}, u32[]{:S(2)}, u32[]{:S(2)}) collective-permute-start(bf16[3072,128]{1,0:T(8,128)(2,1)S(1)} %get-tuple-element.74), channel_id=1, source_target_pairs={{0,1},{1,0},{2,3},{3,2},{4,5},{5,4},{6,7},{7,6},{8,9},{9,8},{10,11... | collective-permute-start | bytes 2359304 | tf_op jit(solution)/shard_map/ppermute | solution.py:738
  23.2 3.9 %collective-permute-start.4 = (bf16[3088,128]{1,0:T(8,128)(2,1)S(1)}, bf16[3088,128]{1,0:T(8,128)(2,1)S(1)}, u32[]{:S(2)}, u32[]{:S(2)}) collective-permute-start(bf16[3088,128]{1,0:T(8,128)(2,1)S(1)} %collective-permute-done.3.buf_c), channel_id=1, source_target_pairs={{0,1},{1,0},{2,3},{3,2},{4,5},{5,4},{6,7},{7,6},{8,9},{9,8},{10,11... | collective-permute-start | bytes 2371592 | tf_op jit(solution)/shard_map/ppermute | solution.py:738
  25.0 13.1 %collective-permute-start.2 = (bf16[1536,128]{1,0:T(8,128)(2,1)S(1)}, bf16[1536,128]{1,0:T(8,128)(2,1)S(1)}, u32[]{:S(2)}, u32[]{:S(2)}) collective-permute-start(bf16[1536,128]{1,0:T(8,128)(2,1)S(1)} %get-tuple-element.76), channel_id=1, source_target_pairs={{0,4},{4,0},{8,12},{12,8},{16,20},{20,16},{24,28},{28,24},{1,5},{5... | collective-permute-start | bytes 1179656 | tf_op jit(solution)/shard_map/ppermute | solution.py:743
  38.1 13.2 %collective-permute-start.8 = (bf16[2304,512]{1,0:T(8,128)(2,1)S(1)}, bf16[2304,512]{1,0:T(8,128)(2,1)S(1)}, u32[]{:S(2)}, u32[]{:S(2)}) collective-permute-start(bf16[2304,512]{1,0:T(8,128)(2,1)S(1)} %get-tuple-element.98.own), channel_id=1, source_target_pairs={{0,1},{1,0},{2,3},{3,2},{4,5},{5,4},{6,7},{7,6},{8,9},{9,8},{10,11... | collective-permute-start | bytes 7077896 | tf_op jit(solution)/shard_map/ppermute | solution.py:738
  38.4 12.2 %collective-permute-start.7 = (bf16[384,128]{1,0:T(8,128)(2,1)S(1)}, bf16[384,128]{1,0:T(8,128)(2,1)S(1)}, u32[]{:S(2)}, u32[]{:S(2)}) collective-permute-start(bf16[384,128]{1,0:T(8,128)(2,1)S(1)} %get-tuple-element.135), channel_id=1, source_target_pairs={{0,24},{4,28},{8,16},{12,20},{16,8},{20,12},{24,0},{28,4},{1,25},{... | collective-permute-start | bytes 294920 | tf_op jit(solution)/shard_map/ppermute | solution.py:743
  42.4 8.9 %collective-permute-start.6 = (bf16[384,128]{1,0:T(8,128)(2,1)S(1)}, bf16[384,128]{1,0:T(8,128)(2,1)S(1)}, u32[]{:S(2)}, u32[]{:S(2)}) collective-permute-start(bf16[384,128]{1,0:T(8,128)(2,1)S(1)} %get-tuple-element.136), channel_id=1, source_target_pairs={{0,16},{4,20},{8,24},{12,28},{16,0},{20,4},{24,8},{28,12},{1,17},{... | collective-permute-start | bytes 294920 | tf_op jit(solution)/shard_map/ppermute | solution.py:743
  42.4 8.9 %collective-permute-start.5 = (bf16[384,128]{1,0:T(8,128)(2,1)S(1)}, bf16[384,128]{1,0:T(8,128)(2,1)S(1)}, u32[]{:S(2)}, u32[]{:S(2)}) collective-permute-start(bf16[384,128]{1,0:T(8,128)(2,1)S(1)} %get-tuple-element.137), channel_id=1, source_target_pairs={{0,8},{4,12},{8,0},{12,4},{16,24},{20,28},{24,16},{28,20},{1,9},{5... | collective-permute-start | bytes 294920 | tf_op jit(solution)/shard_map/ppermute | solution.py:743
  51.3 1.2 %collective-permute-start.9 = (f32[16,512]{1,0:T(8,128)S(1)}, f32[16,512]{1,0:T(8,128)S(1)}, u32[]{:S(2)}, u32[]{:S(2)}) collective-permute-start(f32[16,512]{1,0:T(8,128)S(1)} %get-tuple-element.101), channel_id=1, source_target_pairs={{0,1},{1,0},{2,3},{3,2},{4,5},{5,4},{6,7},{7,6},{8,9},{9,8},{10,11... | collective-permute-start | bytes 98312 | tf_op jit(solution)/shard_map/ppermute | solution.py:738
  52.6 14.1 %collective-permute-start.14 = (bf16[448,128]{1,0:T(8,128)(2,1)S(1)}, bf16[448,128]{1,0:T(8,128)(2,1)S(1)}, u32[]{:S(2)}, u32[]{:S(2)}) collective-permute-start(bf16[448,128]{1,0:T(8,128)(2,1)S(1)} %get-tuple-element.114.refs_0_), channel_id=1, source_target_pairs={{0,12},{4,8},{8,4},{12,0},{16,28},{20,24},{24,20},{28,16},{1,13},{... | collective-permute-start | bytes 344072 | tf_op jit(solution)/shard_map/ppermute | solution.py:743
  53.7 13.0 %collective-permute-start.12 = (bf16[448,128]{1,0:T(8,128)(2,1)S(1)}, bf16[448,128]{1,0:T(8,128)(2,1)S(1)}, u32[]{:S(2)}, u32[]{:S(2)}) collective-permute-start(bf16[448,128]{1,0:T(8,128)(2,1)S(1)} %get-tuple-element.114.refs_0_), channel_id=1, source_target_pairs={{0,24},{4,28},{8,16},{12,20},{16,8},{20,12},{24,0},{28,4},{1,25},{... | collective-permute-start | bytes 344072 | tf_op jit(solution)/shard_map/ppermute | solution.py:743
  56.2 10.8 %collective-permute-start.11 = (bf16[448,128]{1,0:T(8,128)(2,1)S(1)}, bf16[448,128]{1,0:T(8,128)(2,1)S(1)}, u32[]{:S(2)}, u32[]{:S(2)}) collective-permute-start(bf16[448,128]{1,0:T(8,128)(2,1)S(1)} %get-tuple-element.114.refs_0_), channel_id=1, source_target_pairs={{0,16},{4,20},{8,24},{12,28},{16,0},{20,4},{24,8},{28,12},{1,17},{... | collective-permute-start | bytes 344072 | tf_op jit(solution)/shard_map/ppermute | solution.py:743
  56.4 10.6 %collective-permute-start.10 = (bf16[448,128]{1,0:T(8,128)(2,1)S(1)}, bf16[448,128]{1,0:T(8,128)(2,1)S(1)}, u32[]{:S(2)}, u32[]{:S(2)}) collective-permute-start(bf16[448,128]{1,0:T(8,128)(2,1)S(1)} %get-tuple-element.114.refs_0_), channel_id=1, source_target_pairs={{0,8},{4,12},{8,0},{12,4},{16,24},{20,28},{24,16},{28,20},{1,9},{5... | collective-permute-start | bytes 344072 | tf_op jit(solution)/shard_map/ppermute | solution.py:743
  58.1 8.6 %collective-permute-start.13 = (bf16[384,128]{1,0:T(8,128)(2,1)S(1)}, bf16[384,128]{1,0:T(8,128)(2,1)S(1)}, u32[]{:S(2)}, u32[]{:S(2)}) collective-permute-start(bf16[384,128]{1,0:T(8,128)(2,1)S(1)} %get-tuple-element.111.mine), channel_id=1, source_target_pairs={{0,4},{4,0},{8,12},{12,8},{16,20},{20,16},{24,28},{28,24},{1,5},{5... | collective-permute-start | bytes 294920 | tf_op jit(solution)/shard_map/ppermute | solution.py:743
  67.0 4.2 %collective-permute-start.16 = (bf16[8,256,512]{2,1,0:T(8,128)(2,1)S(1)}, bf16[8,256,512]{2,1,0:T(8,128)(2,1)S(1)}, u32[]{:S(2)}, u32[]{:S(2)}) collective-permute-start(bf16[8,256,512]{2,1,0:T(8,128)(2,1)S(1)} %get-tuple-element.118), channel_id=1, source_target_pairs={{0,1},{1,0},{2,3},{3,2},{4,5},{5,4},{6,7},{7,6},{8,9},{9,8},{10,11... | collective-permute-start | bytes 6291464 | tf_op jit(solution)/shard_map/ppermute | solution.py:738
  67.0 7.7 %collective-permute-start.15 = (bf16[832,128]{1,0:T(8,128)(2,1)S(1)}, bf16[832,128]{1,0:T(8,128)(2,1)S(1)}, u32[]{:S(2)}, u32[]{:S(2)}) collective-permute-start(bf16[832,128]{1,0:T(8,128)(2,1)S(1)} %shard_map.220.near), channel_id=1, source_target_pairs={{0,4},{4,0},{8,12},{12,8},{16,20},{20,16},{24,28},{28,24},{1,5},{5... | collective-permute-start | bytes 638984 | tf_op jit(solution)/shard_map/ppermute | solution.py:743

commit v12 on v11

--- a/solution.py
+++ b/solution.py
@@ -253,9 +253,9 @@
         for q in range(wq):
             gbo[:, lane(q)] += accs[q]
 
-    def tile(t, between=()):
+    def tile(t, size, between=()):
         between = list(between)
-        at = pl.ds(pl.multiple_of(t * TILE, TILE), TILE)
+        at = pl.ds(pl.multiple_of(t * TILE, TILE), size)
         a, b = ad[at, :], low[at, :]
         activation, slope = gelu_parts(dot(a, win[...]) + bias_row[...])
         if between:
@@ -276,7 +276,7 @@
             between.pop(0)()
 
     done = offs[n + 2]
-    ready = offs[s] >= (done + 1) * TILE
+    ready = offs[s] >= (done + 2) * TILE
     none = (jnp.zeros((8, LANES), F32),) * wq
 
     def conv_with(chunks, with_tile):
@@ -292,13 +292,13 @@
         cuts = [chunks * k // 4 for k in range(5)]
         parts = [part(cuts[k], cuts[k + 1]) for k in range(4)]
         if with_tile:
-            tile(done, parts)
+            tile(done, 2 * TILE, parts)
         else:
             for run in parts:
                 run()
         add_gbo(state[0])
         if with_tile:
-            offs[n + 2] = done + 1
+            offs[n + 2] = done + 2
 
     all_chunks = frames // CHUNK
     short = count <= (all_chunks - 1) * CHUNK
@@ -317,11 +317,20 @@
         fetch_packed(n - 2).wait()
         fetch_packed(n - 1).start()
 
+        start = offs[n + 2]
+        left = offs[n + 1] - start
+        pairs = lax.shift_right_arithmetic(left, 1)
+
         def rest(t, _):
-            tile(t)
+            tile(start + 2 * t, 2 * TILE)
             return 0
 
-        lax.fori_loop(offs[n + 2], offs[n + 1], rest, 0)
+        lax.fori_loop(0, pairs, rest, 0)
+
+        @pl.when(left > 2 * pairs)
+        def _():
+            tile(offs[n + 1] - 1, TILE)
+
         fetch_packed(n - 1).wait()
         for side, dst in ((0, keep), (1, send)):
             for q in range(wq):

time: 76.6 us -> 76.5 us (level)
  starting transfers between devices: 18.7 us -> 17.6 us
  waiting for transfers between devices: 7.79 us -> 8.61 us
    ppermute x10, starting transfers between devices: 15.2 us -> 14.4 us  [across(): return lax.ppermute(x, 'dp', [(i, i ^ step) for i in range(size)])]
where the time goes in v12:
time: 76.5 us
  Pallas kernels  49.4 us (65%)
  starting transfers between devices  17.6 us (23%)
  waiting for transfers between devices  8.61 us (11%)
  between operations  0.8 us (1%)
    pallas_call x1, Pallas kernels, front(): pl.pallas_call(functools.partial(front_kernel, n), grid_spec=pl.GridSpec(...  16.8 us
    ppermute x10, starting transfers between devices, across(): return lax.ppermute(x, 'dp', [(i, i ^ step) for i in range(size)])  14.4 us
    pallas_call x1, Pallas kernels, mix(): pl.pallas_call(functools.partial(mix_kernel, n, taps), in_specs=[smem()]...  11 us
    pallas_call x1, Pallas kernels, norm_grad(): pl.pallas_call(functools.partial(norm_grad_kernel, n, taps, rates), grid=...  7.71 us
    ppermute x7, waiting for transfers between devices, swap(): return lax.ppermute(x, 'tp', [(i, i ^ step) for i in range(size)])  6.52 us
    pallas_call x1, Pallas kernels, token_grad(): pl.pallas_call(functools.partial(token_grad_kernel, n, taps), grid=(n,),...  4.59 us
    ppermute x7, starting transfers between devices, swap(): return lax.ppermute(x, 'tp', [(i, i ^ step) for i in range(size)])  3.23 us
    pallas_call x1, Pallas kernels, place_out(): pl.pallas_call(functools.partial(place_out_kernel, n), in_specs=[smem(),...  2.73 us
  transfers between devices with their start and end apart: 17, of which 7 were waited for; matrix products, arithmetic and copies ran while one was open for 0% of the time, Pallas kernels for 60%

profile of v12, /device:TPU:0, one launch (start us, length us, event | category | flops | bytes accessed | tf_op | source)
XLA Modules:
  0.0 76.5 jit_solution(16273704677864471006)
XLA Ops:
  0.6 1.3 %shard_map.212.buf_a = bf16[3088,128]{1,0:T(8,128)(2,1)S(1)} custom-call(bf16[512,384]{1,0:T(8,128)(2,1)} %wi.1, bf16[384]{0:T(512)(128)(2,1)} %bi.1, bf16[384,512]{1,0:T(8,128)(2,1)} %wo.1), custom_call_target="tpu_custom_call" | custom-call | tf_op jit(solution)/shard_map/pallas_call | solution.py:110
  1.9 0.5 collective-permute-start
  2.4 2.6 %collective-permute-start.3 = (bf16[3088,128]{1,0:T(8,128)(2,1)S(1)}, bf16[3088,128]{1,0:T(8,128)(2,1)S(1)}, u32[]{:S(2)}, u32[]{:S(2)}) collective-permute-start(bf16[3088,128]{1,0:T(8,128)(2,1)S(1)} %shard_map.212.buf_a), channel_id=1, source_target_pairs={{0,2},{1,3},{2,0},{3,1},{4,6},{5,7},{6,4},{7,5},{8,10},{9,11},{10,... | collective-permute-start | bytes 2371592 | tf_op jit(solution)/shard_map/ppermute | solution.py:747
  5.0 0.0 collective-permute-done.buf_b
  5.0 16.8 %shard_map.213 = (bf16[2304,512]{1,0:T(8,128)(2,1)S(1)}, bf16[2304,512]{1,0:T(8,128)(2,1)S(1)}, bf16[2304,512]{1,0:T(8,128)(2,1)S(1)}, f32[2304,128]{1,0:T(8,128...) custom-call(s32[16]{0:T(128)} %counts_hbm.1, ...), custom_call_target="tpu_custom_call" | custom-call | tf_op jit(solution)/shard_map/pallas_call | solution.py:350
  21.8 0.1 collective-permute-start.1
  21.9 1.3 %collective-permute-done.3.buf_c = bf16[3088,128]{1,0:T(8,128)(2,1)S(1)} collective-permute-done((bf16[3088,128]{1,0:T(8,128)(2,1)S(1)}, bf16[3088,128]{1,0:T(8,128)(2,1)S(1)}, u32[]{:S(2)}, u32[]{:S(2)}) %collective-permute-start.3) | collective-permute-done | bytes 790560 | tf_op jit(solution)/shard_map/ppermute | solution.py:747
  23.2 0.0 collective-permute-start.4
  23.2 0.9 %collective-permute-done.1.recv = bf16[3072,128]{1,0:T(8,128)(2,1)S(1)} collective-permute-done((bf16[3072,128]{1,0:T(8,128)(2,1)S(1)}, bf16[3072,128]{1,0:T(8,128)(2,1)S(1)}, u32[]{:S(2)}, u32[]{:S(2)}) %collective-permute-start.1) | collective-permute-done | bytes 786464 | tf_op jit(solution)/shard_map/ppermute | solution.py:747
  24.2 0.7 shard_map.214
  24.9 1.0 %collective-permute-start.2 = (bf16[1536,128]{1,0:T(8,128)(2,1)S(1)}, bf16[1536,128]{1,0:T(8,128)(2,1)S(1)}, u32[]{:S(2)}, u32[]{:S(2)}) collective-permute-start(bf16[1536,128]{1,0:T(8,128)(2,1)S(1)} %get-tuple-element.76), channel_id=1, source_target_pairs={{0,4},{4,0},{8,12},{12,8},{16,20},{20,16},{24,28},{28,24},{1,5},{5... | collective-permute-start | bytes 1179656 | tf_op jit(solution)/shard_map/ppermute | solution.py:752
  25.8 0.0 collective-permute-done.4.buf_d
  25.8 11.0 %shard_map.215 = (f32[2304,512]{1,0:T(8,128)S(1)}, f32[2304,512]{1,0:T(8,128)S(1)}, bf16[2304,512]{1,0:T(8,128)(2,1)S(1)}) custom-call(s32[34]{0:T(128)S(1)} %get-tuple-element.72.meta, bf16[2304,512]{1,0:T(8,128)(2,1)S(1)} %get-tuple-element.77.ad, bf16[2304,512]{1,0:T(8,128)(2,1)S(1)} %get-tuple-element.78.low, ...), custom_call_target="tpu_custom_call" | custom-call | tf_op jit(solution)/shard_map/pallas_call | solution.py:435
  36.8 0.0 collective-permute-done.2
  36.8 0.1 collective-permute-start.8
  36.9 0.1 fusion
  37.1 5.2 %collective-permute-start.7 = (bf16[384,128]{1,0:T(8,128)(2,1)S(1)}, bf16[384,128]{1,0:T(8,128)(2,1)S(1)}, u32[]{:S(2)}, u32[]{:S(2)}) collective-permute-start(bf16[384,128]{1,0:T(8,128)(2,1)S(1)} %get-tuple-element.135), channel_id=1, source_target_pairs={{0,24},{4,28},{8,16},{12,20},{16,8},{20,12},{24,0},{28,4},{1,25},{... | collective-permute-start | bytes 294920 | tf_op jit(solution)/shard_map/ppermute | solution.py:752
  42.3 0.0 collective-permute-start.6
  42.3 0.6 collective-permute-start.5
  42.9 7.7 %shard_map.216 = (f32[8,4,288,128]{3,2,1,0:T(8,128)S(1)}, f32[16,512]{1,0:T(8,128)S(1)}, f32[16,512]{1,0:T(8,128)S(1)}) custom-call(s32[34]{0:T(128)S(1)} %get-tuple-element.72.meta, bf16[8,256,512]{2,1,0:T(8,128)(2,1)S(1)} %get-tuple-element.88.tok, bf16[8,256,512]{2,1,0:T(8,128)(2,1)S(1)} %get-tuple-element.89.cot, ...), custom_call_target="tpu_custom_call" | custom-call | bytes 40000000 | tf_op jit(solution)/shard_map/pallas_call | solution.py:555
  50.6 0.0 collective-permute-done.7.refs_2_
  50.6 0.2 collective-permute-done.6.refs_1_
  50.9 0.0 collective-permute-done.5.refs_0_
  50.9 0.0 collective-permute-done.8.other
  50.9 0.0 collective-permute-start.9
  50.9 1.2 %collective-permute-done.9.recv = f32[16,512]{1,0:T(8,128)S(1)} collective-permute-done((f32[16,512]{1,0:T(8,128)S(1)}, f32[16,512]{1,0:T(8,128)S(1)}, u32[]{:S(2)}, u32[]{:S(2)}) %collective-permute-start.9) | collective-permute-done | bytes 32800 | tf_op jit(solution)/shard_map/ppermute | solution.py:747
  52.1 0.1 shard_map.217
  52.2 1.2 %collective-permute-start.14 = (bf16[448,128]{1,0:T(8,128)(2,1)S(1)}, bf16[448,128]{1,0:T(8,128)(2,1)S(1)}, u32[]{:S(2)}, u32[]{:S(2)}) collective-permute-start(bf16[448,128]{1,0:T(8,128)(2,1)S(1)} %get-tuple-element.114.refs_0_), channel_id=1, source_target_pairs={{0,12},{4,8},{8,4},{12,0},{16,28},{20,24},{24,20},{28,16},{1,13},{... | collective-permute-start | bytes 344072 | tf_op jit(solution)/shard_map/ppermute | solution.py:752
  53.4 2.4 %collective-permute-start.12 = (bf16[448,128]{1,0:T(8,128)(2,1)S(1)}, bf16[448,128]{1,0:T(8,128)(2,1)S(1)}, u32[]{:S(2)}, u32[]{:S(2)}) collective-permute-start(bf16[448,128]{1,0:T(8,128)(2,1)S(1)} %get-tuple-element.114.refs_0_), channel_id=1, source_target_pairs={{0,24},{4,28},{8,16},{12,20},{16,8},{20,12},{24,0},{28,4},{1,25},{... | collective-permute-start | bytes 344072 | tf_op jit(solution)/shard_map/ppermute | solution.py:752
  55.7 0.6 collective-permute-start.11
  56.3 1.5 %collective-permute-start.10 = (bf16[448,128]{1,0:T(8,128)(2,1)S(1)}, bf16[448,128]{1,0:T(8,128)(2,1)S(1)}, u32[]{:S(2)}, u32[]{:S(2)}) collective-permute-start(bf16[448,128]{1,0:T(8,128)(2,1)S(1)} %get-tuple-element.114.refs_0_), channel_id=1, source_target_pairs={{0,8},{4,12},{8,0},{12,4},{16,24},{20,28},{24,16},{28,20},{1,9},{5... | collective-permute-start | bytes 344072 | tf_op jit(solution)/shard_map/ppermute | solution.py:752
  57.8 0.8 %collective-permute-start.13 = (bf16[384,128]{1,0:T(8,128)(2,1)S(1)}, bf16[384,128]{1,0:T(8,128)(2,1)S(1)}, u32[]{:S(2)}, u32[]{:S(2)}) collective-permute-start(bf16[384,128]{1,0:T(8,128)(2,1)S(1)} %get-tuple-element.111.mine), channel_id=1, source_target_pairs={{0,4},{4,0},{8,12},{12,8},{16,20},{20,16},{24,28},{28,24},{1,5},{5... | collective-permute-start | bytes 294920 | tf_op jit(solution)/shard_map/ppermute | solution.py:752
  58.6 2.7 %shard_map.218 = bf16[16,256,512]{2,1,0:T(8,128)(2,1)} custom-call(s32[34]{0:T(128)S(1)} %get-tuple-element.72.meta, bf16[2304,512]{1,0:T(8,128)(2,1)S(1)} %get-tuple-element.98.own, bf16[2304,512]{1,0:T(8,128)(2,1)S(1)} %collective-permute-done.8.other), custom_call_target="tpu_custom_call" | custom-call | bytes 40000000 | tf_op jit(solution)/shard_map/pallas_call | solution.py:588
  61.4 4.6 %shard_map.219 = (f32[16,256,512]{2,1,0:T(8,128)}, bf16[8,256,512]{2,1,0:T(8,128)(2,1)S(1)}) custom-call(s32[34]{0:T(128)S(1)} %get-tuple-element.72.meta, bf16[8,256,512]{2,1,0:T(8,128)(2,1)S(1)} %get-tuple-element.89.cot, f32[8,4,288,128]{3,2,1,0:T(8,128)S(1)} %get-tuple-element.112.cgp, f32[16,512]{1,0:T(8,128)S(1)} %get-tuple-element.83.consts), custom_call_target="tpu_custom_call" | custom-call | bytes 40000000 | tf_op jit(solution)/shard_map/pallas_call | solution.py:640
  66.0 0.0 collective-permute-done.13.theirs
  66.0 0.0 collective-permute-done.14.far_1
  66.0 0.0 collective-permute-done.12.refs_3_
  66.0 0.9 %collective-permute-done.11.refs_2_ = bf16[448,128]{1,0:T(8,128)(2,1)S(1)} collective-permute-done((bf16[448,128]{1,0:T(8,128)(2,1)S(1)}, bf16[448,128]{1,0:T(8,128)(2,1)S(1)}, u32[]{:S(2)}, u32[]{:S(2)}) %collective-permute-start.11) | collective-permute-done | bytes 114720 | tf_op jit(solution)/shard_map/ppermute | solution.py:752
  66.9 0.0 collective-permute-done.10.refs_1_.near_1
  66.9 0.0 collective-permute-start.16
  66.9 1.1 %collective-permute-start.15 = (bf16[832,128]{1,0:T(8,128)(2,1)S(1)}, bf16[832,128]{1,0:T(8,128)(2,1)S(1)}, u32[]{:S(2)}, u32[]{:S(2)}) collective-permute-start(bf16[832,128]{1,0:T(8,128)(2,1)S(1)} %shard_map.220.near), channel_id=1, source_target_pairs={{0,4},{4,0},{8,12},{12,8},{16,20},{20,16},{24,28},{28,24},{1,5},{5... | collective-permute-start | bytes 638984 | tf_op jit(solution)/shard_map/ppermute | solution.py:752
  68.0 3.0 %collective-permute-done.16.other = bf16[8,256,512]{2,1,0:T(8,128)(2,1)S(1)} collective-permute-done((bf16[8,256,512]{2,1,0:T(8,128)(2,1)S(1)}, bf16[8,256,512]{2,1,0:T(8,128)(2,1)S(1)}, u32[]{:S(2)}, u32[]{:S(2)}) %collective-permute-start.16) | collective-permute-done | bytes 2097184 | tf_op jit(solution)/shard_map/ppermute | solution.py:747
  71.0 2.6 %shard_map.221 = f32[16,256,512]{2,1,0:T(8,128)} custom-call(s32[34]{0:T(128)S(1)} %get-tuple-element.72.meta, bf16[8,256,512]{2,1,0:T(8,128)(2,1)S(1)} %collective-permute-done.16.other, f32[16,256,512]{2,1,0:T(8,128)} %get-tuple-element.119.gtok_in), custom_call_target="tpu_custom_call", output_to_operand_aliasing={{}: (2, {})} | custom-call | bytes 20000000 | tf_op jit(solution)/shard_map/pallas_call | solution.py:660
  73.7 1.0 %collective-permute-done.15.far = bf16[832,128]{1,0:T(8,128)(2,1)S(1)} collective-permute-done((bf16[832,128]{1,0:T(8,128)(2,1)S(1)}, bf16[832,128]{1,0:T(8,128)(2,1)S(1)}, u32[]{:S(2)}, u32[]{:S(2)}) %collective-permute-start.15) | collective-permute-done | bytes 213024 | tf_op jit(solution)/shard_map/ppermute | solution.py:752
  74.6 1.9 %shard_map.222 = (f32[7,512]{1,0:T(8,128)}, f32[512]{0:T(512)}, f32[2,512]{1,0:T(2,128)}, f32[2,512]{1,0:T(2,128)}, f32[512,384]{1,0:T(8,128)}, /*index=5*/f32[3...) custom-call(s32[34]{0:T(128)S(1)} %get-tuple-element.72.meta, bf16[384,128]{1,0:T(8,128)(2,1)S(1)} %get-tuple-element.111.mine, ...), custom_call_target="tpu_custom_call" | custom-call | tf_op jit(solution)/shard_map/pallas_call | solution.py:738
  (2 shorter events, 0.0 us)
Async XLA Ops:
  1.9 3.1 %collective-permute-start = (bf16[3088,128]{1,0:T(8,128)(2,1)S(1)}, bf16[3088,128]{1,0:T(8,128)(2,1)S(1)}, u32[]{:S(2)}, u32[]{:S(2)}) collective-permute-start(bf16[3088,128]{1,0:T(8,128)(2,1)S(1)} %shard_map.212.buf_a), channel_id=1, source_target_pairs={{0,1},{1,0},{2,3},{3,2},{4,5},{5,4},{6,7},{7,6},{8,9},{9,8},{10,11... | collective-permute-start | bytes 2371592 | tf_op jit(solution)/shard_map/ppermute | solution.py:747
  2.4 20.8 %collective-permute-start.3 = (bf16[3088,128]{1,0:T(8,128)(2,1)S(1)}, bf16[3088,128]{1,0:T(8,128)(2,1)S(1)}, u32[]{:S(2)}, u32[]{:S(2)}) collective-permute-start(bf16[3088,128]{1,0:T(8,128)(2,1)S(1)} %shard_map.212.buf_a), channel_id=1, source_target_pairs={{0,2},{1,3},{2,0},{3,1},{4,6},{5,7},{6,4},{7,5},{8,10},{9,11},{10,... | collective-permute-start | bytes 2371592 | tf_op jit(solution)/shard_map/ppermute | solution.py:747
  21.8 2.4 %collective-permute-start.1 = (bf16[3072,128]{1,0:T(8,128)(2,1)S(1)}, bf16[3072,128]{1,0:T(8,128)(2,1)S(1)}, u32[]{:S(2)}, u32[]{:S(2)}) collective-permute-start(bf16[3072,128]{1,0:T(8,128)(2,1)S(1)} %get-tuple-element.74), channel_id=1, source_target_pairs={{0,1},{1,0},{2,3},{3,2},{4,5},{5,4},{6,7},{7,6},{8,9},{9,8},{10,11... | collective-permute-start | bytes 2359304 | tf_op jit(solution)/shard_map/ppermute | solution.py:747
  23.2 2.6 %collective-permute-start.4 = (bf16[3088,128]{1,0:T(8,128)(2,1)S(1)}, bf16[3088,128]{1,0:T(8,128)(2,1)S(1)}, u32[]{:S(2)}, u32[]{:S(2)}) collective-permute-start(bf16[3088,128]{1,0:T(8,128)(2,1)S(1)} %collective-permute-done.3.buf_c), channel_id=1, source_target_pairs={{0,1},{1,0},{2,3},{3,2},{4,5},{5,4},{6,7},{7,6},{8,9},{9,8},{10,11... | collective-permute-start | bytes 2371592 | tf_op jit(solution)/shard_map/ppermute | solution.py:747
  24.9 12.0 %collective-permute-start.2 = (bf16[1536,128]{1,0:T(8,128)(2,1)S(1)}, bf16[1536,128]{1,0:T(8,128)(2,1)S(1)}, u32[]{:S(2)}, u32[]{:S(2)}) collective-permute-start(bf16[1536,128]{1,0:T(8,128)(2,1)S(1)} %get-tuple-element.76), channel_id=1, source_target_pairs={{0,4},{4,0},{8,12},{12,8},{16,20},{20,16},{24,28},{28,24},{1,5},{5... | collective-permute-start | bytes 1179656 | tf_op jit(solution)/shard_map/ppermute | solution.py:752
  36.8 14.0 %collective-permute-start.8 = (bf16[2304,512]{1,0:T(8,128)(2,1)S(1)}, bf16[2304,512]{1,0:T(8,128)(2,1)S(1)}, u32[]{:S(2)}, u32[]{:S(2)}) collective-permute-start(bf16[2304,512]{1,0:T(8,128)(2,1)S(1)} %get-tuple-element.98.own), channel_id=1, source_target_pairs={{0,1},{1,0},{2,3},{3,2},{4,5},{5,4},{6,7},{7,6},{8,9},{9,8},{10,11... | collective-permute-start | bytes 7077896 | tf_op jit(solution)/shard_map/ppermute | solution.py:747
  37.1 13.6 %collective-permute-start.7 = (bf16[384,128]{1,0:T(8,128)(2,1)S(1)}, bf16[384,128]{1,0:T(8,128)(2,1)S(1)}, u32[]{:S(2)}, u32[]{:S(2)}) collective-permute-start(bf16[384,128]{1,0:T(8,128)(2,1)S(1)} %get-tuple-element.135), channel_id=1, source_target_pairs={{0,24},{4,28},{8,16},{12,20},{16,8},{20,12},{24,0},{28,4},{1,25},{... | collective-permute-start | bytes 294920 | tf_op jit(solution)/shard_map/ppermute | solution.py:752
  42.3 8.6 %collective-permute-start.6 = (bf16[384,128]{1,0:T(8,128)(2,1)S(1)}, bf16[384,128]{1,0:T(8,128)(2,1)S(1)}, u32[]{:S(2)}, u32[]{:S(2)}) collective-permute-start(bf16[384,128]{1,0:T(8,128)(2,1)S(1)} %get-tuple-element.136), channel_id=1, source_target_pairs={{0,16},{4,20},{8,24},{12,28},{16,0},{20,4},{24,8},{28,12},{1,17},{... | collective-permute-start | bytes 294920 | tf_op jit(solution)/shard_map/ppermute | solution.py:752
  42.3 8.6 %collective-permute-start.5 = (bf16[384,128]{1,0:T(8,128)(2,1)S(1)}, bf16[384,128]{1,0:T(8,128)(2,1)S(1)}, u32[]{:S(2)}, u32[]{:S(2)}) collective-permute-start(bf16[384,128]{1,0:T(8,128)(2,1)S(1)} %get-tuple-element.137), channel_id=1, source_target_pairs={{0,8},{4,12},{8,0},{12,4},{16,24},{20,28},{24,16},{28,20},{1,9},{5... | collective-permute-start | bytes 294920 | tf_op jit(solution)/shard_map/ppermute | solution.py:752
  50.9 1.2 %collective-permute-start.9 = (f32[16,512]{1,0:T(8,128)S(1)}, f32[16,512]{1,0:T(8,128)S(1)}, u32[]{:S(2)}, u32[]{:S(2)}) collective-permute-start(f32[16,512]{1,0:T(8,128)S(1)} %get-tuple-element.101), channel_id=1, source_target_pairs={{0,1},{1,0},{2,3},{3,2},{4,5},{5,4},{6,7},{7,6},{8,9},{9,8},{10,11... | collective-permute-start | bytes 98312 | tf_op jit(solution)/shard_map/ppermute | solution.py:747
  52.2 13.8 %collective-permute-start.14 = (bf16[448,128]{1,0:T(8,128)(2,1)S(1)}, bf16[448,128]{1,0:T(8,128)(2,1)S(1)}, u32[]{:S(2)}, u32[]{:S(2)}) collective-permute-start(bf16[448,128]{1,0:T(8,128)(2,1)S(1)} %get-tuple-element.114.refs_0_), channel_id=1, source_target_pairs={{0,12},{4,8},{8,4},{12,0},{16,28},{20,24},{24,20},{28,16},{1,13},{... | collective-permute-start | bytes 344072 | tf_op jit(solution)/shard_map/ppermute | solution.py:752
  53.4 12.6 %collective-permute-start.12 = (bf16[448,128]{1,0:T(8,128)(2,1)S(1)}, bf16[448,128]{1,0:T(8,128)(2,1)S(1)}, u32[]{:S(2)}, u32[]{:S(2)}) collective-permute-start(bf16[448,128]{1,0:T(8,128)(2,1)S(1)} %get-tuple-element.114.refs_0_), channel_id=1, source_target_pairs={{0,24},{4,28},{8,16},{12,20},{16,8},{20,12},{24,0},{28,4},{1,25},{... | collective-permute-start | bytes 344072 | tf_op jit(solution)/shard_map/ppermute | solution.py:752
  55.7 11.1 %collective-permute-start.11 = (bf16[448,128]{1,0:T(8,128)(2,1)S(1)}, bf16[448,128]{1,0:T(8,128)(2,1)S(1)}, u32[]{:S(2)}, u32[]{:S(2)}) collective-permute-start(bf16[448,128]{1,0:T(8,128)(2,1)S(1)} %get-tuple-element.114.refs_0_), channel_id=1, source_target_pairs={{0,16},{4,20},{8,24},{12,28},{16,0},{20,4},{24,8},{28,12},{1,17},{... | collective-permute-start | bytes 344072 | tf_op jit(solution)/shard_map/ppermute | solution.py:752
  56.3 10.6 %collective-permute-start.10 = (bf16[448,128]{1,0:T(8,128)(2,1)S(1)}, bf16[448,128]{1,0:T(8,128)(2,1)S(1)}, u32[]{:S(2)}, u32[]{:S(2)}) collective-permute-start(bf16[448,128]{1,0:T(8,128)(2,1)S(1)} %get-tuple-element.114.refs_0_), channel_id=1, source_target_pairs={{0,8},{4,12},{8,0},{12,4},{16,24},{20,28},{24,16},{28,20},{1,9},{5... | collective-permute-start | bytes 344072 | tf_op jit(solution)/shard_map/ppermute | solution.py:752
  57.8 8.2 %collective-permute-start.13 = (bf16[384,128]{1,0:T(8,128)(2,1)S(1)}, bf16[384,128]{1,0:T(8,128)(2,1)S(1)}, u32[]{:S(2)}, u32[]{:S(2)}) collective-permute-start(bf16[384,128]{1,0:T(8,128)(2,1)S(1)} %get-tuple-element.111.mine), channel_id=1, source_target_pairs={{0,4},{4,0},{8,12},{12,8},{16,20},{20,16},{24,28},{28,24},{1,5},{5... | collective-permute-start | bytes 294920 | tf_op jit(solution)/shard_map/ppermute | solution.py:752
  66.9 4.2 %collective-permute-start.16 = (bf16[8,256,512]{2,1,0:T(8,128)(2,1)S(1)}, bf16[8,256,512]{2,1,0:T(8,128)(2,1)S(1)}, u32[]{:S(2)}, u32[]{:S(2)}) collective-permute-start(bf16[8,256,512]{2,1,0:T(8,128)(2,1)S(1)} %get-tuple-element.118), channel_id=1, source_target_pairs={{0,1},{1,0},{2,3},{3,2},{4,5},{5,4},{6,7},{7,6},{8,9},{9,8},{10,11... | collective-permute-start | bytes 6291464 | tf_op jit(solution)/shard_map/ppermute | solution.py:747
  66.9 7.7 %collective-permute-start.15 = (bf16[832,128]{1,0:T(8,128)(2,1)S(1)}, bf16[832,128]{1,0:T(8,128)(2,1)S(1)}, u32[]{:S(2)}, u32[]{:S(2)}) collective-permute-start(bf16[832,128]{1,0:T(8,128)(2,1)S(1)} %shard_map.220.near), channel_id=1, source_target_pairs={{0,4},{4,0},{8,12},{12,8},{16,20},{20,16},{24,28},{28,24},{1,5},{5... | collective-permute-start | bytes 638984 | tf_op jit(solution)/shard_map/ppermute | solution.py:752

commit v13 on v12

--- a/solution.py
+++ b/solution.py
@@ -65,8 +65,9 @@
 
 
 def gelu_parts(pre):
-    cdf = 0.5 + 0.5 * lax.erf(pre * 0.7071067811865476)
-    density = jnp.exp(-0.5 * pre * pre) * 0.3989422804014327
+    scaled = pre * 0.7071067811865476
+    cdf = 0.5 + 0.5 * lax.erf(scaled)
+    density = jnp.exp(-(scaled * scaled)) * 0.3989422804014327
     return pre * cdf, cdf + pre * density
 
 
@@ -406,7 +407,7 @@
         out[at, :] = (tokp[at, :].astype(F32) + consts[taps:taps + 1, :] * value).astype(BF)
         ag[at, :] = own_ag + dot_t(grad.astype(BF), win2[...])
 
-    first = pl.ds(0, TILE)
+    first = pl.ds(0, 2 * TILE)
     branch[first, :], ag[first, :] = own(first)
     for c in copies:
         c.wait()
@@ -414,17 +415,17 @@
     rest(first, branch[first, :], ag[first, :])
 
     def pair(t, _):
-        at = pl.ds(pl.multiple_of((2 * t + 1) * TILE, TILE), 2 * TILE)
+        at = pl.ds(pl.multiple_of((2 * t + 2) * TILE, TILE), 2 * TILE)
         rest(at, *own(at))
         return 0
 
-    left = offs[n + 1] - 1
+    left = jnp.maximum(offs[n + 1] - 2, 0)
     pairs = lax.shift_right_arithmetic(left, 1)
     lax.fori_loop(0, pairs, pair, 0)
 
     @pl.when(left > 2 * pairs)
     def _():
-        at = pl.ds(pl.multiple_of(left * TILE, TILE), TILE)
+        at = pl.ds(pl.multiple_of((left + 1) * TILE, TILE), TILE)
         rest(at, *own(at))
 
 
@@ -487,7 +488,7 @@
         istd = inv[src, :]
         for q in range(wq):
             cg = istd * (ngs[q] - m1 - nrs[q] * m2)
-            cgp[s, q, pl.ds(pl.multiple_of(r0 + PAD, 8), size), :] = jnp.where(live, cg, 0.0)
+            cgp[s, q, pl.ds(pl.multiple_of(r0 + PAD, 8), size), :] = cg
         return tuple(new)
 
     def both_sizes(run, width_of_state, add):

time: 76.5 us -> 77.7 us (1.016)
  starting transfers between devices: 17.6 us -> 19.2 us
  waiting for transfers between devices: 8.61 us -> 7.53 us
    ppermute x7, waiting for transfers between devices: 6.52 us -> 5.38 us  [swap(): return lax.ppermute(x, 'tp', [(i, i ^ step) for i in range(size)])]
    ppermute x10, starting transfers between devices: 14.4 us -> 15.5 us  [across(): return lax.ppermute(x, 'dp', [(i, i ^ step) for i in range(size)])]
where the time goes in v13:
time: 77.7 us; the launch traced here: 77.8 us
  Pallas kernels  50.1 us (64%)
  starting transfers between devices  19.2 us (25%)
  waiting for transfers between devices  7.53 us (10%)
  between operations  0.78 us (1%)
    pallas_call x1, Pallas kernels, front(): pl.pallas_call(functools.partial(front_kernel, n), grid_spec=pl.GridSpec(...  17.6 us
    ppermute x10, starting transfers between devices, across(): return lax.ppermute(x, 'dp', [(i, i ^ step) for i in range(size)])  15.5 us
    pallas_call x1, Pallas kernels, mix(): pl.pallas_call(functools.partial(mix_kernel, n, taps), in_specs=[smem()]...  11.4 us
    pallas_call x1, Pallas kernels, norm_grad(): pl.pallas_call(functools.partial(norm_grad_kernel, n, taps, rates), grid=...  7.4 us
    ppermute x7, waiting for transfers between devices, swap(): return lax.ppermute(x, 'tp', [(i, i ^ step) for i in range(size)])  5.38 us
    pallas_call x1, Pallas kernels, token_grad(): pl.pallas_call(functools.partial(token_grad_kernel, n, taps), grid=(n,),...  4.42 us
    ppermute x7, starting transfers between devices, swap(): return lax.ppermute(x, 'tp', [(i, i ^ step) for i in range(size)])  3.71 us
    pallas_call x1, Pallas kernels, place_out(): pl.pallas_call(functools.partial(place_out_kernel, n), in_specs=[smem(),...  2.73 us
  transfers between devices with their start and end apart: 17, of which 7 were waited for; matrix products, arithmetic and copies ran while one was open for 0% of the time, Pallas kernels for 60%

profile of v13, /device:TPU:0, one launch (start us, length us, event | category | flops | bytes accessed | tf_op | source)
XLA Modules:
  0.0 77.8 jit_solution(3914298418301160542)
XLA Ops:
  0.6 1.3 %shard_map.212.buf_a = bf16[3088,128]{1,0:T(8,128)(2,1)S(1)} custom-call(bf16[512,384]{1,0:T(8,128)(2,1)} %wi.1, bf16[384]{0:T(512)(128)(2,1)} %bi.1, bf16[384,512]{1,0:T(8,128)(2,1)} %wo.1), custom_call_target="tpu_custom_call" | custom-call | tf_op jit(solution)/shard_map/pallas_call | solution.py:111
  1.9 0.5 collective-permute-start
  2.4 2.6 %collective-permute-start.3 = (bf16[3088,128]{1,0:T(8,128)(2,1)S(1)}, bf16[3088,128]{1,0:T(8,128)(2,1)S(1)}, u32[]{:S(2)}, u32[]{:S(2)}) collective-permute-start(bf16[3088,128]{1,0:T(8,128)(2,1)S(1)} %shard_map.212.buf_a), channel_id=1, source_target_pairs={{0,2},{1,3},{2,0},{3,1},{4,6},{5,7},{6,4},{7,5},{8,10},{9,11},{10,... | collective-permute-start | bytes 2371592 | tf_op jit(solution)/shard_map/ppermute | solution.py:748
  5.0 0.0 collective-permute-done.buf_b
  5.0 17.6 %shard_map.213 = (bf16[2304,512]{1,0:T(8,128)(2,1)S(1)}, bf16[2304,512]{1,0:T(8,128)(2,1)S(1)}, bf16[2304,512]{1,0:T(8,128)(2,1)S(1)}, f32[2304,128]{1,0:T(8,128...) custom-call(s32[16]{0:T(128)} %counts_hbm.1, ...), custom_call_target="tpu_custom_call" | custom-call | tf_op jit(solution)/shard_map/pallas_call | solution.py:351
  22.6 0.5 collective-permute-start.1
  23.1 0.1 collective-permute-done.3.buf_c
  23.2 0.0 collective-permute-start.4
  23.2 1.8 %collective-permute-done.1.recv = bf16[3072,128]{1,0:T(8,128)(2,1)S(1)} collective-permute-done((bf16[3072,128]{1,0:T(8,128)(2,1)S(1)}, bf16[3072,128]{1,0:T(8,128)(2,1)S(1)}, u32[]{:S(2)}, u32[]{:S(2)}) %collective-permute-start.1) | collective-permute-done | bytes 786464 | tf_op jit(solution)/shard_map/ppermute | solution.py:748
  25.0 0.7 shard_map.214
  25.7 1.0 %collective-permute-start.2 = (bf16[1536,128]{1,0:T(8,128)(2,1)S(1)}, bf16[1536,128]{1,0:T(8,128)(2,1)S(1)}, u32[]{:S(2)}, u32[]{:S(2)}) collective-permute-start(bf16[1536,128]{1,0:T(8,128)(2,1)S(1)} %get-tuple-element.76), channel_id=1, source_target_pairs={{0,4},{4,0},{8,12},{12,8},{16,20},{20,16},{24,28},{28,24},{1,5},{5... | collective-permute-start | bytes 1179656 | tf_op jit(solution)/shard_map/ppermute | solution.py:753
  26.7 0.0 collective-permute-done.4.buf_d
  26.7 11.4 %shard_map.215 = (f32[2304,512]{1,0:T(8,128)S(1)}, f32[2304,512]{1,0:T(8,128)S(1)}, bf16[2304,512]{1,0:T(8,128)(2,1)S(1)}) custom-call(s32[34]{0:T(128)S(1)} %get-tuple-element.72.meta, bf16[2304,512]{1,0:T(8,128)(2,1)S(1)} %get-tuple-element.77.ad, bf16[2304,512]{1,0:T(8,128)(2,1)S(1)} %get-tuple-element.78.low, ...), custom_call_target="tpu_custom_call" | custom-call | tf_op jit(solution)/shard_map/pallas_call | solution.py:436
  38.1 0.0 collective-permute-done.2
  38.1 0.1 collective-permute-start.8
  38.2 0.1 fusion
  38.4 5.0 %collective-permute-start.7 = (bf16[384,128]{1,0:T(8,128)(2,1)S(1)}, bf16[384,128]{1,0:T(8,128)(2,1)S(1)}, u32[]{:S(2)}, u32[]{:S(2)}) collective-permute-start(bf16[384,128]{1,0:T(8,128)(2,1)S(1)} %get-tuple-element.135), channel_id=1, source_target_pairs={{0,24},{4,28},{8,16},{12,20},{16,8},{20,12},{24,0},{28,4},{1,25},{... | collective-permute-start | bytes 294920 | tf_op jit(solution)/shard_map/ppermute | solution.py:753
  43.4 0.7 collective-permute-start.6
  44.1 0.5 collective-permute-start.5
  44.5 7.4 %shard_map.216 = (f32[8,4,288,128]{3,2,1,0:T(8,128)S(1)}, f32[16,512]{1,0:T(8,128)S(1)}, f32[16,512]{1,0:T(8,128)S(1)}) custom-call(s32[34]{0:T(128)S(1)} %get-tuple-element.72.meta, bf16[8,256,512]{2,1,0:T(8,128)(2,1)S(1)} %get-tuple-element.88.tok, bf16[8,256,512]{2,1,0:T(8,128)(2,1)S(1)} %get-tuple-element.89.cot, ...), custom_call_target="tpu_custom_call" | custom-call | bytes 40000000 | tf_op jit(solution)/shard_map/pallas_call | solution.py:556
  52.0 0.0 collective-permute-done.7.refs_2_
  52.0 0.7 collective-permute-done.6.refs_1_
  52.7 0.0 collective-permute-done.5.refs_0_
  52.7 0.0 collective-permute-done.8.other
  52.7 0.1 collective-permute-start.9
  52.7 1.2 %collective-permute-done.9.recv = f32[16,512]{1,0:T(8,128)S(1)} collective-permute-done((f32[16,512]{1,0:T(8,128)S(1)}, f32[16,512]{1,0:T(8,128)S(1)}, u32[]{:S(2)}, u32[]{:S(2)}) %collective-permute-start.9) | collective-permute-done | bytes 32800 | tf_op jit(solution)/shard_map/ppermute | solution.py:748
  53.9 0.1 shard_map.217
  54.0 1.1 %collective-permute-start.14 = (bf16[448,128]{1,0:T(8,128)(2,1)S(1)}, bf16[448,128]{1,0:T(8,128)(2,1)S(1)}, u32[]{:S(2)}, u32[]{:S(2)}) collective-permute-start(bf16[448,128]{1,0:T(8,128)(2,1)S(1)} %get-tuple-element.114.refs_0_), channel_id=1, source_target_pairs={{0,12},{4,8},{8,4},{12,0},{16,28},{20,24},{24,20},{28,16},{1,13},{... | collective-permute-start | bytes 344072 | tf_op jit(solution)/shard_map/ppermute | solution.py:753
  55.1 2.2 %collective-permute-start.12 = (bf16[448,128]{1,0:T(8,128)(2,1)S(1)}, bf16[448,128]{1,0:T(8,128)(2,1)S(1)}, u32[]{:S(2)}, u32[]{:S(2)}) collective-permute-start(bf16[448,128]{1,0:T(8,128)(2,1)S(1)} %get-tuple-element.114.refs_0_), channel_id=1, source_target_pairs={{0,24},{4,28},{8,16},{12,20},{16,8},{20,12},{24,0},{28,4},{1,25},{... | collective-permute-start | bytes 344072 | tf_op jit(solution)/shard_map/ppermute | solution.py:753
  57.3 0.3 collective-permute-start.11
  57.6 1.9 %collective-permute-start.10 = (bf16[448,128]{1,0:T(8,128)(2,1)S(1)}, bf16[448,128]{1,0:T(8,128)(2,1)S(1)}, u32[]{:S(2)}, u32[]{:S(2)}) collective-permute-start(bf16[448,128]{1,0:T(8,128)(2,1)S(1)} %get-tuple-element.114.refs_0_), channel_id=1, source_target_pairs={{0,8},{4,12},{8,0},{12,4},{16,24},{20,28},{24,16},{28,20},{1,9},{5... | collective-permute-start | bytes 344072 | tf_op jit(solution)/shard_map/ppermute | solution.py:753
  59.5 0.9 %collective-permute-start.13 = (bf16[384,128]{1,0:T(8,128)(2,1)S(1)}, bf16[384,128]{1,0:T(8,128)(2,1)S(1)}, u32[]{:S(2)}, u32[]{:S(2)}) collective-permute-start(bf16[384,128]{1,0:T(8,128)(2,1)S(1)} %get-tuple-element.111.mine), channel_id=1, source_target_pairs={{0,4},{4,0},{8,12},{12,8},{16,20},{20,16},{24,28},{28,24},{1,5},{5... | collective-permute-start | bytes 294920 | tf_op jit(solution)/shard_map/ppermute | solution.py:753
  60.4 2.7 %shard_map.218 = bf16[16,256,512]{2,1,0:T(8,128)(2,1)} custom-call(s32[34]{0:T(128)S(1)} %get-tuple-element.72.meta, bf16[2304,512]{1,0:T(8,128)(2,1)S(1)} %get-tuple-element.98.own, bf16[2304,512]{1,0:T(8,128)(2,1)S(1)} %collective-permute-done.8.other), custom_call_target="tpu_custom_call" | custom-call | bytes 40000000 | tf_op jit(solution)/shard_map/pallas_call | solution.py:589
  63.2 4.4 %shard_map.219 = (f32[16,256,512]{2,1,0:T(8,128)}, bf16[8,256,512]{2,1,0:T(8,128)(2,1)S(1)}) custom-call(s32[34]{0:T(128)S(1)} %get-tuple-element.72.meta, bf16[8,256,512]{2,1,0:T(8,128)(2,1)S(1)} %get-tuple-element.89.cot, f32[8,4,288,128]{3,2,1,0:T(8,128)S(1)} %get-tuple-element.112.cgp, f32[16,512]{1,0:T(8,128)S(1)} %get-tuple-element.83.consts), custom_call_target="tpu_custom_call" | custom-call | bytes 40000000 | tf_op jit(solution)/shard_map/pallas_call | solution.py:641
  67.6 0.0 collective-permute-done.13.theirs
  67.6 0.0 collective-permute-done.14.far_1
  67.6 0.0 collective-permute-done.12.refs_3_
  67.6 0.4 collective-permute-done.11.refs_2_
  68.1 0.0 collective-permute-done.10.refs_1_.near_1
  68.1 0.0 collective-permute-start.16
  68.1 1.8 %collective-permute-start.15 = (bf16[832,128]{1,0:T(8,128)(2,1)S(1)}, bf16[832,128]{1,0:T(8,128)(2,1)S(1)}, u32[]{:S(2)}, u32[]{:S(2)}) collective-permute-start(bf16[832,128]{1,0:T(8,128)(2,1)S(1)} %shard_map.220.near), channel_id=1, source_target_pairs={{0,4},{4,0},{8,12},{12,8},{16,20},{20,16},{24,28},{28,24},{1,5},{5... | collective-permute-start | bytes 638984 | tf_op jit(solution)/shard_map/ppermute | solution.py:753
  69.9 2.3 %collective-permute-done.16.other = bf16[8,256,512]{2,1,0:T(8,128)(2,1)S(1)} collective-permute-done((bf16[8,256,512]{2,1,0:T(8,128)(2,1)S(1)}, bf16[8,256,512]{2,1,0:T(8,128)(2,1)S(1)}, u32[]{:S(2)}, u32[]{:S(2)}) %collective-permute-start.16) | collective-permute-done | bytes 2097184 | tf_op jit(solution)/shard_map/ppermute | solution.py:748
  72.2 2.6 %shard_map.221 = f32[16,256,512]{2,1,0:T(8,128)} custom-call(s32[34]{0:T(128)S(1)} %get-tuple-element.72.meta, bf16[8,256,512]{2,1,0:T(8,128)(2,1)S(1)} %collective-permute-done.16.other, f32[16,256,512]{2,1,0:T(8,128)} %get-tuple-element.119.gtok_in), custom_call_target="tpu_custom_call", output_to_operand_aliasing={{}: (2, {})} | custom-call | bytes 20000000 | tf_op jit(solution)/shard_map/pallas_call | solution.py:661
  74.9 1.0 %collective-permute-done.15.far = bf16[832,128]{1,0:T(8,128)(2,1)S(1)} collective-permute-done((bf16[832,128]{1,0:T(8,128)(2,1)S(1)}, bf16[832,128]{1,0:T(8,128)(2,1)S(1)}, u32[]{:S(2)}, u32[]{:S(2)}) %collective-permute-start.15) | collective-permute-done | bytes 213024 | tf_op jit(solution)/shard_map/ppermute | solution.py:753
  75.9 1.9 %shard_map.222 = (f32[7,512]{1,0:T(8,128)}, f32[512]{0:T(512)}, f32[2,512]{1,0:T(2,128)}, f32[2,512]{1,0:T(2,128)}, f32[512,384]{1,0:T(8,128)}, /*index=5*/f32[3...) custom-call(s32[34]{0:T(128)S(1)} %get-tuple-element.72.meta, bf16[384,128]{1,0:T(8,128)(2,1)S(1)} %get-tuple-element.111.mine, ...), custom_call_target="tpu_custom_call" | custom-call | tf_op jit(solution)/shard_map/pallas_call | solution.py:739
  (2 shorter events, 0.0 us)
Async XLA Ops:
  1.9 3.1 %collective-permute-start = (bf16[3088,128]{1,0:T(8,128)(2,1)S(1)}, bf16[3088,128]{1,0:T(8,128)(2,1)S(1)}, u32[]{:S(2)}, u32[]{:S(2)}) collective-permute-start(bf16[3088,128]{1,0:T(8,128)(2,1)S(1)} %shard_map.212.buf_a), channel_id=1, source_target_pairs={{0,1},{1,0},{2,3},{3,2},{4,5},{5,4},{6,7},{7,6},{8,9},{9,8},{10,11... | collective-permute-start | bytes 2371592 | tf_op jit(solution)/shard_map/ppermute | solution.py:748
  2.4 20.8 %collective-permute-start.3 = (bf16[3088,128]{1,0:T(8,128)(2,1)S(1)}, bf16[3088,128]{1,0:T(8,128)(2,1)S(1)}, u32[]{:S(2)}, u32[]{:S(2)}) collective-permute-start(bf16[3088,128]{1,0:T(8,128)(2,1)S(1)} %shard_map.212.buf_a), channel_id=1, source_target_pairs={{0,2},{1,3},{2,0},{3,1},{4,6},{5,7},{6,4},{7,5},{8,10},{9,11},{10,... | collective-permute-start | bytes 2371592 | tf_op jit(solution)/shard_map/ppermute | solution.py:748
  22.6 2.4 %collective-permute-start.1 = (bf16[3072,128]{1,0:T(8,128)(2,1)S(1)}, bf16[3072,128]{1,0:T(8,128)(2,1)S(1)}, u32[]{:S(2)}, u32[]{:S(2)}) collective-permute-start(bf16[3072,128]{1,0:T(8,128)(2,1)S(1)} %get-tuple-element.74), channel_id=1, source_target_pairs={{0,1},{1,0},{2,3},{3,2},{4,5},{5,4},{6,7},{7,6},{8,9},{9,8},{10,11... | collective-permute-start | bytes 2359304 | tf_op jit(solution)/shard_map/ppermute | solution.py:748
  23.2 3.5 %collective-permute-start.4 = (bf16[3088,128]{1,0:T(8,128)(2,1)S(1)}, bf16[3088,128]{1,0:T(8,128)(2,1)S(1)}, u32[]{:S(2)}, u32[]{:S(2)}) collective-permute-start(bf16[3088,128]{1,0:T(8,128)(2,1)S(1)} %collective-permute-done.3.buf_c), channel_id=1, source_target_pairs={{0,1},{1,0},{2,3},{3,2},{4,5},{5,4},{6,7},{7,6},{8,9},{9,8},{10,11... | collective-permute-start | bytes 2371592 | tf_op jit(solution)/shard_map/ppermute | solution.py:748
  25.7 12.4 %collective-permute-start.2 = (bf16[1536,128]{1,0:T(8,128)(2,1)S(1)}, bf16[1536,128]{1,0:T(8,128)(2,1)S(1)}, u32[]{:S(2)}, u32[]{:S(2)}) collective-permute-start(bf16[1536,128]{1,0:T(8,128)(2,1)S(1)} %get-tuple-element.76), channel_id=1, source_target_pairs={{0,4},{4,0},{8,12},{12,8},{16,20},{20,16},{24,28},{28,24},{1,5},{5... | collective-permute-start | bytes 1179656 | tf_op jit(solution)/shard_map/ppermute | solution.py:753
  38.1 14.6 %collective-permute-start.8 = (bf16[2304,512]{1,0:T(8,128)(2,1)S(1)}, bf16[2304,512]{1,0:T(8,128)(2,1)S(1)}, u32[]{:S(2)}, u32[]{:S(2)}) collective-permute-start(bf16[2304,512]{1,0:T(8,128)(2,1)S(1)} %get-tuple-element.98.own), channel_id=1, source_target_pairs={{0,1},{1,0},{2,3},{3,2},{4,5},{5,4},{6,7},{7,6},{8,9},{9,8},{10,11... | collective-permute-start | bytes 7077896 | tf_op jit(solution)/shard_map/ppermute | solution.py:748
  38.4 13.6 %collective-permute-start.7 = (bf16[384,128]{1,0:T(8,128)(2,1)S(1)}, bf16[384,128]{1,0:T(8,128)(2,1)S(1)}, u32[]{:S(2)}, u32[]{:S(2)}) collective-permute-start(bf16[384,128]{1,0:T(8,128)(2,1)S(1)} %get-tuple-element.135), channel_id=1, source_target_pairs={{0,24},{4,28},{8,16},{12,20},{16,8},{20,12},{24,0},{28,4},{1,25},{... | collective-permute-start | bytes 294920 | tf_op jit(solution)/shard_map/ppermute | solution.py:753
  43.4 9.3 %collective-permute-start.6 = (bf16[384,128]{1,0:T(8,128)(2,1)S(1)}, bf16[384,128]{1,0:T(8,128)(2,1)S(1)}, u32[]{:S(2)}, u32[]{:S(2)}) collective-permute-start(bf16[384,128]{1,0:T(8,128)(2,1)S(1)} %get-tuple-element.136), channel_id=1, source_target_pairs={{0,16},{4,20},{8,24},{12,28},{16,0},{20,4},{24,8},{28,12},{1,17},{... | collective-permute-start | bytes 294920 | tf_op jit(solution)/shard_map/ppermute | solution.py:753
  44.1 8.6 %collective-permute-start.5 = (bf16[384,128]{1,0:T(8,128)(2,1)S(1)}, bf16[384,128]{1,0:T(8,128)(2,1)S(1)}, u32[]{:S(2)}, u32[]{:S(2)}) collective-permute-start(bf16[384,128]{1,0:T(8,128)(2,1)S(1)} %get-tuple-element.137), channel_id=1, source_target_pairs={{0,8},{4,12},{8,0},{12,4},{16,24},{20,28},{24,16},{28,20},{1,9},{5... | collective-permute-start | bytes 294920 | tf_op jit(solution)/shard_map/ppermute | solution.py:753
  52.7 1.2 %collective-permute-start.9 = (f32[16,512]{1,0:T(8,128)S(1)}, f32[16,512]{1,0:T(8,128)S(1)}, u32[]{:S(2)}, u32[]{:S(2)}) collective-permute-start(f32[16,512]{1,0:T(8,128)S(1)} %get-tuple-element.101), channel_id=1, source_target_pairs={{0,1},{1,0},{2,3},{3,2},{4,5},{5,4},{6,7},{7,6},{8,9},{9,8},{10,11... | collective-permute-start | bytes 98312 | tf_op jit(solution)/shard_map/ppermute | solution.py:748
  54.0 13.7 %collective-permute-start.14 = (bf16[448,128]{1,0:T(8,128)(2,1)S(1)}, bf16[448,128]{1,0:T(8,128)(2,1)S(1)}, u32[]{:S(2)}, u32[]{:S(2)}) collective-permute-start(bf16[448,128]{1,0:T(8,128)(2,1)S(1)} %get-tuple-element.114.refs_0_), channel_id=1, source_target_pairs={{0,12},{4,8},{8,4},{12,0},{16,28},{20,24},{24,20},{28,16},{1,13},{... | collective-permute-start | bytes 344072 | tf_op jit(solution)/shard_map/ppermute | solution.py:753
  55.1 12.5 %collective-permute-start.12 = (bf16[448,128]{1,0:T(8,128)(2,1)S(1)}, bf16[448,128]{1,0:T(8,128)(2,1)S(1)}, u32[]{:S(2)}, u32[]{:S(2)}) collective-permute-start(bf16[448,128]{1,0:T(8,128)(2,1)S(1)} %get-tuple-element.114.refs_0_), channel_id=1, source_target_pairs={{0,24},{4,28},{8,16},{12,20},{16,8},{20,12},{24,0},{28,4},{1,25},{... | collective-permute-start | bytes 344072 | tf_op jit(solution)/shard_map/ppermute | solution.py:753
  57.3 10.7 %collective-permute-start.11 = (bf16[448,128]{1,0:T(8,128)(2,1)S(1)}, bf16[448,128]{1,0:T(8,128)(2,1)S(1)}, u32[]{:S(2)}, u32[]{:S(2)}) collective-permute-start(bf16[448,128]{1,0:T(8,128)(2,1)S(1)} %get-tuple-element.114.refs_0_), channel_id=1, source_target_pairs={{0,16},{4,20},{8,24},{12,28},{16,0},{20,4},{24,8},{28,12},{1,17},{... | collective-permute-start | bytes 344072 | tf_op jit(solution)/shard_map/ppermute | solution.py:753
  57.6 10.5 %collective-permute-start.10 = (bf16[448,128]{1,0:T(8,128)(2,1)S(1)}, bf16[448,128]{1,0:T(8,128)(2,1)S(1)}, u32[]{:S(2)}, u32[]{:S(2)}) collective-permute-start(bf16[448,128]{1,0:T(8,128)(2,1)S(1)} %get-tuple-element.114.refs_0_), channel_id=1, source_target_pairs={{0,8},{4,12},{8,0},{12,4},{16,24},{20,28},{24,16},{28,20},{1,9},{5... | collective-permute-start | bytes 344072 | tf_op jit(solution)/shard_map/ppermute | solution.py:753
  59.5 8.1 %collective-permute-start.13 = (bf16[384,128]{1,0:T(8,128)(2,1)S(1)}, bf16[384,128]{1,0:T(8,128)(2,1)S(1)}, u32[]{:S(2)}, u32[]{:S(2)}) collective-permute-start(bf16[384,128]{1,0:T(8,128)(2,1)S(1)} %get-tuple-element.111.mine), channel_id=1, source_target_pairs={{0,4},{4,0},{8,12},{12,8},{16,20},{20,16},{24,28},{28,24},{1,5},{5... | collective-permute-start | bytes 294920 | tf_op jit(solution)/shard_map/ppermute | solution.py:753
  68.1 4.2 %collective-permute-start.16 = (bf16[8,256,512]{2,1,0:T(8,128)(2,1)S(1)}, bf16[8,256,512]{2,1,0:T(8,128)(2,1)S(1)}, u32[]{:S(2)}, u32[]{:S(2)}) collective-permute-start(bf16[8,256,512]{2,1,0:T(8,128)(2,1)S(1)} %get-tuple-element.118), channel_id=1, source_target_pairs={{0,1},{1,0},{2,3},{3,2},{4,5},{5,4},{6,7},{7,6},{8,9},{9,8},{10,11... | collective-permute-start | bytes 6291464 | tf_op jit(solution)/shard_map/ppermute | solution.py:748
  68.1 7.8 %collective-permute-start.15 = (bf16[832,128]{1,0:T(8,128)(2,1)S(1)}, bf16[832,128]{1,0:T(8,128)(2,1)S(1)}, u32[]{:S(2)}, u32[]{:S(2)}) collective-permute-start(bf16[832,128]{1,0:T(8,128)(2,1)S(1)} %shard_map.220.near), channel_id=1, source_target_pairs={{0,4},{4,0},{8,12},{12,8},{16,20},{20,16},{24,28},{28,24},{1,5},{5... | collective-permute-start | bytes 638984 | tf_op jit(solution)/shard_map/ppermute | solution.py:753

commit v14 on v12

--- a/solution.py
+++ b/solution.py
@@ -13,6 +13,7 @@
 LANES = 128
 PAD = 8
 CHUNK = 64
+FRONT_CHUNK = 32
 VMEM_LIMIT = 12 * 1024 * 1024
 
 
@@ -224,21 +225,21 @@
 
     def conv_step(i, acc, consts):
         scale, shift, gam, conv_bias, w = consts
-        r0 = i * CHUNK if isinstance(i, int) else pl.multiple_of(i * CHUNK, CHUNK)
-        here = pl.ds(r0, CHUNK)
-        live = (lax.broadcasted_iota(jnp.int32, (CHUNK, LANES), 0) + r0) < count
+        r0 = i * FRONT_CHUNK if isinstance(i, int) else pl.multiple_of(i * FRONT_CHUNK, FRONT_CHUNK)
+        here = pl.ds(r0, FRONT_CHUNK)
+        live = (lax.broadcasted_iota(jnp.int32, (FRONT_CHUNK, LANES), 0) + r0) < count
         convs = []
         for q in range(wq):
             conv = conv_bias[:, lane(q)]
             for k in range(taps):
-                conv = conv + w[k:k + 1, lane(q)] * pad[q, pl.ds(r0 + (PAD - half + k), CHUNK), :]
+                conv = conv + w[k:k + 1, lane(q)] * pad[q, pl.ds(r0 + (PAD - half + k), FRONT_CHUNK), :]
             convs.append(conv)
         mean = jnp.sum(sum(convs[1:], convs[0]), axis=-1, keepdims=True) * (1.0 / width)
         cents = [c - mean for c in convs]
         sq = [c * c for c in cents]
         var = jnp.sum(sum(sq[1:], sq[0]), axis=-1, keepdims=True) * (1.0 / width)
         istd = lax.rsqrt(var + EPS)
-        inv_s[here, :] = jnp.broadcast_to(istd, (CHUNK, LANES))
+        inv_s[here, :] = jnp.broadcast_to(istd, (FRONT_CHUNK, LANES))
         new = []
         for q in range(wq):
             normed = cents[q] * istd
@@ -300,10 +301,10 @@
         if with_tile:
             offs[n + 2] = done + 2
 
-    all_chunks = frames // CHUNK
-    short = count <= (all_chunks - 1) * CHUNK
+    all_chunks = frames // FRONT_CHUNK
+    short = count <= (all_chunks * 3 // 4) * FRONT_CHUNK
     for with_tile in (True, False):
-        for chunks in (all_chunks - 1, all_chunks):
+        for chunks in (all_chunks * 3 // 4, all_chunks):
             fits = short if chunks < all_chunks else jnp.logical_not(short)
             pl.when((ready == with_tile) & fits)(functools.partial(conv_with, chunks, with_tile))
 
@@ -487,7 +488,7 @@
         istd = inv[src, :]
         for q in range(wq):
             cg = istd * (ngs[q] - m1 - nrs[q] * m2)
-            cgp[s, q, pl.ds(pl.multiple_of(r0 + PAD, 8), size), :] = jnp.where(live, cg, 0.0)
+            cgp[s, q, pl.ds(pl.multiple_of(r0 + PAD, 8), size), :] = cg
         return tuple(new)
 
     def both_sizes(run, width_of_state, add):

time: 76.5 us -> 77.6 us (1.014)
  starting transfers between devices: 17.6 us -> 21.5 us
  Pallas kernels: 49.4 us -> 46.1 us
    ppermute x7, starting transfers between devices: 3.23 us -> 6.07 us  [swap(): return lax.ppermute(x, 'tp', [(i, i ^ step) for i in range(size)])]
    pallas_call x1, Pallas kernels: 16.8 us -> 15.5 us  [front(): pl.pallas_call(functools.partial(front_kernel, n), grid_spec=pl.GridSpec(...]
    pallas_call x1, Pallas kernels: 11 us -> 9.76 us  [mix(): pl.pallas_call(functools.partial(mix_kernel, n, taps), in_specs=[smem()]...]
    ppermute x10, starting transfers between devices: 14.4 us -> 15.4 us  [across(): return lax.ppermute(x, 'dp', [(i, i ^ step) for i in range(size)])]
  transfers between devices with their start and end apart: 17 -> 17, of which waited for: 7 -> 7; matrix products, arithmetic and copies ran while one was open for 0% -> 0% of each run, Pallas kernels for 60% -> 56%
where the time goes in v14:
time: 77.6 us; the launch traced here: 77 us
  Pallas kernels  46.1 us (59%)
  starting transfers between devices  21.5 us (28%)
  waiting for transfers between devices  8.49 us (11%)
  between operations  0.78 us (1%)
    pallas_call x1, Pallas kernels, front(): pl.pallas_call(functools.partial(front_kernel, n), grid_spec=pl.GridSpec(...  15.5 us
    ppermute x10, starting transfers between devices, across(): return lax.ppermute(x, 'dp', [(i, i ^ step) for i in range(size)])  15.4 us
    pallas_call x1, Pallas kernels, mix(): pl.pallas_call(functools.partial(mix_kernel, n, taps), in_specs=[smem()]...  9.76 us
    pallas_call x1, Pallas kernels, norm_grad(): pl.pallas_call(functools.partial(norm_grad_kernel, n, taps, rates), grid=...  7.23 us
    ppermute x7, starting transfers between devices, swap(): return lax.ppermute(x, 'tp', [(i, i ^ step) for i in range(size)])  6.07 us
    ppermute x7, waiting for transfers between devices, swap(): return lax.ppermute(x, 'tp', [(i, i ^ step) for i in range(size)])  6.02 us
    pallas_call x1, Pallas kernels, token_grad(): pl.pallas_call(functools.partial(token_grad_kernel, n, taps), grid=(n,),...  4.34 us
    pallas_call x1, Pallas kernels, place_out(): pl.pallas_call(functools.partial(place_out_kernel, n), in_specs=[smem(),...  2.73 us
  transfers between devices with their start and end apart: 17, of which 7 were waited for; matrix products, arithmetic and copies ran while one was open for 0% of the time, Pallas kernels for 56%

profile of v14, /device:TPU:0, one launch (start us, length us, event | category | flops | bytes accessed | tf_op | source)
XLA Modules:
  0.0 77.0 jit_solution(4074384363177089051)
XLA Ops:
  0.6 1.3 %shard_map.212.buf_a = bf16[3088,128]{1,0:T(8,128)(2,1)S(1)} custom-call(bf16[512,384]{1,0:T(8,128)(2,1)} %wi.1, bf16[384]{0:T(512)(128)(2,1)} %bi.1, bf16[384,512]{1,0:T(8,128)(2,1)} %wo.1), custom_call_target="tpu_custom_call" | custom-call | tf_op jit(solution)/shard_map/pallas_call | solution.py:111
  1.9 0.5 collective-permute-start
  2.4 2.6 %collective-permute-start.3 = (bf16[3088,128]{1,0:T(8,128)(2,1)S(1)}, bf16[3088,128]{1,0:T(8,128)(2,1)S(1)}, u32[]{:S(2)}, u32[]{:S(2)}) collective-permute-start(bf16[3088,128]{1,0:T(8,128)(2,1)S(1)} %shard_map.212.buf_a), channel_id=1, source_target_pairs={{0,2},{1,3},{2,0},{3,1},{4,6},{5,7},{6,4},{7,5},{8,10},{9,11},{10,... | collective-permute-start | bytes 2371592 | tf_op jit(solution)/shard_map/ppermute | solution.py:748
  5.0 0.0 collective-permute-done.buf_b
  5.0 15.5 %shard_map.213 = (bf16[2304,512]{1,0:T(8,128)(2,1)S(1)}, bf16[2304,512]{1,0:T(8,128)(2,1)S(1)}, bf16[2304,512]{1,0:T(8,128)(2,1)S(1)}, f32[2304,128]{1,0:T(8,128...) custom-call(s32[16]{0:T(128)} %counts_hbm.1, ...), custom_call_target="tpu_custom_call" | custom-call | tf_op jit(solution)/shard_map/pallas_call | solution.py:351
  20.5 1.8 %collective-permute-start.1 = (bf16[3072,128]{1,0:T(8,128)(2,1)S(1)}, bf16[3072,128]{1,0:T(8,128)(2,1)S(1)}, u32[]{:S(2)}, u32[]{:S(2)}) collective-permute-start(bf16[3072,128]{1,0:T(8,128)(2,1)S(1)} %get-tuple-element.74), channel_id=1, source_target_pairs={{0,1},{1,0},{2,3},{3,2},{4,5},{5,4},{6,7},{7,6},{8,9},{9,8},{10,11... | collective-permute-start | bytes 2359304 | tf_op jit(solution)/shard_map/ppermute | solution.py:748
  22.3 0.9 %collective-permute-done.3.buf_c = bf16[3088,128]{1,0:T(8,128)(2,1)S(1)} collective-permute-done((bf16[3088,128]{1,0:T(8,128)(2,1)S(1)}, bf16[3088,128]{1,0:T(8,128)(2,1)S(1)}, u32[]{:S(2)}, u32[]{:S(2)}) %collective-permute-start.3) | collective-permute-done | bytes 790560 | tf_op jit(solution)/shard_map/ppermute | solution.py:748
  23.2 0.0 collective-permute-start.4
  23.2 1.0 %collective-permute-done.1.recv = bf16[3072,128]{1,0:T(8,128)(2,1)S(1)} collective-permute-done((bf16[3072,128]{1,0:T(8,128)(2,1)S(1)}, bf16[3072,128]{1,0:T(8,128)(2,1)S(1)}, u32[]{:S(2)}, u32[]{:S(2)}) %collective-permute-start.1) | collective-permute-done | bytes 786464 | tf_op jit(solution)/shard_map/ppermute | solution.py:748
  24.2 0.7 shard_map.214
  24.9 2.3 %collective-permute-start.2 = (bf16[1536,128]{1,0:T(8,128)(2,1)S(1)}, bf16[1536,128]{1,0:T(8,128)(2,1)S(1)}, u32[]{:S(2)}, u32[]{:S(2)}) collective-permute-start(bf16[1536,128]{1,0:T(8,128)(2,1)S(1)} %get-tuple-element.76), channel_id=1, source_target_pairs={{0,4},{4,0},{8,12},{12,8},{16,20},{20,16},{24,28},{28,24},{1,5},{5... | collective-permute-start | bytes 1179656 | tf_op jit(solution)/shard_map/ppermute | solution.py:753
  27.3 0.0 collective-permute-done.4.buf_d
  27.3 9.8 %shard_map.215 = (f32[2304,512]{1,0:T(8,128)S(1)}, f32[2304,512]{1,0:T(8,128)S(1)}, bf16[2304,512]{1,0:T(8,128)(2,1)S(1)}) custom-call(s32[34]{0:T(128)S(1)} %get-tuple-element.72.meta, bf16[2304,512]{1,0:T(8,128)(2,1)S(1)} %get-tuple-element.77.ad, bf16[2304,512]{1,0:T(8,128)(2,1)S(1)} %get-tuple-element.78.low, ...), custom_call_target="tpu_custom_call" | custom-call | tf_op jit(solution)/shard_map/pallas_call | solution.py:436
  37.0 0.0 collective-permute-done.2
  37.0 1.2 %collective-permute-start.8 = (bf16[2304,512]{1,0:T(8,128)(2,1)S(1)}, bf16[2304,512]{1,0:T(8,128)(2,1)S(1)}, u32[]{:S(2)}, u32[]{:S(2)}) collective-permute-start(bf16[2304,512]{1,0:T(8,128)(2,1)S(1)} %get-tuple-element.98.own), channel_id=1, source_target_pairs={{0,1},{1,0},{2,3},{3,2},{4,5},{5,4},{6,7},{7,6},{8,9},{9,8},{10,11... | collective-permute-start | bytes 7077896 | tf_op jit(solution)/shard_map/ppermute | solution.py:748
  38.2 0.1 fusion
  38.3 4.2 %collective-permute-start.7 = (bf16[384,128]{1,0:T(8,128)(2,1)S(1)}, bf16[384,128]{1,0:T(8,128)(2,1)S(1)}, u32[]{:S(2)}, u32[]{:S(2)}) collective-permute-start(bf16[384,128]{1,0:T(8,128)(2,1)S(1)} %get-tuple-element.135), channel_id=1, source_target_pairs={{0,24},{4,28},{8,16},{12,20},{16,8},{20,12},{24,0},{28,4},{1,25},{... | collective-permute-start | bytes 294920 | tf_op jit(solution)/shard_map/ppermute | solution.py:753
  42.5 0.0 collective-permute-start.6
  42.5 0.6 collective-permute-start.5
  43.1 7.2 %shard_map.216 = (f32[8,4,288,128]{3,2,1,0:T(8,128)S(1)}, f32[16,512]{1,0:T(8,128)S(1)}, f32[16,512]{1,0:T(8,128)S(1)}) custom-call(s32[34]{0:T(128)S(1)} %get-tuple-element.72.meta, bf16[8,256,512]{2,1,0:T(8,128)(2,1)S(1)} %get-tuple-element.88.tok, bf16[8,256,512]{2,1,0:T(8,128)(2,1)S(1)} %get-tuple-element.89.cot, ...), custom_call_target="tpu_custom_call" | custom-call | bytes 40000000 | tf_op jit(solution)/shard_map/pallas_call | solution.py:556
  50.4 0.0 collective-permute-done.7.refs_2_
  50.4 0.8 %collective-permute-done.6.refs_1_ = bf16[384,128]{1,0:T(8,128)(2,1)S(1)} collective-permute-done((bf16[384,128]{1,0:T(8,128)(2,1)S(1)}, bf16[384,128]{1,0:T(8,128)(2,1)S(1)}, u32[]{:S(2)}, u32[]{:S(2)}) %collective-permute-start.6) | collective-permute-done | bytes 98336 | tf_op jit(solution)/shard_map/ppermute | solution.py:753
  51.2 0.0 collective-permute-done.5.refs_0_
  51.2 0.0 collective-permute-done.8.other
  51.2 0.0 collective-permute-start.9
  51.2 1.2 %collective-permute-done.9.recv = f32[16,512]{1,0:T(8,128)S(1)} collective-permute-done((f32[16,512]{1,0:T(8,128)S(1)}, f32[16,512]{1,0:T(8,128)S(1)}, u32[]{:S(2)}, u32[]{:S(2)}) %collective-permute-start.9) | collective-permute-done | bytes 32800 | tf_op jit(solution)/shard_map/ppermute | solution.py:748
  52.5 0.1 shard_map.217
  52.5 1.3 %collective-permute-start.14 = (bf16[448,128]{1,0:T(8,128)(2,1)S(1)}, bf16[448,128]{1,0:T(8,128)(2,1)S(1)}, u32[]{:S(2)}, u32[]{:S(2)}) collective-permute-start(bf16[448,128]{1,0:T(8,128)(2,1)S(1)} %get-tuple-element.114.refs_0_), channel_id=1, source_target_pairs={{0,12},{4,8},{8,4},{12,0},{16,28},{20,24},{24,20},{28,16},{1,13},{... | collective-permute-start | bytes 344072 | tf_op jit(solution)/shard_map/ppermute | solution.py:753
  53.8 2.1 %collective-permute-start.12 = (bf16[448,128]{1,0:T(8,128)(2,1)S(1)}, bf16[448,128]{1,0:T(8,128)(2,1)S(1)}, u32[]{:S(2)}, u32[]{:S(2)}) collective-permute-start(bf16[448,128]{1,0:T(8,128)(2,1)S(1)} %get-tuple-element.114.refs_0_), channel_id=1, source_target_pairs={{0,24},{4,28},{8,16},{12,20},{16,8},{20,12},{24,0},{28,4},{1,25},{... | collective-permute-start | bytes 344072 | tf_op jit(solution)/shard_map/ppermute | solution.py:753
  56.0 0.8 %collective-permute-start.11 = (bf16[448,128]{1,0:T(8,128)(2,1)S(1)}, bf16[448,128]{1,0:T(8,128)(2,1)S(1)}, u32[]{:S(2)}, u32[]{:S(2)}) collective-permute-start(bf16[448,128]{1,0:T(8,128)(2,1)S(1)} %get-tuple-element.114.refs_0_), channel_id=1, source_target_pairs={{0,16},{4,20},{8,24},{12,28},{16,0},{20,4},{24,8},{28,12},{1,17},{... | collective-permute-start | bytes 344072 | tf_op jit(solution)/shard_map/ppermute | solution.py:753
  56.8 1.5 %collective-permute-start.10 = (bf16[448,128]{1,0:T(8,128)(2,1)S(1)}, bf16[448,128]{1,0:T(8,128)(2,1)S(1)}, u32[]{:S(2)}, u32[]{:S(2)}) collective-permute-start(bf16[448,128]{1,0:T(8,128)(2,1)S(1)} %get-tuple-element.114.refs_0_), channel_id=1, source_target_pairs={{0,8},{4,12},{8,0},{12,4},{16,24},{20,28},{24,16},{28,20},{1,9},{5... | collective-permute-start | bytes 344072 | tf_op jit(solution)/shard_map/ppermute | solution.py:753
  58.2 1.3 %collective-permute-start.13 = (bf16[384,128]{1,0:T(8,128)(2,1)S(1)}, bf16[384,128]{1,0:T(8,128)(2,1)S(1)}, u32[]{:S(2)}, u32[]{:S(2)}) collective-permute-start(bf16[384,128]{1,0:T(8,128)(2,1)S(1)} %get-tuple-element.111.mine), channel_id=1, source_target_pairs={{0,4},{4,0},{8,12},{12,8},{16,20},{20,16},{24,28},{28,24},{1,5},{5... | collective-permute-start | bytes 294920 | tf_op jit(solution)/shard_map/ppermute | solution.py:753
  59.6 2.7 %shard_map.218 = bf16[16,256,512]{2,1,0:T(8,128)(2,1)} custom-call(s32[34]{0:T(128)S(1)} %get-tuple-element.72.meta, bf16[2304,512]{1,0:T(8,128)(2,1)S(1)} %get-tuple-element.98.own, bf16[2304,512]{1,0:T(8,128)(2,1)S(1)} %collective-permute-done.8.other), custom_call_target="tpu_custom_call" | custom-call | bytes 40000000 | tf_op jit(solution)/shard_map/pallas_call | solution.py:589
  62.3 4.3 %shard_map.219 = (f32[16,256,512]{2,1,0:T(8,128)}, bf16[8,256,512]{2,1,0:T(8,128)(2,1)S(1)}) custom-call(s32[34]{0:T(128)S(1)} %get-tuple-element.72.meta, bf16[8,256,512]{2,1,0:T(8,128)(2,1)S(1)} %get-tuple-element.89.cot, f32[8,4,288,128]{3,2,1,0:T(8,128)S(1)} %get-tuple-element.112.cgp, f32[16,512]{1,0:T(8,128)S(1)} %get-tuple-element.83.consts), custom_call_target="tpu_custom_call" | custom-call | bytes 40000000 | tf_op jit(solution)/shard_map/pallas_call | solution.py:641
  66.6 0.0 collective-permute-done.13.theirs
  66.7 0.0 collective-permute-done.14.far_1
  66.7 0.0 collective-permute-done.12.refs_3_
  66.7 0.6 collective-permute-done.11.refs_2_
  67.3 0.0 collective-permute-done.10.refs_1_.near_1
  67.3 0.0 collective-permute-start.16
  67.4 1.2 %collective-permute-start.15 = (bf16[832,128]{1,0:T(8,128)(2,1)S(1)}, bf16[832,128]{1,0:T(8,128)(2,1)S(1)}, u32[]{:S(2)}, u32[]{:S(2)}) collective-permute-start(bf16[832,128]{1,0:T(8,128)(2,1)S(1)} %shard_map.220.near), channel_id=1, source_target_pairs={{0,4},{4,0},{8,12},{12,8},{16,20},{20,16},{24,28},{28,24},{1,5},{5... | collective-permute-start | bytes 638984 | tf_op jit(solution)/shard_map/ppermute | solution.py:753
  68.6 2.9 %collective-permute-done.16.other = bf16[8,256,512]{2,1,0:T(8,128)(2,1)S(1)} collective-permute-done((bf16[8,256,512]{2,1,0:T(8,128)(2,1)S(1)}, bf16[8,256,512]{2,1,0:T(8,128)(2,1)S(1)}, u32[]{:S(2)}, u32[]{:S(2)}) %collective-permute-start.16) | collective-permute-done | bytes 2097184 | tf_op jit(solution)/shard_map/ppermute | solution.py:748
  71.5 2.6 %shard_map.221 = f32[16,256,512]{2,1,0:T(8,128)} custom-call(s32[34]{0:T(128)S(1)} %get-tuple-element.72.meta, bf16[8,256,512]{2,1,0:T(8,128)(2,1)S(1)} %collective-permute-done.16.other, f32[16,256,512]{2,1,0:T(8,128)} %get-tuple-element.119.gtok_in), custom_call_target="tpu_custom_call", output_to_operand_aliasing={{}: (2, {})} | custom-call | bytes 20000000 | tf_op jit(solution)/shard_map/pallas_call | solution.py:661
  74.1 1.0 %collective-permute-done.15.far = bf16[832,128]{1,0:T(8,128)(2,1)S(1)} collective-permute-done((bf16[832,128]{1,0:T(8,128)(2,1)S(1)}, bf16[832,128]{1,0:T(8,128)(2,1)S(1)}, u32[]{:S(2)}, u32[]{:S(2)}) %collective-permute-start.15) | collective-permute-done | bytes 213024 | tf_op jit(solution)/shard_map/ppermute | solution.py:753
  75.1 1.9 %shard_map.222 = (f32[7,512]{1,0:T(8,128)}, f32[512]{0:T(512)}, f32[2,512]{1,0:T(2,128)}, f32[2,512]{1,0:T(2,128)}, f32[512,384]{1,0:T(8,128)}, /*index=5*/f32[3...) custom-call(s32[34]{0:T(128)S(1)} %get-tuple-element.72.meta, bf16[384,128]{1,0:T(8,128)(2,1)S(1)} %get-tuple-element.111.mine, ...), custom_call_target="tpu_custom_call" | custom-call | tf_op jit(solution)/shard_map/pallas_call | solution.py:739
  (2 shorter events, 0.0 us)
Async XLA Ops:
  1.9 3.1 %collective-permute-start = (bf16[3088,128]{1,0:T(8,128)(2,1)S(1)}, bf16[3088,128]{1,0:T(8,128)(2,1)S(1)}, u32[]{:S(2)}, u32[]{:S(2)}) collective-permute-start(bf16[3088,128]{1,0:T(8,128)(2,1)S(1)} %shard_map.212.buf_a), channel_id=1, source_target_pairs={{0,1},{1,0},{2,3},{3,2},{4,5},{5,4},{6,7},{7,6},{8,9},{9,8},{10,11... | collective-permute-start | bytes 2371592 | tf_op jit(solution)/shard_map/ppermute | solution.py:748
  2.4 20.8 %collective-permute-start.3 = (bf16[3088,128]{1,0:T(8,128)(2,1)S(1)}, bf16[3088,128]{1,0:T(8,128)(2,1)S(1)}, u32[]{:S(2)}, u32[]{:S(2)}) collective-permute-start(bf16[3088,128]{1,0:T(8,128)(2,1)S(1)} %shard_map.212.buf_a), channel_id=1, source_target_pairs={{0,2},{1,3},{2,0},{3,1},{4,6},{5,7},{6,4},{7,5},{8,10},{9,11},{10,... | collective-permute-start | bytes 2371592 | tf_op jit(solution)/shard_map/ppermute | solution.py:748
  20.5 3.7 %collective-permute-start.1 = (bf16[3072,128]{1,0:T(8,128)(2,1)S(1)}, bf16[3072,128]{1,0:T(8,128)(2,1)S(1)}, u32[]{:S(2)}, u32[]{:S(2)}) collective-permute-start(bf16[3072,128]{1,0:T(8,128)(2,1)S(1)} %get-tuple-element.74), channel_id=1, source_target_pairs={{0,1},{1,0},{2,3},{3,2},{4,5},{5,4},{6,7},{7,6},{8,9},{9,8},{10,11... | collective-permute-start | bytes 2359304 | tf_op jit(solution)/shard_map/ppermute | solution.py:748
  23.2 4.0 %collective-permute-start.4 = (bf16[3088,128]{1,0:T(8,128)(2,1)S(1)}, bf16[3088,128]{1,0:T(8,128)(2,1)S(1)}, u32[]{:S(2)}, u32[]{:S(2)}) collective-permute-start(bf16[3088,128]{1,0:T(8,128)(2,1)S(1)} %collective-permute-done.3.buf_c), channel_id=1, source_target_pairs={{0,1},{1,0},{2,3},{3,2},{4,5},{5,4},{6,7},{7,6},{8,9},{9,8},{10,11... | collective-permute-start | bytes 2371592 | tf_op jit(solution)/shard_map/ppermute | solution.py:748
  24.9 12.1 %collective-permute-start.2 = (bf16[1536,128]{1,0:T(8,128)(2,1)S(1)}, bf16[1536,128]{1,0:T(8,128)(2,1)S(1)}, u32[]{:S(2)}, u32[]{:S(2)}) collective-permute-start(bf16[1536,128]{1,0:T(8,128)(2,1)S(1)} %get-tuple-element.76), channel_id=1, source_target_pairs={{0,4},{4,0},{8,12},{12,8},{16,20},{20,16},{24,28},{28,24},{1,5},{5... | collective-permute-start | bytes 1179656 | tf_op jit(solution)/shard_map/ppermute | solution.py:753
  37.0 14.2 %collective-permute-start.8 = (bf16[2304,512]{1,0:T(8,128)(2,1)S(1)}, bf16[2304,512]{1,0:T(8,128)(2,1)S(1)}, u32[]{:S(2)}, u32[]{:S(2)}) collective-permute-start(bf16[2304,512]{1,0:T(8,128)(2,1)S(1)} %get-tuple-element.98.own), channel_id=1, source_target_pairs={{0,1},{1,0},{2,3},{3,2},{4,5},{5,4},{6,7},{7,6},{8,9},{9,8},{10,11... | collective-permute-start | bytes 7077896 | tf_op jit(solution)/shard_map/ppermute | solution.py:748
  38.3 12.0 %collective-permute-start.7 = (bf16[384,128]{1,0:T(8,128)(2,1)S(1)}, bf16[384,128]{1,0:T(8,128)(2,1)S(1)}, u32[]{:S(2)}, u32[]{:S(2)}) collective-permute-start(bf16[384,128]{1,0:T(8,128)(2,1)S(1)} %get-tuple-element.135), channel_id=1, source_target_pairs={{0,24},{4,28},{8,16},{12,20},{16,8},{20,12},{24,0},{28,4},{1,25},{... | collective-permute-start | bytes 294920 | tf_op jit(solution)/shard_map/ppermute | solution.py:753
  42.5 8.7 %collective-permute-start.6 = (bf16[384,128]{1,0:T(8,128)(2,1)S(1)}, bf16[384,128]{1,0:T(8,128)(2,1)S(1)}, u32[]{:S(2)}, u32[]{:S(2)}) collective-permute-start(bf16[384,128]{1,0:T(8,128)(2,1)S(1)} %get-tuple-element.136), channel_id=1, source_target_pairs={{0,16},{4,20},{8,24},{12,28},{16,0},{20,4},{24,8},{28,12},{1,17},{... | collective-permute-start | bytes 294920 | tf_op jit(solution)/shard_map/ppermute | solution.py:753
  42.5 8.7 %collective-permute-start.5 = (bf16[384,128]{1,0:T(8,128)(2,1)S(1)}, bf16[384,128]{1,0:T(8,128)(2,1)S(1)}, u32[]{:S(2)}, u32[]{:S(2)}) collective-permute-start(bf16[384,128]{1,0:T(8,128)(2,1)S(1)} %get-tuple-element.137), channel_id=1, source_target_pairs={{0,8},{4,12},{8,0},{12,4},{16,24},{20,28},{24,16},{28,20},{1,9},{5... | collective-permute-start | bytes 294920 | tf_op jit(solution)/shard_map/ppermute | solution.py:753
  51.2 1.2 %collective-permute-start.9 = (f32[16,512]{1,0:T(8,128)S(1)}, f32[16,512]{1,0:T(8,128)S(1)}, u32[]{:S(2)}, u32[]{:S(2)}) collective-permute-start(f32[16,512]{1,0:T(8,128)S(1)} %get-tuple-element.101), channel_id=1, source_target_pairs={{0,1},{1,0},{2,3},{3,2},{4,5},{5,4},{6,7},{7,6},{8,9},{9,8},{10,11... | collective-permute-start | bytes 98312 | tf_op jit(solution)/shard_map/ppermute | solution.py:748
  52.5 14.2 %collective-permute-start.14 = (bf16[448,128]{1,0:T(8,128)(2,1)S(1)}, bf16[448,128]{1,0:T(8,128)(2,1)S(1)}, u32[]{:S(2)}, u32[]{:S(2)}) collective-permute-start(bf16[448,128]{1,0:T(8,128)(2,1)S(1)} %get-tuple-element.114.refs_0_), channel_id=1, source_target_pairs={{0,12},{4,8},{8,4},{12,0},{16,28},{20,24},{24,20},{28,16},{1,13},{... | collective-permute-start | bytes 344072 | tf_op jit(solution)/shard_map/ppermute | solution.py:753
  53.8 12.8 %collective-permute-start.12 = (bf16[448,128]{1,0:T(8,128)(2,1)S(1)}, bf16[448,128]{1,0:T(8,128)(2,1)S(1)}, u32[]{:S(2)}, u32[]{:S(2)}) collective-permute-start(bf16[448,128]{1,0:T(8,128)(2,1)S(1)} %get-tuple-element.114.refs_0_), channel_id=1, source_target_pairs={{0,24},{4,28},{8,16},{12,20},{16,8},{20,12},{24,0},{28,4},{1,25},{... | collective-permute-start | bytes 344072 | tf_op jit(solution)/shard_map/ppermute | solution.py:753
  56.0 11.4 %collective-permute-start.11 = (bf16[448,128]{1,0:T(8,128)(2,1)S(1)}, bf16[448,128]{1,0:T(8,128)(2,1)S(1)}, u32[]{:S(2)}, u32[]{:S(2)}) collective-permute-start(bf16[448,128]{1,0:T(8,128)(2,1)S(1)} %get-tuple-element.114.refs_0_), channel_id=1, source_target_pairs={{0,16},{4,20},{8,24},{12,28},{16,0},{20,4},{24,8},{28,12},{1,17},{... | collective-permute-start | bytes 344072 | tf_op jit(solution)/shard_map/ppermute | solution.py:753
  56.8 10.6 %collective-permute-start.10 = (bf16[448,128]{1,0:T(8,128)(2,1)S(1)}, bf16[448,128]{1,0:T(8,128)(2,1)S(1)}, u32[]{:S(2)}, u32[]{:S(2)}) collective-permute-start(bf16[448,128]{1,0:T(8,128)(2,1)S(1)} %get-tuple-element.114.refs_0_), channel_id=1, source_target_pairs={{0,8},{4,12},{8,0},{12,4},{16,24},{20,28},{24,16},{28,20},{1,9},{5... | collective-permute-start | bytes 344072 | tf_op jit(solution)/shard_map/ppermute | solution.py:753
  58.2 8.4 %collective-permute-start.13 = (bf16[384,128]{1,0:T(8,128)(2,1)S(1)}, bf16[384,128]{1,0:T(8,128)(2,1)S(1)}, u32[]{:S(2)}, u32[]{:S(2)}) collective-permute-start(bf16[384,128]{1,0:T(8,128)(2,1)S(1)} %get-tuple-element.111.mine), channel_id=1, source_target_pairs={{0,4},{4,0},{8,12},{12,8},{16,20},{20,16},{24,28},{28,24},{1,5},{5... | collective-permute-start | bytes 294920 | tf_op jit(solution)/shard_map/ppermute | solution.py:753
  67.3 4.2 %collective-permute-start.16 = (bf16[8,256,512]{2,1,0:T(8,128)(2,1)S(1)}, bf16[8,256,512]{2,1,0:T(8,128)(2,1)S(1)}, u32[]{:S(2)}, u32[]{:S(2)}) collective-permute-start(bf16[8,256,512]{2,1,0:T(8,128)(2,1)S(1)} %get-tuple-element.118), channel_id=1, source_target_pairs={{0,1},{1,0},{2,3},{3,2},{4,5},{5,4},{6,7},{7,6},{8,9},{9,8},{10,11... | collective-permute-start | bytes 6291464 | tf_op jit(solution)/shard_map/ppermute | solution.py:748
  67.4 7.7 %collective-permute-start.15 = (bf16[832,128]{1,0:T(8,128)(2,1)S(1)}, bf16[832,128]{1,0:T(8,128)(2,1)S(1)}, u32[]{:S(2)}, u32[]{:S(2)}) collective-permute-start(bf16[832,128]{1,0:T(8,128)(2,1)S(1)} %shard_map.220.near), channel_id=1, source_target_pairs={{0,4},{4,0},{8,12},{12,8},{16,20},{20,16},{24,28},{28,24},{1,5},{5... | collective-permute-start | bytes 638984 | tf_op jit(solution)/shard_map/ppermute | solution.py:753

commit v15 on v14

--- a/solution.py
+++ b/solution.py
@@ -785,7 +785,7 @@
     m = pieces[0].shape[0]
     near = [message] + [across(message, 2 * d) for d in range(1, dp // 2)]
     theirs = across(mine, 1)
-    far_1 = across(message, 3)
+    far_1 = across(mine, 3)
     out = place_out(meta, out_own, out_b, n, tokens.shape[1])
     cgp, out = lax.optimization_barrier((cgp, out))
     gtok, gtok_own = token_grad(meta, cot, cgp, consts, taps)

time: 77.6 us -> 76.9 us (level)
  Pallas kernels: 46.1 us -> 49.3 us
  starting transfers between devices: 21.5 us -> 19.1 us
  waiting for transfers between devices: 8.49 us -> 7.07 us
    ppermute x7, starting transfers between devices: 6.07 us -> 3.52 us  [swap(): return lax.ppermute(x, 'tp', [(i, i ^ step) for i in range(size)])]
    ppermute x10, waiting for transfers between devices: 2.46 us -> 0.97 us  [across(): return lax.ppermute(x, 'dp', [(i, i ^ step) for i in range(size)])]
    pallas_call x1, Pallas kernels: 15.5 us -> 16.9 us  [front(): pl.pallas_call(functools.partial(front_kernel, n), grid_spec=pl.GridSpec(...]
    pallas_call x1, Pallas kernels: 9.76 us -> 11 us  [mix(): pl.pallas_call(functools.partial(mix_kernel, n, taps), in_specs=[smem()]...]
  transfers between devices with their start and end apart: 17 -> 17, of which waited for: 7 -> 5; matrix products, arithmetic and copies ran while one was open for 0% -> 0% of each run, Pallas kernels for 56% -> 60%
where the time goes in v15:
time: 76.9 us; the launch traced here: 76.4 us
  Pallas kernels  49.3 us (64%)
  starting transfers between devices  19.1 us (25%)
  waiting for transfers between devices  7.07 us (9%)
  between operations  0.84 us (1%)
    pallas_call x1, Pallas kernels, front(): pl.pallas_call(functools.partial(front_kernel, n), grid_spec=pl.GridSpec(...  16.9 us
    ppermute x10, starting transfers between devices, across(): return lax.ppermute(x, 'dp', [(i, i ^ step) for i in range(size)])  15.6 us
    pallas_call x1, Pallas kernels, mix(): pl.pallas_call(functools.partial(mix_kernel, n, taps), in_specs=[smem()]...  11 us
    pallas_call x1, Pallas kernels, norm_grad(): pl.pallas_call(functools.partial(norm_grad_kernel, n, taps, rates), grid=...  7.57 us
    ppermute x7, waiting for transfers between devices, swap(): return lax.ppermute(x, 'tp', [(i, i ^ step) for i in range(size)])  6.09 us
    pallas_call x1, Pallas kernels, token_grad(): pl.pallas_call(functools.partial(token_grad_kernel, n, taps), grid=(n,),...  4.51 us
    ppermute x7, starting transfers between devices, swap(): return lax.ppermute(x, 'tp', [(i, i ^ step) for i in range(size)])  3.52 us
    pallas_call x1, Pallas kernels, place_out(): pl.pallas_call(functools.partial(place_out_kernel, n), in_specs=[smem(),...  2.73 us
  transfers between devices with their start and end apart: 17, of which 5 were waited for; matrix products, arithmetic and copies ran while one was open for 0% of the time, Pallas kernels for 60%

profile of v15, /device:TPU:0, one launch (start us, length us, event | category | flops | bytes accessed | tf_op | source)
XLA Modules:
  0.0 76.4 jit_solution(6946565253202321645)
XLA Ops:
  0.6 1.3 %shard_map.212.buf_a = bf16[3088,128]{1,0:T(8,128)(2,1)S(1)} custom-call(bf16[512,384]{1,0:T(8,128)(2,1)} %wi.1, bf16[384]{0:T(512)(128)(2,1)} %bi.1, bf16[384,512]{1,0:T(8,128)(2,1)} %wo.1), custom_call_target="tpu_custom_call" | custom-call | tf_op jit(solution)/shard_map/pallas_call | solution.py:111
  1.9 0.5 collective-permute-start
  2.4 2.6 %collective-permute-start.3 = (bf16[3088,128]{1,0:T(8,128)(2,1)S(1)}, bf16[3088,128]{1,0:T(8,128)(2,1)S(1)}, u32[]{:S(2)}, u32[]{:S(2)}) collective-permute-start(bf16[3088,128]{1,0:T(8,128)(2,1)S(1)} %shard_map.212.buf_a), channel_id=1, source_target_pairs={{0,2},{1,3},{2,0},{3,1},{4,6},{5,7},{6,4},{7,5},{8,10},{9,11},{10,... | collective-permute-start | bytes 2371592 | tf_op jit(solution)/shard_map/ppermute | solution.py:748
  5.0 0.0 collective-permute-done.buf_b
  5.0 16.9 %shard_map.213 = (bf16[2304,512]{1,0:T(8,128)(2,1)S(1)}, bf16[2304,512]{1,0:T(8,128)(2,1)S(1)}, bf16[2304,512]{1,0:T(8,128)(2,1)S(1)}, f32[2304,128]{1,0:T(8,128...) custom-call(s32[16]{0:T(128)} %counts_hbm.1, ...), custom_call_target="tpu_custom_call" | custom-call | tf_op jit(solution)/shard_map/pallas_call | solution.py:351
  21.9 0.2 collective-permute-start.1
  22.2 1.1 %collective-permute-done.3.buf_c = bf16[3088,128]{1,0:T(8,128)(2,1)S(1)} collective-permute-done((bf16[3088,128]{1,0:T(8,128)(2,1)S(1)}, bf16[3088,128]{1,0:T(8,128)(2,1)S(1)}, u32[]{:S(2)}, u32[]{:S(2)}) %collective-permute-start.3) | collective-permute-done | bytes 790560 | tf_op jit(solution)/shard_map/ppermute | solution.py:748
  23.2 0.0 collective-permute-start.4
  23.2 1.1 %collective-permute-done.1.recv = bf16[3072,128]{1,0:T(8,128)(2,1)S(1)} collective-permute-done((bf16[3072,128]{1,0:T(8,128)(2,1)S(1)}, bf16[3072,128]{1,0:T(8,128)(2,1)S(1)}, u32[]{:S(2)}, u32[]{:S(2)}) %collective-permute-start.1) | collective-permute-done | bytes 786464 | tf_op jit(solution)/shard_map/ppermute | solution.py:748
  24.3 0.7 shard_map.214
  25.0 2.3 %collective-permute-start.2 = (bf16[1536,128]{1,0:T(8,128)(2,1)S(1)}, bf16[1536,128]{1,0:T(8,128)(2,1)S(1)}, u32[]{:S(2)}, u32[]{:S(2)}) collective-permute-start(bf16[1536,128]{1,0:T(8,128)(2,1)S(1)} %get-tuple-element.76), channel_id=1, source_target_pairs={{0,4},{4,0},{8,12},{12,8},{16,20},{20,16},{24,28},{28,24},{1,5},{5... | collective-permute-start | bytes 1179656 | tf_op jit(solution)/shard_map/ppermute | solution.py:753
  27.3 0.0 collective-permute-done.4.buf_d
  27.3 11.0 %shard_map.215 = (f32[2304,512]{1,0:T(8,128)S(1)}, f32[2304,512]{1,0:T(8,128)S(1)}, bf16[2304,512]{1,0:T(8,128)(2,1)S(1)}) custom-call(s32[34]{0:T(128)S(1)} %get-tuple-element.72.meta, bf16[2304,512]{1,0:T(8,128)(2,1)S(1)} %get-tuple-element.77.ad, bf16[2304,512]{1,0:T(8,128)(2,1)S(1)} %get-tuple-element.78.low, ...), custom_call_target="tpu_custom_call" | custom-call | tf_op jit(solution)/shard_map/pallas_call | solution.py:436
  38.2 0.0 collective-permute-done.2
  38.3 0.1 collective-permute-start.8
  38.3 0.1 fusion
  38.5 3.8 %collective-permute-start.7 = (bf16[384,128]{1,0:T(8,128)(2,1)S(1)}, bf16[384,128]{1,0:T(8,128)(2,1)S(1)}, u32[]{:S(2)}, u32[]{:S(2)}) collective-permute-start(bf16[384,128]{1,0:T(8,128)(2,1)S(1)} %get-tuple-element.135), channel_id=1, source_target_pairs={{0,24},{4,28},{8,16},{12,20},{16,8},{20,12},{24,0},{28,4},{1,25},{... | collective-permute-start | bytes 294920 | tf_op jit(solution)/shard_map/ppermute | solution.py:753
  42.3 0.0 collective-permute-start.6
  42.3 0.6 collective-permute-start.5
  43.0 7.6 %shard_map.216 = (f32[8,4,288,128]{3,2,1,0:T(8,128)S(1)}, f32[16,512]{1,0:T(8,128)S(1)}, f32[16,512]{1,0:T(8,128)S(1)}) custom-call(s32[34]{0:T(128)S(1)} %get-tuple-element.72.meta, bf16[8,256,512]{2,1,0:T(8,128)(2,1)S(1)} %get-tuple-element.88.tok, bf16[8,256,512]{2,1,0:T(8,128)(2,1)S(1)} %get-tuple-element.89.cot, ...), custom_call_target="tpu_custom_call" | custom-call | bytes 40000000 | tf_op jit(solution)/shard_map/pallas_call | solution.py:556
  50.5 0.0 collective-permute-done.7.refs_2_
  50.6 0.0 collective-permute-done.6.refs_1_
  50.6 0.0 collective-permute-done.5.refs_0_
  50.6 0.0 collective-permute-done.8.other
  50.6 0.1 collective-permute-start.9
  50.7 1.2 %collective-permute-done.9.recv = f32[16,512]{1,0:T(8,128)S(1)} collective-permute-done((f32[16,512]{1,0:T(8,128)S(1)}, f32[16,512]{1,0:T(8,128)S(1)}, u32[]{:S(2)}, u32[]{:S(2)}) %collective-permute-start.9) | collective-permute-done | bytes 32800 | tf_op jit(solution)/shard_map/ppermute | solution.py:748
  51.9 0.1 shard_map.217
  51.9 4.0 %collective-permute-start.12 = (bf16[448,128]{1,0:T(8,128)(2,1)S(1)}, bf16[448,128]{1,0:T(8,128)(2,1)S(1)}, u32[]{:S(2)}, u32[]{:S(2)}) collective-permute-start(bf16[448,128]{1,0:T(8,128)(2,1)S(1)} %get-tuple-element.114.refs_0_), channel_id=1, source_target_pairs={{0,24},{4,28},{8,16},{12,20},{16,8},{20,12},{24,0},{28,4},{1,25},{... | collective-permute-start | bytes 344072 | tf_op jit(solution)/shard_map/ppermute | solution.py:753
  55.9 0.0 collective-permute-start.11
  55.9 0.6 collective-permute-start.10
  56.5 1.3 %collective-permute-start.14 = (bf16[384,128]{1,0:T(8,128)(2,1)S(1)}, bf16[384,128]{1,0:T(8,128)(2,1)S(1)}, u32[]{:S(2)}, u32[]{:S(2)}) collective-permute-start(bf16[384,128]{1,0:T(8,128)(2,1)S(1)} %get-tuple-element.111.mine), channel_id=1, source_target_pairs={{0,12},{4,8},{8,4},{12,0},{16,28},{20,24},{24,20},{28,16},{1,13},{... | collective-permute-start | bytes 294920 | tf_op jit(solution)/shard_map/ppermute | solution.py:753
  57.9 1.5 %collective-permute-start.13 = (bf16[384,128]{1,0:T(8,128)(2,1)S(1)}, bf16[384,128]{1,0:T(8,128)(2,1)S(1)}, u32[]{:S(2)}, u32[]{:S(2)}) collective-permute-start(bf16[384,128]{1,0:T(8,128)(2,1)S(1)} %get-tuple-element.111.mine), channel_id=1, source_target_pairs={{0,4},{4,0},{8,12},{12,8},{16,20},{20,16},{24,28},{28,24},{1,5},{5... | collective-permute-start | bytes 294920 | tf_op jit(solution)/shard_map/ppermute | solution.py:753
  59.4 2.7 %shard_map.218 = bf16[16,256,512]{2,1,0:T(8,128)(2,1)} custom-call(s32[34]{0:T(128)S(1)} %get-tuple-element.72.meta, bf16[2304,512]{1,0:T(8,128)(2,1)S(1)} %get-tuple-element.98.own, bf16[2304,512]{1,0:T(8,128)(2,1)S(1)} %collective-permute-done.8.other), custom_call_target="tpu_custom_call" | custom-call | bytes 40000000 | tf_op jit(solution)/shard_map/pallas_call | solution.py:589
  62.1 4.5 %shard_map.219 = (f32[16,256,512]{2,1,0:T(8,128)}, bf16[8,256,512]{2,1,0:T(8,128)(2,1)S(1)}) custom-call(s32[34]{0:T(128)S(1)} %get-tuple-element.72.meta, bf16[8,256,512]{2,1,0:T(8,128)(2,1)S(1)} %get-tuple-element.89.cot, f32[8,4,288,128]{3,2,1,0:T(8,128)S(1)} %get-tuple-element.112.cgp, f32[16,512]{1,0:T(8,128)S(1)} %get-tuple-element.83.consts), custom_call_target="tpu_custom_call" | custom-call | bytes 40000000 | tf_op jit(solution)/shard_map/pallas_call | solution.py:641
  66.6 0.0 collective-permute-done.14.far_1
  66.7 0.0 collective-permute-done.13.theirs
  66.7 0.0 collective-permute-done.12.refs_3_
  66.7 0.0 collective-permute-done.11.refs_2_
  66.7 0.0 collective-permute-done.10.refs_1_.near_1
  66.7 0.1 collective-permute-start.16
  66.8 1.3 %collective-permute-start.15 = (bf16[832,128]{1,0:T(8,128)(2,1)S(1)}, bf16[832,128]{1,0:T(8,128)(2,1)S(1)}, u32[]{:S(2)}, u32[]{:S(2)}) collective-permute-start(bf16[832,128]{1,0:T(8,128)(2,1)S(1)} %shard_map.220.near), channel_id=1, source_target_pairs={{0,4},{4,0},{8,12},{12,8},{16,20},{20,16},{24,28},{28,24},{1,5},{5... | collective-permute-start | bytes 638984 | tf_op jit(solution)/shard_map/ppermute | solution.py:753
  68.2 2.8 %collective-permute-done.16.other = bf16[8,256,512]{2,1,0:T(8,128)(2,1)S(1)} collective-permute-done((bf16[8,256,512]{2,1,0:T(8,128)(2,1)S(1)}, bf16[8,256,512]{2,1,0:T(8,128)(2,1)S(1)}, u32[]{:S(2)}, u32[]{:S(2)}) %collective-permute-start.16) | collective-permute-done | bytes 2097184 | tf_op jit(solution)/shard_map/ppermute | solution.py:748
  70.9 2.6 %shard_map.221 = f32[16,256,512]{2,1,0:T(8,128)} custom-call(s32[34]{0:T(128)S(1)} %get-tuple-element.72.meta, bf16[8,256,512]{2,1,0:T(8,128)(2,1)S(1)} %collective-permute-done.16.other, f32[16,256,512]{2,1,0:T(8,128)} %get-tuple-element.119.gtok_in), custom_call_target="tpu_custom_call", output_to_operand_aliasing={{}: (2, {})} | custom-call | bytes 20000000 | tf_op jit(solution)/shard_map/pallas_call | solution.py:661
  73.6 1.0 %collective-permute-done.15.far = bf16[832,128]{1,0:T(8,128)(2,1)S(1)} collective-permute-done((bf16[832,128]{1,0:T(8,128)(2,1)S(1)}, bf16[832,128]{1,0:T(8,128)(2,1)S(1)}, u32[]{:S(2)}, u32[]{:S(2)}) %collective-permute-start.15) | collective-permute-done | bytes 213024 | tf_op jit(solution)/shard_map/ppermute | solution.py:753
  74.5 1.9 %shard_map.222 = (f32[7,512]{1,0:T(8,128)}, f32[512]{0:T(512)}, f32[2,512]{1,0:T(2,128)}, f32[2,512]{1,0:T(2,128)}, f32[512,384]{1,0:T(8,128)}, /*index=5*/f32[3...) custom-call(s32[34]{0:T(128)S(1)} %get-tuple-element.72.meta, bf16[384,128]{1,0:T(8,128)(2,1)S(1)} %get-tuple-element.111.mine, ...), custom_call_target="tpu_custom_call" | custom-call | tf_op jit(solution)/shard_map/pallas_call | solution.py:739
  (2 shorter events, 0.0 us)
Async XLA Ops:
  1.9 3.1 %collective-permute-start = (bf16[3088,128]{1,0:T(8,128)(2,1)S(1)}, bf16[3088,128]{1,0:T(8,128)(2,1)S(1)}, u32[]{:S(2)}, u32[]{:S(2)}) collective-permute-start(bf16[3088,128]{1,0:T(8,128)(2,1)S(1)} %shard_map.212.buf_a), channel_id=1, source_target_pairs={{0,1},{1,0},{2,3},{3,2},{4,5},{5,4},{6,7},{7,6},{8,9},{9,8},{10,11... | collective-permute-start | bytes 2371592 | tf_op jit(solution)/shard_map/ppermute | solution.py:748
  2.4 20.8 %collective-permute-start.3 = (bf16[3088,128]{1,0:T(8,128)(2,1)S(1)}, bf16[3088,128]{1,0:T(8,128)(2,1)S(1)}, u32[]{:S(2)}, u32[]{:S(2)}) collective-permute-start(bf16[3088,128]{1,0:T(8,128)(2,1)S(1)} %shard_map.212.buf_a), channel_id=1, source_target_pairs={{0,2},{1,3},{2,0},{3,1},{4,6},{5,7},{6,4},{7,5},{8,10},{9,11},{10,... | collective-permute-start | bytes 2371592 | tf_op jit(solution)/shard_map/ppermute | solution.py:748
  21.9 2.4 %collective-permute-start.1 = (bf16[3072,128]{1,0:T(8,128)(2,1)S(1)}, bf16[3072,128]{1,0:T(8,128)(2,1)S(1)}, u32[]{:S(2)}, u32[]{:S(2)}) collective-permute-start(bf16[3072,128]{1,0:T(8,128)(2,1)S(1)} %get-tuple-element.74), channel_id=1, source_target_pairs={{0,1},{1,0},{2,3},{3,2},{4,5},{5,4},{6,7},{7,6},{8,9},{9,8},{10,11... | collective-permute-start | bytes 2359304 | tf_op jit(solution)/shard_map/ppermute | solution.py:748
  23.2 4.0 %collective-permute-start.4 = (bf16[3088,128]{1,0:T(8,128)(2,1)S(1)}, bf16[3088,128]{1,0:T(8,128)(2,1)S(1)}, u32[]{:S(2)}, u32[]{:S(2)}) collective-permute-start(bf16[3088,128]{1,0:T(8,128)(2,1)S(1)} %collective-permute-done.3.buf_c), channel_id=1, source_target_pairs={{0,1},{1,0},{2,3},{3,2},{4,5},{5,4},{6,7},{7,6},{8,9},{9,8},{10,11... | collective-permute-start | bytes 2371592 | tf_op jit(solution)/shard_map/ppermute | solution.py:748
  25.0 13.3 %collective-permute-start.2 = (bf16[1536,128]{1,0:T(8,128)(2,1)S(1)}, bf16[1536,128]{1,0:T(8,128)(2,1)S(1)}, u32[]{:S(2)}, u32[]{:S(2)}) collective-permute-start(bf16[1536,128]{1,0:T(8,128)(2,1)S(1)} %get-tuple-element.76), channel_id=1, source_target_pairs={{0,4},{4,0},{8,12},{12,8},{16,20},{20,16},{24,28},{28,24},{1,5},{5... | collective-permute-start | bytes 1179656 | tf_op jit(solution)/shard_map/ppermute | solution.py:753
  38.3 12.3 %collective-permute-start.8 = (bf16[2304,512]{1,0:T(8,128)(2,1)S(1)}, bf16[2304,512]{1,0:T(8,128)(2,1)S(1)}, u32[]{:S(2)}, u32[]{:S(2)}) collective-permute-start(bf16[2304,512]{1,0:T(8,128)(2,1)S(1)} %get-tuple-element.98.own), channel_id=1, source_target_pairs={{0,1},{1,0},{2,3},{3,2},{4,5},{5,4},{6,7},{7,6},{8,9},{9,8},{10,11... | collective-permute-start | bytes 7077896 | tf_op jit(solution)/shard_map/ppermute | solution.py:748
  38.5 12.1 %collective-permute-start.7 = (bf16[384,128]{1,0:T(8,128)(2,1)S(1)}, bf16[384,128]{1,0:T(8,128)(2,1)S(1)}, u32[]{:S(2)}, u32[]{:S(2)}) collective-permute-start(bf16[384,128]{1,0:T(8,128)(2,1)S(1)} %get-tuple-element.135), channel_id=1, source_target_pairs={{0,24},{4,28},{8,16},{12,20},{16,8},{20,12},{24,0},{28,4},{1,25},{... | collective-permute-start | bytes 294920 | tf_op jit(solution)/shard_map/ppermute | solution.py:753
  42.3 8.2 %collective-permute-start.6 = (bf16[384,128]{1,0:T(8,128)(2,1)S(1)}, bf16[384,128]{1,0:T(8,128)(2,1)S(1)}, u32[]{:S(2)}, u32[]{:S(2)}) collective-permute-start(bf16[384,128]{1,0:T(8,128)(2,1)S(1)} %get-tuple-element.136), channel_id=1, source_target_pairs={{0,16},{4,20},{8,24},{12,28},{16,0},{20,4},{24,8},{28,12},{1,17},{... | collective-permute-start | bytes 294920 | tf_op jit(solution)/shard_map/ppermute | solution.py:753
  42.3 8.2 %collective-permute-start.5 = (bf16[384,128]{1,0:T(8,128)(2,1)S(1)}, bf16[384,128]{1,0:T(8,128)(2,1)S(1)}, u32[]{:S(2)}, u32[]{:S(2)}) collective-permute-start(bf16[384,128]{1,0:T(8,128)(2,1)S(1)} %get-tuple-element.137), channel_id=1, source_target_pairs={{0,8},{4,12},{8,0},{12,4},{16,24},{20,28},{24,16},{28,20},{1,9},{5... | collective-permute-start | bytes 294920 | tf_op jit(solution)/shard_map/ppermute | solution.py:753
  50.6 1.3 %collective-permute-start.9 = (f32[16,512]{1,0:T(8,128)S(1)}, f32[16,512]{1,0:T(8,128)S(1)}, u32[]{:S(2)}, u32[]{:S(2)}) collective-permute-start(f32[16,512]{1,0:T(8,128)S(1)} %get-tuple-element.101), channel_id=1, source_target_pairs={{0,1},{1,0},{2,3},{3,2},{4,5},{5,4},{6,7},{7,6},{8,9},{9,8},{10,11... | collective-permute-start | bytes 98312 | tf_op jit(solution)/shard_map/ppermute | solution.py:748
  51.9 14.8 %collective-permute-start.12 = (bf16[448,128]{1,0:T(8,128)(2,1)S(1)}, bf16[448,128]{1,0:T(8,128)(2,1)S(1)}, u32[]{:S(2)}, u32[]{:S(2)}) collective-permute-start(bf16[448,128]{1,0:T(8,128)(2,1)S(1)} %get-tuple-element.114.refs_0_), channel_id=1, source_target_pairs={{0,24},{4,28},{8,16},{12,20},{16,8},{20,12},{24,0},{28,4},{1,25},{... | collective-permute-start | bytes 344072 | tf_op jit(solution)/shard_map/ppermute | solution.py:753
  55.9 10.8 %collective-permute-start.11 = (bf16[448,128]{1,0:T(8,128)(2,1)S(1)}, bf16[448,128]{1,0:T(8,128)(2,1)S(1)}, u32[]{:S(2)}, u32[]{:S(2)}) collective-permute-start(bf16[448,128]{1,0:T(8,128)(2,1)S(1)} %get-tuple-element.114.refs_0_), channel_id=1, source_target_pairs={{0,16},{4,20},{8,24},{12,28},{16,0},{20,4},{24,8},{28,12},{1,17},{... | collective-permute-start | bytes 344072 | tf_op jit(solution)/shard_map/ppermute | solution.py:753
  55.9 10.8 %collective-permute-start.10 = (bf16[448,128]{1,0:T(8,128)(2,1)S(1)}, bf16[448,128]{1,0:T(8,128)(2,1)S(1)}, u32[]{:S(2)}, u32[]{:S(2)}) collective-permute-start(bf16[448,128]{1,0:T(8,128)(2,1)S(1)} %get-tuple-element.114.refs_0_), channel_id=1, source_target_pairs={{0,8},{4,12},{8,0},{12,4},{16,24},{20,28},{24,16},{28,20},{1,9},{5... | collective-permute-start | bytes 344072 | tf_op jit(solution)/shard_map/ppermute | solution.py:753
  56.5 10.1 %collective-permute-start.14 = (bf16[384,128]{1,0:T(8,128)(2,1)S(1)}, bf16[384,128]{1,0:T(8,128)(2,1)S(1)}, u32[]{:S(2)}, u32[]{:S(2)}) collective-permute-start(bf16[384,128]{1,0:T(8,128)(2,1)S(1)} %get-tuple-element.111.mine), channel_id=1, source_target_pairs={{0,12},{4,8},{8,4},{12,0},{16,28},{20,24},{24,20},{28,16},{1,13},{... | collective-permute-start | bytes 294920 | tf_op jit(solution)/shard_map/ppermute | solution.py:753
  57.9 8.8 %collective-permute-start.13 = (bf16[384,128]{1,0:T(8,128)(2,1)S(1)}, bf16[384,128]{1,0:T(8,128)(2,1)S(1)}, u32[]{:S(2)}, u32[]{:S(2)}) collective-permute-start(bf16[384,128]{1,0:T(8,128)(2,1)S(1)} %get-tuple-element.111.mine), channel_id=1, source_target_pairs={{0,4},{4,0},{8,12},{12,8},{16,20},{20,16},{24,28},{28,24},{1,5},{5... | collective-permute-start | bytes 294920 | tf_op jit(solution)/shard_map/ppermute | solution.py:753
  66.7 4.2 %collective-permute-start.16 = (bf16[8,256,512]{2,1,0:T(8,128)(2,1)S(1)}, bf16[8,256,512]{2,1,0:T(8,128)(2,1)S(1)}, u32[]{:S(2)}, u32[]{:S(2)}) collective-permute-start(bf16[8,256,512]{2,1,0:T(8,128)(2,1)S(1)} %get-tuple-element.118), channel_id=1, source_target_pairs={{0,1},{1,0},{2,3},{3,2},{4,5},{5,4},{6,7},{7,6},{8,9},{9,8},{10,11... | collective-permute-start | bytes 6291464 | tf_op jit(solution)/shard_map/ppermute | solution.py:748
  66.8 7.7 %collective-permute-start.15 = (bf16[832,128]{1,0:T(8,128)(2,1)S(1)}, bf16[832,128]{1,0:T(8,128)(2,1)S(1)}, u32[]{:S(2)}, u32[]{:S(2)}) collective-permute-start(bf16[832,128]{1,0:T(8,128)(2,1)S(1)} %shard_map.220.near), channel_id=1, source_target_pairs={{0,4},{4,0},{8,12},{12,8},{16,20},{20,16},{24,28},{28,24},{1,5},{5... | collective-permute-start | bytes 638984 | tf_op jit(solution)/shard_map/ppermute | solution.py:753

commit v16 on v15

--- a/solution.py
+++ b/solution.py
@@ -414,19 +414,19 @@
     spread_bias(bias, bias_row)
     rest(first, branch[first, :], ag[first, :])
 
-    def pair(t, _):
-        at = pl.ds(pl.multiple_of((2 * t + 1) * TILE, TILE), 2 * TILE)
+    def block(start, tiles):
+        at = pl.ds(pl.multiple_of(start * TILE, TILE), tiles * TILE)
         rest(at, *own(at))
+
+    def triple(t, _):
+        block(3 * t + 1, 3)
         return 0
 
     left = offs[n + 1] - 1
-    pairs = lax.shift_right_arithmetic(left, 1)
-    lax.fori_loop(0, pairs, pair, 0)
-
-    @pl.when(left > 2 * pairs)
-    def _():
-        at = pl.ds(pl.multiple_of(left * TILE, TILE), TILE)
-        rest(at, *own(at))
+    triples = lax.div(left, 3)
+    lax.fori_loop(0, triples, triple, 0)
+    for tiles in (1, 2):
+        pl.when(left - 3 * triples == tiles)(functools.partial(block, 3 * triples + 1, tiles))
 
 
 def mix(meta, ad, low, act, pre, win, wout, consts, tokp, buf_c, buf_d, n, taps):

time: 76.9 us -> 76.4 us (level)
  starting transfers between devices: 19.1 us -> 17.7 us
  waiting for transfers between devices: 7.07 us -> 8.33 us
    ppermute x10, starting transfers between devices: 15.6 us -> 14.3 us  [across(): return lax.ppermute(x, 'dp', [(i, i ^ step) for i in range(size)])]
    ppermute x10, waiting for transfers between devices: 0.97 us -> 1.8 us  [across(): return lax.ppermute(x, 'dp', [(i, i ^ step) for i in range(size)])]
  transfers between devices with their start and end apart: 17 -> 17, of which waited for: 5 -> 7; matrix products, arithmetic and copies ran while one was open for 0% -> 0% of each run, Pallas kernels for 60% -> 60%
where the time goes in v16:
time: 76.4 us; the launch traced here: 76.2 us
  Pallas kernels  49.3 us (65%)
  starting transfers between devices  17.7 us (23%)
  waiting for transfers between devices  8.33 us (11%)
  between operations  0.79 us (1%)
    pallas_call x1, Pallas kernels, front(): pl.pallas_call(functools.partial(front_kernel, n), grid_spec=pl.GridSpec(...  17.1 us
    ppermute x10, starting transfers between devices, across(): return lax.ppermute(x, 'dp', [(i, i ^ step) for i in range(size)])  14.3 us
    pallas_call x1, Pallas kernels, mix(): pl.pallas_call(functools.partial(mix_kernel, n, taps), in_specs=[smem()]...  10.6 us
    pallas_call x1, Pallas kernels, norm_grad(): pl.pallas_call(functools.partial(norm_grad_kernel, n, taps, rates), grid=...  7.73 us
    ppermute x7, waiting for transfers between devices, swap(): return lax.ppermute(x, 'tp', [(i, i ^ step) for i in range(size)])  6.53 us
    pallas_call x1, Pallas kernels, token_grad(): pl.pallas_call(functools.partial(token_grad_kernel, n, taps), grid=(n,),...  4.59 us
    ppermute x7, starting transfers between devices, swap(): return lax.ppermute(x, 'tp', [(i, i ^ step) for i in range(size)])  3.31 us
    pallas_call x1, Pallas kernels, place_out(): pl.pallas_call(functools.partial(place_out_kernel, n), in_specs=[smem(),...  2.73 us
  transfers between devices with their start and end apart: 17, of which 7 were waited for; matrix products, arithmetic and copies ran while one was open for 0% of the time, Pallas kernels for 60%

profile of v16, /device:TPU:0, one launch (start us, length us, event | category | flops | bytes accessed | tf_op | source)
XLA Modules:
  0.0 76.2 jit_solution(1238445101805019458)
XLA Ops:
  0.6 1.3 %shard_map.212.buf_a = bf16[3088,128]{1,0:T(8,128)(2,1)S(1)} custom-call(bf16[512,384]{1,0:T(8,128)(2,1)} %wi.1, bf16[384]{0:T(512)(128)(2,1)} %bi.1, bf16[384,512]{1,0:T(8,128)(2,1)} %wo.1), custom_call_target="tpu_custom_call" | custom-call | tf_op jit(solution)/shard_map/pallas_call | solution.py:111
  1.9 0.5 collective-permute-start
  2.4 2.6 %collective-permute-start.3 = (bf16[3088,128]{1,0:T(8,128)(2,1)S(1)}, bf16[3088,128]{1,0:T(8,128)(2,1)S(1)}, u32[]{:S(2)}, u32[]{:S(2)}) collective-permute-start(bf16[3088,128]{1,0:T(8,128)(2,1)S(1)} %shard_map.212.buf_a), channel_id=1, source_target_pairs={{0,2},{1,3},{2,0},{3,1},{4,6},{5,7},{6,4},{7,5},{8,10},{9,11},{10,... | collective-permute-start | bytes 2371592 | tf_op jit(solution)/shard_map/ppermute | solution.py:748
  5.0 0.0 collective-permute-done.buf_b
  5.0 17.1 %shard_map.213 = (bf16[2304,512]{1,0:T(8,128)(2,1)S(1)}, bf16[2304,512]{1,0:T(8,128)(2,1)S(1)}, bf16[2304,512]{1,0:T(8,128)(2,1)S(1)}, f32[2304,128]{1,0:T(8,128...) custom-call(s32[16]{0:T(128)} %counts_hbm.1, ...), custom_call_target="tpu_custom_call" | custom-call | tf_op jit(solution)/shard_map/pallas_call | solution.py:351
  22.1 0.1 collective-permute-start.1
  22.2 1.1 %collective-permute-done.3.buf_c = bf16[3088,128]{1,0:T(8,128)(2,1)S(1)} collective-permute-done((bf16[3088,128]{1,0:T(8,128)(2,1)S(1)}, bf16[3088,128]{1,0:T(8,128)(2,1)S(1)}, u32[]{:S(2)}, u32[]{:S(2)}) %collective-permute-start.3) | collective-permute-done | bytes 790560 | tf_op jit(solution)/shard_map/ppermute | solution.py:748
  23.2 0.0 collective-permute-start.4
  23.2 1.2 %collective-permute-done.1.recv = bf16[3072,128]{1,0:T(8,128)(2,1)S(1)} collective-permute-done((bf16[3072,128]{1,0:T(8,128)(2,1)S(1)}, bf16[3072,128]{1,0:T(8,128)(2,1)S(1)}, u32[]{:S(2)}, u32[]{:S(2)}) %collective-permute-start.1) | collective-permute-done | bytes 786464 | tf_op jit(solution)/shard_map/ppermute | solution.py:748
  24.4 0.7 shard_map.214
  25.1 2.1 %collective-permute-start.2 = (bf16[1536,128]{1,0:T(8,128)(2,1)S(1)}, bf16[1536,128]{1,0:T(8,128)(2,1)S(1)}, u32[]{:S(2)}, u32[]{:S(2)}) collective-permute-start(bf16[1536,128]{1,0:T(8,128)(2,1)S(1)} %get-tuple-element.76), channel_id=1, source_target_pairs={{0,4},{4,0},{8,12},{12,8},{16,20},{20,16},{24,28},{28,24},{1,5},{5... | collective-permute-start | bytes 1179656 | tf_op jit(solution)/shard_map/ppermute | solution.py:753
  27.3 0.0 collective-permute-done.4.buf_d
  27.3 10.6 %shard_map.215 = (f32[2304,512]{1,0:T(8,128)S(1)}, f32[2304,512]{1,0:T(8,128)S(1)}, bf16[2304,512]{1,0:T(8,128)(2,1)S(1)}) custom-call(s32[34]{0:T(128)S(1)} %get-tuple-element.72.meta, bf16[2304,512]{1,0:T(8,128)(2,1)S(1)} %get-tuple-element.77.ad, bf16[2304,512]{1,0:T(8,128)(2,1)S(1)} %get-tuple-element.78.low, ...), custom_call_target="tpu_custom_call" | custom-call | tf_op jit(solution)/shard_map/pallas_call | solution.py:436
  37.9 0.0 collective-permute-done.2
  37.9 0.1 collective-permute-start.8
  38.0 0.1 fusion
  38.1 3.7 %collective-permute-start.7 = (bf16[384,128]{1,0:T(8,128)(2,1)S(1)}, bf16[384,128]{1,0:T(8,128)(2,1)S(1)}, u32[]{:S(2)}, u32[]{:S(2)}) collective-permute-start(bf16[384,128]{1,0:T(8,128)(2,1)S(1)} %get-tuple-element.135), channel_id=1, source_target_pairs={{0,24},{4,28},{8,16},{12,20},{16,8},{20,12},{24,0},{28,4},{1,25},{... | collective-permute-start | bytes 294920 | tf_op jit(solution)/shard_map/ppermute | solution.py:753
  41.8 0.0 collective-permute-start.6
  41.8 0.8 %collective-permute-start.5 = (bf16[384,128]{1,0:T(8,128)(2,1)S(1)}, bf16[384,128]{1,0:T(8,128)(2,1)S(1)}, u32[]{:S(2)}, u32[]{:S(2)}) collective-permute-start(bf16[384,128]{1,0:T(8,128)(2,1)S(1)} %get-tuple-element.137), channel_id=1, source_target_pairs={{0,8},{4,12},{8,0},{12,4},{16,24},{20,28},{24,16},{28,20},{1,9},{5... | collective-permute-start | bytes 294920 | tf_op jit(solution)/shard_map/ppermute | solution.py:753
  42.5 7.7 %shard_map.216 = (f32[8,4,288,128]{3,2,1,0:T(8,128)S(1)}, f32[16,512]{1,0:T(8,128)S(1)}, f32[16,512]{1,0:T(8,128)S(1)}) custom-call(s32[34]{0:T(128)S(1)} %get-tuple-element.72.meta, bf16[8,256,512]{2,1,0:T(8,128)(2,1)S(1)} %get-tuple-element.88.tok, bf16[8,256,512]{2,1,0:T(8,128)(2,1)S(1)} %get-tuple-element.89.cot, ...), custom_call_target="tpu_custom_call" | custom-call | bytes 40000000 | tf_op jit(solution)/shard_map/pallas_call | solution.py:556
  50.3 0.0 collective-permute-done.7.refs_2_
  50.3 0.2 collective-permute-done.6.refs_1_
  50.5 0.0 collective-permute-done.5.refs_0_
  50.5 0.0 collective-permute-done.8.other
  50.5 0.0 collective-permute-start.9
  50.5 1.2 %collective-permute-done.9.recv = f32[16,512]{1,0:T(8,128)S(1)} collective-permute-done((f32[16,512]{1,0:T(8,128)S(1)}, f32[16,512]{1,0:T(8,128)S(1)}, u32[]{:S(2)}, u32[]{:S(2)}) %collective-permute-start.9) | collective-permute-done | bytes 32800 | tf_op jit(solution)/shard_map/ppermute | solution.py:748
  51.7 0.1 shard_map.217
  51.8 3.2 %collective-permute-start.12 = (bf16[448,128]{1,0:T(8,128)(2,1)S(1)}, bf16[448,128]{1,0:T(8,128)(2,1)S(1)}, u32[]{:S(2)}, u32[]{:S(2)}) collective-permute-start(bf16[448,128]{1,0:T(8,128)(2,1)S(1)} %get-tuple-element.114.refs_0_), channel_id=1, source_target_pairs={{0,24},{4,28},{8,16},{12,20},{16,8},{20,12},{24,0},{28,4},{1,25},{... | collective-permute-start | bytes 344072 | tf_op jit(solution)/shard_map/ppermute | solution.py:753
  55.0 0.0 collective-permute-start.11
  55.0 1.2 %collective-permute-start.10 = (bf16[448,128]{1,0:T(8,128)(2,1)S(1)}, bf16[448,128]{1,0:T(8,128)(2,1)S(1)}, u32[]{:S(2)}, u32[]{:S(2)}) collective-permute-start(bf16[448,128]{1,0:T(8,128)(2,1)S(1)} %get-tuple-element.114.refs_0_), channel_id=1, source_target_pairs={{0,8},{4,12},{8,0},{12,4},{16,24},{20,28},{24,16},{28,20},{1,9},{5... | collective-permute-start | bytes 344072 | tf_op jit(solution)/shard_map/ppermute | solution.py:753
  56.2 0.9 %collective-permute-start.14 = (bf16[384,128]{1,0:T(8,128)(2,1)S(1)}, bf16[384,128]{1,0:T(8,128)(2,1)S(1)}, u32[]{:S(2)}, u32[]{:S(2)}) collective-permute-start(bf16[384,128]{1,0:T(8,128)(2,1)S(1)} %get-tuple-element.111.mine), channel_id=1, source_target_pairs={{0,12},{4,8},{8,4},{12,0},{16,28},{20,24},{24,20},{28,16},{1,13},{... | collective-permute-start | bytes 294920 | tf_op jit(solution)/shard_map/ppermute | solution.py:753
  57.1 1.4 %collective-permute-start.13 = (bf16[384,128]{1,0:T(8,128)(2,1)S(1)}, bf16[384,128]{1,0:T(8,128)(2,1)S(1)}, u32[]{:S(2)}, u32[]{:S(2)}) collective-permute-start(bf16[384,128]{1,0:T(8,128)(2,1)S(1)} %get-tuple-element.111.mine), channel_id=1, source_target_pairs={{0,4},{4,0},{8,12},{12,8},{16,20},{20,16},{24,28},{28,24},{1,5},{5... | collective-permute-start | bytes 294920 | tf_op jit(solution)/shard_map/ppermute | solution.py:753
  58.5 2.7 %shard_map.218 = bf16[16,256,512]{2,1,0:T(8,128)(2,1)} custom-call(s32[34]{0:T(128)S(1)} %get-tuple-element.72.meta, bf16[2304,512]{1,0:T(8,128)(2,1)S(1)} %get-tuple-element.98.own, bf16[2304,512]{1,0:T(8,128)(2,1)S(1)} %collective-permute-done.8.other), custom_call_target="tpu_custom_call" | custom-call | bytes 40000000 | tf_op jit(solution)/shard_map/pallas_call | solution.py:589
  61.2 4.6 %shard_map.219 = (f32[16,256,512]{2,1,0:T(8,128)}, bf16[8,256,512]{2,1,0:T(8,128)(2,1)S(1)}) custom-call(s32[34]{0:T(128)S(1)} %get-tuple-element.72.meta, bf16[8,256,512]{2,1,0:T(8,128)(2,1)S(1)} %get-tuple-element.89.cot, f32[8,4,288,128]{3,2,1,0:T(8,128)S(1)} %get-tuple-element.112.cgp, f32[16,512]{1,0:T(8,128)S(1)} %get-tuple-element.83.consts), custom_call_target="tpu_custom_call" | custom-call | bytes 40000000 | tf_op jit(solution)/shard_map/pallas_call | solution.py:641
  65.8 0.6 collective-permute-done.14.far_1
  66.5 0.0 collective-permute-done.13.theirs
  66.5 0.0 collective-permute-done.12.refs_3_
  66.5 0.0 collective-permute-done.11.refs_2_
  66.5 0.0 collective-permute-done.10.refs_1_.near_1
  66.5 0.1 collective-permute-start.16
  66.6 1.1 %collective-permute-start.15 = (bf16[832,128]{1,0:T(8,128)(2,1)S(1)}, bf16[832,128]{1,0:T(8,128)(2,1)S(1)}, u32[]{:S(2)}, u32[]{:S(2)}) collective-permute-start(bf16[832,128]{1,0:T(8,128)(2,1)S(1)} %shard_map.220.near), channel_id=1, source_target_pairs={{0,4},{4,0},{8,12},{12,8},{16,20},{20,16},{24,28},{28,24},{1,5},{5... | collective-permute-start | bytes 638984 | tf_op jit(solution)/shard_map/ppermute | solution.py:753
  67.6 3.1 %collective-permute-done.16.other = bf16[8,256,512]{2,1,0:T(8,128)(2,1)S(1)} collective-permute-done((bf16[8,256,512]{2,1,0:T(8,128)(2,1)S(1)}, bf16[8,256,512]{2,1,0:T(8,128)(2,1)S(1)}, u32[]{:S(2)}, u32[]{:S(2)}) %collective-permute-start.16) | collective-permute-done | bytes 2097184 | tf_op jit(solution)/shard_map/ppermute | solution.py:748
  70.7 2.6 %shard_map.221 = f32[16,256,512]{2,1,0:T(8,128)} custom-call(s32[34]{0:T(128)S(1)} %get-tuple-element.72.meta, bf16[8,256,512]{2,1,0:T(8,128)(2,1)S(1)} %collective-permute-done.16.other, f32[16,256,512]{2,1,0:T(8,128)} %get-tuple-element.119.gtok_in), custom_call_target="tpu_custom_call", output_to_operand_aliasing={{}: (2, {})} | custom-call | bytes 20000000 | tf_op jit(solution)/shard_map/pallas_call | solution.py:661
  73.3 1.0 %collective-permute-done.15.far = bf16[832,128]{1,0:T(8,128)(2,1)S(1)} collective-permute-done((bf16[832,128]{1,0:T(8,128)(2,1)S(1)}, bf16[832,128]{1,0:T(8,128)(2,1)S(1)}, u32[]{:S(2)}, u32[]{:S(2)}) %collective-permute-start.15) | collective-permute-done | bytes 213024 | tf_op jit(solution)/shard_map/ppermute | solution.py:753
  74.3 1.9 %shard_map.222 = (f32[7,512]{1,0:T(8,128)}, f32[512]{0:T(512)}, f32[2,512]{1,0:T(2,128)}, f32[2,512]{1,0:T(2,128)}, f32[512,384]{1,0:T(8,128)}, /*index=5*/f32[3...) custom-call(s32[34]{0:T(128)S(1)} %get-tuple-element.72.meta, bf16[384,128]{1,0:T(8,128)(2,1)S(1)} %get-tuple-element.111.mine, ...), custom_call_target="tpu_custom_call" | custom-call | tf_op jit(solution)/shard_map/pallas_call | solution.py:739
  (2 shorter events, 0.0 us)
Async XLA Ops:
  1.9 3.1 %collective-permute-start = (bf16[3088,128]{1,0:T(8,128)(2,1)S(1)}, bf16[3088,128]{1,0:T(8,128)(2,1)S(1)}, u32[]{:S(2)}, u32[]{:S(2)}) collective-permute-start(bf16[3088,128]{1,0:T(8,128)(2,1)S(1)} %shard_map.212.buf_a), channel_id=1, source_target_pairs={{0,1},{1,0},{2,3},{3,2},{4,5},{5,4},{6,7},{7,6},{8,9},{9,8},{10,11... | collective-permute-start | bytes 2371592 | tf_op jit(solution)/shard_map/ppermute | solution.py:748
  2.4 20.8 %collective-permute-start.3 = (bf16[3088,128]{1,0:T(8,128)(2,1)S(1)}, bf16[3088,128]{1,0:T(8,128)(2,1)S(1)}, u32[]{:S(2)}, u32[]{:S(2)}) collective-permute-start(bf16[3088,128]{1,0:T(8,128)(2,1)S(1)} %shard_map.212.buf_a), channel_id=1, source_target_pairs={{0,2},{1,3},{2,0},{3,1},{4,6},{5,7},{6,4},{7,5},{8,10},{9,11},{10,... | collective-permute-start | bytes 2371592 | tf_op jit(solution)/shard_map/ppermute | solution.py:748
  22.1 2.4 %collective-permute-start.1 = (bf16[3072,128]{1,0:T(8,128)(2,1)S(1)}, bf16[3072,128]{1,0:T(8,128)(2,1)S(1)}, u32[]{:S(2)}, u32[]{:S(2)}) collective-permute-start(bf16[3072,128]{1,0:T(8,128)(2,1)S(1)} %get-tuple-element.74), channel_id=1, source_target_pairs={{0,1},{1,0},{2,3},{3,2},{4,5},{5,4},{6,7},{7,6},{8,9},{9,8},{10,11... | collective-permute-start | bytes 2359304 | tf_op jit(solution)/shard_map/ppermute | solution.py:748
  23.2 4.0 %collective-permute-start.4 = (bf16[3088,128]{1,0:T(8,128)(2,1)S(1)}, bf16[3088,128]{1,0:T(8,128)(2,1)S(1)}, u32[]{:S(2)}, u32[]{:S(2)}) collective-permute-start(bf16[3088,128]{1,0:T(8,128)(2,1)S(1)} %collective-permute-done.3.buf_c), channel_id=1, source_target_pairs={{0,1},{1,0},{2,3},{3,2},{4,5},{5,4},{6,7},{7,6},{8,9},{9,8},{10,11... | collective-permute-start | bytes 2371592 | tf_op jit(solution)/shard_map/ppermute | solution.py:748
  25.1 12.7 %collective-permute-start.2 = (bf16[1536,128]{1,0:T(8,128)(2,1)S(1)}, bf16[1536,128]{1,0:T(8,128)(2,1)S(1)}, u32[]{:S(2)}, u32[]{:S(2)}) collective-permute-start(bf16[1536,128]{1,0:T(8,128)(2,1)S(1)} %get-tuple-element.76), channel_id=1, source_target_pairs={{0,4},{4,0},{8,12},{12,8},{16,20},{20,16},{24,28},{28,24},{1,5},{5... | collective-permute-start | bytes 1179656 | tf_op jit(solution)/shard_map/ppermute | solution.py:753
  37.9 12.6 %collective-permute-start.8 = (bf16[2304,512]{1,0:T(8,128)(2,1)S(1)}, bf16[2304,512]{1,0:T(8,128)(2,1)S(1)}, u32[]{:S(2)}, u32[]{:S(2)}) collective-permute-start(bf16[2304,512]{1,0:T(8,128)(2,1)S(1)} %get-tuple-element.98.own), channel_id=1, source_target_pairs={{0,1},{1,0},{2,3},{3,2},{4,5},{5,4},{6,7},{7,6},{8,9},{9,8},{10,11... | collective-permute-start | bytes 7077896 | tf_op jit(solution)/shard_map/ppermute | solution.py:748
  38.1 12.2 %collective-permute-start.7 = (bf16[384,128]{1,0:T(8,128)(2,1)S(1)}, bf16[384,128]{1,0:T(8,128)(2,1)S(1)}, u32[]{:S(2)}, u32[]{:S(2)}) collective-permute-start(bf16[384,128]{1,0:T(8,128)(2,1)S(1)} %get-tuple-element.135), channel_id=1, source_target_pairs={{0,24},{4,28},{8,16},{12,20},{16,8},{20,12},{24,0},{28,4},{1,25},{... | collective-permute-start | bytes 294920 | tf_op jit(solution)/shard_map/ppermute | solution.py:753
  41.8 8.7 %collective-permute-start.6 = (bf16[384,128]{1,0:T(8,128)(2,1)S(1)}, bf16[384,128]{1,0:T(8,128)(2,1)S(1)}, u32[]{:S(2)}, u32[]{:S(2)}) collective-permute-start(bf16[384,128]{1,0:T(8,128)(2,1)S(1)} %get-tuple-element.136), channel_id=1, source_target_pairs={{0,16},{4,20},{8,24},{12,28},{16,0},{20,4},{24,8},{28,12},{1,17},{... | collective-permute-start | bytes 294920 | tf_op jit(solution)/shard_map/ppermute | solution.py:753
  41.8 8.7 %collective-permute-start.5 = (bf16[384,128]{1,0:T(8,128)(2,1)S(1)}, bf16[384,128]{1,0:T(8,128)(2,1)S(1)}, u32[]{:S(2)}, u32[]{:S(2)}) collective-permute-start(bf16[384,128]{1,0:T(8,128)(2,1)S(1)} %get-tuple-element.137), channel_id=1, source_target_pairs={{0,8},{4,12},{8,0},{12,4},{16,24},{20,28},{24,16},{28,20},{1,9},{5... | collective-permute-start | bytes 294920 | tf_op jit(solution)/shard_map/ppermute | solution.py:753
  50.5 1.2 %collective-permute-start.9 = (f32[16,512]{1,0:T(8,128)S(1)}, f32[16,512]{1,0:T(8,128)S(1)}, u32[]{:S(2)}, u32[]{:S(2)}) collective-permute-start(f32[16,512]{1,0:T(8,128)S(1)} %get-tuple-element.101), channel_id=1, source_target_pairs={{0,1},{1,0},{2,3},{3,2},{4,5},{5,4},{6,7},{7,6},{8,9},{9,8},{10,11... | collective-permute-start | bytes 98312 | tf_op jit(solution)/shard_map/ppermute | solution.py:748
  51.8 14.7 %collective-permute-start.12 = (bf16[448,128]{1,0:T(8,128)(2,1)S(1)}, bf16[448,128]{1,0:T(8,128)(2,1)S(1)}, u32[]{:S(2)}, u32[]{:S(2)}) collective-permute-start(bf16[448,128]{1,0:T(8,128)(2,1)S(1)} %get-tuple-element.114.refs_0_), channel_id=1, source_target_pairs={{0,24},{4,28},{8,16},{12,20},{16,8},{20,12},{24,0},{28,4},{1,25},{... | collective-permute-start | bytes 344072 | tf_op jit(solution)/shard_map/ppermute | solution.py:753
  55.0 11.5 %collective-permute-start.11 = (bf16[448,128]{1,0:T(8,128)(2,1)S(1)}, bf16[448,128]{1,0:T(8,128)(2,1)S(1)}, u32[]{:S(2)}, u32[]{:S(2)}) collective-permute-start(bf16[448,128]{1,0:T(8,128)(2,1)S(1)} %get-tuple-element.114.refs_0_), channel_id=1, source_target_pairs={{0,16},{4,20},{8,24},{12,28},{16,0},{20,4},{24,8},{28,12},{1,17},{... | collective-permute-start | bytes 344072 | tf_op jit(solution)/shard_map/ppermute | solution.py:753
  55.0 11.5 %collective-permute-start.10 = (bf16[448,128]{1,0:T(8,128)(2,1)S(1)}, bf16[448,128]{1,0:T(8,128)(2,1)S(1)}, u32[]{:S(2)}, u32[]{:S(2)}) collective-permute-start(bf16[448,128]{1,0:T(8,128)(2,1)S(1)} %get-tuple-element.114.refs_0_), channel_id=1, source_target_pairs={{0,8},{4,12},{8,0},{12,4},{16,24},{20,28},{24,16},{28,20},{1,9},{5... | collective-permute-start | bytes 344072 | tf_op jit(solution)/shard_map/ppermute | solution.py:753
  56.2 10.2 %collective-permute-start.14 = (bf16[384,128]{1,0:T(8,128)(2,1)S(1)}, bf16[384,128]{1,0:T(8,128)(2,1)S(1)}, u32[]{:S(2)}, u32[]{:S(2)}) collective-permute-start(bf16[384,128]{1,0:T(8,128)(2,1)S(1)} %get-tuple-element.111.mine), channel_id=1, source_target_pairs={{0,12},{4,8},{8,4},{12,0},{16,28},{20,24},{24,20},{28,16},{1,13},{... | collective-permute-start | bytes 294920 | tf_op jit(solution)/shard_map/ppermute | solution.py:753
  57.1 9.4 %collective-permute-start.13 = (bf16[384,128]{1,0:T(8,128)(2,1)S(1)}, bf16[384,128]{1,0:T(8,128)(2,1)S(1)}, u32[]{:S(2)}, u32[]{:S(2)}) collective-permute-start(bf16[384,128]{1,0:T(8,128)(2,1)S(1)} %get-tuple-element.111.mine), channel_id=1, source_target_pairs={{0,4},{4,0},{8,12},{12,8},{16,20},{20,16},{24,28},{28,24},{1,5},{5... | collective-permute-start | bytes 294920 | tf_op jit(solution)/shard_map/ppermute | solution.py:753
  66.5 4.2 %collective-permute-start.16 = (bf16[8,256,512]{2,1,0:T(8,128)(2,1)S(1)}, bf16[8,256,512]{2,1,0:T(8,128)(2,1)S(1)}, u32[]{:S(2)}, u32[]{:S(2)}) collective-permute-start(bf16[8,256,512]{2,1,0:T(8,128)(2,1)S(1)} %get-tuple-element.118), channel_id=1, source_target_pairs={{0,1},{1,0},{2,3},{3,2},{4,5},{5,4},{6,7},{7,6},{8,9},{9,8},{10,11... | collective-permute-start | bytes 6291464 | tf_op jit(solution)/shard_map/ppermute | solution.py:748
  66.6 7.7 %collective-permute-start.15 = (bf16[832,128]{1,0:T(8,128)(2,1)S(1)}, bf16[832,128]{1,0:T(8,128)(2,1)S(1)}, u32[]{:S(2)}, u32[]{:S(2)}) collective-permute-start(bf16[832,128]{1,0:T(8,128)(2,1)S(1)} %shard_map.220.near), channel_id=1, source_target_pairs={{0,4},{4,0},{8,12},{12,8},{16,20},{20,16},{24,28},{28,24},{1,5},{5... | collective-permute-start | bytes 638984 | tf_op jit(solution)/shard_map/ppermute | solution.py:753

commit v17 on v16

--- a/solution.py
+++ b/solution.py
@@ -320,7 +320,7 @@
 
         start = offs[n + 2]
         left = offs[n + 1] - start
-        pairs = lax.shift_right_arithmetic(left, 1)
+        pairs = jnp.where(left == 3, 0, lax.shift_right_arithmetic(left, 1))
 
         def rest(t, _):
             tile(start + 2 * t, 2 * TILE)
@@ -328,7 +328,11 @@
 
         lax.fori_loop(0, pairs, rest, 0)
 
-        @pl.when(left > 2 * pairs)
+        @pl.when(left == 3)
+        def _():
+            tile(start, 3 * TILE)
+
+        @pl.when((left != 3) & (left > 2 * pairs))
         def _():
             tile(offs[n + 1] - 1, TILE)
 

time: 76.4 us -> 76.2 us (level)
  transfers between devices with their start and end apart: 17 -> 17, of which waited for: 7 -> 6; matrix products, arithmetic and copies ran while one was open for 0% -> 0% of each run, Pallas kernels for 60% -> 60%
where the time goes in v17:
time: 76.2 us; the launch traced here: 76.1 us
  Pallas kernels  49 us (64%)
  starting transfers between devices  17.4 us (23%)
  waiting for transfers between devices  8.83 us (12%)
  between operations  0.81 us (1%)
    pallas_call x1, Pallas kernels, front(): pl.pallas_call(functools.partial(front_kernel, n), grid_spec=pl.GridSpec(...  17.2 us
    ppermute x10, starting transfers between devices, across(): return lax.ppermute(x, 'dp', [(i, i ^ step) for i in range(size)])  14 us
    pallas_call x1, Pallas kernels, mix(): pl.pallas_call(functools.partial(mix_kernel, n, taps), in_specs=[smem()]...  10.4 us
    pallas_call x1, Pallas kernels, norm_grad(): pl.pallas_call(functools.partial(norm_grad_kernel, n, taps, rates), grid=...  7.57 us
    ppermute x7, waiting for transfers between devices, swap(): return lax.ppermute(x, 'tp', [(i, i ^ step) for i in range(size)])  6.45 us
    pallas_call x1, Pallas kernels, token_grad(): pl.pallas_call(functools.partial(token_grad_kernel, n, taps), grid=(n,),...  4.51 us
    ppermute x7, starting transfers between devices, swap(): return lax.ppermute(x, 'tp', [(i, i ^ step) for i in range(size)])  3.38 us
    pallas_call x1, Pallas kernels, place_out(): pl.pallas_call(functools.partial(place_out_kernel, n), in_specs=[smem(),...  2.73 us
  transfers between devices with their start and end apart: 17, of which 6 were waited for; matrix products, arithmetic and copies ran while one was open for 0% of the time, Pallas kernels for 60%

profile of v17, /device:TPU:0, one launch (start us, length us, event | category | flops | bytes accessed | tf_op | source)
XLA Modules:
  0.0 76.1 jit_solution(10737476323298339131)
XLA Ops:
  0.6 1.3 %shard_map.212.buf_a = bf16[3088,128]{1,0:T(8,128)(2,1)S(1)} custom-call(bf16[512,384]{1,0:T(8,128)(2,1)} %wi.1, bf16[384]{0:T(512)(128)(2,1)} %bi.1, bf16[384,512]{1,0:T(8,128)(2,1)} %wo.1), custom_call_target="tpu_custom_call" | custom-call | tf_op jit(solution)/shard_map/pallas_call | solution.py:111
  1.9 0.5 collective-permute-start
  2.4 2.6 %collective-permute-start.3 = (bf16[3088,128]{1,0:T(8,128)(2,1)S(1)}, bf16[3088,128]{1,0:T(8,128)(2,1)S(1)}, u32[]{:S(2)}, u32[]{:S(2)}) collective-permute-start(bf16[3088,128]{1,0:T(8,128)(2,1)S(1)} %shard_map.212.buf_a), channel_id=1, source_target_pairs={{0,2},{1,3},{2,0},{3,1},{4,6},{5,7},{6,4},{7,5},{8,10},{9,11},{10,... | collective-permute-start | bytes 2371592 | tf_op jit(solution)/shard_map/ppermute | solution.py:752
  5.0 0.0 collective-permute-done.buf_b
  5.0 17.2 %shard_map.213 = (bf16[2304,512]{1,0:T(8,128)(2,1)S(1)}, bf16[2304,512]{1,0:T(8,128)(2,1)S(1)}, bf16[2304,512]{1,0:T(8,128)(2,1)S(1)}, f32[2304,128]{1,0:T(8,128...) custom-call(s32[16]{0:T(128)} %counts_hbm.1, ...), custom_call_target="tpu_custom_call" | custom-call | tf_op jit(solution)/shard_map/pallas_call | solution.py:355
  22.2 0.1 collective-permute-start.1
  22.3 0.9 %collective-permute-done.3.buf_c = bf16[3088,128]{1,0:T(8,128)(2,1)S(1)} collective-permute-done((bf16[3088,128]{1,0:T(8,128)(2,1)S(1)}, bf16[3088,128]{1,0:T(8,128)(2,1)S(1)}, u32[]{:S(2)}, u32[]{:S(2)}) %collective-permute-start.3) | collective-permute-done | bytes 790560 | tf_op jit(solution)/shard_map/ppermute | solution.py:752
  23.2 0.0 collective-permute-start.4
  23.2 1.3 %collective-permute-done.1.recv = bf16[3072,128]{1,0:T(8,128)(2,1)S(1)} collective-permute-done((bf16[3072,128]{1,0:T(8,128)(2,1)S(1)}, bf16[3072,128]{1,0:T(8,128)(2,1)S(1)}, u32[]{:S(2)}, u32[]{:S(2)}) %collective-permute-start.1) | collective-permute-done | bytes 786464 | tf_op jit(solution)/shard_map/ppermute | solution.py:752
  24.6 0.7 shard_map.214
  25.2 2.5 %collective-permute-start.2 = (bf16[1536,128]{1,0:T(8,128)(2,1)S(1)}, bf16[1536,128]{1,0:T(8,128)(2,1)S(1)}, u32[]{:S(2)}, u32[]{:S(2)}) collective-permute-start(bf16[1536,128]{1,0:T(8,128)(2,1)S(1)} %get-tuple-element.76), channel_id=1, source_target_pairs={{0,4},{4,0},{8,12},{12,8},{16,20},{20,16},{24,28},{28,24},{1,5},{5... | collective-permute-start | bytes 1179656 | tf_op jit(solution)/shard_map/ppermute | solution.py:757
  27.7 0.0 collective-permute-done.4.buf_d
  27.7 10.4 %shard_map.215 = (f32[2304,512]{1,0:T(8,128)S(1)}, f32[2304,512]{1,0:T(8,128)S(1)}, bf16[2304,512]{1,0:T(8,128)(2,1)S(1)}) custom-call(s32[34]{0:T(128)S(1)} %get-tuple-element.72.meta, bf16[2304,512]{1,0:T(8,128)(2,1)S(1)} %get-tuple-element.77.ad, bf16[2304,512]{1,0:T(8,128)(2,1)S(1)} %get-tuple-element.78.low, ...), custom_call_target="tpu_custom_call" | custom-call | tf_op jit(solution)/shard_map/pallas_call | solution.py:440
  38.1 0.0 collective-permute-done.2
  38.2 0.1 collective-permute-start.8
  38.2 0.1 fusion
  38.4 1.3 %collective-permute-start.7 = (bf16[384,128]{1,0:T(8,128)(2,1)S(1)}, bf16[384,128]{1,0:T(8,128)(2,1)S(1)}, u32[]{:S(2)}, u32[]{:S(2)}) collective-permute-start(bf16[384,128]{1,0:T(8,128)(2,1)S(1)} %get-tuple-element.135), channel_id=1, source_target_pairs={{0,24},{4,28},{8,16},{12,20},{16,8},{20,12},{24,0},{28,4},{1,25},{... | collective-permute-start | bytes 294920 | tf_op jit(solution)/shard_map/ppermute | solution.py:757
  39.6 1.5 %collective-permute-start.6 = (bf16[384,128]{1,0:T(8,128)(2,1)S(1)}, bf16[384,128]{1,0:T(8,128)(2,1)S(1)}, u32[]{:S(2)}, u32[]{:S(2)}) collective-permute-start(bf16[384,128]{1,0:T(8,128)(2,1)S(1)} %get-tuple-element.136), channel_id=1, source_target_pairs={{0,16},{4,20},{8,24},{12,28},{16,0},{20,4},{24,8},{28,12},{1,17},{... | collective-permute-start | bytes 294920 | tf_op jit(solution)/shard_map/ppermute | solution.py:757
  41.2 1.7 %collective-permute-start.5 = (bf16[384,128]{1,0:T(8,128)(2,1)S(1)}, bf16[384,128]{1,0:T(8,128)(2,1)S(1)}, u32[]{:S(2)}, u32[]{:S(2)}) collective-permute-start(bf16[384,128]{1,0:T(8,128)(2,1)S(1)} %get-tuple-element.137), channel_id=1, source_target_pairs={{0,8},{4,12},{8,0},{12,4},{16,24},{20,28},{24,16},{28,20},{1,9},{5... | collective-permute-start | bytes 294920 | tf_op jit(solution)/shard_map/ppermute | solution.py:757
  42.8 7.6 %shard_map.216 = (f32[8,4,288,128]{3,2,1,0:T(8,128)S(1)}, f32[16,512]{1,0:T(8,128)S(1)}, f32[16,512]{1,0:T(8,128)S(1)}) custom-call(s32[34]{0:T(128)S(1)} %get-tuple-element.72.meta, bf16[8,256,512]{2,1,0:T(8,128)(2,1)S(1)} %get-tuple-element.88.tok, bf16[8,256,512]{2,1,0:T(8,128)(2,1)S(1)} %get-tuple-element.89.cot, ...), custom_call_target="tpu_custom_call" | custom-call | bytes 40000000 | tf_op jit(solution)/shard_map/pallas_call | solution.py:560
  50.4 0.0 collective-permute-done.7.refs_2_
  50.4 0.0 collective-permute-done.6.refs_1_
  50.4 0.0 collective-permute-done.5.refs_0_
  50.4 0.0 collective-permute-done.8.other
  50.4 0.1 collective-permute-start.9
  50.5 1.2 %collective-permute-done.9.recv = f32[16,512]{1,0:T(8,128)S(1)} collective-permute-done((f32[16,512]{1,0:T(8,128)S(1)}, f32[16,512]{1,0:T(8,128)S(1)}, u32[]{:S(2)}, u32[]{:S(2)}) %collective-permute-start.9) | collective-permute-done | bytes 32800 | tf_op jit(solution)/shard_map/ppermute | solution.py:752
  51.7 0.1 shard_map.217
  51.8 1.8 %collective-permute-start.12 = (bf16[448,128]{1,0:T(8,128)(2,1)S(1)}, bf16[448,128]{1,0:T(8,128)(2,1)S(1)}, u32[]{:S(2)}, u32[]{:S(2)}) collective-permute-start(bf16[448,128]{1,0:T(8,128)(2,1)S(1)} %get-tuple-element.114.refs_0_), channel_id=1, source_target_pairs={{0,24},{4,28},{8,16},{12,20},{16,8},{20,12},{24,0},{28,4},{1,25},{... | collective-permute-start | bytes 344072 | tf_op jit(solution)/shard_map/ppermute | solution.py:757
  53.5 0.1 collective-permute-start.11
  53.7 2.6 %collective-permute-start.10 = (bf16[448,128]{1,0:T(8,128)(2,1)S(1)}, bf16[448,128]{1,0:T(8,128)(2,1)S(1)}, u32[]{:S(2)}, u32[]{:S(2)}) collective-permute-start(bf16[448,128]{1,0:T(8,128)(2,1)S(1)} %get-tuple-element.114.refs_0_), channel_id=1, source_target_pairs={{0,8},{4,12},{8,0},{12,4},{16,24},{20,28},{24,16},{28,20},{1,9},{5... | collective-permute-start | bytes 344072 | tf_op jit(solution)/shard_map/ppermute | solution.py:757
  56.2 0.5 collective-permute-start.14
  56.7 1.0 %collective-permute-start.13 = (bf16[384,128]{1,0:T(8,128)(2,1)S(1)}, bf16[384,128]{1,0:T(8,128)(2,1)S(1)}, u32[]{:S(2)}, u32[]{:S(2)}) collective-permute-start(bf16[384,128]{1,0:T(8,128)(2,1)S(1)} %get-tuple-element.111.mine), channel_id=1, source_target_pairs={{0,4},{4,0},{8,12},{12,8},{16,20},{20,16},{24,28},{28,24},{1,5},{5... | collective-permute-start | bytes 294920 | tf_op jit(solution)/shard_map/ppermute | solution.py:757
  57.7 2.7 %shard_map.218 = bf16[16,256,512]{2,1,0:T(8,128)(2,1)} custom-call(s32[34]{0:T(128)S(1)} %get-tuple-element.72.meta, bf16[2304,512]{1,0:T(8,128)(2,1)S(1)} %get-tuple-element.98.own, bf16[2304,512]{1,0:T(8,128)(2,1)S(1)} %collective-permute-done.8.other), custom_call_target="tpu_custom_call" | custom-call | bytes 40000000 | tf_op jit(solution)/shard_map/pallas_call | solution.py:593
  60.4 4.5 %shard_map.219 = (f32[16,256,512]{2,1,0:T(8,128)}, bf16[8,256,512]{2,1,0:T(8,128)(2,1)S(1)}) custom-call(s32[34]{0:T(128)S(1)} %get-tuple-element.72.meta, bf16[8,256,512]{2,1,0:T(8,128)(2,1)S(1)} %get-tuple-element.89.cot, f32[8,4,288,128]{3,2,1,0:T(8,128)S(1)} %get-tuple-element.112.cgp, f32[16,512]{1,0:T(8,128)S(1)} %get-tuple-element.83.consts), custom_call_target="tpu_custom_call" | custom-call | bytes 40000000 | tf_op jit(solution)/shard_map/pallas_call | solution.py:645
  65.0 1.4 %collective-permute-done.14.far_1 = bf16[384,128]{1,0:T(8,128)(2,1)S(1)} collective-permute-done((bf16[384,128]{1,0:T(8,128)(2,1)S(1)}, bf16[384,128]{1,0:T(8,128)(2,1)S(1)}, u32[]{:S(2)}, u32[]{:S(2)}) %collective-permute-start.14) | collective-permute-done | bytes 98336 | tf_op jit(solution)/shard_map/ppermute | solution.py:757
  66.4 0.0 collective-permute-done.13.theirs
  66.4 0.0 collective-permute-done.12.refs_3_
  66.4 0.0 collective-permute-done.11.refs_2_
  66.4 0.0 collective-permute-done.10.refs_1_.near_1
  66.4 0.1 collective-permute-start.16
  66.5 1.1 %collective-permute-start.15 = (bf16[832,128]{1,0:T(8,128)(2,1)S(1)}, bf16[832,128]{1,0:T(8,128)(2,1)S(1)}, u32[]{:S(2)}, u32[]{:S(2)}) collective-permute-start(bf16[832,128]{1,0:T(8,128)(2,1)S(1)} %shard_map.220.near), channel_id=1, source_target_pairs={{0,4},{4,0},{8,12},{12,8},{16,20},{20,16},{24,28},{28,24},{1,5},{5... | collective-permute-start | bytes 638984 | tf_op jit(solution)/shard_map/ppermute | solution.py:757
  67.6 3.0 %collective-permute-done.16.other = bf16[8,256,512]{2,1,0:T(8,128)(2,1)S(1)} collective-permute-done((bf16[8,256,512]{2,1,0:T(8,128)(2,1)S(1)}, bf16[8,256,512]{2,1,0:T(8,128)(2,1)S(1)}, u32[]{:S(2)}, u32[]{:S(2)}) %collective-permute-start.16) | collective-permute-done | bytes 2097184 | tf_op jit(solution)/shard_map/ppermute | solution.py:752
  70.6 2.6 %shard_map.221 = f32[16,256,512]{2,1,0:T(8,128)} custom-call(s32[34]{0:T(128)S(1)} %get-tuple-element.72.meta, bf16[8,256,512]{2,1,0:T(8,128)(2,1)S(1)} %collective-permute-done.16.other, f32[16,256,512]{2,1,0:T(8,128)} %get-tuple-element.119.gtok_in), custom_call_target="tpu_custom_call", output_to_operand_aliasing={{}: (2, {})} | custom-call | bytes 20000000 | tf_op jit(solution)/shard_map/pallas_call | solution.py:665
  73.3 1.0 %collective-permute-done.15.far = bf16[832,128]{1,0:T(8,128)(2,1)S(1)} collective-permute-done((bf16[832,128]{1,0:T(8,128)(2,1)S(1)}, bf16[832,128]{1,0:T(8,128)(2,1)S(1)}, u32[]{:S(2)}, u32[]{:S(2)}) %collective-permute-start.15) | collective-permute-done | bytes 213024 | tf_op jit(solution)/shard_map/ppermute | solution.py:757
  74.2 1.9 %shard_map.222 = (f32[7,512]{1,0:T(8,128)}, f32[512]{0:T(512)}, f32[2,512]{1,0:T(2,128)}, f32[2,512]{1,0:T(2,128)}, f32[512,384]{1,0:T(8,128)}, /*index=5*/f32[3...) custom-call(s32[34]{0:T(128)S(1)} %get-tuple-element.72.meta, bf16[384,128]{1,0:T(8,128)(2,1)S(1)} %get-tuple-element.111.mine, ...), custom_call_target="tpu_custom_call" | custom-call | tf_op jit(solution)/shard_map/pallas_call | solution.py:743
  (2 shorter events, 0.0 us)
Async XLA Ops:
  1.9 3.1 %collective-permute-start = (bf16[3088,128]{1,0:T(8,128)(2,1)S(1)}, bf16[3088,128]{1,0:T(8,128)(2,1)S(1)}, u32[]{:S(2)}, u32[]{:S(2)}) collective-permute-start(bf16[3088,128]{1,0:T(8,128)(2,1)S(1)} %shard_map.212.buf_a), channel_id=1, source_target_pairs={{0,1},{1,0},{2,3},{3,2},{4,5},{5,4},{6,7},{7,6},{8,9},{9,8},{10,11... | collective-permute-start | bytes 2371592 | tf_op jit(solution)/shard_map/ppermute | solution.py:752
  2.4 20.8 %collective-permute-start.3 = (bf16[3088,128]{1,0:T(8,128)(2,1)S(1)}, bf16[3088,128]{1,0:T(8,128)(2,1)S(1)}, u32[]{:S(2)}, u32[]{:S(2)}) collective-permute-start(bf16[3088,128]{1,0:T(8,128)(2,1)S(1)} %shard_map.212.buf_a), channel_id=1, source_target_pairs={{0,2},{1,3},{2,0},{3,1},{4,6},{5,7},{6,4},{7,5},{8,10},{9,11},{10,... | collective-permute-start | bytes 2371592 | tf_op jit(solution)/shard_map/ppermute | solution.py:752
  22.2 2.4 %collective-permute-start.1 = (bf16[3072,128]{1,0:T(8,128)(2,1)S(1)}, bf16[3072,128]{1,0:T(8,128)(2,1)S(1)}, u32[]{:S(2)}, u32[]{:S(2)}) collective-permute-start(bf16[3072,128]{1,0:T(8,128)(2,1)S(1)} %get-tuple-element.74), channel_id=1, source_target_pairs={{0,1},{1,0},{2,3},{3,2},{4,5},{5,4},{6,7},{7,6},{8,9},{9,8},{10,11... | collective-permute-start | bytes 2359304 | tf_op jit(solution)/shard_map/ppermute | solution.py:752
  23.2 4.5 %collective-permute-start.4 = (bf16[3088,128]{1,0:T(8,128)(2,1)S(1)}, bf16[3088,128]{1,0:T(8,128)(2,1)S(1)}, u32[]{:S(2)}, u32[]{:S(2)}) collective-permute-start(bf16[3088,128]{1,0:T(8,128)(2,1)S(1)} %collective-permute-done.3.buf_c), channel_id=1, source_target_pairs={{0,1},{1,0},{2,3},{3,2},{4,5},{5,4},{6,7},{7,6},{8,9},{9,8},{10,11... | collective-permute-start | bytes 2371592 | tf_op jit(solution)/shard_map/ppermute | solution.py:752
  25.2 12.9 %collective-permute-start.2 = (bf16[1536,128]{1,0:T(8,128)(2,1)S(1)}, bf16[1536,128]{1,0:T(8,128)(2,1)S(1)}, u32[]{:S(2)}, u32[]{:S(2)}) collective-permute-start(bf16[1536,128]{1,0:T(8,128)(2,1)S(1)} %get-tuple-element.76), channel_id=1, source_target_pairs={{0,4},{4,0},{8,12},{12,8},{16,20},{20,16},{24,28},{28,24},{1,5},{5... | collective-permute-start | bytes 1179656 | tf_op jit(solution)/shard_map/ppermute | solution.py:757
  38.2 12.3 %collective-permute-start.8 = (bf16[2304,512]{1,0:T(8,128)(2,1)S(1)}, bf16[2304,512]{1,0:T(8,128)(2,1)S(1)}, u32[]{:S(2)}, u32[]{:S(2)}) collective-permute-start(bf16[2304,512]{1,0:T(8,128)(2,1)S(1)} %get-tuple-element.98.own), channel_id=1, source_target_pairs={{0,1},{1,0},{2,3},{3,2},{4,5},{5,4},{6,7},{7,6},{8,9},{9,8},{10,11... | collective-permute-start | bytes 7077896 | tf_op jit(solution)/shard_map/ppermute | solution.py:752
  38.4 12.0 %collective-permute-start.7 = (bf16[384,128]{1,0:T(8,128)(2,1)S(1)}, bf16[384,128]{1,0:T(8,128)(2,1)S(1)}, u32[]{:S(2)}, u32[]{:S(2)}) collective-permute-start(bf16[384,128]{1,0:T(8,128)(2,1)S(1)} %get-tuple-element.135), channel_id=1, source_target_pairs={{0,24},{4,28},{8,16},{12,20},{16,8},{20,12},{24,0},{28,4},{1,25},{... | collective-permute-start | bytes 294920 | tf_op jit(solution)/shard_map/ppermute | solution.py:757
  39.6 10.8 %collective-permute-start.6 = (bf16[384,128]{1,0:T(8,128)(2,1)S(1)}, bf16[384,128]{1,0:T(8,128)(2,1)S(1)}, u32[]{:S(2)}, u32[]{:S(2)}) collective-permute-start(bf16[384,128]{1,0:T(8,128)(2,1)S(1)} %get-tuple-element.136), channel_id=1, source_target_pairs={{0,16},{4,20},{8,24},{12,28},{16,0},{20,4},{24,8},{28,12},{1,17},{... | collective-permute-start | bytes 294920 | tf_op jit(solution)/shard_map/ppermute | solution.py:757
  41.2 9.3 %collective-permute-start.5 = (bf16[384,128]{1,0:T(8,128)(2,1)S(1)}, bf16[384,128]{1,0:T(8,128)(2,1)S(1)}, u32[]{:S(2)}, u32[]{:S(2)}) collective-permute-start(bf16[384,128]{1,0:T(8,128)(2,1)S(1)} %get-tuple-element.137), channel_id=1, source_target_pairs={{0,8},{4,12},{8,0},{12,4},{16,24},{20,28},{24,16},{28,20},{1,9},{5... | collective-permute-start | bytes 294920 | tf_op jit(solution)/shard_map/ppermute | solution.py:757
  50.4 1.3 %collective-permute-start.9 = (f32[16,512]{1,0:T(8,128)S(1)}, f32[16,512]{1,0:T(8,128)S(1)}, u32[]{:S(2)}, u32[]{:S(2)}) collective-permute-start(f32[16,512]{1,0:T(8,128)S(1)} %get-tuple-element.101), channel_id=1, source_target_pairs={{0,1},{1,0},{2,3},{3,2},{4,5},{5,4},{6,7},{7,6},{8,9},{9,8},{10,11... | collective-permute-start | bytes 98312 | tf_op jit(solution)/shard_map/ppermute | solution.py:752
  51.8 14.6 %collective-permute-start.12 = (bf16[448,128]{1,0:T(8,128)(2,1)S(1)}, bf16[448,128]{1,0:T(8,128)(2,1)S(1)}, u32[]{:S(2)}, u32[]{:S(2)}) collective-permute-start(bf16[448,128]{1,0:T(8,128)(2,1)S(1)} %get-tuple-element.114.refs_0_), channel_id=1, source_target_pairs={{0,24},{4,28},{8,16},{12,20},{16,8},{20,12},{24,0},{28,4},{1,25},{... | collective-permute-start | bytes 344072 | tf_op jit(solution)/shard_map/ppermute | solution.py:757
  53.5 12.8 %collective-permute-start.11 = (bf16[448,128]{1,0:T(8,128)(2,1)S(1)}, bf16[448,128]{1,0:T(8,128)(2,1)S(1)}, u32[]{:S(2)}, u32[]{:S(2)}) collective-permute-start(bf16[448,128]{1,0:T(8,128)(2,1)S(1)} %get-tuple-element.114.refs_0_), channel_id=1, source_target_pairs={{0,16},{4,20},{8,24},{12,28},{16,0},{20,4},{24,8},{28,12},{1,17},{... | collective-permute-start | bytes 344072 | tf_op jit(solution)/shard_map/ppermute | solution.py:757
  53.7 12.7 %collective-permute-start.10 = (bf16[448,128]{1,0:T(8,128)(2,1)S(1)}, bf16[448,128]{1,0:T(8,128)(2,1)S(1)}, u32[]{:S(2)}, u32[]{:S(2)}) collective-permute-start(bf16[448,128]{1,0:T(8,128)(2,1)S(1)} %get-tuple-element.114.refs_0_), channel_id=1, source_target_pairs={{0,8},{4,12},{8,0},{12,4},{16,24},{20,28},{24,16},{28,20},{1,9},{5... | collective-permute-start | bytes 344072 | tf_op jit(solution)/shard_map/ppermute | solution.py:757
  56.2 10.1 %collective-permute-start.14 = (bf16[384,128]{1,0:T(8,128)(2,1)S(1)}, bf16[384,128]{1,0:T(8,128)(2,1)S(1)}, u32[]{:S(2)}, u32[]{:S(2)}) collective-permute-start(bf16[384,128]{1,0:T(8,128)(2,1)S(1)} %get-tuple-element.111.mine), channel_id=1, source_target_pairs={{0,12},{4,8},{8,4},{12,0},{16,28},{20,24},{24,20},{28,16},{1,13},{... | collective-permute-start | bytes 294920 | tf_op jit(solution)/shard_map/ppermute | solution.py:757
  56.7 9.6 %collective-permute-start.13 = (bf16[384,128]{1,0:T(8,128)(2,1)S(1)}, bf16[384,128]{1,0:T(8,128)(2,1)S(1)}, u32[]{:S(2)}, u32[]{:S(2)}) collective-permute-start(bf16[384,128]{1,0:T(8,128)(2,1)S(1)} %get-tuple-element.111.mine), channel_id=1, source_target_pairs={{0,4},{4,0},{8,12},{12,8},{16,20},{20,16},{24,28},{28,24},{1,5},{5... | collective-permute-start | bytes 294920 | tf_op jit(solution)/shard_map/ppermute | solution.py:757
  66.4 4.2 %collective-permute-start.16 = (bf16[8,256,512]{2,1,0:T(8,128)(2,1)S(1)}, bf16[8,256,512]{2,1,0:T(8,128)(2,1)S(1)}, u32[]{:S(2)}, u32[]{:S(2)}) collective-permute-start(bf16[8,256,512]{2,1,0:T(8,128)(2,1)S(1)} %get-tuple-element.118), channel_id=1, source_target_pairs={{0,1},{1,0},{2,3},{3,2},{4,5},{5,4},{6,7},{7,6},{8,9},{9,8},{10,11... | collective-permute-start | bytes 6291464 | tf_op jit(solution)/shard_map/ppermute | solution.py:752
  66.5 7.7 %collective-permute-start.15 = (bf16[832,128]{1,0:T(8,128)(2,1)S(1)}, bf16[832,128]{1,0:T(8,128)(2,1)S(1)}, u32[]{:S(2)}, u32[]{:S(2)}) collective-permute-start(bf16[832,128]{1,0:T(8,128)(2,1)S(1)} %shard_map.220.near), channel_id=1, source_target_pairs={{0,4},{4,0},{8,12},{12,8},{16,20},{20,16},{24,28},{28,24},{1,5},{5... | collective-permute-start | bytes 638984 | tf_op jit(solution)/shard_map/ppermute | solution.py:757
